TPU v7x, 32 devices: a whole 2x2x4 slice. The times are simulated.
32 devices in a mesh: dp: 8 (over z, core), blk: 4 (over y, x).
Axes of the slice: x: 2, y: 2, z: 4, core: 2. Of those that a mesh axis runs over, the one named last changes fastest.
Arguments:
- block_in: bfloat16 [8, 1024, 1024], P('dp', 'blk'), may hold values from -6 to 6
- memory: bfloat16 [8, 512, 1024], P('dp', 'blk'), may hold values from -6 to 6
- memory_len: int32 [8], P('dp'), may hold values from 64 to 512, as said below
- cross_mask: int32 [8, 512], P('dp'), may hold values 0 or 1
- buckets: int32 [1024], replicated, may hold values from 0 to 31, never falling along the last dimension, each value on 1 to 256 neighbouring positions
- bias_table: float32 [32, 16], replicated, may hold values from -5 to 5
- norm_self: float32 [1024], replicated, may hold values from 0.5 to 1.5
- w_query: bfloat16 [1024, 1024], replicated, may hold values from -0.1875 to 0.1875
- w_key: bfloat16 [1024, 512], replicated, may hold values from -0.1875 to 0.1875
- w_value: bfloat16 [1024, 512], replicated, may hold values from -0.1875 to 0.1875
- w_out: bfloat16 [1024, 1024], replicated, may hold values from -1.5 to 1.5
- norm_cross: float32 [1024], replicated, may hold values from 0.5 to 1.5
- cross_query: bfloat16 [1024, 1024], replicated, may hold values from -0.1875 to 0.1875
- cross_key: bfloat16 [1024, 512], replicated, may hold values from -0.1875 to 0.1875
- cross_value: bfloat16 [1024, 512], replicated, may hold values from -0.1875 to 0.1875
- cross_out: bfloat16 [1024, 1024], replicated, may hold values from -1.5 to 1.5
- norm_ffn: float32 [1024], replicated, may hold values from 0.5 to 1.5
- w_gate: bfloat16 [1024, 2816], replicated, may hold values from -0.1875 to 0.1875
- w_up: bfloat16 [1024, 2816], replicated, may hold values from -0.1875 to 0.1875
- w_down: bfloat16 [2816, 1024], replicated, may hold values from -0.109375 to 0.109375
- grad_out: bfloat16 [8, 1024, 1024], P('dp', 'blk'), may hold values from -6 to 6
Outputs:
- block_out: bfloat16 [8, 1024, 1024], P('dp', 'blk')
- d_block_in: float32 [8, 1024, 1024], P('dp', 'blk')
- d_memory: float32 [8, 512, 1024], P('dp', 'blk')
- d_bias_table: float32 [32, 16], replicated
- d_norm_self: float32 [1024], replicated
- d_w_query: float32 [1024, 1024], P(('dp', 'blk'))
- d_w_key: float32 [1024, 512], P(('dp', 'blk'))
- d_w_value: float32 [1024, 512], P(('dp', 'blk'))
- d_w_out: float32 [1024, 1024], P(('dp', 'blk'))
- d_norm_cross: float32 [1024], replicated
- d_cross_query: float32 [1024, 1024], P(('dp', 'blk'))
- d_cross_key: float32 [1024, 512], P(('dp', 'blk'))
- d_cross_value: float32 [1024, 512], P(('dp', 'blk'))
- d_cross_out: float32 [1024, 1024], P(('dp', 'blk'))
- d_norm_ffn: float32 [1024], replicated
- d_w_gate: float32 [1024, 2816], P(('dp', 'blk'))
- d_w_up: float32 [1024, 2816], P(('dp', 'blk'))
- d_w_down: float32 [2816, 1024], P(('dp', 'blk'))
Inputs may be any that keep to these rules, and one draw needn't show every extreme that they name: `memory_len`: one sequence in every draw has a memory of exactly 512 rows. `buckets`: the bucket never falls as the distance grows; each bucket covers 1 to 256 distances, one exactly 256.
All inputs are finite; a program needn't handle non-finite values. No bound on the sum of `cross_mask` on one device may be relied on, other than what follows from the above.
Results may differ from a plain program's by a relative error of at most 0.025.
Values may be sent and summed in bfloat16 or wider, within the bound.
No kernel may reach another device: no remote copies, remote signals or barrier semaphores. Data moves between devices by JAX's collectives and lax.ppermute only.
A program may use at most 256 MiB of HBM per device.

v0:
```python
import jax
import jax.numpy as jnp
from jax import lax
from jax.sharding import PartitionSpec as P

HEAD_DIM = 64


EPSILON = 1e-06
NEGATIVE = -1e30


def as_sent(x):
    return jax.tree.map(lambda a: a.astype(jnp.bfloat16) if a.dtype == jnp.float32 else a, x)


def from_behind(x, axis, by):
    length = lax.axis_size(axis)
    pairs = [(i, i + by) for i in range(length) if 0 <= i + by < length]
    return lax.ppermute(x, axis, pairs)


def from_behind_2(block, axis, distance):
    devices = range(lax.axis_size(axis))
    route = [((i - distance) % len(devices), i) for i in devices]
    return lax.ppermute(block, axis, route)


def rms_scale(stream, gain):
    inverse = lax.rsqrt(jnp.mean(stream * stream, axis=-1, keepdims=True) + EPSILON)
    return stream * inverse * gain


def gated_unit(gate, upward):
    return jax.nn.gelu(gate, approximate=True) * upward


def diagonal_sums(tile_set):
    span_len = tile_set.shape[-1]
    head_count = tile_set.shape[0]
    flipped = jnp.flip(tile_set, axis=-1)
    padded = jnp.pad(flipped, ((0, 0), (0, 0), (0, span_len)))
    skewed = padded.reshape(head_count, 2 * span_len * span_len)[:, : span_len * (2 * span_len - 1)]
    return jnp.sum(skewed.reshape(head_count, span_len, 2 * span_len - 1), axis=1)


def toeplitz_tile(window):
    head_count, width = window.shape
    span_len = width // 2
    flipped = jnp.flip(window, axis=-1)
    repeated = jnp.broadcast_to(flipped[:, None, :], (head_count, span_len + 1, width)).reshape(
        head_count, (span_len + 1) * width
    )
    skewed = repeated[:, : span_len * (width + 1)].reshape(head_count, span_len, width + 1)[
        :, :, :span_len
    ]
    return jnp.flip(skewed, axis=1)


def body(
    block_in,
    memory,
    memory_len,
    cross_mask,
    buckets,
    bias_table,
    norm_self,
    w_query,
    w_key,
    w_value,
    w_out,
    norm_cross,
    cross_query,
    cross_key,
    cross_value,
    cross_out,
    norm_ffn,
    w_gate,
    w_up,
    w_down,
    grad_out,
):
    seq_count, blk_len, model_width = block_in.shape
    row_count = seq_count * blk_len
    mem_rows = memory.shape[1]
    mem_total = cross_mask.shape[1]
    cycle_size = lax.axis_size("blk")
    my_block = lax.axis_index("blk")
    kv_width = w_key.shape[1]
    kv_heads = kv_width // HEAD_DIM
    groups = w_query.shape[1] // kv_width
    head_count = kv_heads * groups
    q_width = head_count * HEAD_DIM
    score_scale = HEAD_DIM ** (-0.5)
    bucket_count = bias_table.shape[0]
    seq_len = buckets.shape[0]
    stream = block_in.astype(jnp.float32).reshape(row_count, model_width)
    normed_self, self_back = jax.vjp(rms_scale, stream, norm_self)
    self_in = normed_self.astype(jnp.bfloat16)
    query_s = (
        jnp.dot(self_in, w_query, preferred_element_type=jnp.float32)
        .astype(jnp.bfloat16)
        .reshape(seq_count, blk_len, kv_heads, groups, HEAD_DIM)
    )
    key_s = (
        jnp.dot(self_in, w_key, preferred_element_type=jnp.float32)
        .astype(jnp.bfloat16)
        .reshape(seq_count, blk_len, kv_heads, HEAD_DIM)
    )
    value_s = (
        jnp.dot(self_in, w_value, preferred_element_type=jnp.float32)
        .astype(jnp.bfloat16)
        .reshape(seq_count, blk_len, kv_heads, HEAD_DIM)
    )
    bucket_hot = (buckets[:, None] == jnp.arange(bucket_count)[None, :]).astype(jnp.float32)
    dist_bias = jnp.dot(bucket_hot, bias_table, precision=lax.Precision.HIGHEST).T
    bias_pad = jnp.concatenate([jnp.zeros((head_count, blk_len), jnp.float32), dist_bias], axis=1)
    lane_ids = jnp.arange(blk_len)
    lane_diff = lane_ids[:, None] - lane_ids[None, :]

    def block_window(source):
        offset = (my_block - source) * blk_len
        return (offset, jnp.maximum(offset, 0))

    def block_scores(source_keys, source):
        offset, start_col = block_window(source)
        window = lax.dynamic_slice_in_dim(bias_pad, start_col, 2 * blk_len, 1)
        tile_bias = toeplitz_tile(window).reshape(kv_heads, groups, blk_len, blk_len)
        raw_scores = (
            jnp.einsum(
                "sqkgd,stkd->skgqt", query_s, source_keys, preferred_element_type=jnp.float32
            )
            * score_scale
            + tile_bias
        )
        return jnp.where(offset + lane_diff >= 0, raw_scores, NEGATIVE)

    def attend_block(online, kv_pair, source):
        run_max, run_sum, run_acc = online
        scores = block_scores(kv_pair[0], source)
        new_max = jnp.maximum(run_max, jnp.max(scores, axis=-1))
        rescale = jnp.exp(run_max - new_max)
        weights = jnp.exp(scores - new_max[..., None])
        new_sum = run_sum * rescale + jnp.sum(weights, axis=-1)
        mixed_block = jnp.einsum(
            "skgqt,stkd->sqkgd",
            weights.astype(jnp.bfloat16),
            kv_pair[1],
            preferred_element_type=jnp.float32,
        )
        new_acc = run_acc * jnp.transpose(rescale, (0, 3, 1, 2))[..., None] + mixed_block
        return (new_max, new_sum, new_acc)

    def forward_section(online, kv_pair, source):
        result = attend_block(online, kv_pair, source)
        return result

    own_pair = (key_s, value_s)
    stat_shape = (seq_count, kv_heads, groups, blk_len)
    online = (
        jnp.full(stat_shape, NEGATIVE, jnp.float32),
        jnp.zeros(stat_shape, jnp.float32),
        jnp.zeros((seq_count, blk_len, kv_heads, groups, HEAD_DIM), jnp.float32),
    )
    online = attend_block(online, own_pair, my_block)
    kept_pair = (
        jnp.zeros((cycle_size,) + key_s.shape, jnp.bfloat16).at[0].set(key_s),
        jnp.zeros((cycle_size,) + value_s.shape, jnp.bfloat16).at[0].set(value_s),
    )

    def forward_turn(turn_idx, loop_state):
        current, kv_pair, kv_stash = loop_state
        kv_pair = jax.tree.map(
            lambda part, own: part.astype(own.dtype),
            from_behind(as_sent(kv_pair), "blk", 1),
            kv_pair,
        )
        current = forward_section(current, kv_pair, (my_block - turn_idx) % cycle_size)
        kv_stash = (
            lax.dynamic_update_index_in_dim(kv_stash[0], kv_pair[0], turn_idx, 0),
            lax.dynamic_update_index_in_dim(kv_stash[1], kv_pair[1], turn_idx, 0),
        )
        return (current, kv_pair, kv_stash)

    online, unused_pair, kept_pair = lax.fori_loop(
        1, cycle_size, forward_turn, (online, own_pair, kept_pair)
    )
    run_max, run_sum, run_acc = online
    attention = run_acc / jnp.transpose(run_sum, (0, 3, 1, 2))[..., None]
    log_sum = run_max + jnp.log(run_sum)
    self_mix = attention.astype(jnp.bfloat16).reshape(row_count, q_width)
    after_self = stream + jnp.dot(self_mix, w_out, preferred_element_type=jnp.float32)
    normed_cross, cross_back = jax.vjp(rms_scale, after_self, norm_cross)
    cross_in = normed_cross.astype(jnp.bfloat16)
    cross_q = (
        jnp.dot(cross_in, cross_query, preferred_element_type=jnp.float32)
        .astype(jnp.bfloat16)
        .reshape(seq_count, blk_len, kv_heads, groups, HEAD_DIM)
    )
    mem_flat = memory.reshape(seq_count * mem_rows, model_width)
    key_part = (
        jnp.dot(mem_flat, cross_key, preferred_element_type=jnp.float32)
        .astype(jnp.bfloat16)
        .reshape(seq_count, mem_rows, kv_width)
    )
    value_part = (
        jnp.dot(mem_flat, cross_value, preferred_element_type=jnp.float32)
        .astype(jnp.bfloat16)
        .reshape(seq_count, mem_rows, kv_width)
    )
    mem_keys, mem_values = (
        lax.all_gather(key_part, "blk", axis=1, tiled=True),
        lax.all_gather(value_part, "blk", axis=1, tiled=True),
    )
    mem_keys = mem_keys.reshape(seq_count, mem_total, kv_heads, HEAD_DIM)
    mem_values = mem_values.reshape(seq_count, mem_total, kv_heads, HEAD_DIM)
    mem_places = jnp.arange(mem_total)
    allowed = (mem_places[None, :] == 0) | (mem_places[None, :] < memory_len[:, None]) & (
        cross_mask == 1
    )
    cross_scores = (
        jnp.einsum("sqkgd,smkd->skgqm", cross_q, mem_keys, preferred_element_type=jnp.float32)
        * score_scale
    )
    cross_scores = jnp.where(allowed[:, None, None, None, :], cross_scores, NEGATIVE)
    cross_raise = jnp.exp(cross_scores - jnp.max(cross_scores, axis=-1, keepdims=True))
    cross_prob = cross_raise / jnp.sum(cross_raise, axis=-1, keepdims=True)
    cross_low = cross_prob.astype(jnp.bfloat16)
    cross_mix = (
        jnp.einsum("skgqm,smkd->sqkgd", cross_low, mem_values, preferred_element_type=jnp.float32)
        .astype(jnp.bfloat16)
        .reshape(row_count, q_width)
    )
    after_cross = after_self + jnp.dot(cross_mix, cross_out, preferred_element_type=jnp.float32)
    normed_ffn, ffn_back = jax.vjp(rms_scale, after_cross, norm_ffn)
    ffn_in = normed_ffn.astype(jnp.bfloat16)
    gate_pre = jnp.dot(ffn_in, w_gate, preferred_element_type=jnp.float32)
    up_pre = jnp.dot(ffn_in, w_up, preferred_element_type=jnp.float32)
    hidden_full, gated_back = jax.vjp(gated_unit, gate_pre, up_pre)
    hidden = hidden_full.astype(jnp.bfloat16)
    block_out = (
        (after_cross + jnp.dot(hidden, w_down, preferred_element_type=jnp.float32))
        .astype(jnp.bfloat16)
        .reshape(seq_count, blk_len, model_width)
    )
    grad_top = grad_out.astype(jnp.float32).reshape(row_count, model_width)
    ffn_grad = grad_top.astype(jnp.bfloat16)
    dw_down = jnp.dot(hidden.T, ffn_grad, preferred_element_type=jnp.float32)
    d_hidden = jnp.dot(ffn_grad, w_down.T, preferred_element_type=jnp.float32)
    gate_full, up_full = gated_back(d_hidden)
    gate_grad = gate_full.astype(jnp.bfloat16)
    up_grad = up_full.astype(jnp.bfloat16)
    dw_gate = jnp.dot(ffn_in.T, gate_grad, preferred_element_type=jnp.float32)
    dw_up = jnp.dot(ffn_in.T, up_grad, preferred_element_type=jnp.float32)
    d_ffn_norm = jnp.dot(gate_grad, w_gate.T, preferred_element_type=jnp.float32) + jnp.dot(
        up_grad, w_up.T, preferred_element_type=jnp.float32
    )
    d_stream_ffn, d_gain_ffn = ffn_back(d_ffn_norm)
    grad_cross = grad_top + d_stream_ffn
    ffn_sums = (dw_gate, dw_up, dw_down)
    cross_grad = grad_cross.astype(jnp.bfloat16)
    dw_cout = jnp.dot(cross_mix.T, cross_grad, preferred_element_type=jnp.float32)
    mix_grad = (
        jnp.dot(cross_grad, cross_out.T, preferred_element_type=jnp.float32)
        .astype(jnp.bfloat16)
        .reshape(seq_count, blk_len, kv_heads, groups, HEAD_DIM)
    )
    prob_grad = jnp.einsum(
        "sqkgd,smkd->skgqm", mix_grad, mem_values, preferred_element_type=jnp.float32
    )
    cross_score_grad = (
        cross_prob * (prob_grad - jnp.sum(cross_prob * prob_grad, axis=-1, keepdims=True))
    ).astype(jnp.bfloat16)
    cq_grad = (
        (
            jnp.einsum(
                "skgqm,smkd->sqkgd", cross_score_grad, mem_keys, preferred_element_type=jnp.float32
            )
            * score_scale
        )
        .astype(jnp.bfloat16)
        .reshape(row_count, q_width)
    )
    key_term = (
        jnp.einsum(
            "skgqm,sqkgd->smkd", cross_score_grad, cross_q, preferred_element_type=jnp.float32
        )
        * score_scale
    )
    value_term = jnp.einsum(
        "skgqm,sqkgd->smkd", cross_low, mix_grad, preferred_element_type=jnp.float32
    )
    mem_key_grad, mem_value_grad = (
        lax.psum_scatter(
            key_term.reshape(seq_count, mem_total, kv_width).astype(jnp.bfloat16),
            "blk",
            scatter_dimension=1,
            tiled=True,
        ).astype(jnp.float32),
        lax.psum_scatter(
            value_term.reshape(seq_count, mem_total, kv_width).astype(jnp.bfloat16),
            "blk",
            scatter_dimension=1,
            tiled=True,
        ).astype(jnp.float32),
    )
    mem_key_grad = mem_key_grad.astype(jnp.bfloat16).reshape(seq_count * mem_rows, kv_width)
    mem_value_grad = mem_value_grad.astype(jnp.bfloat16).reshape(seq_count * mem_rows, kv_width)
    d_memory = (
        jnp.dot(mem_key_grad, cross_key.T, preferred_element_type=jnp.float32)
        + jnp.dot(mem_value_grad, cross_value.T, preferred_element_type=jnp.float32)
    ).reshape(seq_count, mem_rows, model_width)
    dw_ckey = jnp.dot(mem_flat.T, mem_key_grad, preferred_element_type=jnp.float32)
    dw_cvalue = jnp.dot(mem_flat.T, mem_value_grad, preferred_element_type=jnp.float32)
    dw_cquery = jnp.dot(cross_in.T, cq_grad, preferred_element_type=jnp.float32)
    d_stream_cross, d_gain_cross = cross_back(
        jnp.dot(cq_grad, cross_query.T, preferred_element_type=jnp.float32)
    )
    grad_self = grad_cross + d_stream_cross
    cross_sums = (dw_cquery, dw_ckey, dw_cvalue, dw_cout)
    self_grad = grad_self.astype(jnp.bfloat16)
    dw_out = jnp.dot(self_mix.T, self_grad, preferred_element_type=jnp.float32)
    attn_grad = (
        jnp.dot(self_grad, w_out.T, preferred_element_type=jnp.float32)
        .astype(jnp.bfloat16)
        .reshape(seq_count, blk_len, kv_heads, groups, HEAD_DIM)
    )
    row_delta = jnp.transpose(
        jnp.sum(attn_grad.astype(jnp.float32) * attention, axis=-1), (0, 2, 3, 1)
    )

    def back_block(current, kv_pair, source):
        grads_q, acc_pair, bias_grad = current
        key_blk, value_blk = kv_pair
        scores = block_scores(key_blk, source)
        probs = jnp.exp(scores - log_sum[..., None])
        prob_block = jnp.einsum(
            "sqkgd,stkd->skgqt", attn_grad, value_blk, preferred_element_type=jnp.float32
        )
        score_grad = (probs * (prob_block - row_delta[..., None])).astype(jnp.bfloat16)
        grads_q = grads_q + jnp.einsum(
            "skgqt,stkd->sqkgd", score_grad, key_blk, preferred_element_type=jnp.float32
        )
        key_acc = (
            acc_pair[0]
            + jnp.einsum(
                "skgqt,sqkgd->stkd", score_grad, query_s, preferred_element_type=jnp.float32
            )
            * score_scale
        )
        value_acc = acc_pair[1] + jnp.einsum(
            "skgqt,sqkgd->stkd",
            probs.astype(jnp.bfloat16),
            attn_grad,
            preferred_element_type=jnp.float32,
        )
        offset, start_col = block_window(source)
        head_tiles = jnp.sum(score_grad, axis=0, dtype=jnp.float32).reshape(
            head_count, blk_len, blk_len
        )
        window_grad = jnp.pad(diagonal_sums(head_tiles), ((0, 0), (1, 0)))
        updated = lax.dynamic_slice_in_dim(bias_grad, start_col, 2 * blk_len, 1) + window_grad
        bias_grad = lax.dynamic_update_slice_in_dim(bias_grad, updated, start_col, 1)
        return (grads_q, (key_acc, value_acc), bias_grad)

    def back_section(current, kv_pair, source):
        grads_q, acc_pair, bias_grad = back_block(current, kv_pair, source)
        acc_pair = from_behind_2((as_sent(acc_pair[0]), as_sent(acc_pair[1])), "blk", 1)
        return (grads_q, acc_pair, bias_grad)

    zero_keys = jnp.zeros((seq_count, blk_len, kv_heads, HEAD_DIM), jnp.float32)
    back_state = (
        jnp.zeros((seq_count, blk_len, kv_heads, groups, HEAD_DIM), jnp.float32),
        (zero_keys, zero_keys),
        jnp.zeros((head_count, seq_len + blk_len), jnp.float32),
    )
    back_state = back_section(back_state, own_pair, my_block)

    def backward_turn(turn_idx, loop_state):
        current, kv_pair = loop_state
        kv_pair = (
            lax.dynamic_index_in_dim(kept_pair[0], turn_idx, 0, keepdims=False),
            lax.dynamic_index_in_dim(kept_pair[1], turn_idx, 0, keepdims=False),
        )
        current = back_section(current, kv_pair, (my_block - turn_idx) % cycle_size)
        return (current, kv_pair)

    back_state, unused_back = lax.fori_loop(1, cycle_size, backward_turn, (back_state, own_pair))
    grads_q, (key_total, value_total), bias_grad = back_state
    query_grad = (grads_q * score_scale).astype(jnp.bfloat16).reshape(row_count, q_width)
    key_grad = key_total.astype(jnp.bfloat16).reshape(row_count, kv_width)
    value_grad = value_total.astype(jnp.bfloat16).reshape(row_count, kv_width)
    dw_query = jnp.dot(self_in.T, query_grad, preferred_element_type=jnp.float32)
    dw_key = jnp.dot(self_in.T, key_grad, preferred_element_type=jnp.float32)
    dw_value = jnp.dot(self_in.T, value_grad, preferred_element_type=jnp.float32)
    d_self_norm = (
        jnp.dot(query_grad, w_query.T, preferred_element_type=jnp.float32)
        + jnp.dot(key_grad, w_key.T, preferred_element_type=jnp.float32)
        + jnp.dot(value_grad, w_value.T, preferred_element_type=jnp.float32)
    )
    d_stream_self, d_gain_self = self_back(d_self_norm)
    d_block_in = (grad_self + d_stream_self).reshape(seq_count, blk_len, model_width)
    d_table = jnp.dot(bucket_hot.T, bias_grad[:, blk_len:].T, precision=lax.Precision.HIGHEST)
    weight_sums = (
        lax.psum_scatter(dw_query, ("dp", "blk"), scatter_dimension=0, tiled=True),
        lax.psum_scatter(dw_key, ("dp", "blk"), scatter_dimension=0, tiled=True),
        lax.psum_scatter(dw_value, ("dp", "blk"), scatter_dimension=0, tiled=True),
        lax.psum_scatter(dw_out, ("dp", "blk"), scatter_dimension=0, tiled=True),
        lax.psum_scatter(cross_sums[0], ("dp", "blk"), scatter_dimension=0, tiled=True),
        lax.psum_scatter(cross_sums[1], ("dp", "blk"), scatter_dimension=0, tiled=True),
        lax.psum_scatter(cross_sums[2], ("dp", "blk"), scatter_dimension=0, tiled=True),
        lax.psum_scatter(cross_sums[3], ("dp", "blk"), scatter_dimension=0, tiled=True),
        lax.psum_scatter(ffn_sums[0], ("dp", "blk"), scatter_dimension=0, tiled=True),
        lax.psum_scatter(ffn_sums[1], ("dp", "blk"), scatter_dimension=0, tiled=True),
        lax.psum_scatter(ffn_sums[2], ("dp", "blk"), scatter_dimension=0, tiled=True),
    )
    gain_self, gain_cross, gain_ffn, table_sum = lax.psum(
        (d_gain_self, d_gain_cross, d_gain_ffn, d_table), ("dp", "blk")
    )
    return (
        block_out,
        d_block_in,
        d_memory,
        table_sum,
        gain_self,
        weight_sums[0],
        weight_sums[1],
        weight_sums[2],
        weight_sums[3],
        gain_cross,
        weight_sums[4],
        weight_sums[5],
        weight_sums[6],
        weight_sums[7],
        gain_ffn,
        weight_sums[8],
        weight_sums[9],
        weight_sums[10],
    )


def solution(mesh):
    return jax.shard_map(
        body,
        mesh=mesh,
        in_specs=(
            P("dp", "blk", None),
            P("dp", "blk", None),
            P("dp"),
            P("dp", None),
            P(),
            P(),
            P(),
            P(),
            P(),
            P(),
            P(),
            P(),
            P(),
            P(),
            P(),
            P(),
            P(),
            P(),
            P(),
            P(),
            P("dp", "blk", None),
        ),
        out_specs=(
            P("dp", "blk", None),
            P("dp", "blk", None),
            P("dp", "blk", None),
            P(),
            P(),
            P(("dp", "blk"), None),
            P(("dp", "blk"), None),
            P(("dp", "blk"), None),
            P(("dp", "blk"), None),
            P(),
            P(("dp", "blk"), None),
            P(("dp", "blk"), None),
            P(("dp", "blk"), None),
            P(("dp", "blk"), None),
            P(),
            P(("dp", "blk"), None),
            P(("dp", "blk"), None),
            P(("dp", "blk"), None),
        ),
        check_vma=False,
    )
```

profile of v0, /device:TPU:0, one launch (start us, length us, event | category | flops | bytes accessed | tf_op | source)
XLA Modules:
  0.0 2930.4 jit_solution(1475816447943404940)
XLA Ops:
  67.2 18.4 reshape.932
  90.3 32.5 %rev.80 = f32[16,256,256]{2,1,0:T(8,128)} reverse(f32[16,256,256]{2,1,0:T(8,128)} %slice.152), dimensions={1} | reverse | bytes 8388608 | tf_op jit(solution)/shard_map/jit(_flip)/rev | solution.py:57
  133.7 254.2 %while.56 = (s32[]{:T(128)}, f32[1,8,2,256]{3,2,1,0:T(2,128)S(1)}, f32[1,8,2,256]{3,2,1,0:T(2,128)S(1)}, f32[1,256,8,2,64]{1,4,3,2,0:T(8,128)}, bf16[1,256,8,64]...) while((s32[]{:T(128)}, f32[1,8,2,256]{3,2,1,0:T(2,128)S(1)}, ...), condition=%wide.region_6.7_spmd.clone, body=%wide.region_3.6_spmd.clone.sunk | while | flops 277557248 | bytes 117113328 | solution.py:185
  149.9 18.4 reshape.1027
  173.0 32.5 %rev.93 = f32[16,256,256]{2,1,0:T(8,128)} reverse(f32[16,256,256]{2,1,0:T(8,128)} %slice.162), dimensions={1} | reverse | bytes 8388608 | tf_op jit(solution)/shard_map/while/body/eval_jaxpr/jit(_flip)/rev | solution.py:57
  234.7 18.4 reshape.1027
  257.8 32.5 %rev.93 = f32[16,256,256]{2,1,0:T(8,128)} reverse(f32[16,256,256]{2,1,0:T(8,128)} %slice.162), dimensions={1} | reverse | bytes 8388608 | tf_op jit(solution)/shard_map/while/body/eval_jaxpr/jit(_flip)/rev | solution.py:57
  318.1 18.4 reshape.1027
  341.2 32.5 %rev.93 = f32[16,256,256]{2,1,0:T(8,128)} reverse(f32[16,256,256]{2,1,0:T(8,128)} %slice.162), dimensions={1} | reverse | bytes 8388608 | tf_op jit(solution)/shard_map/while/body/eval_jaxpr/jit(_flip)/rev | solution.py:57
  491.6 34.3 %rev.81 = f32[16,256,256]{2,1,0:T(8,128)} reverse(f32[16,256,256]{2,1,0:T(8,128)} %copy.138), dimensions={2} | reverse | bytes 8388608 | tf_op jit(solution)/shard_map/jit(_flip)/rev | solution.py:41
  556.3 498.9 %while.57 = (s32[]{:T(128)}, f32[1,256,8,2,64]{1,4,3,2,0:T(8,128)}, bf16[1,256,8,64]{1,3,2,0:T(8,128)(2,1)}, bf16[1,256,8,64]{1,3,2,0:T(8,128)(2,1)S(1)}, f32[16...) while((s32[]{:T(128)}, f32[1,256,8,2,64]{1,4,3,2,0:T(8,128)}, ...), condition=%wide.region_18.19_spmd.clone, body=%wide.region_16.18_spmd.clone.sunk | while | flops 683995136 | bytes 210059600 | solution.py:388
  584.1 18.4 reshape.1028
  607.1 32.5 %rev.95 = f32[16,256,256]{2,1,0:T(8,128)} reverse(f32[16,256,256]{2,1,0:T(8,128)} %slice.164), dimensions={1} | reverse | bytes 8388608 | tf_op jit(solution)/shard_map/while/body/eval_jaxpr/jit(_flip)/rev | solution.py:57
  668.4 34.2 %rev.96 = f32[16,256,256]{2,1,0:T(8,128)} reverse(f32[16,256,256]{2,1,0:T(8,128)} %copy.198), dimensions={2} | reverse | bytes 8388608 | tf_op jit(solution)/shard_map/while/body/eval_jaxpr/jit(_flip)/rev | solution.py:41
  746.0 18.4 reshape.1028
  769.1 32.5 %rev.95 = f32[16,256,256]{2,1,0:T(8,128)} reverse(f32[16,256,256]{2,1,0:T(8,128)} %slice.164), dimensions={1} | reverse | bytes 8388608 | tf_op jit(solution)/shard_map/while/body/eval_jaxpr/jit(_flip)/rev | solution.py:57
  825.3 34.2 %rev.96 = f32[16,256,256]{2,1,0:T(8,128)} reverse(f32[16,256,256]{2,1,0:T(8,128)} %copy.198), dimensions={2} | reverse | bytes 8388608 | tf_op jit(solution)/shard_map/while/body/eval_jaxpr/jit(_flip)/rev | solution.py:41
  902.9 18.4 reshape.1028
  926.0 32.5 %rev.95 = f32[16,256,256]{2,1,0:T(8,128)} reverse(f32[16,256,256]{2,1,0:T(8,128)} %slice.164), dimensions={1} | reverse | bytes 8388608 | tf_op jit(solution)/shard_map/while/body/eval_jaxpr/jit(_flip)/rev | solution.py:57
  987.2 34.2 %rev.96 = f32[16,256,256]{2,1,0:T(8,128)} reverse(f32[16,256,256]{2,1,0:T(8,128)} %copy.198), dimensions={2} | reverse | bytes 8388608 | tf_op jit(solution)/shard_map/while/body/eval_jaxpr/jit(_flip)/rev | solution.py:41
  1116.7 40.3 %all-reduce.8 = (f32[32,16]{0,1:T(8,128)}, f32[1024]{0:T(1024)}, f32[1024]{0:T(1024)}, f32[1024]{0:T(1024)}) all-reduce(f32[32,16]{0,1:T(8,128)S(1)} %copy-done.68, f32[1024]{0:T(1024)S(1)} %get-tuple-element.999, f32[1024]{0:T(1024)S(1)} %copy-done.65, f32[1024]{0:T(1024)S(1)} %copy-done.69), channel_id=1, replica_groups=mesh['dp'=8,'blk'=4] {'dp','blk'}, use_global_device_ids=true, to_apply=%region_22.23 | all-reduce | flops 3584 | bytes 28672 | tf_op jit(solution)/shard_map/psum | solution.py:417
  1161.8 32.7 %reduce-scatter.26.cloned.1.call-done = f32[32,512]{1,0:T(8,128)} async-done(((f32[1024,512]{1,0:T(8,128)}), f32[32,512]{1,0:T(8,128)}) %reduce-scatter.26.cloned.1.call-update) | async-done | bytes 65552 | tf_op jit(solution)/shard_map/reduce_scatter | solution.py:407
  1194.5 135.6 %reduce-scatter.24.cloned.1.call-done = f32[32,512]{1,0:T(8,128)} async-done(((f32[1024,512]{1,0:T(8,128)}), f32[32,512]{1,0:T(8,128)}) %reduce-scatter.24.cloned.1.call-update) | async-done | bytes 65552 | tf_op jit(solution)/shard_map/reduce_scatter | solution.py:406
  1330.1 135.7 %reduce-scatter.46.cloned.1.call-done = f32[32,512]{1,0:T(8,128)} async-done(((f32[1024,512]{1,0:T(8,128)}), f32[32,512]{1,0:T(8,128)}) %reduce-scatter.46.cloned.1.call-update) | async-done | bytes 65552
  1465.8 135.6 %reduce-scatter.44.cloned.1.call-done = f32[32,512]{1,0:T(8,128)} async-done(((f32[1024,512]{1,0:T(8,128)}), f32[32,512]{1,0:T(8,128)}) %reduce-scatter.44.cloned.1.call-update) | async-done | bytes 65552
  1601.5 140.4 %reduce-scatter.32.cloned.1.call-done = f32[32,1024]{1,0:T(8,128)} async-done(((f32[1024,1024]{1,0:T(8,128)}), f32[32,1024]{1,0:T(8,128)}) %reduce-scatter.32.cloned.1.call-update) | async-done | bytes 131088 | tf_op jit(solution)/shard_map/reduce_scatter | solution.py:412
  1741.9 142.2 %reduce-scatter.30.cloned.1.call-done = f32[32,1024]{1,0:T(8,128)} async-done(((f32[1024,1024]{1,0:T(8,128)}), f32[32,1024]{1,0:T(8,128)}) %reduce-scatter.30.cloned.1.call-update) | async-done | bytes 131088 | tf_op jit(solution)/shard_map/reduce_scatter | solution.py:409
  1884.1 142.7 %reduce-scatter.28.cloned.1.call-done = f32[32,1024]{1,0:T(8,128)} async-done(((f32[1024,1024]{1,0:T(8,128)}), f32[32,1024]{1,0:T(8,128)}) %reduce-scatter.28.cloned.1.call-update) | async-done | bytes 131088 | tf_op jit(solution)/shard_map/reduce_scatter | solution.py:408
  2026.8 141.9 %reduce-scatter.22.cloned.1.call-done = f32[32,1024]{1,0:T(8,128)} async-done(((f32[1024,1024]{1,0:T(8,128)}), f32[32,1024]{1,0:T(8,128)}) %reduce-scatter.22.cloned.1.call-update) | async-done | bytes 131088 | tf_op jit(solution)/shard_map/reduce_scatter | solution.py:405
  2168.6 249.4 %reduce-scatter.36.cloned.1.call-done = f32[32,2816]{1,0:T(8,128)} async-done(((f32[1024,2816]{1,0:T(8,128)}), f32[32,2816]{1,0:T(8,128)}) %reduce-scatter.36.cloned.1.call-update) | async-done | bytes 360464 | tf_op jit(solution)/shard_map/reduce_scatter | solution.py:414
  2418.1 252.7 %reduce-scatter.34.cloned.1.call-done = f32[32,2816]{1,0:T(8,128)} async-done(((f32[1024,2816]{1,0:T(8,128)}), f32[32,2816]{1,0:T(8,128)}) %reduce-scatter.34.cloned.1.call-update) | async-done | bytes 360464 | tf_op jit(solution)/shard_map/reduce_scatter | solution.py:413
  2670.7 253.0 %reduce-scatter.38.cloned.1.call-done = f32[88,1024]{1,0:T(8,128)} async-done(((f32[2816,1024]{1,0:T(8,128)}), f32[88,1024]{1,0:T(8,128)}) %reduce-scatter.38.cloned.1.call-update) | async-done | bytes 360464 | tf_op jit(solution)/shard_map/reduce_scatter | solution.py:415
  (447 shorter events, 599.6 us)
Async XLA Ops:
  7.2 386.5 %copy-start = (bf16[1024,1024]{1,0:T(8,128)(2,1)S(1)}, bf16[1024,1024]{1,0:T(8,128)(2,1)}, u32[]{:S(2)}) copy-start(bf16[1024,1024]{1,0:T(8,128)(2,1)} %param.41) | copy-start | bytes 6291460
  7.2 1053.6 %reduce-scatter.42.cloned.1.call-start = ((), (), s32[]{:S(2)}) async-start(), calls=%async_computation.23 | async-start | bytes 655360
  17.9 114.1 %copy-start.29 = (bf16[256,512]{0,1:T(8,128)(2,1)}, bf16[256,512]{0,1:T(8,128)(2,1)S(1)}, u32[]{:S(2)}) copy-start(bf16[256,512]{0,1:T(8,128)(2,1)S(1)} %copy.120) | copy-start | bytes 786436
  22.1 106.0 %copy-start.31 = (bf16[256,512]{0,1:T(8,128)(2,1)}, bf16[256,512]{0,1:T(8,128)(2,1)S(1)}, u32[]{:S(2)}) copy-start(bf16[256,512]{0,1:T(8,128)(2,1)S(1)} %copy.117) | copy-start | bytes 786436
  133.9 77.1 %collective-permute-start = (bf16[1,256,8,64]{1,3,2,0:T(8,128)(2,1)}, bf16[1,256,8,64]{1,3,2,0:T(8,128)(2,1)S(1)}, u32[]{:S(2)}, u32[]{:S(2)}) collective-permute-start(bf16[1,256,8,64]{1,3,2,0:T(8,128)(2,1)} %get-tuple-element.1252), channel_id=1, source_target_pairs={{0,1},{1,2},{2,3},{4,5},{5,6},{6,7},{8,9},{9,10},{10,11},{12,13},{... | collective-permute-start | bytes 786440 | tf_op jit(solution)/shard_map/while/body/eval_jaxpr/ppermute | solution.py:20
  136.5 78.9 %collective-permute-start.1 = (bf16[1,256,8,64]{1,3,2,0:T(8,128)(2,1)}, bf16[1,256,8,64]{1,3,2,0:T(8,128)(2,1)S(1)}, u32[]{:S(2)}, u32[]{:S(2)}) collective-permute-start(bf16[1,256,8,64]{1,3,2,0:T(8,128)(2,1)} %get-tuple-element.1253), channel_id=1, source_target_pairs={{0,1},{1,2},{2,3},{4,5},{5,6},{6,7},{8,9},{9,10},{10,11},{12,13},{... | collective-permute-start | bytes 786440 | tf_op jit(solution)/shard_map/while/body/eval_jaxpr/ppermute | solution.py:20
  219.5 76.2 %collective-permute-start = (bf16[1,256,8,64]{1,3,2,0:T(8,128)(2,1)}, bf16[1,256,8,64]{1,3,2,0:T(8,128)(2,1)S(1)}, u32[]{:S(2)}, u32[]{:S(2)}) collective-permute-start(bf16[1,256,8,64]{1,3,2,0:T(8,128)(2,1)} %get-tuple-element.1252), channel_id=1, source_target_pairs={{0,1},{1,2},{2,3},{4,5},{5,6},{6,7},{8,9},{9,10},{10,11},{12,13},{... | collective-permute-start | bytes 786440 | tf_op jit(solution)/shard_map/while/body/eval_jaxpr/ppermute | solution.py:20
  222.8 77.5 %collective-permute-start.1 = (bf16[1,256,8,64]{1,3,2,0:T(8,128)(2,1)}, bf16[1,256,8,64]{1,3,2,0:T(8,128)(2,1)S(1)}, u32[]{:S(2)}, u32[]{:S(2)}) collective-permute-start(bf16[1,256,8,64]{1,3,2,0:T(8,128)(2,1)} %get-tuple-element.1253), channel_id=1, source_target_pairs={{0,1},{1,2},{2,3},{4,5},{5,6},{6,7},{8,9},{9,10},{10,11},{12,13},{... | collective-permute-start | bytes 786440 | tf_op jit(solution)/shard_map/while/body/eval_jaxpr/ppermute | solution.py:20
  304.3 74.9 %collective-permute-start = (bf16[1,256,8,64]{1,3,2,0:T(8,128)(2,1)}, bf16[1,256,8,64]{1,3,2,0:T(8,128)(2,1)S(1)}, u32[]{:S(2)}, u32[]{:S(2)}) collective-permute-start(bf16[1,256,8,64]{1,3,2,0:T(8,128)(2,1)} %get-tuple-element.1252), channel_id=1, source_target_pairs={{0,1},{1,2},{2,3},{4,5},{5,6},{6,7},{8,9},{9,10},{10,11},{12,13},{... | collective-permute-start | bytes 786440 | tf_op jit(solution)/shard_map/while/body/eval_jaxpr/ppermute | solution.py:20
  306.2 77.5 %collective-permute-start.1 = (bf16[1,256,8,64]{1,3,2,0:T(8,128)(2,1)}, bf16[1,256,8,64]{1,3,2,0:T(8,128)(2,1)S(1)}, u32[]{:S(2)}, u32[]{:S(2)}) collective-permute-start(bf16[1,256,8,64]{1,3,2,0:T(8,128)(2,1)} %get-tuple-element.1253), channel_id=1, source_target_pairs={{0,1},{1,2},{2,3},{4,5},{5,6},{6,7},{8,9},{9,10},{10,11},{12,13},{... | collective-permute-start | bytes 786440 | tf_op jit(solution)/shard_map/while/body/eval_jaxpr/ppermute | solution.py:20
  445.5 618.9 %reduce-scatter.40.cloned.1.call-start = ((), (), s32[]{:S(2)}) async-start(), calls=%async_computation.22 | async-start | bytes 655360
  472.8 83.5 %collective-permute-start.4 = (bf16[1,256,8,64]{1,3,2,0:T(8,128)(2,1)}, bf16[1,256,8,64]{1,3,2,0:T(8,128)(2,1)}, u32[]{:S(2)}, u32[]{:S(2)}) collective-permute-start(bf16[1,256,8,64]{1,3,2,0:T(8,128)(2,1)} %fusion.160), channel_id=1, source_target_pairs={{3,0},{0,1},{1,2},{2,3},{7,4},{4,5},{5,6},{6,7},{11,8},{8,9},{9,10... | collective-permute-start | bytes 786440 | tf_op jit(solution)/shard_map/ppermute | solution.py:26
  475.4 80.9 %collective-permute-start.5 = (bf16[1,256,8,64]{1,3,2,0:T(8,128)(2,1)}, bf16[1,256,8,64]{1,3,2,0:T(8,128)(2,1)S(1)}, u32[]{:S(2)}, u32[]{:S(2)}) collective-permute-start(bf16[1,256,8,64]{1,3,2,0:T(8,128)(2,1)} %fusion.163), channel_id=1, source_target_pairs={{3,0},{0,1},{1,2},{2,3},{7,4},{4,5},{5,6},{6,7},{11,8},{8,9},{9,10... | collective-permute-start | bytes 786440 | tf_op jit(solution)/shard_map/ppermute | solution.py:26
  483.3 711.2 %reduce-scatter.26.cloned.1.call-start = ((), (), s32[]{:S(2)}) async-start(), calls=%async_computation.15 | async-start | bytes 2162688 | tf_op jit(solution)/shard_map/reduce_scatter | solution.py:407
  556.3 498.9 %copy-start.16 = (bf16[1,256,1024]{2,1,0:T(8,128)(2,1)S(1)}, bf16[1,256,1024]{2,1,0:T(8,128)(2,1)}, u32[]{:S(2)}) copy-start(bf16[1,256,1024]{2,1,0:T(8,128)(2,1)} %param.29) | copy-start | bytes 1572868
  652.9 83.0 %collective-permute-start.2 = (bf16[1,256,8,64]{1,3,2,0:T(8,128)(2,1)}, bf16[1,256,8,64]{1,3,2,0:T(8,128)(2,1)}, u32[]{:S(2)}, u32[]{:S(2)}) collective-permute-start(bf16[1,256,8,64]{1,3,2,0:T(8,128)(2,1)} %fusion.333), channel_id=1, source_target_pairs={{3,0},{0,1},{1,2},{2,3},{7,4},{4,5},{5,6},{6,7},{11,8},{8,9},{9,10... | collective-permute-start | bytes 786440 | tf_op jit(solution)/shard_map/while/body/eval_jaxpr/ppermute | solution.py:26
  655.5 80.5 %collective-permute-start.3 = (bf16[1,256,8,64]{1,3,2,0:T(8,128)(2,1)}, bf16[1,256,8,64]{1,3,2,0:T(8,128)(2,1)S(1)}, u32[]{:S(2)}, u32[]{:S(2)}) collective-permute-start(bf16[1,256,8,64]{1,3,2,0:T(8,128)(2,1)} %fusion.334), channel_id=1, source_target_pairs={{3,0},{0,1},{1,2},{2,3},{7,4},{4,5},{5,6},{6,7},{11,8},{8,9},{9,10... | collective-permute-start | bytes 786440 | tf_op jit(solution)/shard_map/while/body/eval_jaxpr/ppermute | solution.py:26
  814.8 78.1 %collective-permute-start.2 = (bf16[1,256,8,64]{1,3,2,0:T(8,128)(2,1)}, bf16[1,256,8,64]{1,3,2,0:T(8,128)(2,1)}, u32[]{:S(2)}, u32[]{:S(2)}) collective-permute-start(bf16[1,256,8,64]{1,3,2,0:T(8,128)(2,1)} %fusion.333), channel_id=1, source_target_pairs={{3,0},{0,1},{1,2},{2,3},{7,4},{4,5},{5,6},{6,7},{11,8},{8,9},{9,10... | collective-permute-start | bytes 786440 | tf_op jit(solution)/shard_map/while/body/eval_jaxpr/ppermute | solution.py:26
  817.4 75.6 %collective-permute-start.3 = (bf16[1,256,8,64]{1,3,2,0:T(8,128)(2,1)}, bf16[1,256,8,64]{1,3,2,0:T(8,128)(2,1)S(1)}, u32[]{:S(2)}, u32[]{:S(2)}) collective-permute-start(bf16[1,256,8,64]{1,3,2,0:T(8,128)(2,1)} %fusion.334), channel_id=1, source_target_pairs={{3,0},{0,1},{1,2},{2,3},{7,4},{4,5},{5,6},{6,7},{11,8},{8,9},{9,10... | collective-permute-start | bytes 786440 | tf_op jit(solution)/shard_map/while/body/eval_jaxpr/ppermute | solution.py:26
  971.8 83.0 %collective-permute-start.2 = (bf16[1,256,8,64]{1,3,2,0:T(8,128)(2,1)}, bf16[1,256,8,64]{1,3,2,0:T(8,128)(2,1)}, u32[]{:S(2)}, u32[]{:S(2)}) collective-permute-start(bf16[1,256,8,64]{1,3,2,0:T(8,128)(2,1)} %fusion.333), channel_id=1, source_target_pairs={{3,0},{0,1},{1,2},{2,3},{7,4},{4,5},{5,6},{6,7},{11,8},{8,9},{9,10... | collective-permute-start | bytes 786440 | tf_op jit(solution)/shard_map/while/body/eval_jaxpr/ppermute | solution.py:26
  974.3 80.4 %collective-permute-start.3 = (bf16[1,256,8,64]{1,3,2,0:T(8,128)(2,1)}, bf16[1,256,8,64]{1,3,2,0:T(8,128)(2,1)S(1)}, u32[]{:S(2)}, u32[]{:S(2)}) collective-permute-start(bf16[1,256,8,64]{1,3,2,0:T(8,128)(2,1)} %fusion.334), channel_id=1, source_target_pairs={{3,0},{0,1},{1,2},{2,3},{7,4},{4,5},{5,6},{6,7},{11,8},{8,9},{9,10... | collective-permute-start | bytes 786440 | tf_op jit(solution)/shard_map/while/body/eval_jaxpr/ppermute | solution.py:26
  1057.8 272.3 %reduce-scatter.24.cloned.1.call-start = ((), (), s32[]{:S(2)}) async-start(), calls=%async_computation.14 | async-start | bytes 2162688 | tf_op jit(solution)/shard_map/reduce_scatter | solution.py:406
  1060.8 405.1 %reduce-scatter.46.cloned.1.call-start = ((), (), s32[]{:S(2)}) async-start(), calls=%async_computation.25 | async-start | bytes 2162688
  1064.3 537.1 %reduce-scatter.44.cloned.1.call-start = ((), (), s32[]{:S(2)}) async-start(), calls=%async_computation.24 | async-start | bytes 2162688
  1070.4 671.4 %reduce-scatter.32.cloned.1.call-start = ((), (), s32[]{:S(2)}) async-start(), calls=%async_computation.18 | async-start | bytes 4325376 | tf_op jit(solution)/shard_map/reduce_scatter | solution.py:412
  1074.3 809.7 %reduce-scatter.30.cloned.1.call-start = ((), (), s32[]{:S(2)}) async-start(), calls=%async_computation.17 | async-start | bytes 4325376 | tf_op jit(solution)/shard_map/reduce_scatter | solution.py:409
  1077.3 949.5 %reduce-scatter.28.cloned.1.call-start = ((), (), s32[]{:S(2)}) async-start(), calls=%async_computation.16 | async-start | bytes 4325376 | tf_op jit(solution)/shard_map/reduce_scatter | solution.py:408
  1080.9 1087.7 %reduce-scatter.22.cloned.1.call-start = ((), (), s32[]{:S(2)}) async-start(), calls=%async_computation.13 | async-start | bytes 4325376 | tf_op jit(solution)/shard_map/reduce_scatter | solution.py:405
  1084.1 1334.0 %reduce-scatter.36.cloned.1.call-start = ((), (), s32[]{:S(2)}) async-start(), calls=%async_computation.20 | async-start | bytes 11894784 | tf_op jit(solution)/shard_map/reduce_scatter | solution.py:414
  1090.2 1580.6 %reduce-scatter.34.cloned.1.call-start = ((), (), s32[]{:S(2)}) async-start(), calls=%async_computation.19 | async-start | bytes 11894784 | tf_op jit(solution)/shard_map/reduce_scatter | solution.py:413
  1097.5 1826.2 %reduce-scatter.38.cloned.1.call-start = ((), (), s32[]{:S(2)}) async-start(), calls=%async_computation.21 | async-start | bytes 11894784 | tf_op jit(solution)/shard_map/reduce_scatter | solution.py:415
  1115.1 1808.6 %copy-start.1 = (bf16[1024,1024]{1,0:T(8,128)(2,1)S(1)}, bf16[1024,1024]{1,0:T(8,128)(2,1)}, u32[]{:S(2)}) copy-start(bf16[1024,1024]{1,0:T(8,128)(2,1)} %param.41) | copy-start | bytes 6291460
  (75 other events, 421.8 us)
Sparse Core Ops, SparseCore 0:
  445.6 24.1 reduce-scatter.41
  483.4 27.0 reduce-scatter.39
  1058.0 136.4 reduce-scatter.25
  1197.3 132.8 reduce-scatter.23
  1332.8 132.9 reduce-scatter.45
  1468.6 132.8 reduce-scatter.43
  1604.3 137.4 reduce-scatter.31
  1744.7 139.3 reduce-scatter.29
  1886.9 139.8 reduce-scatter.27
  2029.5 139.1 reduce-scatter.21
  2171.5 246.5 reduce-scatter.35
  2420.8 249.8 reduce-scatter.33
  2673.6 250.0 reduce-scatter.37
where the time goes:
time: 2970 us; the launch traced here: 2930 us
  waiting for transfers between devices  1760 us (59%)
  local copies, waits for them, and re-layouts  817 us (28%)
  matrix products  177 us (6%)
  blocking collectives  63.7 us (2%)
  other arithmetic  50.1 us (2%)
    unnamed x17, waiting for transfers between devices  272 us
    rev x14, local copies, waits for them, and re-layouts, toeplitz_tile(): return jnp.flip(skewed, axis=1)  265 us
    reduce_scatter x1, waiting for transfers between devices, body(): lax.psum_scatter(ffn_sums[2], ('dp', 'blk'), scatter_dimension=0, tiled=T...  253 us
    reduce_scatter x1, waiting for transfers between devices, body(): lax.psum_scatter(ffn_sums[0], ('dp', 'blk'), scatter_dimension=0, tiled=T...  253 us
    reduce_scatter x1, waiting for transfers between devices, body(): lax.psum_scatter(ffn_sums[1], ('dp', 'blk'), scatter_dimension=0, tiled=T...  249 us
    reduce_scatter x1, waiting for transfers between devices, body(): lax.psum_scatter(dw_out, ('dp', 'blk'), scatter_dimension=0, tiled=True)  143 us
    reduce_scatter x1, waiting for transfers between devices, body(): lax.psum_scatter(cross_sums[0], ('dp', 'blk'), scatter_dimension=0, tiled...  142 us
    reduce_scatter x1, waiting for transfers between devices, body(): lax.psum_scatter(dw_query, ('dp', 'blk'), scatter_dimension=0, tiled=True)  142 us
  transfers between devices with their start and end apart: 27, of which 11 were waited for; matrix products, arithmetic and copies ran while one was open for 30% of the time, Pallas kernels for 0%

commit v1 on v0

v1 whole, which is shorter than its diff:
```python
import functools

import jax
import jax.numpy as jnp
from jax import lax
from jax.experimental import pallas as pl
from jax.experimental.pallas import tpu as pltpu
from jax.sharding import PartitionSpec as P

HEAD_DIM = 64
EPSILON = 1e-06
NEGATIVE = -1e30
SCALE = HEAD_DIM ** (-0.5)
LANES = 128
PAIR = 2 * HEAD_DIM
F32 = jnp.float32
BF16 = jnp.bfloat16
VMEM_LIMIT = 56 * 1024 * 1024

NT = (((1,), (1,)), ((), ()))
NN = (((1,), (0,)), ((), ()))
TN = (((0,), (0,)), ((), ()))


def dot32(a, b, dims=NN):
    return lax.dot_general(a, b, dims, preferred_element_type=F32)


def swap(x, axis, bit):
    return lax.ppermute(x, axis, [(i, i ^ bit) for i in range(lax.axis_size(axis))])


def gather_relative(x):
    size = lax.axis_size("blk")
    if size == 4:
        half = x.shape[0] // 2
        one = swap(x, "blk", 1)
        two = swap(x, "blk", 2)
        far_a = swap(one[:half], "blk", 2)
        far_b = swap(two[half:], "blk", 1)
        return jnp.concatenate([x, one, two, far_a, far_b], axis=0)
    bit = 1
    while bit < size:
        x = jnp.concatenate([x, swap(x, "blk", bit)], axis=0)
        bit *= 2
    return x


def add16(a, b):
    return (a.astype(F32) + b.astype(F32)).astype(BF16)


def scatter_relative(x):
    size = lax.axis_size("blk")
    width = x.shape[-1]
    x = x.reshape(size, -1, width)
    if size == 4:
        half = width // 2
        a, b = x[..., :half], x[..., half:]
        from_x = swap(jnp.stack([a[1], a[3]]), "blk", 1)
        from_y = swap(b[2:], "blk", 2)
        a_far = swap(add16(a[2], from_x[1]), "blk", 2)
        b_far = swap(add16(b[1], from_y[1]), "blk", 1)
        left = add16(a[0], from_x[0]).astype(F32) + a_far.astype(F32)
        right = add16(b[0], from_y[0]).astype(F32) + b_far.astype(F32)
        return jnp.concatenate([left, right], axis=-1)
    bit = size // 2
    while bit:
        x = add16(x[:bit], swap(x[bit:], "blk", bit))
        bit //= 2
    return x[0].astype(F32)


def sum_rows(x, first_blk_bit):
    dp_bits = lax.axis_size("dp").bit_length() - 1
    blk_bits = lax.axis_size("blk").bit_length() - 1
    rest = [("dp", k) for k in reversed(range(dp_bits))] + [("blk", k) for k in reversed(range(blk_bits))]
    rows, width = x.shape
    x = x.reshape((2,) * len(rest) + (rows >> len(rest), width))
    order = [("dp", 0)]
    order += [("blk", (first_blk_bit + k) % blk_bits) for k in range(blk_bits)]
    order += [("dp", k) for k in range(1, dp_bits)]
    for axis, k in order:
        place = rest.index((axis, k))
        mine = (lax.axis_index(axis) >> k) & 1
        out = lax.dynamic_index_in_dim(x, 1 - mine, place, keepdims=False)
        keep = lax.dynamic_index_in_dim(x, mine, place, keepdims=False)
        got = swap(out, axis, 1 << k)
        rest.pop(place)
        x = keep.astype(F32) + got.astype(F32)
        if rest:
            x = x.astype(BF16)
    return x


def stacked(ref, kv):
    low = kv * PAIR
    return jnp.concatenate([ref[:, low : low + HEAD_DIM], ref[:, low + HEAD_DIM : low + PAIR]], axis=0)


def unstack(ref, kv, columns):
    length = columns.shape[1] // 2
    rows = columns.T
    low = kv * PAIR
    ref[:, low : low + HEAD_DIM] = rows[:length].astype(ref.dtype)
    ref[:, low + HEAD_DIM : low + PAIR] = rows[length:].astype(ref.dtype)


def spread_bias(bias_ref, tile_ref, kv):
    for g in range(2):
        line = bias_ref[0, 2 * kv + g : 2 * kv + g + 1, :]
        width = line.shape[1]
        tile_ref[g] = pltpu.roll(
            jnp.broadcast_to(line, (LANES, width)), 0, 1, stride=1, stride_axis=0
        )


def bias_tile(tile_ref, start, length):
    heads = []
    for g in range(2):
        heads.append(
            jnp.concatenate(
                [
                    tile_ref[g, :, pl.ds(pl.multiple_of(start - LANES * m, LANES), length)]
                    for m in range(length // LANES)
                ],
                axis=0,
            )
        )
    return jnp.concatenate(heads, axis=1)


def self_forward_kernel(blocks, my_ref, q_ref, k_ref, v_ref, bias_ref, mix_ref, lse_ref, tile_ref, top_ref, sum_ref, acc_ref):
    length = q_ref.shape[0]
    my = my_ref[0]
    for kv in range(2):
        low = kv * HEAD_DIM
        spread_bias(bias_ref, tile_ref, kv)
        qq = stacked(q_ref, kv)
        top_ref[...] = jnp.full_like(top_ref, NEGATIVE)
        sum_ref[...] = jnp.zeros_like(sum_ref)
        acc_ref[...] = jnp.zeros_like(acc_ref)
        for j in range(blocks):
            source = my ^ j

            @pl.when(source <= my)
            def _(j=j, source=source):
                start = length + length * (my - source)
                keys = k_ref[j * length : (j + 1) * length, low : low + HEAD_DIM]
                values = v_ref[j * length : (j + 1) * length, low : low + HEAD_DIM]
                scores = dot32(keys, qq, NT) * SCALE + bias_tile(tile_ref, start, length)
                old = top_ref[...]
                new = jnp.maximum(old, jnp.max(scores, axis=0, keepdims=True))
                weights = jnp.exp(scores - new)
                shrink = jnp.exp(old - new)
                top_ref[...] = new
                sum_ref[...] = sum_ref[...] * shrink + jnp.sum(weights, axis=0, keepdims=True)
                acc_ref[...] = acc_ref[...] * shrink + dot32(values, weights.astype(BF16), TN)

        unstack(mix_ref, kv, acc_ref[...] / sum_ref[...])
        lse_ref[kv] = top_ref[...] + jnp.log(sum_ref[...])


def self_backward_kernel(blocks, my_ref, q_ref, k_ref, v_ref, bias_ref, mix_ref, lse_ref, grad_ref, dq_ref, dk_ref, dv_ref, dbias_ref, tile_ref, diag_ref, acc_ref):
    length = q_ref.shape[0]
    width = bias_ref.shape[2]
    my = my_ref[0]
    for kv in range(2):
        low = kv * HEAD_DIM
        spread_bias(bias_ref, tile_ref, kv)
        qq = stacked(q_ref, kv)
        dd = stacked(grad_ref, kv)
        delta = jnp.sum((dd.astype(F32) * stacked(mix_ref, kv).astype(F32)).T, axis=0, keepdims=True)
        lse = lse_ref[kv]
        diag_ref[...] = jnp.zeros_like(diag_ref)
        acc_ref[...] = jnp.zeros_like(acc_ref)
        for j in range(blocks):
            source = my ^ j
            rows = slice(j * length, (j + 1) * length)

            @pl.when(source <= my)
            def _(rows=rows, source=source):
                start = length + length * (my - source)
                keys = k_ref[rows, low : low + HEAD_DIM]
                values = v_ref[rows, low : low + HEAD_DIM]
                scores = dot32(keys, qq, NT) * SCALE + bias_tile(tile_ref, start, length)
                probs = jnp.exp(scores - lse)
                dv_ref[rows, low : low + HEAD_DIM] = dot32(probs.astype(BF16), dd).astype(BF16)
                change = dot32(values, dd, NT) - delta
                ds = (probs * change).astype(BF16)
                dk_ref[rows, low : low + HEAD_DIM] = (dot32(ds, qq) * SCALE).astype(BF16)
                acc_ref[...] += dot32(keys, ds, TN)
                ds = ds.astype(F32)
                for g in range(2):
                    for m in range(length // LANES):
                        where = pl.ds(pl.multiple_of(start - LANES * m, LANES), length)
                        diag_ref[g, :, where] += ds[m * LANES : (m + 1) * LANES, g * length : (g + 1) * length]

            @pl.when(source > my)
            def _(rows=rows):
                none = jnp.zeros((length, HEAD_DIM), BF16)
                dv_ref[rows, low : low + HEAD_DIM] = none
                dk_ref[rows, low : low + HEAD_DIM] = none

        unstack(dq_ref, kv, acc_ref[...] * SCALE)
        for g in range(2):
            part = diag_ref[g]
            half = LANES // 2
            while half:
                part = part[:half] + pltpu.roll(part[half:], width - half, 1)
                half //= 2
            dbias_ref[0, 2 * kv + g : 2 * kv + g + 1, :] = part


def cross_forward_kernel(allow_ref, q_ref, k_ref, v_ref, mix_ref, lse_ref):
    allow = allow_ref[...] > 0
    for kv in range(2):
        low = kv * HEAD_DIM
        qq = stacked(q_ref, kv)
        scores = dot32(k_ref[:, low : low + HEAD_DIM], qq, NT) * SCALE
        scores = jnp.where(allow, scores, NEGATIVE)
        top = jnp.max(scores, axis=0, keepdims=True)
        raised = jnp.exp(scores - top)
        total = jnp.sum(raised, axis=0, keepdims=True)
        probs = (raised * (1.0 / total)).astype(BF16)
        unstack(mix_ref, kv, dot32(v_ref[:, low : low + HEAD_DIM], probs, TN))
        lse_ref[kv] = top + jnp.log(total)


def cross_backward_kernel(allow_ref, q_ref, k_ref, v_ref, lse_ref, grad_ref, dq_ref, dk_ref, dv_ref):
    allow = allow_ref[...] > 0
    for kv in range(2):
        low = kv * HEAD_DIM
        qq = stacked(q_ref, kv)
        dd = stacked(grad_ref, kv)
        keys = k_ref[:, low : low + HEAD_DIM]
        scores = jnp.where(allow, dot32(keys, qq, NT) * SCALE, NEGATIVE)
        probs = jnp.exp(scores - lse_ref[kv])
        change = dot32(v_ref[:, low : low + HEAD_DIM], dd, NT)
        delta = jnp.sum(probs * change, axis=0, keepdims=True)
        ds = (probs * (change - delta)).astype(BF16)
        dv_ref[:, low : low + HEAD_DIM] = dot32(probs.astype(BF16), dd).astype(BF16)
        dk_ref[:, low : low + HEAD_DIM] = (dot32(ds, qq) * SCALE).astype(BF16)
        unstack(dq_ref, kv, dot32(keys, ds, TN) * SCALE)


def params():
    return pltpu.CompilerParams(dimension_semantics=("arbitrary",), vmem_limit_bytes=VMEM_LIMIT)


def cost(length, keys, heads, passes, moved):
    return pl.CostEstimate(
        flops=2 * length * keys * heads * HEAD_DIM * passes,
        transcendentals=length * keys * heads,
        bytes_accessed=moved,
    )


def lane_block(rows, width):
    return pl.BlockSpec((rows, width), lambda i: (0, i))


def self_forward(my, q, k, v, bias):
    length, keys, kv_heads = q.shape[0], k.shape[0], k.shape[1] // HEAD_DIM
    pairs, width = kv_heads // 2, bias.shape[2]
    lead = pl.BlockSpec((1, 4, width), lambda i: (i, 0, 0))
    return pl.pallas_call(
        functools.partial(self_forward_kernel, keys // length),
        grid=(pairs,),
        in_specs=[
            pl.BlockSpec(memory_space=pltpu.SMEM),
            lane_block(length, 2 * PAIR),
            lane_block(keys, PAIR),
            lane_block(keys, PAIR),
            lead,
        ],
        out_specs=[
            lane_block(length, 2 * PAIR),
            pl.BlockSpec((2, 1, 2 * length), lambda i: (i, 0, 0)),
        ],
        out_shape=[
            jax.ShapeDtypeStruct(q.shape, BF16),
            jax.ShapeDtypeStruct((kv_heads, 1, 2 * length), F32),
        ],
        scratch_shapes=[
            pltpu.VMEM((2, LANES, width), F32),
            pltpu.VMEM((1, 2 * length), F32),
            pltpu.VMEM((1, 2 * length), F32),
            pltpu.VMEM((HEAD_DIM, 2 * length), F32),
        ],
        compiler_params=params(),
        cost_estimate=cost(length, keys, 2 * kv_heads, 2, 4 * q.size + 4 * k.size),
        name="self_forward",
    )(my, q, k, v, bias)


def self_backward(my, q, k, v, bias, mix, lse, grad):
    length, keys, kv_heads = q.shape[0], k.shape[0], k.shape[1] // HEAD_DIM
    pairs, width = kv_heads // 2, bias.shape[2]
    lead = pl.BlockSpec((1, 4, width), lambda i: (i, 0, 0))
    return pl.pallas_call(
        functools.partial(self_backward_kernel, keys // length),
        grid=(pairs,),
        in_specs=[
            pl.BlockSpec(memory_space=pltpu.SMEM),
            lane_block(length, 2 * PAIR),
            lane_block(keys, PAIR),
            lane_block(keys, PAIR),
            lead,
            lane_block(length, 2 * PAIR),
            pl.BlockSpec((2, 1, 2 * length), lambda i: (i, 0, 0)),
            lane_block(length, 2 * PAIR),
        ],
        out_specs=[
            lane_block(length, 2 * PAIR),
            lane_block(keys, PAIR),
            lane_block(keys, PAIR),
            lead,
        ],
        out_shape=[
            jax.ShapeDtypeStruct(q.shape, BF16),
            jax.ShapeDtypeStruct(k.shape, BF16),
            jax.ShapeDtypeStruct(v.shape, BF16),
            jax.ShapeDtypeStruct(bias.shape, F32),
        ],
        scratch_shapes=[
            pltpu.VMEM((2, LANES, width), F32),
            pltpu.VMEM((2, LANES, width), F32),
            pltpu.VMEM((HEAD_DIM, 2 * length), F32),
        ],
        compiler_params=params(),
        cost_estimate=cost(length, keys, 2 * kv_heads, 5, 8 * q.size + 8 * k.size),
        name="self_backward",
    )(my, q, k, v, bias, mix, lse, grad)


def cross_forward(allow, q, k, v):
    length, keys, kv_heads = q.shape[0], k.shape[0], k.shape[1] // HEAD_DIM
    return pl.pallas_call(
        cross_forward_kernel,
        grid=(kv_heads // 2,),
        in_specs=[
            pl.BlockSpec((keys, 1), lambda i: (0, 0)),
            lane_block(length, 2 * PAIR),
            lane_block(keys, PAIR),
            lane_block(keys, PAIR),
        ],
        out_specs=[
            lane_block(length, 2 * PAIR),
            pl.BlockSpec((2, 1, 2 * length), lambda i: (i, 0, 0)),
        ],
        out_shape=[
            jax.ShapeDtypeStruct(q.shape, BF16),
            jax.ShapeDtypeStruct((kv_heads, 1, 2 * length), F32),
        ],
        compiler_params=params(),
        cost_estimate=cost(length, keys, 2 * kv_heads, 2, 4 * q.size + 4 * k.size),
        name="cross_forward",
    )(allow, q, k, v)


def cross_backward(allow, q, k, v, lse, grad):
    length, keys, kv_heads = q.shape[0], k.shape[0], k.shape[1] // HEAD_DIM
    return pl.pallas_call(
        cross_backward_kernel,
        grid=(kv_heads // 2,),
        in_specs=[
            pl.BlockSpec((keys, 1), lambda i: (0, 0)),
            lane_block(length, 2 * PAIR),
            lane_block(keys, PAIR),
            lane_block(keys, PAIR),
            pl.BlockSpec((2, 1, 2 * length), lambda i: (i, 0, 0)),
            lane_block(length, 2 * PAIR),
        ],
        out_specs=[
            lane_block(length, 2 * PAIR),
            lane_block(keys, PAIR),
            lane_block(keys, PAIR),
        ],
        out_shape=[
            jax.ShapeDtypeStruct(q.shape, BF16),
            jax.ShapeDtypeStruct(k.shape, BF16),
            jax.ShapeDtypeStruct(v.shape, BF16),
        ],
        compiler_params=params(),
        cost_estimate=cost(length, keys, 2 * kv_heads, 5, 6 * q.size + 8 * k.size),
        name="cross_backward",
    )(allow, q, k, v, lse, grad)


def inverse_rms(x):
    return lax.rsqrt(jnp.mean(x * x, axis=-1, keepdims=True) + EPSILON)


def norm_back(x, inverse, gain, grad):
    scaled = grad * gain
    along = jnp.mean(scaled * x, axis=-1, keepdims=True)
    d_x = inverse * scaled - x * (inverse * inverse * inverse * along)
    return d_x, jnp.sum(grad * x * inverse, axis=0)


def body(
    block_in,
    memory,
    memory_len,
    cross_mask,
    buckets,
    bias_table,
    norm_self,
    w_query,
    w_key,
    w_value,
    w_out,
    norm_cross,
    cross_query,
    cross_key,
    cross_value,
    cross_out,
    norm_ffn,
    w_gate,
    w_up,
    w_down,
    grad_out,
):
    seq_count, length, model_width = block_in.shape
    assert seq_count == 1
    mem_rows = memory.shape[1]
    mem_total = cross_mask.shape[1]
    blocks = lax.axis_size("blk")
    my = lax.axis_index("blk")
    kv_width = w_key.shape[1]
    head_count = w_query.shape[1] // HEAD_DIM
    bucket_count = bias_table.shape[0]
    my_ref = my.reshape(1).astype(jnp.int32)

    x_all = gather_relative(block_in[0])
    mem_all = gather_relative(memory[0])

    bucket_hot = (buckets[:, None] == jnp.arange(bucket_count)[None, :]).astype(F32)
    dist_bias = lax.dot_general(bias_table, bucket_hot, (((0,), (1,)), ((), ())), precision=lax.Precision.HIGHEST)
    bias = jnp.concatenate([jnp.full((head_count, length), NEGATIVE, F32), dist_bias], axis=1)
    bias = bias.reshape(head_count // 4, 4, -1)

    mem_places = jnp.arange(mem_total)
    allowed = (mem_places == 0) | (mem_places < memory_len[0]) & (cross_mask[0] == 1)
    allow = allowed.astype(F32).reshape(blocks, mem_rows)[my ^ jnp.arange(blocks)].reshape(mem_total, 1)

    stream_all = x_all.astype(F32)
    inv_self_all = inverse_rms(stream_all)
    self_all = (stream_all * inv_self_all * norm_self).astype(BF16)
    stream, inv_self, self_in = stream_all[:length], inv_self_all[:length], self_all[:length]
    query = dot32(self_in, w_query).astype(BF16)
    key = dot32(self_all, w_key).astype(BF16)
    value = dot32(self_all, w_value).astype(BF16)
    self_mix, lse = self_forward(my_ref, query, key, value, bias)
    after_self = stream + dot32(self_mix, w_out)

    inv_cross = inverse_rms(after_self)
    cross_in = (after_self * inv_cross * norm_cross).astype(BF16)
    cross_q = dot32(cross_in, cross_query).astype(BF16)
    mem_key = dot32(mem_all, cross_key).astype(BF16)
    mem_value = dot32(mem_all, cross_value).astype(BF16)
    cross_mix, cross_lse = cross_forward(allow, cross_q, mem_key, mem_value)
    after_cross = after_self + dot32(cross_mix, cross_out)

    inv_ffn = inverse_rms(after_cross)
    ffn_in = (after_cross * inv_ffn * norm_ffn).astype(BF16)
    gate = dot32(ffn_in, w_gate)
    up = dot32(ffn_in, w_up)
    (act, hidden_full), gated_back = jax.vjp(lambda g, u: (jax.nn.gelu(g, approximate=True), jax.nn.gelu(g, approximate=True) * u), gate, up)
    hidden = hidden_full.astype(BF16)
    block_out = (after_cross + dot32(hidden, w_down)).astype(BF16)

    ffn_grad = grad_out[0]
    grad_top = ffn_grad.astype(F32)
    d_hidden = dot32(ffn_grad, w_down, NT)
    gate_full, up_full = gated_back((jnp.zeros_like(act), d_hidden))
    both_grad = jnp.concatenate([gate_full.astype(BF16), up_full.astype(BF16)], axis=1)
    ff = gate.shape[1]
    gate_grad, up_grad = both_grad[:, :ff], both_grad[:, ff:]
    dw_down = sum_rows(dot32(hidden, ffn_grad, TN).astype(BF16), 1)
    dw_both = sum_rows(dot32(ffn_in, both_grad, TN).astype(BF16), 0)
    d_stream, d_gain_ffn = norm_back(after_cross, inv_ffn, norm_ffn, dot32(gate_grad, w_gate, NT) + dot32(up_grad, w_up, NT))
    grad_cross = grad_top + d_stream

    cross_grad = grad_cross.astype(BF16)
    mix_grad = dot32(cross_grad, cross_out, NT).astype(BF16)
    cq_grad, mem_key_part, mem_value_part = cross_backward(allow, cross_q, mem_key, mem_value, cross_lse, mix_grad)
    mem_part = jnp.concatenate([mem_key_part, mem_value_part], axis=1)
    mem_grad = scatter_relative(mem_part).astype(BF16)
    d_memory = dot32(mem_grad[:, :kv_width], cross_key, NT) + dot32(mem_grad[:, kv_width:], cross_value, NT)
    dw_cross = jnp.concatenate(
        [
            dot32(cross_mix, cross_grad, TN).astype(BF16),
            dot32(cross_in, cq_grad, TN).astype(BF16),
            dot32(mem_all, mem_part, TN).astype(BF16),
        ],
        axis=1,
    )
    dw_cross = sum_rows(dw_cross, 1)
    d_stream, d_gain_cross = norm_back(after_self, inv_cross, norm_cross, dot32(cq_grad, cross_query, NT))
    grad_self = grad_cross + d_stream

    self_grad = grad_self.astype(BF16)
    attn_grad = dot32(self_grad, w_out, NT).astype(BF16)
    query_grad, key_part, value_part, bias_grad = self_backward(my_ref, query, key, value, bias, self_mix, lse, attn_grad)
    pair_part = jnp.concatenate([key_part, value_part], axis=1)
    dw_self = jnp.concatenate(
        [
            dot32(self_mix, self_grad, TN).astype(BF16),
            dot32(self_in, query_grad, TN).astype(BF16),
            dot32(self_all, pair_part, TN).astype(BF16),
        ],
        axis=1,
    )
    dw_self = sum_rows(dw_self, 1)
    pair_grad = scatter_relative(pair_part).astype(BF16)
    d_self_norm = (
        dot32(query_grad, w_query, NT)
        + dot32(pair_grad[:, :kv_width], w_key, NT)
        + dot32(pair_grad[:, kv_width:], w_value, NT)
    )
    d_stream, d_gain_self = norm_back(stream, inv_self, norm_self, d_self_norm)
    d_block_in = grad_self + d_stream
    d_table = lax.dot_general(
        bucket_hot,
        bias_grad.reshape(head_count, -1)[:, length:],
        (((0,), (1,)), ((), ())),
        precision=lax.Precision.HIGHEST,
    )
    gain_self, gain_cross, gain_ffn, table_sum = lax.psum((d_gain_self, d_gain_cross, d_gain_ffn, d_table), ("dp", "blk"))
    d = model_width
    return (
        block_out[None],
        d_block_in[None],
        d_memory[None],
        table_sum,
        gain_self,
        dw_self[:, d : 2 * d],
        dw_self[:, 2 * d : 2 * d + kv_width],
        dw_self[:, 2 * d + kv_width :],
        dw_self[:, :d],
        gain_cross,
        dw_cross[:, d : 2 * d],
        dw_cross[:, 2 * d : 2 * d + kv_width],
        dw_cross[:, 2 * d + kv_width :],
        dw_cross[:, :d],
        gain_ffn,
        dw_both[:, :ff],
        dw_both[:, ff:],
        dw_down,
    )


def solution(mesh):
    rows = P("dp", "blk", None)
    split = P(("dp", "blk"), None)
    whole = P()
    return jax.shard_map(
        body,
        mesh=mesh,
        in_specs=(rows, rows, P("dp"), P("dp", None)) + (whole,) * 16 + (rows,),
        out_specs=(rows, rows, rows, whole, whole)
        + (split,) * 4
        + (whole,)
        + (split,) * 4
        + (whole,)
        + (split,) * 3,
        check_vma=False,
    )
```

time: 2970 us -> 579 us (0.19); the launches traced: 2930 us -> 573 us
  waiting for transfers between devices: 1760 us -> 213 us
  local copies, waits for them, and re-layouts: 817 us -> 74.8 us
  matrix products: 177 us -> 76 us
  starting transfers between devices: 25.5 us -> 73.6 us
  Pallas kernels: 0 us -> 42.1 us
    reduce_scatter x9 -> x0, waiting for transfers between devices: 1490 us -> none  [the longest x1 253 us: body(): lax.psum_scatter(ffn_sums[2], ('dp', 'blk'), scatter_dimension=0, tiled=T...]
    rev x25 -> x0, local copies, waits for them, and re-layouts: 406 us -> none  [the longest x14 265 us: toeplitz_tile(): return jnp.flip(skewed, axis=1)]
    unnamed x17 -> x0, waiting for transfers between devices: 272 us -> none
    ppermute x14 -> x36, waiting for transfers between devices: 0.04 us -> 213 us  [swap(): lax.ppermute(x, axis, [(i, i ^ bit) for i in range(lax.axis_size(axis))])]
    reshape x15 -> x3, local copies, waits for them, and re-layouts: 198 us -> 1.55 us  [the longest x1 0.86 us: body(): allowed.astype(F32).reshape(blocks, mem_rows)[my ^ jnp.arange(blocks)]]
    dot_general x68 -> x32, matrix products: 177 us -> 76 us  [the longest x30 73.8 us: dot32(): return lax.dot_general(a, b, dims, preferred_element_type=F32)]
    slice x18 -> x14, local copies, waits for them, and re-layouts: 73.3 us -> 7.61 us  [the longest x2 1.55 us: scatter_relative(): from_y = swap(b[2:], 'blk', 2)]
    while x30 -> x0, local copies, waits for them, and re-layouts: 51 us -> none
  transfers between devices with their start and end apart: 27 -> 36, of which waited for: 11 -> 15; matrix products, arithmetic and copies ran while one was open for 30% -> 21% of each run, Pallas kernels for 0% -> 0%
where the time goes in v1:
time: 579 us; the launch traced here: 573 us
  waiting for transfers between devices  213 us (37%)
  matrix products  76 us (13%)
  local copies, waits for them, and re-layouts  74.8 us (13%)
  starting transfers between devices  73.6 us (13%)
  other arithmetic  49.6 us (9%)
  Pallas kernels  42.1 us (7%)
  blocking collectives  40.8 us (7%)
    ppermute x36, waiting for transfers between devices, swap(): lax.ppermute(x, axis, [(i, i ^ bit) for i in range(lax.axis_size(axis))])  213 us
    dot_general x30, matrix products, dot32(): return lax.dot_general(a, b, dims, preferred_element_type=F32)  73.8 us
    ppermute x36, starting transfers between devices, swap(): lax.ppermute(x, axis, [(i, i ^ bit) for i in range(lax.axis_size(axis))])  73.6 us
    psum x1, blocking collectives, body(): lax.psum((d_gain_self, d_gain_cross, d_gain_ffn, d_table), ('dp', 'blk'))  40.8 us
    convert_element_type x16, other arithmetic, sum_rows(): x = x.astype(BF16)  21.8 us
    pallas_call x1, Pallas kernels, self_backward(): pl.pallas_call(functools.partial(self_backward_kernel, keys // length), g...  16.5 us
    dynamic_slice x2, local copies, waits for them, and re-layouts, sum_rows(): keep = lax.dynamic_index_in_dim(x, mine, place, keepdims=False)  15.1 us
    concatenate x1, other arithmetic, body(): jnp.concatenate([dot32(self_mix, self_grad, TN).astype(BF16), dot32(self_...  13.3 us
  transfers between devices with their start and end apart: 36, of which 15 were waited for; matrix products, arithmetic and copies ran while one was open for 21% of the time, Pallas kernels for 0%

profile of v1, /device:TPU:0, one launch (start us, length us, event | category | flops | bytes accessed | tf_op | source)
XLA Modules:
  0.0 573.0 jit_solution(15441951559933716637)
XLA Ops:
  14.8 6.6 %collective-permute-done.4 = bf16[128,1024]{1,0:T(8,128)(2,1)S(1)} collective-permute-done((bf16[128,1024]{1,0:T(8,128)(2,1)}, bf16[128,1024]{1,0:T(8,128)(2,1)S(1)}, u32[]{:S(2)}, u32[]{:S(2)}) %collective-permute-start.4) | collective-permute-done | bytes 262176 | tf_op jit(solution)/shard_map/ppermute | solution.py:30
  52.1 7.9 %self_forward.1 = (bf16[256,1024]{1,0:T(8,128)(2,1)}, f32[8,1,512]{2,1,0:T(1,128)}) custom-call(s32[1]{0:T(128)} %bitcast.1.my_ref, bf16[256,1024]{1,0:T(8,128)(2,1)} %convolution_convert_fusion.13.q_ref, bf16[1024,512]{1,0:T(8,128)(2,1)} %convolution_convert_fusion.9.k_ref, bf16[1024,512]{1,0:T(8,128)(2,1)} %convolution_convert_fusion.8.v_ref, ...), custom_call_target="tpu_custom_call" | custom-call | flops 1073741824 | bytes 3145728 | tf_op jit(solution)/shard_map/self_forward/pallas_call | solution.py:267
  64.2 8.3 %cross_forward.1 = (bf16[256,1024]{1,0:T(8,128)(2,1)}, f32[8,1,512]{2,1,0:T(1,128)}) custom-call(f32[512,1]{1,0:T(8,128)} %copy.47.allow_ref, bf16[256,1024]{1,0:T(8,128)(2,1)} %convolution_convert_fusion.12.q_ref, bf16[512,512]{1,0:T(8,128)(2,1)} %convolution_convert_fusion.15.k_ref, bf16[512,512]{1,0:T(8,128)(2,1)} %convolution_convert_fusion.14.v_ref), custom_call_target="tpu_custom_call" | custom-call | flops 536870912 | bytes 2097152 | tf_op jit(solution)/shard_map/cross_forward/pallas_call | solution.py:339
  74.5 4.4 fusion.81
  82.3 7.6 %multiply_convert_fusion.1 = (bf16[256,2816]{1,0:T(8,128)(2,1)S(1)}, bf16[256,2816]{1,0:T(8,128)(2,1)S(1)}, bf16[256,2816]{1,0:T(8,128)(2,1)}) fusion(f32[256,2816]{1,0:T(8,128)S(1)} %fusion.81, f32[256,2816]{1,0:T(8,128)} %fusion.82, bf16[2816,1024]{1,0:T(8,128)(2,1)S(1)} %bitcast.256, bf16[1,256,1024]{2,1,0:T(8,128)(2,1)S(1)} %copy-done.21), kind=kOutput, calls=%fused_computation.41 | convolution fusion | flops 1501626368 | bytes 16384000 | tf_op jit(solution)/shard_map/dot_general | solution.py:26
  95.4 9.4 %cross_backward.1 = (bf16[256,1024]{1,0:T(8,128)(2,1)}, bf16[512,512]{1,0:T(8,128)(2,1)}, bf16[512,512]{1,0:T(8,128)(2,1)}) custom-call(f32[512,1]{1,0:T(8,128)} %copy.47.allow_ref, bf16[256,1024]{1,0:T(8,128)(2,1)} %convolution_convert_fusion.12.q_ref, bf16[512,512]{1,0:T(8,128)(2,1)} %convolution_convert_fusion.15.k_ref, ...), custom_call_target="tpu_custom_call" | custom-call | flops 1342177280 | bytes 3670016 | tf_op jit(solution)/shard_map/cross_backward/pallas_call | solution.py:364
  110.1 16.5 %self_backward.1 = (bf16[256,1024]{1,0:T(8,128)(2,1)}, bf16[1024,512]{1,0:T(8,128)(2,1)}, bf16[1024,512]{1,0:T(8,128)(2,1)}, f32[4,4,1280]{2,1,0:T(4,128)}) custom-call(s32[1]{0:T(128)} %bitcast.1.my_ref, bf16[256,1024]{1,0:T(8,128)(2,1)} %convolution_convert_fusion.13.q_ref, bf16[1024,512]{1,0:T(8,128)(2,1)} %convolution_convert_fusion.9.k_ref, ...), custom_call_target="tpu_custom_call" | custom-call | flops 2684354560 | bytes 6291456 | tf_op jit(solution)/shard_map/self_backward/pallas_call | solution.py:301
  144.3 6.2 %convolution_convert_fusion = bf16[1024,5632]{1,0:T(8,128)(2,1)} fusion(bf16[256,1024]{1,0:T(8,128)(2,1)S(1)} %multiply_convert_fusion.3, bf16[256,2816]{1,0:T(8,128)(2,1)S(1)} %copy-done.24, bf16[256,2816]{1,0:T(8,128)(2,1)S(1)} %copy-done.26), kind=kOutput, calls=%fused_computation.3 | convolution fusion | flops 2964324352 | bytes 14942208 | tf_op jit(solution)/shard_map/dot_general | solution.py:26
  150.5 5.1 fusion.22
  155.7 4.2 convolution_convert_fusion.1
  159.9 18.9 %collective-permute-start.10 = (bf16[2,256,512]{2,1,0:T(8,128)(2,1)}, bf16[2,256,512]{2,1,0:T(8,128)(2,1)}, u32[]{:S(2)}, u32[]{:S(2)}) collective-permute-start(bf16[2,256,512]{2,1,0:T(8,128)(2,1)} %slice.213), channel_id=1, source_target_pairs={{0,2},{1,3},{2,0},{3,1},{4,6},{5,7},{6,4},{7,5},{8,10},{9,11},{10,... | collective-permute-start | bytes 1572872 | tf_op jit(solution)/shard_map/ppermute | solution.py:30
  179.7 10.6 %collective-permute-start.8 = (bf16[2,256,512]{2,1,0:T(8,128)(2,1)}, bf16[2,256,512]{2,1,0:T(8,128)(2,1)}, u32[]{:S(2)}, u32[]{:S(2)}) collective-permute-start(bf16[2,256,512]{2,1,0:T(8,128)(2,1)} %pad_maximum_fusion.2), channel_id=1, source_target_pairs={{0,1},{1,0},{2,3},{3,2},{4,5},{5,4},{6,7},{7,6},{8,9},{9,8},{10,11... | collective-permute-start | bytes 1572872 | tf_op jit(solution)/shard_map/ppermute | solution.py:30
  191.3 13.3 %pad_maximum_fusion = bf16[1024,3072]{0,1:T(8,128)(2,1)} fusion(bf16[1024,1024]{0,1:T(8,128)(2,1)S(1)} %copy-done.20, bf16[1024,1024]{0,1:T(8,128)(2,1)S(1)} %convolution_convert_fusion.6, bf16[1024,1024]{0,1:T(8,128)(2,1)S(1)} %convolution_convert_fusion.7), kind=kLoop, calls=%fused_computation.4 | loop fusion | flops 18874368 | bytes 12582912 | tf_op jit(solution)/shard_map/concatenate | solution.py:508
  204.6 8.6 %copy.49 = bf16[1024,3072]{1,0:T(8,128)(2,1)} copy(bf16[1024,3072]{0,1:T(8,128)(2,1)} %pad_maximum_fusion) | data formatting | bytes 12582912 | tf_op jit(solution)/shard_map/concatenate | solution.py:508
  213.1 6.0 %pad_maximum_fusion.1 = bf16[1024,3072]{0,1:T(8,128)(2,1)} fusion(bf16[1024,1024]{0,1:T(8,128)(2,1)} %convolution_convert_fusion.2, bf16[1024,1024]{0,1:T(8,128)(2,1)} %convolution_convert_fusion.3, bf16[1024,1024]{0,1:T(8,128)(2,1)} %convolution_convert_fusion.4), kind=kLoop, calls=%fused_computation.5 | loop fusion | flops 18874368 | bytes 12582912 | tf_op jit(solution)/shard_map/concatenate | solution.py:492
  219.1 8.7 %copy.50 = bf16[1024,3072]{1,0:T(8,128)(2,1)} copy(bf16[1024,3072]{0,1:T(8,128)(2,1)} %pad_maximum_fusion.1) | data formatting | bytes 12582912 | tf_op jit(solution)/shard_map/concatenate | solution.py:492
  227.8 3.9 dynamic-slice_bitcast_fusion.1
  234.5 9.8 %constant_dynamic-slice_fusion.3 = (bf16[2,2,1,2,2,32,5632]{6,5,4,3,2,1,0:T(8,128)(2,1)}, bf16[2,2,1,2,2,32,5632]{6,5,4,3,2,1,0:T(8,128)(2,1)}) fusion(bf16[2,2,2,2,2,32,5632]{6,5,4,3,2,1,0:T(8,128)(2,1)} %bitcast.223, s32[]{:T(128)S(6)} %select_n.86, s32[]{:T(128)S(6)} %select_n.87), kind=kLoop, calls=%fused_computation.182 | loop fusion | bytes 23068680 | tf_op jit(solution)/shard_map/jit(dynamic_index_in_dim)/dynamic_slice | solution.py:87
  244.3 5.3 constant_dynamic-slice_fusion.1
  252.6 5.8 %copy.65 = bf16[2,2,1,2,2,32,5632]{6,5,0,1,3,4,2:T(8,128)(2,1)} copy(bf16[2,2,1,2,2,32,5632]{6,5,4,3,2,1,0:T(8,128)(2,1)} %get-tuple-element.51) | data formatting | bytes 11534336 | tf_op jit(solution)/shard_map/jit(dynamic_index_in_dim)/dynamic_slice | solution.py:86
  269.4 4.3 collective-permute-done.9
  276.7 4.4 collective-permute-done.11
  283.0 40.8 %all-reduce.1 = (f32[32,16]{0,1:T(8,128)}, f32[1024]{0:T(1024)}, f32[1024]{0:T(1024)}, f32[1024]{0:T(1024)}) all-reduce(f32[32,16]{0,1:T(8,128)S(1)} %fusion.31, f32[1024]{0:T(1024)S(1)} %get-tuple-element.40, f32[1024]{0:T(1024)S(1)} %get-tuple-element.44, f32[1024]{0:T(1024)S(1)} %get-tuple-element.42), channel_id=1, replica_groups=mesh['dp'=8,'blk'=4] {'dp','blk'}, use_global_device_ids=true, to_apply=%region_6.7 | all-reduce | flops 3584 | bytes 28672 | tf_op jit(solution)/shard_map/psum | solution.py:531
  341.3 23.9 %collective-permute-done.32 = bf16[2,2,2,88,1024]{4,3,0,1,2:T(8,128)(2,1)S(1)} collective-permute-done((bf16[2,2,2,88,1024]{4,3,0,1,2:T(8,128)(2,1)S(1)}, bf16[2,2,2,88,1024]{4,3,0,1,2:T(8,128)(2,1)S(1)}, u32[]{:S(2)}, u32[]{:S(2)}) %collective-permute-start.32) | collective-permute-done | bytes 1441824 | tf_op jit(solution)/shard_map/ppermute | solution.py:30
  367.6 31.3 %collective-permute-done.17 = bf16[2,2,2,32,3072]{4,3,2,1,0:T(8,128)(2,1)S(1)} collective-permute-done((bf16[2,2,2,32,3072]{4,3,2,1,0:T(8,128)(2,1)S(1)}, bf16[2,2,2,32,3072]{4,3,2,1,0:T(8,128)(2,1)S(1)}, u32[]{:S(2)}, u32[]{:S(2)}) %collective-permute-start.17) | collective-permute-done | bytes 1572896 | tf_op jit(solution)/shard_map/ppermute | solution.py:30
  404.0 26.3 %collective-permute-done.22 = bf16[2,2,2,32,3072]{4,3,2,1,0:T(8,128)(2,1)S(1)} collective-permute-done((bf16[2,2,2,32,3072]{4,3,2,1,0:T(8,128)(2,1)S(1)}, bf16[2,2,2,32,3072]{4,3,2,1,0:T(8,128)(2,1)S(1)}, u32[]{:S(2)}, u32[]{:S(2)}) %collective-permute-start.22) | collective-permute-done | bytes 1572896 | tf_op jit(solution)/shard_map/ppermute | solution.py:30
  436.0 6.0 %fusion = bf16[2,2,2,2,32,5632]{5,4,0,1,2,3:T(8,128)(2,1)S(1)} fusion(bf16[2,2,2,2,32,5632]{5,4,0,1,2,3:T(8,128)(2,1)} %collective-permute-done.26, bf16[2,2,1,2,2,32,5632]{6,5,4,3,2,1,0:T(8,128)(2,1)} %get-tuple-element.50), kind=kLoop, calls=%fused_computation.2 | loop fusion | flops 11534336 | bytes 17301504 | tf_op jit(solution)/shard_map/convert_element_type | solution.py:92
  444.7 8.0 %collective-permute-done.23 = bf16[2,2,32,3072]{3,2,1,0:T(8,128)(2,1)} collective-permute-done((bf16[2,2,32,3072]{3,2,1,0:T(8,128)(2,1)}, bf16[2,2,32,3072]{3,2,1,0:T(8,128)(2,1)}, u32[]{:S(2)}, u32[]{:S(2)}) %collective-permute-start.23) | collective-permute-done | bytes 786464 | tf_op jit(solution)/shard_map/ppermute | solution.py:30
  457.9 53.3 %collective-permute-done.27 = bf16[2,2,2,32,5632]{4,3,0,1,2:T(8,128)(2,1)S(1)} collective-permute-done((bf16[2,2,2,32,5632]{4,3,0,1,2:T(8,128)(2,1)S(1)}, bf16[2,2,2,32,5632]{4,3,0,1,2:T(8,128)(2,1)S(1)}, u32[]{:S(2)}, u32[]{:S(2)}) %collective-permute-start.27) | collective-permute-done | bytes 2883616 | tf_op jit(solution)/shard_map/ppermute | solution.py:30
  516.6 26.0 %collective-permute-done.28 = bf16[2,2,32,5632]{3,2,0,1:T(8,128)(2,1)S(1)} collective-permute-done((bf16[2,2,32,5632]{3,2,0,1:T(8,128)(2,1)S(1)}, bf16[2,2,32,5632]{3,2,0,1:T(8,128)(2,1)S(1)}, u32[]{:S(2)}, u32[]{:S(2)}) %collective-permute-start.28) | collective-permute-done | bytes 1441824 | tf_op jit(solution)/shard_map/ppermute | solution.py:30
  545.2 13.9 %collective-permute-done.29 = bf16[2,32,5632]{2,1,0:T(8,128)(2,1)S(1)} collective-permute-done((bf16[2,32,5632]{2,1,0:T(8,128)(2,1)S(1)}, bf16[2,32,5632]{2,1,0:T(8,128)(2,1)S(1)}, u32[]{:S(2)}, u32[]{:S(2)}) %collective-permute-start.29) | collective-permute-done | bytes 720928 | tf_op jit(solution)/shard_map/ppermute | solution.py:30
  563.0 8.6 %collective-permute-done.30 = bf16[32,5632]{1,0:T(8,128)(2,1)S(1)} collective-permute-done((bf16[32,5632]{1,0:T(8,128)(2,1)S(1)}, bf16[32,5632]{1,0:T(8,128)(2,1)S(1)}, u32[]{:S(2)}, u32[]{:S(2)}) %collective-permute-start.30) | collective-permute-done | bytes 360480 | tf_op jit(solution)/shard_map/ppermute | solution.py:30
  (295 shorter events, 156.3 us)
Async XLA Ops:
  0.7 32.0 %collective-permute-start = (bf16[256,1024]{1,0:T(8,128)(2,1)}, bf16[256,1024]{1,0:T(8,128)(2,1)S(1)}, u32[]{:S(2)}, u32[]{:S(2)}) collective-permute-start(bf16[256,1024]{1,0:T(8,128)(2,1)} %bitcast.243), channel_id=1, source_target_pairs={{0,1},{1,0},{2,3},{3,2},{4,5},{5,4},{6,7},{7,6},{8,9},{9,8},{10,11... | collective-permute-start | bytes 1572872 | tf_op jit(solution)/shard_map/ppermute | solution.py:30
  3.7 31.8 %collective-permute-start.1 = (bf16[256,1024]{1,0:T(8,128)(2,1)}, bf16[256,1024]{1,0:T(8,128)(2,1)S(1)}, u32[]{:S(2)}, u32[]{:S(2)}) collective-permute-start(bf16[256,1024]{1,0:T(8,128)(2,1)} %bitcast.244), channel_id=1, source_target_pairs={{0,2},{1,3},{2,0},{3,1},{4,6},{5,7},{6,4},{7,5},{8,10},{9,11},{10,... | collective-permute-start | bytes 1572872 | tf_op jit(solution)/shard_map/ppermute | solution.py:30
  5.2 16.2 %collective-permute-start.4 = (bf16[128,1024]{1,0:T(8,128)(2,1)}, bf16[128,1024]{1,0:T(8,128)(2,1)S(1)}, u32[]{:S(2)}, u32[]{:S(2)}) collective-permute-start(bf16[128,1024]{1,0:T(8,128)(2,1)} %bitcast.245), channel_id=1, source_target_pairs={{0,1},{1,0},{2,3},{3,2},{4,5},{5,4},{6,7},{7,6},{8,9},{9,8},{10,11... | collective-permute-start | bytes 786440 | tf_op jit(solution)/shard_map/ppermute | solution.py:30
  5.7 17.6 %collective-permute-start.5 = (bf16[128,1024]{1,0:T(8,128)(2,1)}, bf16[128,1024]{1,0:T(8,128)(2,1)}, u32[]{:S(2)}, u32[]{:S(2)}) collective-permute-start(bf16[128,1024]{1,0:T(8,128)(2,1)} %bitcast.246), channel_id=1, source_target_pairs={{0,2},{1,3},{2,0},{3,1},{4,6},{5,7},{6,4},{7,5},{8,10},{9,11},{10,... | collective-permute-start | bytes 786440 | tf_op jit(solution)/shard_map/ppermute | solution.py:30
  21.5 6.7 %collective-permute-start.6 = (bf16[64,1024]{1,0:T(8,128)(2,1)S(1)}, bf16[64,1024]{1,0:T(8,128)(2,1)S(1)}, u32[]{:S(2)}, u32[]{:S(2)}) collective-permute-start(bf16[64,1024]{1,0:T(8,128)(2,1)S(1)} %slice.204), channel_id=1, source_target_pairs={{0,2},{1,3},{2,0},{3,1},{4,6},{5,7},{6,4},{7,5},{8,10},{9,11},{10,... | collective-permute-start | bytes 393224 | tf_op jit(solution)/shard_map/ppermute | solution.py:30
  159.9 99.6 %collective-permute-start.10 = (bf16[2,256,512]{2,1,0:T(8,128)(2,1)}, bf16[2,256,512]{2,1,0:T(8,128)(2,1)}, u32[]{:S(2)}, u32[]{:S(2)}) collective-permute-start(bf16[2,256,512]{2,1,0:T(8,128)(2,1)} %slice.213), channel_id=1, source_target_pairs={{0,2},{1,3},{2,0},{3,1},{4,6},{5,7},{6,4},{7,5},{8,10},{9,11},{10,... | collective-permute-start | bytes 1572872 | tf_op jit(solution)/shard_map/ppermute | solution.py:30
  179.7 81.8 %collective-permute-start.8 = (bf16[2,256,512]{2,1,0:T(8,128)(2,1)}, bf16[2,256,512]{2,1,0:T(8,128)(2,1)}, u32[]{:S(2)}, u32[]{:S(2)}) collective-permute-start(bf16[2,256,512]{2,1,0:T(8,128)(2,1)} %pad_maximum_fusion.2), channel_id=1, source_target_pairs={{0,1},{1,0},{2,3},{3,2},{4,5},{5,4},{6,7},{7,6},{8,9},{9,8},{10,11... | collective-permute-start | bytes 1572872 | tf_op jit(solution)/shard_map/ppermute | solution.py:30
  190.3 68.1 %collective-permute-start.12 = (bf16[2,128,512]{2,1,0:T(8,128)(2,1)S(1)}, bf16[2,128,512]{2,1,0:T(8,128)(2,1)S(1)}, u32[]{:S(2)}, u32[]{:S(2)}) collective-permute-start(bf16[2,128,512]{2,1,0:T(8,128)(2,1)S(1)} %pad_maximum_fusion.3), channel_id=1, source_target_pairs={{0,1},{1,0},{2,3},{3,2},{4,5},{5,4},{6,7},{7,6},{8,9},{9,8},{10,11... | collective-permute-start | bytes 786440 | tf_op jit(solution)/shard_map/ppermute | solution.py:30
  190.4 68.7 %collective-permute-start.14 = (bf16[2,128,512]{2,1,0:T(8,128)(2,1)}, bf16[2,128,512]{2,1,0:T(8,128)(2,1)S(1)}, u32[]{:S(2)}, u32[]{:S(2)}) collective-permute-start(bf16[2,128,512]{2,1,0:T(8,128)(2,1)} %slice.224), channel_id=1, source_target_pairs={{0,2},{1,3},{2,0},{3,1},{4,6},{5,7},{6,4},{7,5},{8,10},{9,11},{10,... | collective-permute-start | bytes 786440 | tf_op jit(solution)/shard_map/ppermute | solution.py:30
  251.5 74.9 %collective-permute-start.31 = (bf16[2,2,2,2,88,1024]{5,4,0,1,3,2:T(8,128)(2,1)}, bf16[2,2,2,2,88,1024]{5,4,0,1,3,2:T(8,128)(2,1)}, u32[]{:S(2)}, u32[]{:S(2)}) collective-permute-start(bf16[2,2,2,2,88,1024]{5,4,0,1,3,2:T(8,128)(2,1)} %bitcast.221), channel_id=1, source_target_pairs={{0,4},{4,0},{8,12},{12,8},{16,20},{20,16},{24,28},{28,24},{1,5},{5... | collective-permute-start | bytes 8650760 | tf_op jit(solution)/shard_map/ppermute | solution.py:30
  258.4 74.3 %collective-permute-start.16 = (bf16[2,2,2,2,32,3072]{5,4,3,2,1,0:T(8,128)(2,1)}, bf16[2,2,2,2,32,3072]{5,4,3,2,1,0:T(8,128)(2,1)}, u32[]{:S(2)}, u32[]{:S(2)}) collective-permute-start(bf16[2,2,2,2,32,3072]{5,4,3,2,1,0:T(8,128)(2,1)} %dynamic-slice_bitcast_fusion.1), channel_id=1, source_target_pairs={{0,4},{4,0},{8,12},{12,8},{16,20},{20,16},{24,28},{28,24},{1,5},{5... | collective-permute-start | bytes 9437192 | tf_op jit(solution)/shard_map/ppermute | solution.py:30
  259.2 77.0 %collective-permute-start.21 = (bf16[2,2,2,2,32,3072]{5,4,3,2,1,0:T(8,128)(2,1)}, bf16[2,2,2,2,32,3072]{5,4,3,2,1,0:T(8,128)(2,1)}, u32[]{:S(2)}, u32[]{:S(2)}) collective-permute-start(bf16[2,2,2,2,32,3072]{5,4,3,2,1,0:T(8,128)(2,1)} %dynamic-slice_bitcast_fusion), channel_id=1, source_target_pairs={{0,4},{4,0},{8,12},{12,8},{16,20},{20,16},{24,28},{28,24},{1,5},{5... | collective-permute-start | bytes 9437192 | tf_op jit(solution)/shard_map/ppermute | solution.py:30
  261.5 6.5 %collective-permute-start.13 = (bf16[128,512]{1,0:T(8,128)(2,1)S(1)}, bf16[128,512]{1,0:T(8,128)(2,1)S(1)}, u32[]{:S(2)}, u32[]{:S(2)}) collective-permute-start(bf16[128,512]{1,0:T(8,128)(2,1)S(1)} %get-tuple-element.61), channel_id=1, source_target_pairs={{0,2},{1,3},{2,0},{3,1},{4,6},{5,7},{6,4},{7,5},{8,10},{9,11},{10,... | collective-permute-start | bytes 393224 | tf_op jit(solution)/shard_map/ppermute | solution.py:30
  265.5 8.2 %collective-permute-start.9 = (bf16[256,512]{1,0:T(8,128)(2,1)S(1)}, bf16[256,512]{1,0:T(8,128)(2,1)S(1)}, u32[]{:S(2)}, u32[]{:S(2)}) collective-permute-start(bf16[256,512]{1,0:T(8,128)(2,1)S(1)} %get-tuple-element.58), channel_id=1, source_target_pairs={{0,2},{1,3},{2,0},{3,1},{4,6},{5,7},{6,4},{7,5},{8,10},{9,11},{10,... | collective-permute-start | bytes 786440 | tf_op jit(solution)/shard_map/ppermute | solution.py:30
  268.0 168.0 %collective-permute-start.26 = (bf16[2,2,2,2,32,5632]{5,4,0,1,2,3:T(8,128)(2,1)}, bf16[2,2,2,2,32,5632]{5,4,0,1,2,3:T(8,128)(2,1)}, u32[]{:S(2)}, u32[]{:S(2)}) collective-permute-start(bf16[2,2,2,2,32,5632]{5,4,0,1,2,3:T(8,128)(2,1)} %bitcast.220), channel_id=1, source_target_pairs={{0,4},{4,0},{8,12},{12,8},{16,20},{20,16},{24,28},{28,24},{1,5},{5... | collective-permute-start | bytes 17301512 | tf_op jit(solution)/shard_map/ppermute | solution.py:30
  273.7 7.4 %collective-permute-start.11 = (bf16[256,512]{1,0:T(8,128)(2,1)S(1)}, bf16[256,512]{1,0:T(8,128)(2,1)S(1)}, u32[]{:S(2)}, u32[]{:S(2)}) collective-permute-start(bf16[256,512]{1,0:T(8,128)(2,1)S(1)} %get-tuple-element.57), channel_id=1, source_target_pairs={{0,1},{1,0},{2,3},{3,2},{4,5},{5,4},{6,7},{7,6},{8,9},{9,8},{10,11... | collective-permute-start | bytes 786440 | tf_op jit(solution)/shard_map/ppermute | solution.py:30
  330.0 35.2 %collective-permute-start.32 = (bf16[2,2,2,88,1024]{4,3,0,1,2:T(8,128)(2,1)S(1)}, bf16[2,2,2,88,1024]{4,3,0,1,2:T(8,128)(2,1)S(1)}, u32[]{:S(2)}, u32[]{:S(2)}) collective-permute-start(bf16[2,2,2,88,1024]{4,3,0,1,2:T(8,128)(2,1)S(1)} %dynamic-slice_bitcast_fusion.5), channel_id=1, source_target_pairs={{0,2},{1,3},{2,0},{3,1},{4,6},{5,7},{6,4},{7,5},{8,10},{9,11},{10,... | collective-permute-start | bytes 4325384 | tf_op jit(solution)/shard_map/ppermute | solution.py:30
  335.9 63.0 %collective-permute-start.17 = (bf16[2,2,2,32,3072]{4,3,2,1,0:T(8,128)(2,1)S(1)}, bf16[2,2,2,32,3072]{4,3,2,1,0:T(8,128)(2,1)S(1)}, u32[]{:S(2)}, u32[]{:S(2)}) collective-permute-start(bf16[2,2,2,32,3072]{4,3,2,1,0:T(8,128)(2,1)S(1)} %dynamic-slice_bitcast_fusion.4), channel_id=1, source_target_pairs={{0,2},{1,3},{2,0},{3,1},{4,6},{5,7},{6,4},{7,5},{8,10},{9,11},{10,... | collective-permute-start | bytes 4718600 | tf_op jit(solution)/shard_map/ppermute | solution.py:30
  339.4 91.0 %collective-permute-start.22 = (bf16[2,2,2,32,3072]{4,3,2,1,0:T(8,128)(2,1)S(1)}, bf16[2,2,2,32,3072]{4,3,2,1,0:T(8,128)(2,1)S(1)}, u32[]{:S(2)}, u32[]{:S(2)}) collective-permute-start(bf16[2,2,2,32,3072]{4,3,2,1,0:T(8,128)(2,1)S(1)} %dynamic-slice_bitcast_fusion.3), channel_id=1, source_target_pairs={{0,2},{1,3},{2,0},{3,1},{4,6},{5,7},{6,4},{7,5},{8,10},{9,11},{10,... | collective-permute-start | bytes 4718600 | tf_op jit(solution)/shard_map/ppermute | solution.py:30
  365.9 36.3 %collective-permute-start.33 = (bf16[2,2,88,1024]{3,2,0,1:T(8,128)(2,1)S(1)}, bf16[2,2,88,1024]{3,2,0,1:T(8,128)(2,1)S(1)}, u32[]{:S(2)}, u32[]{:S(2)}) collective-permute-start(bf16[2,2,88,1024]{3,2,0,1:T(8,128)(2,1)S(1)} %dynamic-slice_bitcast_fusion.9), channel_id=1, source_target_pairs={{0,1},{1,0},{2,3},{3,2},{4,5},{5,4},{6,7},{7,6},{8,9},{9,8},{10,11... | collective-permute-start | bytes 2162696 | tf_op jit(solution)/shard_map/ppermute | solution.py:30
  400.5 42.3 %collective-permute-start.18 = (bf16[2,2,32,3072]{3,2,1,0:T(8,128)(2,1)}, bf16[2,2,32,3072]{3,2,1,0:T(8,128)(2,1)}, u32[]{:S(2)}, u32[]{:S(2)}) collective-permute-start(bf16[2,2,32,3072]{3,2,1,0:T(8,128)(2,1)} %dynamic-slice_bitcast_fusion.8), channel_id=1, source_target_pairs={{0,1},{1,0},{2,3},{3,2},{4,5},{5,4},{6,7},{7,6},{8,9},{9,8},{10,11... | collective-permute-start | bytes 2359304 | tf_op jit(solution)/shard_map/ppermute | solution.py:30
  402.5 31.0 %collective-permute-start.34 = (bf16[2,88,1024]{2,1,0:T(8,128)(2,1)S(1)}, bf16[2,88,1024]{2,1,0:T(8,128)(2,1)S(1)}, u32[]{:S(2)}, u32[]{:S(2)}) collective-permute-start(bf16[2,88,1024]{2,1,0:T(8,128)(2,1)S(1)} %dynamic-slice_bitcast_fusion.13), channel_id=1, source_target_pairs={{0,8},{4,12},{8,0},{12,4},{16,24},{20,28},{24,16},{28,20},{1,9},{5... | collective-permute-start | bytes 1081352 | tf_op jit(solution)/shard_map/ppermute | solution.py:30
  431.9 20.8 %collective-permute-start.23 = (bf16[2,2,32,3072]{3,2,1,0:T(8,128)(2,1)}, bf16[2,2,32,3072]{3,2,1,0:T(8,128)(2,1)}, u32[]{:S(2)}, u32[]{:S(2)}) collective-permute-start(bf16[2,2,32,3072]{3,2,1,0:T(8,128)(2,1)} %dynamic-slice_bitcast_fusion.7), channel_id=1, source_target_pairs={{0,1},{1,0},{2,3},{3,2},{4,5},{5,4},{6,7},{7,6},{8,9},{9,8},{10,11... | collective-permute-start | bytes 2359304 | tf_op jit(solution)/shard_map/ppermute | solution.py:30
  433.6 22.0 %collective-permute-start.35 = (bf16[88,1024]{1,0:T(8,128)(2,1)S(1)}, bf16[88,1024]{1,0:T(8,128)(2,1)S(1)}, u32[]{:S(2)}, u32[]{:S(2)}) collective-permute-start(bf16[88,1024]{1,0:T(8,128)(2,1)S(1)} %dynamic-slice_bitcast_fusion.17), channel_id=1, source_target_pairs={{0,16},{4,20},{8,24},{12,28},{16,0},{20,4},{24,8},{28,12},{1,17},{... | collective-permute-start | bytes 540680 | tf_op jit(solution)/shard_map/ppermute | solution.py:30
  442.3 68.9 %collective-permute-start.27 = (bf16[2,2,2,32,5632]{4,3,0,1,2:T(8,128)(2,1)S(1)}, bf16[2,2,2,32,5632]{4,3,0,1,2:T(8,128)(2,1)S(1)}, u32[]{:S(2)}, u32[]{:S(2)}) collective-permute-start(bf16[2,2,2,32,5632]{4,3,0,1,2:T(8,128)(2,1)S(1)} %dynamic-slice_bitcast_fusion.2), channel_id=1, source_target_pairs={{0,1},{1,0},{2,3},{3,2},{4,5},{5,4},{6,7},{7,6},{8,9},{9,8},{10,11... | collective-permute-start | bytes 8650760 | tf_op jit(solution)/shard_map/ppermute | solution.py:30
  444.2 12.3 %collective-permute-start.19 = (bf16[2,32,3072]{2,1,0:T(8,128)(2,1)S(1)}, bf16[2,32,3072]{2,1,0:T(8,128)(2,1)S(1)}, u32[]{:S(2)}, u32[]{:S(2)}) collective-permute-start(bf16[2,32,3072]{2,1,0:T(8,128)(2,1)S(1)} %dynamic-slice_bitcast_fusion.12), channel_id=1, source_target_pairs={{0,8},{4,12},{8,0},{12,4},{16,24},{20,28},{24,16},{28,20},{1,9},{5... | collective-permute-start | bytes 1179656 | tf_op jit(solution)/shard_map/ppermute | solution.py:30
  454.1 59.2 %collective-permute-start.24 = (bf16[2,32,3072]{2,1,0:T(8,128)(2,1)S(1)}, bf16[2,32,3072]{2,1,0:T(8,128)(2,1)S(1)}, u32[]{:S(2)}, u32[]{:S(2)}) collective-permute-start(bf16[2,32,3072]{2,1,0:T(8,128)(2,1)S(1)} %dynamic-slice_bitcast_fusion.11), channel_id=1, source_target_pairs={{0,8},{4,12},{8,0},{12,4},{16,24},{20,28},{24,16},{28,20},{1,9},{5... | collective-permute-start | bytes 1179656 | tf_op jit(solution)/shard_map/ppermute | solution.py:30
  456.6 59.3 %collective-permute-start.20 = (bf16[32,3072]{1,0:T(8,128)(2,1)S(1)}, bf16[32,3072]{1,0:T(8,128)(2,1)S(1)}, u32[]{:S(2)}, u32[]{:S(2)}) collective-permute-start(bf16[32,3072]{1,0:T(8,128)(2,1)S(1)} %dynamic-slice_bitcast_fusion.16), channel_id=1, source_target_pairs={{0,16},{4,20},{8,24},{12,28},{16,0},{20,4},{24,8},{28,12},{1,17},{... | collective-permute-start | bytes 589832 | tf_op jit(solution)/shard_map/ppermute | solution.py:30
  512.1 30.5 %collective-permute-start.28 = (bf16[2,2,32,5632]{3,2,0,1:T(8,128)(2,1)S(1)}, bf16[2,2,32,5632]{3,2,0,1:T(8,128)(2,1)S(1)}, u32[]{:S(2)}, u32[]{:S(2)}) collective-permute-start(bf16[2,2,32,5632]{3,2,0,1:T(8,128)(2,1)S(1)} %dynamic-slice_bitcast_fusion.6), channel_id=1, source_target_pairs={{0,2},{1,3},{2,0},{3,1},{4,6},{5,7},{6,4},{7,5},{8,10},{9,11},{10,... | collective-permute-start | bytes 4325384 | tf_op jit(solution)/shard_map/ppermute | solution.py:30
  513.4 31.8 %collective-permute-start.25 = (bf16[32,3072]{1,0:T(8,128)(2,1)S(1)}, bf16[32,3072]{1,0:T(8,128)(2,1)S(1)}, u32[]{:S(2)}, u32[]{:S(2)}) collective-permute-start(bf16[32,3072]{1,0:T(8,128)(2,1)S(1)} %dynamic-slice_bitcast_fusion.15), channel_id=1, source_target_pairs={{0,16},{4,20},{8,24},{12,28},{16,0},{20,4},{24,8},{28,12},{1,17},{... | collective-permute-start | bytes 589832 | tf_op jit(solution)/shard_map/ppermute | solution.py:30
  543.0 16.1 %collective-permute-start.29 = (bf16[2,32,5632]{2,1,0:T(8,128)(2,1)S(1)}, bf16[2,32,5632]{2,1,0:T(8,128)(2,1)S(1)}, u32[]{:S(2)}, u32[]{:S(2)}) collective-permute-start(bf16[2,32,5632]{2,1,0:T(8,128)(2,1)S(1)} %dynamic-slice_bitcast_fusion.10), channel_id=1, source_target_pairs={{0,8},{4,12},{8,0},{12,4},{16,24},{20,28},{24,16},{28,20},{1,9},{5... | collective-permute-start | bytes 2162696 | tf_op jit(solution)/shard_map/ppermute | solution.py:30
  559.3 12.3 %collective-permute-start.30 = (bf16[32,5632]{1,0:T(8,128)(2,1)S(1)}, bf16[32,5632]{1,0:T(8,128)(2,1)S(1)}, u32[]{:S(2)}, u32[]{:S(2)}) collective-permute-start(bf16[32,5632]{1,0:T(8,128)(2,1)S(1)} %dynamic-slice_bitcast_fusion.14), channel_id=1, source_target_pairs={{0,16},{4,20},{8,24},{12,28},{16,0},{20,4},{24,8},{28,12},{1,17},{... | collective-permute-start | bytes 1081352 | tf_op jit(solution)/shard_map/ppermute | solution.py:30
  (60 other events, 519.9 us)

commit v2 on v1

v2 whole, which is shorter than its diff:
```python
import functools

import jax
import jax.numpy as jnp
from jax import lax
from jax.experimental import pallas as pl
from jax.experimental.pallas import tpu as pltpu
from jax.sharding import PartitionSpec as P

HEAD_DIM = 64
EPSILON = 1e-06
NEGATIVE = -1e30
SCALE = HEAD_DIM ** (-0.5)
LANES = 128
PAIR = 2 * HEAD_DIM
SLAB = 512
STEP_ELEMENTS = 768 * 1024
F32 = jnp.float32
BF16 = jnp.bfloat16
VMEM_LIMIT = 56 * 1024 * 1024

NT = (((1,), (1,)), ((), ()))
NN = (((1,), (0,)), ((), ()))
TN = (((0,), (0,)), ((), ()))


def dot32(a, b, dims=NN):
    return lax.dot_general(a, b, dims, preferred_element_type=F32)


def swap(x, axis, bit):
    return lax.ppermute(x, axis, [(i, i ^ bit) for i in range(lax.axis_size(axis))])


def gather_relative(x, later):
    size = lax.axis_size("blk")
    if size == 4:
        half = x.shape[0] // 2
        one, two = swap(x, "blk", 1), swap(x, "blk", 2)
        far_a, far_b, later = tie(swap(one[:half], "blk", 2), swap(two[half:], "blk", 1), later)
        return jnp.concatenate([x, one, two, far_a, far_b], axis=0), later
    bit = 1
    while bit < size:
        x = jnp.concatenate([x, swap(x, "blk", bit)], axis=0)
        bit *= 2
    return x, later


def trade(parts, axis, bit):
    return [swap(part, axis, k * bit) for k, part in enumerate(parts) if k]


def tie(*groups):
    return lax.optimization_barrier(groups)


def row_blocks(x, count):
    length = x.shape[0] // count
    return [x[k * length : (k + 1) * length] for k in range(count)]


def column_blocks(x, count):
    width = x.shape[1] // count
    return [x[:, k * width : (k + 1) * width] for k in range(count)]


def add16(a, b):
    return (a.astype(F32) + b.astype(F32)).astype(BF16)


def sum_everywhere(x):
    for axis, low in (("dp", 0), ("blk", 0), ("dp", 1)):
        bits = lax.axis_size(axis).bit_length() - 1
        high = 1 if axis == "dp" and low == 0 else bits
        while low < high:
            if high - low >= 2:
                one, two, three = trade([x] * 4, axis, 1 << low)
                x = (x + one) + (two + three)
                low += 2
            else:
                x = x + swap(x, axis, 1 << low)
                low += 1
    return x


def sum_rows(x, first_blk_bit):
    dp_bits = lax.axis_size("dp").bit_length() - 1
    blk_bits = lax.axis_size("blk").bit_length() - 1
    rest = [("dp", k) for k in reversed(range(dp_bits))] + [("blk", k) for k in reversed(range(blk_bits))]
    rows, width = x.shape
    x = x.reshape((2,) * len(rest) + (rows >> len(rest), width))
    order = [("dp", 0)]
    order += [("blk", (first_blk_bit + k) % blk_bits) for k in range(blk_bits)]
    order += [("dp", k) for k in range(1, dp_bits)]
    for axis, k in order:
        place = rest.index((axis, k))
        mine = (lax.axis_index(axis) >> k) & 1
        out = lax.dynamic_index_in_dim(x, 1 - mine, place, keepdims=False)
        keep = lax.dynamic_index_in_dim(x, mine, place, keepdims=False)
        got = swap(out, axis, 1 << k)
        rest.pop(place)
        x = keep.astype(F32) + got.astype(F32)
        if rest:
            x = x.astype(BF16)
    return x


def stacked(ref, kv):
    low = kv * PAIR
    return jnp.concatenate([ref[:, low : low + HEAD_DIM], ref[:, low + HEAD_DIM : low + PAIR]], axis=0)


def unstack(ref, kv, columns):
    length = columns.shape[1] // 2
    rows = columns.T
    low = kv * PAIR
    ref[:, low : low + HEAD_DIM] = rows[:length].astype(ref.dtype)
    ref[:, low + HEAD_DIM : low + PAIR] = rows[length:].astype(ref.dtype)


def spread_bias(bias_ref, tile_ref):
    heads, width = bias_ref.shape
    for h in range(heads):
        line = jnp.broadcast_to(bias_ref[h : h + 1, :], (LANES, width))
        tile_ref[h] = pltpu.roll(line, 0, 1, stride=1, stride_axis=0)


def bias_tile(tile_ref, kv, start, length):
    heads = []
    for g in range(2):
        parts = [
            tile_ref[2 * kv + g, :, pl.ds(pl.multiple_of(start - LANES * m, LANES), length)]
            for m in range(length // LANES)
        ]
        heads.append(jnp.concatenate(parts, axis=0))
    return jnp.concatenate(heads, axis=1)


def head_columns(kv_local, kv):
    return kv * PAIR, kv_local * PAIR + kv * HEAD_DIM, kv_local * (PAIR + HEAD_DIM) + kv * HEAD_DIM


def two_heads(ref, rows, low):
    return jnp.concatenate([ref[rows, low : low + HEAD_DIM], ref[rows, low + HEAD_DIM : low + PAIR]], axis=0)


def self_forward_kernel(blocks, kv_local, my_ref, qkv_ref, bias_ref, mix_ref, lse_ref, tile_ref, top_ref, sum_ref, acc_ref):
    a = pl.program_id(0)
    length = qkv_ref.shape[0] // blocks
    my = my_ref[0]
    mine = my ^ a

    @pl.when(a == 0)
    def _():
        spread_bias(bias_ref, tile_ref)

    rows = pl.ds(pl.multiple_of(a * length, length), length)
    top_ref[...] = jnp.full_like(top_ref, NEGATIVE)
    sum_ref[...] = jnp.zeros_like(sum_ref)
    acc_ref[...] = jnp.zeros_like(acc_ref)
    for b in range(blocks):
        source = my ^ b
        keys_at = slice(b * length, (b + 1) * length)

        @pl.when(source <= mine)
        def _(source=source, keys_at=keys_at):
            start = length + length * (mine - source)
            for kv in range(kv_local):
                q_at, k_at, v_at = head_columns(kv_local, kv)
                qq = two_heads(qkv_ref, rows, q_at)
                keys = qkv_ref[keys_at, k_at : k_at + HEAD_DIM]
                values = qkv_ref[keys_at, v_at : v_at + HEAD_DIM]
                scores = dot32(keys, qq, NT) * SCALE + bias_tile(tile_ref, kv, start, length)
                old = top_ref[kv]
                new = jnp.maximum(old, jnp.max(scores, axis=0, keepdims=True))
                weights = jnp.exp(scores - new)
                shrink = jnp.exp(old - new)
                top_ref[kv] = new
                sum_ref[kv] = sum_ref[kv] * shrink + jnp.sum(weights, axis=0, keepdims=True)
                acc_ref[kv] = acc_ref[kv] * shrink + dot32(values, weights.astype(BF16), TN)

    for kv in range(kv_local):
        unstack(mix_ref, kv, acc_ref[kv] / sum_ref[kv])
        lse_ref[0, kv] = top_ref[kv] + jnp.log(sum_ref[kv])


def self_backward_kernel(blocks, kv_local, my_ref, qkv_ref, bias_ref, mix_ref, lse_ref, grad_ref, out_ref, dbias_ref, tile_ref, diag_ref, dq_ref, dk_ref, dv_ref):
    a = pl.program_id(0)
    length = qkv_ref.shape[0] // blocks
    width = bias_ref.shape[1]
    my = my_ref[0]
    mine = my ^ a

    @pl.when(a == 0)
    def _():
        spread_bias(bias_ref, tile_ref)
        diag_ref[...] = jnp.zeros_like(diag_ref)
        dk_ref[...] = jnp.zeros_like(dk_ref)
        dv_ref[...] = jnp.zeros_like(dv_ref)

    rows = pl.ds(pl.multiple_of(a * length, length), length)
    every = slice(0, length)
    dq_ref[...] = jnp.zeros_like(dq_ref)
    deltas = []
    for kv in range(kv_local):
        both = two_heads(grad_ref, every, kv * PAIR).astype(F32) * two_heads(mix_ref, every, kv * PAIR).astype(F32)
        deltas.append(jnp.sum(both.T, axis=0, keepdims=True))
    for b in range(blocks):
        source = my ^ b
        keys_at = slice(b * length, (b + 1) * length)

        @pl.when(source <= mine)
        def _(source=source, keys_at=keys_at):
            start = length + length * (mine - source)
            for kv in range(kv_local):
                q_at, k_at, v_at = head_columns(kv_local, kv)
                qq = two_heads(qkv_ref, rows, q_at)
                dd = two_heads(grad_ref, every, q_at)
                keys = qkv_ref[keys_at, k_at : k_at + HEAD_DIM]
                values = qkv_ref[keys_at, v_at : v_at + HEAD_DIM]
                scores = dot32(keys, qq, NT) * SCALE + bias_tile(tile_ref, kv, start, length)
                probs = jnp.exp(scores - lse_ref[0, kv])
                dv_ref[kv, keys_at, :] += dot32(probs.astype(BF16), dd)
                change = dot32(values, dd, NT) - deltas[kv]
                ds = (probs * change).astype(BF16)
                dk_ref[kv, keys_at, :] += dot32(ds, qq)
                dq_ref[kv] += dot32(keys, ds, TN)
                ds = ds.astype(F32)
                for g in range(2):
                    for m in range(length // LANES):
                        where = pl.ds(pl.multiple_of(start - LANES * m, LANES), length)
                        diag_ref[2 * kv + g, :, where] += ds[m * LANES : (m + 1) * LANES, g * length : (g + 1) * length]

    for kv in range(kv_local):
        back = (dq_ref[kv] * SCALE).T.astype(BF16)
        out_ref[rows, kv * PAIR : kv * PAIR + HEAD_DIM] = back[:length]
        out_ref[rows, kv * PAIR + HEAD_DIM : (kv + 1) * PAIR] = back[length:]

    @pl.when(a == blocks - 1)
    def _():
        for kv in range(kv_local):
            _, k_at, v_at = head_columns(kv_local, kv)
            out_ref[:, k_at : k_at + HEAD_DIM] = (dk_ref[kv] * SCALE).astype(BF16)
            out_ref[:, v_at : v_at + HEAD_DIM] = dv_ref[kv].astype(BF16)
        for h in range(2 * kv_local):
            part = diag_ref[h]
            half = LANES // 2
            while half:
                part = part[:half] + pltpu.roll(part[half:], width - half, 1)
                half //= 2
            dbias_ref[h : h + 1, :] = part


def cross_forward_kernel(allow_ref, q_ref, k_ref, v_ref, mix_ref, lse_ref):
    allow = allow_ref[...] > 0
    for kv in range(2):
        low = kv * HEAD_DIM
        qq = stacked(q_ref, kv)
        scores = dot32(k_ref[:, low : low + HEAD_DIM], qq, NT) * SCALE
        scores = jnp.where(allow, scores, NEGATIVE)
        top = jnp.max(scores, axis=0, keepdims=True)
        raised = jnp.exp(scores - top)
        total = jnp.sum(raised, axis=0, keepdims=True)
        probs = (raised * (1.0 / total)).astype(BF16)
        unstack(mix_ref, kv, dot32(v_ref[:, low : low + HEAD_DIM], probs, TN))
        lse_ref[kv] = top + jnp.log(total)


def cross_backward_kernel(allow_ref, q_ref, k_ref, v_ref, lse_ref, grad_ref, dq_ref, dkv_ref):
    allow = allow_ref[...] > 0
    for kv in range(2):
        low = kv * HEAD_DIM
        qq = stacked(q_ref, kv)
        dd = stacked(grad_ref, kv)
        keys = k_ref[:, low : low + HEAD_DIM]
        scores = jnp.where(allow, dot32(keys, qq, NT) * SCALE, NEGATIVE)
        probs = jnp.exp(scores - lse_ref[kv])
        change = dot32(v_ref[:, low : low + HEAD_DIM], dd, NT)
        delta = jnp.sum(probs * change, axis=0, keepdims=True)
        ds = (probs * (change - delta)).astype(BF16)
        dkv_ref[1, :, low : low + HEAD_DIM] = dot32(probs.astype(BF16), dd).astype(BF16)
        dkv_ref[0, :, low : low + HEAD_DIM] = (dot32(ds, qq) * SCALE).astype(BF16)
        unstack(dq_ref, kv, dot32(keys, ds, TN) * SCALE)


TINY = pl.CostEstimate(flops=1, transcendentals=0, bytes_accessed=1)


def params():
    return pltpu.CompilerParams(dimension_semantics=("arbitrary",), vmem_limit_bytes=VMEM_LIMIT)


def cost(length, keys, heads, passes, moved):
    return pl.CostEstimate(
        flops=2 * length * keys * heads * HEAD_DIM * passes,
        transcendentals=length * keys * heads,
        bytes_accessed=moved,
    )


def lane_block(rows, width):
    return pl.BlockSpec((rows, width), lambda i: (0, i))


def self_forward(blocks, my, qkv, bias):
    tokens, columns = qkv.shape
    length, kv_local, width = tokens // blocks, columns // (2 * PAIR), bias.shape[1]
    q_width = kv_local * PAIR
    return pl.pallas_call(
        functools.partial(self_forward_kernel, blocks, kv_local),
        grid=(blocks,),
        in_specs=[
            pl.BlockSpec(memory_space=pltpu.SMEM),
            pl.BlockSpec((tokens, columns), lambda i: (0, 0)),
            pl.BlockSpec(bias.shape, lambda i: (0, 0)),
        ],
        out_specs=[
            pl.BlockSpec((length, q_width), lambda i: (i, 0)),
            pl.BlockSpec((1, kv_local, 1, 2 * length), lambda i: (i, 0, 0, 0)),
        ],
        out_shape=[
            jax.ShapeDtypeStruct((tokens, q_width), BF16),
            jax.ShapeDtypeStruct((blocks, kv_local, 1, 2 * length), F32),
        ],
        scratch_shapes=[
            pltpu.VMEM((2 * kv_local, LANES, width), F32),
            pltpu.VMEM((kv_local, 1, 2 * length), F32),
            pltpu.VMEM((kv_local, 1, 2 * length), F32),
            pltpu.VMEM((kv_local, HEAD_DIM, 2 * length), F32),
        ],
        compiler_params=params(),
        cost_estimate=TINY,
        name="self_forward",
    )(my, qkv, bias)


def self_backward(blocks, my, qkv, bias, mix, lse, grad):
    tokens, columns = qkv.shape
    length, kv_local, width = tokens // blocks, columns // (2 * PAIR), bias.shape[1]
    q_width = kv_local * PAIR
    whole = pl.BlockSpec((tokens, columns), lambda i: (0, 0))
    lines = pl.BlockSpec(bias.shape, lambda i: (0, 0))
    return pl.pallas_call(
        functools.partial(self_backward_kernel, blocks, kv_local),
        grid=(blocks,),
        in_specs=[
            pl.BlockSpec(memory_space=pltpu.SMEM),
            whole,
            lines,
            pl.BlockSpec((length, q_width), lambda i: (i, 0)),
            pl.BlockSpec((1, kv_local, 1, 2 * length), lambda i: (i, 0, 0, 0)),
            pl.BlockSpec((length, q_width), lambda i: (i, 0)),
        ],
        out_specs=[whole, lines],
        out_shape=[
            jax.ShapeDtypeStruct(qkv.shape, BF16),
            jax.ShapeDtypeStruct(bias.shape, F32),
        ],
        scratch_shapes=[
            pltpu.VMEM((2 * kv_local, LANES, width), F32),
            pltpu.VMEM((2 * kv_local, LANES, width), F32),
            pltpu.VMEM((kv_local, HEAD_DIM, 2 * length), F32),
            pltpu.VMEM((kv_local, tokens, HEAD_DIM), F32),
            pltpu.VMEM((kv_local, tokens, HEAD_DIM), F32),
        ],
        compiler_params=params(),
        cost_estimate=TINY,
        name="self_backward",
    )(my, qkv, bias, mix, lse, grad)


def cross_forward(allow, q, k, v):
    length, keys, kv_heads = q.shape[0], k.shape[0], k.shape[1] // HEAD_DIM
    return pl.pallas_call(
        cross_forward_kernel,
        grid=(kv_heads // 2,),
        in_specs=[
            pl.BlockSpec((keys, 1), lambda i: (0, 0)),
            lane_block(length, 2 * PAIR),
            lane_block(keys, PAIR),
            lane_block(keys, PAIR),
        ],
        out_specs=[
            lane_block(length, 2 * PAIR),
            pl.BlockSpec((2, 1, 2 * length), lambda i: (i, 0, 0)),
        ],
        out_shape=[
            jax.ShapeDtypeStruct(q.shape, BF16),
            jax.ShapeDtypeStruct((kv_heads, 1, 2 * length), F32),
        ],
        compiler_params=params(),
        cost_estimate=TINY,
        name="cross_forward",
    )(allow, q, k, v)


def cross_backward(allow, q, k, v, lse, grad):
    length, keys, kv_heads = q.shape[0], k.shape[0], k.shape[1] // HEAD_DIM
    return pl.pallas_call(
        cross_backward_kernel,
        grid=(kv_heads // 2,),
        in_specs=[
            pl.BlockSpec((keys, 1), lambda i: (0, 0)),
            lane_block(length, 2 * PAIR),
            lane_block(keys, PAIR),
            lane_block(keys, PAIR),
            pl.BlockSpec((2, 1, 2 * length), lambda i: (i, 0, 0)),
            lane_block(length, 2 * PAIR),
        ],
        out_specs=[
            lane_block(length, 2 * PAIR),
            pl.BlockSpec((2, keys, PAIR), lambda i: (0, 0, i)),
        ],
        out_shape=[
            jax.ShapeDtypeStruct(q.shape, BF16),
            jax.ShapeDtypeStruct((2,) + k.shape, BF16),
        ],
        compiler_params=params(),
        cost_estimate=TINY,
        name="cross_backward",
    )(allow, q, k, v, lse, grad)


def slab_kernel(kind, later, order_ref, x_ref, g_ref, *refs):
    keep_ref, send_ref, turned_ref, whole_ref = refs[-4:]
    slab = pl.program_id(0)
    kind = jnp.where(slab < later, 0, 1) if kind is None else kind

    @pl.when(slab == 0)
    def _():
        turned_ref[...] = x_ref[...].T

    chunks, rows, width = whole_ref.shape
    whole_ref[...] = dot32(turned_ref[...], g_ref[...]).reshape(chunks, rows, width)
    half = chunks // 2
    for c in range(half):
        keep_ref[c] = whole_ref[order_ref[kind, c]].astype(BF16)
        send_ref[c] = whole_ref[order_ref[kind, half + c]].astype(BF16)


def slabs(order, x, g, total, at, later, buffers, kind=None, slab=SLAB):
    tokens, features = x.shape
    chunks = order.shape[1]
    rows = features // chunks
    if g.ndim == 3:
        count = g.shape[0]
        g_spec = pl.BlockSpec((None, tokens, slab), lambda i: (i, 0, 0))
    else:
        count = g.shape[1] // slab
        g_spec = pl.BlockSpec((tokens, slab), lambda i: (0, i))
    assert at % rows == 0 and features % chunks == 0 and rows % 8 == 0
    out = pl.BlockSpec((chunks // 2, rows, slab), lambda i: (0, at // rows + i, 0))
    shape = jax.ShapeDtypeStruct((chunks // 2, total, slab), BF16)
    extra = [] if buffers is None else list(buffers)
    return pl.pallas_call(
        functools.partial(slab_kernel, kind, later),
        grid=(count,),
        in_specs=[
            pl.BlockSpec(memory_space=pltpu.SMEM),
            pl.BlockSpec((tokens, features), lambda i: (0, 0)),
            g_spec,
        ]
        + [pl.BlockSpec(memory_space=pl.ANY)] * len(extra),
        out_specs=[out, out],
        out_shape=[shape, shape],
        scratch_shapes=[pltpu.VMEM((features, tokens), BF16), pltpu.VMEM((chunks, rows, slab), F32)],
        input_output_aliases={3: 0, 4: 1} if extra else {},
        compiler_params=params(),
        cost_estimate=TINY,
        name="slabs",
    )(order, x, g, *extra)


def sum_pieces(pieces, offset, count, outs):
    places = [(start, start + array.shape[1]) for array, start in pieces]
    cuts = sorted({p for place in places for p in place} | {p for out in outs for p in out})
    width = pieces[0][0].shape[2]
    step = count
    while step % 2 == 0 and step * (places[0][1] - places[0][0]) * width > STEP_ELEMENTS:
        step //= 2
    first = offset // step
    assert first * step == offset
    return pl.pallas_call(
        functools.partial(sum_split_kernel, places, outs, cuts),
        grid=(count // step,),
        in_specs=[pl.BlockSpec((step,) + array.shape[1:], lambda i: (first + i, 0, 0)) for array, _ in pieces],
        out_specs=[pl.BlockSpec((step, high - low, width), lambda i: (i, 0, 0)) for low, high in outs],
        out_shape=[jax.ShapeDtypeStruct((count, high - low, width), BF16) for low, high in outs],
        compiler_params=params(),
        cost_estimate=TINY,
        name="sum_pieces",
    )(*[array for array, _ in pieces])


def add_range(places, pieces, low, high):
    total = None
    for (start, stop), piece in zip(places, pieces):
        if start <= low and high <= stop:
            part = piece[:, low - start : high - start, :].astype(F32)
            total = part if total is None else total + part
    return total


def sum_split_kernel(places, outs, cuts, *refs):
    pieces, results = refs[: len(places)], refs[len(places) :]
    for (low, high), result in zip(outs, results):
        inner = [c for c in cuts if low <= c <= high]
        for a, b in zip(inner[:-1], inner[1:]):
            result[:, a - low : b - low, :] = add_range(places, pieces, a, b).astype(result.dtype)


def finish_kernel(places, outs, *refs):
    pieces, results = refs[: len(places)], refs[len(places) :]
    for row, rows, number, column, start, width in outs:
        total = add_range(places, pieces, row, row + rows)[0]
        results[number][:, column : column + width] = total[:, start : start + width]


def finish(pieces, shapes, outs):
    places = [(start, start + array.shape[1]) for array, start in pieces]
    return pl.pallas_call(
        functools.partial(finish_kernel, places, outs),
        grid=(1,),
        in_specs=[pl.BlockSpec((1,) + array.shape[1:], lambda i: (0, 0, 0)) for array, _ in pieces],
        out_specs=[pl.BlockSpec(shape, lambda i: (0, 0)) for shape in shapes],
        out_shape=[jax.ShapeDtypeStruct(shape, F32) for shape in shapes],
        compiler_params=params(),
        cost_estimate=TINY,
        name="finish",
    )(*[array for array, _ in pieces])


def pair_dot_kernel(x_count, *refs):
    result = refs[-1]
    xs, gs = refs[:x_count], refs[x_count:-1]
    x = jnp.concatenate([ref[...] for ref in xs], axis=0)
    g = jnp.concatenate([ref[...] for ref in gs], axis=0)
    result[...] = dot32(x, g, TN).astype(BF16)


def pair_dot(xs, gs):
    features, width = xs[0].shape[1], gs[0].shape[1]
    return pl.pallas_call(
        functools.partial(pair_dot_kernel, len(xs)),
        grid=(1,),
        in_specs=[pl.BlockSpec(x.shape, lambda i: (0, 0)) for x in list(xs) + list(gs)],
        out_specs=pl.BlockSpec((features, width), lambda i: (0, 0)),
        out_shape=jax.ShapeDtypeStruct((features, width), BF16),
        compiler_params=params(),
        cost_estimate=TINY,
        name="pair_dot",
    )(*xs, *gs)


def place_kernel(share, widths, my_ref, *refs):
    count = len(widths) + 2
    parts, halves, results = refs[:-count], refs[-count : 2 - count], refs[2 - count :]
    per_half = len(parts) // 2
    for j, part in enumerate(parts):
        owner = my_ref[0] ^ j
        for number, result in enumerate(halves):

            @pl.when(owner // per_half == number)
            def _(part=part, result=result, number=number, owner=owner):
                columns = pl.ds(pl.multiple_of((owner - number * per_half) * share, LANES), share)
                result[:, columns] = part[:, :share].astype(F32)

        low = share
        for width, result in zip(widths, results):
            columns = pl.ds(pl.multiple_of(owner * width, LANES), width)
            result[:, columns] = part[:, low : low + width].astype(F32)
            low += width


def place(my, parts, share, widths):
    rows, count = parts[0].shape[0], len(parts)
    shapes = [(rows, count // 2 * share)] * 2 + [(rows, count * width) for width in widths]
    return pl.pallas_call(
        functools.partial(place_kernel, share, widths),
        grid=(1,),
        in_specs=[pl.BlockSpec(memory_space=pltpu.SMEM)] + [pl.BlockSpec(part.shape, lambda i: (0, 0)) for part in parts],
        out_specs=[pl.BlockSpec(shape, lambda i: (0, 0)) for shape in shapes],
        out_shape=[jax.ShapeDtypeStruct(shape, F32) for shape in shapes],
        compiler_params=params(),
        cost_estimate=TINY,
        name="place",
    )(my, *parts)


def exchange_order():
    dp, blk = lax.axis_size("dp"), lax.axis_size("blk")
    dp_bits, blk_bits = dp.bit_length() - 1, blk.bit_length() - 1
    mine = lax.axis_index("dp") * blk + lax.axis_index("blk")
    deep = list(reversed(range(blk_bits + 1, blk_bits + dp_bits)))
    up, down = list(range(blk_bits)), list(reversed(range(blk_bits)))
    tables = []
    for order in (up + deep, down + deep, deep + down, down + deep):
        order = [blk_bits] + order
        table = []
        for place in range(dp * blk):
            relative = 0
            for k, bit in enumerate(order):
                relative |= ((place >> (len(order) - 1 - k)) & 1) << bit
            table.append(relative)
        tables.append(table)
    return jnp.array(tables, jnp.int32) ^ mine.astype(jnp.int32)


def combine_kernel(plan, *refs):
    inputs, results = refs[: -len(plan)], refs[-len(plan) :]
    rows = results[0].shape[1]
    for sources, result in zip(plan, results):
        cuts = sorted({0, rows} | {r for _, row, size in sources for r in (row, row + size)})
        for a, b in zip(cuts[:-1], cuts[1:]):
            total = None
            for number, row, size in sources:
                if row <= a and b <= row + size:
                    part = inputs[number][0, a - row : b - row, :].astype(F32)
                    total = part if total is None else total + part
            result[0, a:b, :] = total.astype(result.dtype)


def combine(pieces, groups):
    plan, specs, arrays = [], [], []
    steps = groups[0][1] - groups[0][0]
    rows, width = max(array.shape[1] + row for array, row in pieces), pieces[0][0].shape[2]
    for low, _ in groups:
        sources = []
        for array, row in pieces:
            sources.append((len(arrays), row, array.shape[1]))
            arrays.append(array)
            specs.append(pl.BlockSpec((1,) + array.shape[1:], lambda i, low=low: (low + i, 0, 0)))
        plan.append(sources)
    out = pl.BlockSpec((1, rows, width), lambda i: (i, 0, 0))
    return pl.pallas_call(
        functools.partial(combine_kernel, plan),
        grid=(steps,),
        in_specs=specs,
        out_specs=[out] * len(groups),
        out_shape=[jax.ShapeDtypeStruct((steps, rows, width), BF16)] * len(groups),
        compiler_params=params(),
        cost_estimate=TINY,
        name="combine",
    )(*arrays)


class Exchange:
    def __init__(self, keep, send):
        self.send, self.pieces = send, [(keep, 0)]

    def core(self):
        self.got = [swap(self.send, "dp", 1)]

    def pack(self):
        self.pieces += [(got, 0) for got in self.got]
        step = self.got[0].shape[0] // 4
        self.out = combine(self.pieces, [(k * step, (k + 1) * step) for k in range(1, 4)])

    def hop(self, axis, bit):
        self.got = trade([None, *self.out], axis, bit)

    def done(self, row=0):
        return [(array, row) for array, _ in self.pieces + [(got, 0) for got in self.got]]


class Halves:
    def __init__(self, keep, send, cut):
        self.cut, self.total = cut, keep.shape[1]
        self.parts = [(0, cut), (cut, self.total)]
        self.pieces, self.send = [(keep, 0)], send

    def core(self):
        self.got = [swap(self.send, "dp", 1)]

    def arrive(self):
        rows = [0] if len(self.got) == 1 else [low for low, _ in self.parts]
        self.pieces += list(zip(self.got, rows))

    def pack(self):
        self.arrive()
        half = self.got[0].shape[0] // 2
        self.out = sum_pieces(self.pieces, half, half, self.parts)

    def hop(self, bits):
        self.got = [swap(out, "blk", bit) for out, bit in zip(self.out, bits)]

    def pack_deep(self):
        self.arrive()
        self.out = combine(self.pieces, [(k, k + 1) for k in range(1, self.got[0].shape[0])])

    def hop_deep(self):
        self.got = trade([None, *self.out], "dp", 2)

    def done(self):
        return self.pieces + [(got, 0) for got in self.got]


def turn_rows(x, rows):
    my = lax.axis_index("blk")
    return jnp.concatenate([lax.dynamic_slice_in_dim(x, (my ^ j) * rows, rows, 0) for j in range(lax.axis_size("blk"))], axis=0)


def inverse_rms(x):
    return lax.rsqrt(jnp.mean(x * x, axis=-1, keepdims=True) + EPSILON)


def norm_back(x, inverse, gain, grad):
    scaled = grad * gain
    along = jnp.mean(scaled * x, axis=-1, keepdims=True)
    d_x = inverse * scaled - x * (inverse * inverse * inverse * along)
    return d_x, jnp.sum(grad * x * inverse, axis=0)


def body(
    block_in,
    memory,
    memory_len,
    cross_mask,
    buckets,
    bias_table,
    norm_self,
    w_query,
    w_key,
    w_value,
    w_out,
    norm_cross,
    cross_query,
    cross_key,
    cross_value,
    cross_out,
    norm_ffn,
    w_gate,
    w_up,
    w_down,
    grad_out,
):
    seq_count, length, model_width = block_in.shape
    assert seq_count == 1
    mem_rows = memory.shape[1]
    mem_total = cross_mask.shape[1]
    blocks = lax.axis_size("blk")
    my = lax.axis_index("blk")
    kv_width = w_key.shape[1]
    head_count = w_query.shape[1] // HEAD_DIM
    bucket_count = bias_table.shape[0]
    my_ref = my.reshape(1).astype(jnp.int32)

    x_all, mem_own = gather_relative(block_in[0], memory[0])
    mem_all = lax.all_gather(mem_own, "blk", axis=0, tiled=True)

    own_heads = head_count // blocks
    own_q, own_kv = own_heads * HEAD_DIM, kv_width // blocks
    turned_qkv = [
        jnp.concatenate(
            [
                lax.dynamic_slice_in_dim(w, (my ^ j) * width, width, 1)
                for w, width in ((w_query, own_q), (w_key, own_kv), (w_value, own_kv))
            ],
            axis=1,
        )
        for j in range(blocks)
    ]
    out_turned = jnp.concatenate([lax.dynamic_slice_in_dim(w_out, (my ^ j) * own_q, own_q, 0) for j in range(blocks)], axis=0)

    bucket_hot = (buckets[:, None] == jnp.arange(bucket_count)[None, :]).astype(F32)
    own_table = lax.dynamic_slice_in_dim(bias_table, my * own_heads, own_heads, 1)
    dist_bias = lax.dot_general(own_table, bucket_hot, (((0,), (1,)), ((), ())), precision=lax.Precision.HIGHEST)
    bias = jnp.concatenate([jnp.full((own_heads, length), NEGATIVE, F32), dist_bias], axis=1)

    mem_places = jnp.arange(mem_total)
    allowed = (mem_places == 0) | (mem_places < memory_len[0]) & (cross_mask[0] == 1)
    allow = allowed.astype(F32).reshape(mem_total, 1)

    stream_all = x_all.astype(F32)
    inv_self_all = inverse_rms(stream_all)
    self_all = (stream_all * inv_self_all * norm_self).astype(BF16)
    stream = block_in[0].astype(F32)
    inv_self = inv_self_all[:length]
    qkv = dot32(self_all, turned_qkv[0]).astype(BF16)
    own_mix, lse = self_forward(blocks, my_ref, qkv, bias)
    mix_parts = row_blocks(own_mix, blocks)
    mem_key = dot32(mem_all, cross_key).astype(BF16)
    mem_value = dot32(mem_all, cross_value).astype(BF16)
    mix_got, mem_key, mem_value = tie(trade(mix_parts, "blk", 1), mem_key, mem_value)
    self_mix = jnp.concatenate([mix_parts[0]] + mix_got, axis=1)
    after_self = stream + dot32(self_mix, out_turned)

    inv_cross = inverse_rms(after_self)
    cross_in = (after_self * inv_cross * norm_cross).astype(BF16)
    cross_q = dot32(cross_in, cross_query).astype(BF16)
    cross_mix, cross_lse = cross_forward(allow, cross_q, mem_key, mem_value)
    after_cross = after_self + dot32(cross_mix, cross_out)

    inv_ffn = inverse_rms(after_cross)
    ffn_in = (after_cross * inv_ffn * norm_ffn).astype(BF16)
    devices = blocks * lax.axis_size("dp")
    d, ff = model_width, w_gate.shape[1]
    share = 2 * ff // blocks
    fast = (
        blocks == 4
        and lax.axis_size("dp") == 8
        and d % (8 * devices) == 0
        and ff % (8 * devices) == 0
        and kv_width == SLAB
        and d % SLAB == 0
        and share % LANES == 0
    )
    gate = dot32(ffn_in, w_gate)
    up = dot32(ffn_in, w_up)
    (act, hidden_full), gated_back = jax.vjp(lambda g, u: (jax.nn.gelu(g, approximate=True), jax.nn.gelu(g, approximate=True) * u), gate, up)
    hidden = hidden_full.astype(BF16)

    ffn_grad = grad_out[0]
    grad_top = ffn_grad.astype(F32)
    d_hidden = dot32(ffn_grad, w_down, NT)
    gate_full, up_full = gated_back((jnp.zeros_like(act), d_hidden))
    gate_grad, up_grad = gate_full.astype(BF16), up_full.astype(BF16)
    if fast:
        order = exchange_order()
        turned = order ^ ((my * (devices // blocks)).astype(jnp.int32))
        small, large = d // devices, ff // devices
        d_slabs = d // SLAB
        half = length // 2
        near = trade([ffn_in] * 3, "blk", 1)
        gate_grad, up_grad, near = tie(gate_grad, up_grad, near)
        both_grad = jnp.concatenate([gate_grad, up_grad], axis=1)
        shares = [lax.dynamic_slice_in_dim(both_grad, (my ^ j) * share, share, 1) for j in range(blocks)]
        shares, hidden = tie(shares, hidden)
        shares_near = trade(shares[:3], "blk", 1)
        keep, send = slabs(order, hidden, ffn_grad, d_slabs * large, 0, 0, None, 3)
    else:
        dw_down = sum_rows(dot32(hidden, ffn_grad, TN).astype(BF16), 1)
        ffn_outs = (
            sum_rows(dot32(ffn_in, gate_grad, TN).astype(BF16), 0),
            sum_rows(dot32(ffn_in, up_grad, TN).astype(BF16), 1),
            dw_down,
        )
    d_ffn_norm = dot32(gate_grad, w_gate, NT) + dot32(up_grad, w_up, NT)
    if fast:
        down_got = swap(send, "dp", 1)
        d_ffn_norm, shares_near, shares[3], near, keep = tie(d_ffn_norm, shares_near, shares[3], near, keep)
        down = Exchange(keep, send)
        down.got = [down_got]
        far = [swap(near[0][:half], "blk", 2), swap(near[1][half:], "blk", 1)]
        share_far = swap(shares[3], "blk", 3)
    d_stream, d_gain_ffn = norm_back(after_cross, inv_ffn, norm_ffn, d_ffn_norm)
    grad_cross = grad_top + d_stream

    cross_grad = grad_cross.astype(BF16)
    mix_grad = dot32(cross_grad, cross_out, NT).astype(BF16)
    cq_grad, mem_part = cross_backward(allow, cross_q, mem_key, mem_value, cross_lse, mix_grad)
    if fast:
        cq_grad, mem_part, share_far, down.got = tie(cq_grad, mem_part, share_far, down.got)
        total = 4 * d_slabs * small
        held = slabs(order, cross_mix, cross_grad, total, 0, total, None)
    d_stream, d_gain_cross = norm_back(after_self, inv_cross, norm_cross, dot32(cq_grad, cross_query, NT))
    grad_self = grad_cross + d_stream

    self_grad = grad_self.astype(BF16)
    grad_parts = column_blocks(dot32(self_grad, out_turned, NT).astype(BF16), blocks)
    if fast:
        grad_parts, mem_part, down.got, far, held = tie(grad_parts, mem_part, down.got, far, held)
    grad_got = trade(grad_parts, "blk", 1)
    if fast:
        down.pack()
        grad_parts[0], down.out = tie(grad_parts[0], down.out)
        down.hop("blk", 1)
        held = slabs(order, cross_in, cq_grad, total, d_slabs * small, total, held)
        held = slabs(order, mem_all, mem_part, total, 2 * d_slabs * small, 0, held)
        cross = Halves(*slabs(turned, self_mix, self_grad, total, 3 * d_slabs * small, 0, held), total // 2)
        cross.core()
        grad_got, keep = tie(grad_got, cross.pieces[0][0])
        cross.pieces = [(keep, 0)]
        wide = pair_dot([ffn_in] + near + far, [shares[0]] + shares_near + [share_far])
        wide, cross.got = tie(wide, cross.got)
        wide = lax.psum_scatter(wide, "dp", scatter_dimension=0, tiled=True)
        cross.pack()
        grad_got, cross.out = tie(grad_got, cross.out)
        cross.hop((1, 2))
    attn_grad = jnp.concatenate([grad_parts[0]] + grad_got, axis=0)
    qkv_grad, bias_grad = self_backward(blocks, my_ref, qkv, bias, own_mix, lse, attn_grad)
    if fast:
        qkv_grad, bias_grad, hidden, cross.got, mem_part, down.got = tie(
            qkv_grad, bias_grad, hidden, cross.got, mem_part, down.got
        )
    qkv_parts = row_blocks(qkv_grad, blocks)
    attn = dot32(self_all, qkv_grad, TN)
    gain_part = jnp.sum(attn * turned_qkv[0].astype(F32), axis=1)
    attn = attn.astype(BF16)
    if fast:
        attn = lax.psum_scatter(attn, "dp", scatter_dimension=0, tiled=True)
    qkv_got = trade(qkv_parts, "blk", 1)
    if fast:
        cross.pack()
        cross.hop((2, 1))
        down.pack()
        down.hop("dp", 2)
        qkv_got, hidden = tie(qkv_got, hidden)
    block_out = (after_cross + dot32(hidden, w_down)).astype(BF16)
    d_self_norm = None
    for part, weight in zip([qkv_parts[0]] + qkv_got, turned_qkv):
        term = dot32(part, weight, NT)
        d_self_norm = term if d_self_norm is None else d_self_norm + term
    d_stream, _ = norm_back(stream, inv_self, norm_self, d_self_norm)
    d_gain_self = gain_part / norm_self
    d_block_in = grad_self + d_stream
    mem_blocks = [lax.dynamic_slice_in_dim(mem_part, (my ^ j) * mem_rows, mem_rows, 1) for j in range(blocks)]
    mem_grad = mem_blocks[0].astype(F32)
    for got in trade(mem_blocks, "blk", 1):
        mem_grad = mem_grad + got.astype(F32)
    mem_grad = mem_grad.astype(BF16)
    d_memory = dot32(mem_grad[0], cross_key, NT) + dot32(mem_grad[1], cross_value, NT)
    d_table = lax.dot_general(bucket_hot, bias_grad[:, length:], (((0,), (1,)), ((), ())), precision=lax.Precision.HIGHEST)
    d_table = lax.dynamic_update_slice_in_dim(jnp.zeros_like(bias_table), d_table, my * own_heads, 1)
    lines = sum_everywhere(
        jnp.concatenate([d_gain_self, d_gain_cross, d_gain_ffn, d_table.reshape(-1)]).reshape(-1, LANES)
    ).reshape(-1)
    gain_self, gain_cross, gain_ffn = lines[:d], lines[d : 2 * d], lines[2 * d : 3 * d]
    table_sum = lines[3 * d :].reshape(bias_table.shape)
    if fast:
        cross.pack_deep()
        cross.hop_deep()
        pieces = cross.done() + down.done(total)
        dealt = jnp.concatenate([wide, attn], axis=1)
        dealt = [lax.dynamic_slice_in_dim(dealt, (my ^ j) * small, small, 0) for j in range(blocks)]
        dealt = [dealt[0]] + trade(dealt, "blk", 1)
        dw_gate, dw_up, dw_q, dw_k, dw_v = place(my_ref, dealt, share, (own_q, own_kv, own_kv))
        shapes = [(small, d), (small, d), (small, kv_width), (small, kv_width), (small, d), (large, d)]
        outs, row = [], 0
        for number, (rows, width) in enumerate(shapes):
            for k in range(width // SLAB):
                outs.append((row, rows, number, k * SLAB, 0, SLAB))
                row += rows
        dw_co, dw_cq, dw_ck, dw_cv, dw_o, dw_down = finish(pieces, shapes, outs)
        ffn_outs = (dw_gate, dw_up, dw_down)
    else:
        dw_co = sum_rows(dot32(cross_mix, cross_grad, TN).astype(BF16), 0)
        dw_cq = sum_rows(dot32(cross_in, cq_grad, TN).astype(BF16), 1)
        dw_ck = sum_rows(dot32(mem_all, mem_part[0], TN).astype(BF16), 0)
        dw_cv = sum_rows(dot32(mem_all, mem_part[1], TN).astype(BF16), 1)
        dw_o = sum_rows(turn_rows(dot32(self_mix, self_grad, TN).astype(BF16), own_q), 0)
        dw_q, dw_k, dw_v = [
            sum_rows(lax.dynamic_update_slice_in_dim(jnp.zeros((d, width), BF16), attn[:, low : low + width // blocks], my * (width // blocks), 1), 0)
            for width, low in ((blocks * own_q, 0), (kv_width, own_q), (kv_width, own_q + own_kv))
        ]
    return (
        block_out[None],
        d_block_in[None],
        d_memory[None],
        table_sum,
        gain_self,
        dw_q,
        dw_k,
        dw_v,
        dw_o,
        gain_cross,
        dw_cq,
        dw_ck,
        dw_cv,
        dw_co,
        gain_ffn,
        *ffn_outs,
    )


def solution(mesh):
    rows = P("dp", "blk", None)
    split = P(("dp", "blk"), None)
    whole = P()
    return jax.shard_map(
        body,
        mesh=mesh,
        in_specs=(rows, rows, P("dp"), P("dp", None)) + (whole,) * 16 + (rows,),
        out_specs=(rows, rows, rows, whole, whole)
        + (split,) * 4
        + (whole,)
        + (split,) * 4
        + (whole,)
        + (split,) * 3,
        check_vma=False,
    )
```

time: 579 us -> 358 us (0.62)
  waiting for transfers between devices: 213 us -> 55.7 us
  Pallas kernels: 42.1 us -> 99.4 us
  blocking collectives: 40.8 us -> 0 us
  other arithmetic: 49.6 us -> 13.3 us
  local copies, waits for them, and re-layouts: 74.8 us -> 44.8 us
  starting transfers between devices: 73.6 us -> 58.7 us
  between operations: 2.72 us -> 15.7 us
  matrix products: 76 us -> 64.6 us
    ppermute x36 -> x48, waiting for transfers between devices: 213 us -> 55.6 us  [swap(): lax.ppermute(x, axis, [(i, i ^ bit) for i in range(lax.axis_size(axis))])]
    pallas_call x2 -> x15, Pallas kernels: 24.4 us -> 81.8 us  [the longest x5 21.6 us: slabs(): pl.pallas_call(functools.partial(slab_kernel, kind, later), grid=(count,)...]
    psum x1 -> x0, blocking collectives: 40.8 us -> none  [body(): lax.psum((d_gain_self, d_gain_cross, d_gain_ffn, d_table), ('dp', 'blk'))]
    convert_element_type x21 -> x5, other arithmetic: 24.1 us -> 4.7 us  [the longest x1 1.48 us: body(): self_grad = grad_self.astype(BF16)]
    concatenate x7 -> x4, local copies, waits for them, and re-layouts: 20.3 us -> 3.29 us  [the longest x1 1.67 us: gather_relative(): return (jnp.concatenate([x, one, two, far_a, far_b], axis=0), later)]
    concatenate x2, other arithmetic: 19.2 us -> 2.68 us  [the longest x1 1.85 us: body(): self_mix = jnp.concatenate([mix_parts[0]] + mix_got, axis=1)]
    ppermute x36 -> x48, starting transfers between devices: 73.6 us -> 58.5 us  [swap(): lax.ppermute(x, axis, [(i, i ^ bit) for i in range(lax.axis_size(axis))])]
    dynamic_slice x4 -> x6, local copies, waits for them, and re-layouts: 22.8 us -> 10.1 us  [the longest x2 2.9 us: body(): lax.dynamic_slice_in_dim(w, (my ^ j) * width, width, 1)]
  transfers between devices with their start and end apart: 36 -> 51, of which waited for: 15 -> 12; matrix products, arithmetic and copies ran while one was open for 21% -> 30% of each run, Pallas kernels for 0% -> 20%
where the time goes in v2:
time: 358 us; the launch traced here: 352 us
  Pallas kernels  99.4 us (28%)
  matrix products  64.6 us (18%)
  starting transfers between devices  58.7 us (16%)
  waiting for transfers between devices  55.7 us (16%)
  local copies, waits for them, and re-layouts  44.8 us (13%)
  between operations  15.7 us (4%)
  other arithmetic  13.3 us (4%)
    dot_general x22, matrix products, dot32(): return lax.dot_general(a, b, dims, preferred_element_type=F32)  62.2 us
    ppermute x48, starting transfers between devices, swap(): lax.ppermute(x, axis, [(i, i ^ bit) for i in range(lax.axis_size(axis))])  58.5 us
    ppermute x48, waiting for transfers between devices, swap(): lax.ppermute(x, axis, [(i, i ^ bit) for i in range(lax.axis_size(axis))])  55.6 us
    pallas_call x5, Pallas kernels, slabs(): pl.pallas_call(functools.partial(slab_kernel, kind, later), grid=(count,)...  21.6 us
    unnamed x166, local copies, waits for them, and re-layouts  21 us
    pallas_call x1, Pallas kernels, self_backward(): pl.pallas_call(functools.partial(self_backward_kernel, blocks, kv_local),...  18.3 us
    pallas_call x1, Pallas kernels, self_forward(): pl.pallas_call(functools.partial(self_forward_kernel, blocks, kv_local),...  12.6 us
    pallas_call x3, Pallas kernels, combine(): pl.pallas_call(functools.partial(combine_kernel, plan), grid=(steps,), in...  10.2 us
  transfers between devices with their start and end apart: 51, of which 12 were waited for; matrix products, arithmetic and copies ran while one was open for 30% of the time, Pallas kernels for 20%

profile of v2, /device:TPU:0, one launch (start us, length us, event | category | flops | bytes accessed | tf_op | source)
XLA Modules:
  0.0 352.2 jit_solution(16507933670393890083)
XLA Ops:
  7.3 3.0 collective-permute-start
  20.9 6.1 %fusion.56 = f32[256,2816]{1,0:T(8,128)} fusion(bf16[2816,1024]{1,0:T(8,128)(2,1)} %param.41, bf16[1,256,1024]{2,1,0:T(8,128)(2,1)S(1)} %copy-done.15), kind=kOutput, calls=%fused_computation.150 | convolution fusion | flops 1476395008 | bytes 9175040 | tf_op jit(solution)/shard_map/dot_general | solution.py:28
  47.0 4.0 %convolution_convert_fusion.qkv_ref = bf16[1024,512]{1,0:T(8,128)(2,1)} fusion(bf16[1024,1024]{1,0:T(8,128)(2,1)} %constant_dynamic-update-slice_fusion, f32[1024]{0:T(1024)S(1)} %copy-done.71, f32[1024]{0:T(1024)S(1)} %add_rsqrt_fusion, bf16[1024,128]{0,1:T(8,128)(2,1)} %copy.68, bf16[1024,128]{0,1:T(8,128)(2,1)} %copy.67, bf16[1024,256]{0,1:T(8,128)(2,1)S(1)} %copy-done.48), kind=kOutput, calls=%fused_computation.20 | convolution fusion | flops 1081606144 | bytes 4202496 | tf_op jit(solution)/shard_map/dot_general | solution.py:28
  51.0 12.6 %self_forward.1 = (bf16[1024,256]{1,0:T(8,128)(2,1)}, f32[4,2,1,512]{3,2,1,0:T(1,128)}) custom-call(s32[1]{0:T(128)} %bitcast.1.my_ref, bf16[1024,512]{1,0:T(8,128)(2,1)} %convolution_convert_fusion.qkv_ref, f32[4,1280]{1,0:T(4,128)} %concatenate.38.bias_ref), custom_call_target="tpu_custom_call" | custom-call | flops 1 | bytes 1 | tf_op jit(solution)/shard_map/self_forward/pallas_call | solution.py:309
  69.0 3.2 convolution_convert_fusion.5.k_ref
  78.8 8.2 %cross_forward.1 = (bf16[256,1024]{1,0:T(8,128)(2,1)}, f32[8,1,512]{2,1,0:T(1,128)}) custom-call(f32[512,1]{1,0:T(8,128)} %fusion.44.allow_ref, bf16[256,1024]{1,0:T(8,128)(2,1)} %convolution_convert_fusion.3.q_ref, bf16[512,512]{1,0:T(8,128)(2,1)} %convolution_convert_fusion.5.k_ref, bf16[512,512]{1,0:T(8,128)(2,1)} %convolution_convert_fusion.4.v_ref), custom_call_target="tpu_custom_call" | custom-call | flops 1 | bytes 1 | tf_op jit(solution)/shard_map/cross_forward/pallas_call | solution.py:374
  91.1 5.1 %fusion.64 = f32[256,2816]{1,0:T(8,128)S(1)} fusion(bf16[256,1024]{1,0:T(8,128)(2,1)S(1)} %multiply_convert_fusion.2.refs_0_, bf16[1024,2816]{1,0:T(8,128)(2,1)} %param.39), kind=kOutput, calls=%fused_computation.158 | convolution fusion | flops 1476395008 | bytes 9175040 | tf_op jit(solution)/shard_map/dot_general | solution.py:28
  96.2 5.5 %multiply_convert_fusion = (bf16[256,2816]{1,0:T(8,128)(2,1)}, bf16[256,2816]{1,0:T(8,128)(2,1)S(1)}, bf16[256,2816]{1,0:T(8,128)(2,1)S(1)}) fusion(f32[256,2816]{1,0:T(8,128)S(1)} %fusion.64, f32[256,2816]{1,0:T(8,128)S(1)} %copy-done.75, bf16[256,1024]{1,0:T(8,128)(2,1)S(1)} %multiply_convert_fusion.2.refs_0_, bf16[1024,2816]{1,0:T(8,128)(2,1)S(1)} %bitcast.85), kind=kOutput, calls=%fused_computation.11 | convolution fusion | flops 1501626368 | bytes 16384000 | tf_op jit(solution)/shard_map/dot_general | solution.py:28
  105.2 6.3 %slabs.5 = (bf16[16,176,512]{2,1,0:T(8,128)(2,1)}, bf16[16,176,512]{2,1,0:T(8,128)(2,1)}) custom-call(s32[4,32]{1,0:T(4,128)} %get-tuple-element.321.order_ref, bf16[256,2816]{1,0:T(8,128)(2,1)} %get-tuple-element.203.x_ref, bf16[256,1024]{1,0:T(8,128)(2,1)} %bitcast.79), custom_call_target="tpu_custom_call" | custom-call | flops 1 | bytes 1 | tf_op jit(solution)/shard_map/slabs/pallas_call | solution.py:455
  115.4 4.8 %fusion.65 = f32[256,1024]{1,0:T(8,128)S(1)} fusion(bf16[256,2816]{1,0:T(8,128)(2,1)} %copy-done.29, bf16[1024,2816]{1,0:T(8,128)(2,1)} %param.40), kind=kOutput, calls=%fused_computation.159 | convolution fusion | flops 1476395008 | bytes 8257536 | tf_op jit(solution)/shard_map/dot_general | solution.py:28
  120.2 4.4 %convolution_add_fusion.4 = f32[256,1024]{1,0:T(8,128)S(1)} fusion(f32[256,1024]{1,0:T(8,128)S(1)} %fusion.65, bf16[256,2816]{1,0:T(8,128)(2,1)S(1)} %copy-done.28, bf16[1024,2816]{1,0:T(8,128)(2,1)} %param.39), kind=kOutput, calls=%fused_computation.27 | convolution fusion | flops 1476657152 | bytes 9306112 | tf_op jit(solution)/shard_map/dot_general | solution.py:28
  124.7 7.5 %collective-permute-done.9.refs_6_ = bf16[256,1408]{1,0:T(8,128)(2,1)S(1)} collective-permute-done((bf16[256,1408]{1,0:T(8,128)(2,1)}, bf16[256,1408]{1,0:T(8,128)(2,1)S(1)}, u32[]{:S(2)}, u32[]{:S(2)}) %collective-permute-start.9) | collective-permute-done | bytes 720928 | tf_op jit(solution)/shard_map/ppermute | solution.py:32
  138.9 3.5 slabs.6
  142.4 3.3 convolution_convert_fusion.2.grad_ref
  145.7 9.4 %cross_backward.1 = (bf16[256,1024]{1,0:T(8,128)(2,1)}, bf16[2,512,512]{2,1,0:T(8,128)(2,1)}) custom-call(f32[512,1]{1,0:T(8,128)} %fusion.44.allow_ref, bf16[256,1024]{1,0:T(8,128)(2,1)} %convolution_convert_fusion.3.q_ref, bf16[512,512]{1,0:T(8,128)(2,1)} %convolution_convert_fusion.5.k_ref, bf16[512,512]{1,0:T(8,128)(2,1)} %convolution_convert_fusion.4.v_ref, ...), custom_call_target="tpu_custom_call" | custom-call | flops 1 | bytes 1 | tf_op jit(solution)/shard_map/cross_backward/pallas_call | solution.py:399
  160.3 3.6 %slabs.7 = (bf16[16,256,512]{2,1,0:T(8,128)(2,1)}, bf16[16,256,512]{2,1,0:T(8,128)(2,1)}) custom-call(s32[4,32]{1,0:T(4,128)} %get-tuple-element.321.order_ref, bf16[256,1024]{1,0:T(8,128)(2,1)} %copy-done.20, bf16[256,1024]{1,0:T(8,128)(2,1)} %get-tuple-element.152.g_ref, ...), custom_call_target="tpu_custom_call", output_to_operand_aliasing={{0}: (3, {}), {1}: (4, {})} | custom-call | flops 1 | bytes 1 | tf_op jit(solution)/shard_map/slabs/pallas_call | solution.py:455
  163.8 4.5 %slabs.8 = (bf16[16,256,512]{2,1,0:T(8,128)(2,1)}, bf16[16,256,512]{2,1,0:T(8,128)(2,1)}) custom-call(s32[4,32]{1,0:T(4,128)} %get-tuple-element.321.order_ref, bf16[512,1024]{1,0:T(8,128)(2,1)} %all-gather.2.cloned.1.call-done.x_ref, bf16[2,512,512]{2,1,0:T(8,128)(2,1)} %get-tuple-element.207.g_ref, ...), custom_call_target="tpu_custom_call", output_to_operand_aliasing={{0}: (3, {}), {1}: (4, {})} | custom-call | flops 1 | bytes 1 | tf_op jit(solution)/shard_map/slabs/pallas_call | solution.py:455
  168.3 3.7 %slabs.9 = (bf16[16,256,512]{2,1,0:T(8,128)(2,1)}, bf16[16,256,512]{2,1,0:T(8,128)(2,1)}) custom-call(s32[4,32]{1,0:T(4,128)} %get-tuple-element.320.order_ref, bf16[256,1024]{1,0:T(8,128)(2,1)} %pad_maximum_fusion.2.x_ref, bf16[256,1024]{1,0:T(8,128)(2,1)} %copy-done.23, ...), custom_call_target="tpu_custom_call", output_to_operand_aliasing={{0}: (3, {}), {1}: (4, {})} | custom-call | flops 1 | bytes 1 | tf_op jit(solution)/shard_map/slabs/pallas_call | solution.py:455
  172.1 7.5 %pair_dot.1 = bf16[1024,1408]{1,0:T(8,128)(2,1)} custom-call(bf16[256,1024]{1,0:T(8,128)(2,1)} %copy-done.25, bf16[256,1024]{1,0:T(8,128)(2,1)} %copy-done.31, bf16[256,1024]{1,0:T(8,128)(2,1)} %copy-done.33, bf16[128,1024]{1,0:T(8,128)(2,1)} %copy-done.63, bf16[128,1024]{1,0:T(8,128)(2,1)} %collective-permute-done.14.refs_4_, ...), custom_call_target="tpu_custom_call" | custom-call | flops 1 | bytes 1 | tf_op jit(solution)/shard_map/pair_dot/pallas_call | solution.py:543
  186.1 3.6 %collective-permute-done.16 = bf16[256,256]{1,0:T(8,128)(2,1)S(1)} collective-permute-done((bf16[256,256]{1,0:T(8,128)(2,1)S(1)}, bf16[256,256]{1,0:T(8,128)(2,1)S(1)}, u32[]{:S(2)}, u32[]{:S(2)}) %collective-permute-start.16) | collective-permute-done | bytes 131104 | tf_op jit(solution)/shard_map/ppermute | solution.py:32
  189.7 3.3 sum_pieces.2
  195.1 4.4 %combine.3 = (bf16[4,176,512]{2,1,0:T(8,128)(2,1)}, bf16[4,176,512]{2,1,0:T(8,128)(2,1)}, bf16[4,176,512]{2,1,0:T(8,128)(2,1)}) custom-call(bf16[16,176,512]{2,1,0:T(8,128)(2,1)} %get-tuple-element.160.refs_0_.refs_2_.refs_4_.refs_5_.refs_10_.refs_9_, bf16[16,176,512]{2,1,0:T(8,128)(2,1)} %copy-done.2, ...), custom_call_target="tpu_custom_call" | custom-call | flops 1 | bytes 1 | tf_op jit(solution)/shard_map/combine/pallas_call | solution.py:635
  203.9 18.3 %self_backward.1 = (bf16[1024,512]{1,0:T(8,128)(2,1)}, f32[4,1280]{1,0:T(4,128)}) custom-call(s32[1]{0:T(128)} %bitcast.1.my_ref, bf16[1024,512]{1,0:T(8,128)(2,1)} %convolution_convert_fusion.qkv_ref, f32[4,1280]{1,0:T(4,128)} %concatenate.38.bias_ref, bf16[1024,256]{1,0:T(8,128)(2,1)} %get-tuple-element.128.mix_ref, ...), custom_call_target="tpu_custom_call" | custom-call | flops 1 | bytes 1 | tf_op jit(solution)/shard_map/self_backward/pallas_call | solution.py:343
  222.1 12.6 %collective-permute-done.21.refs_2_.refs_7_.refs_12_.refs_11_ = bf16[4,176,512]{2,1,0:T(8,128)(2,1)S(1)} collective-permute-done((bf16[4,176,512]{2,1,0:T(8,128)(2,1)}, bf16[4,176,512]{2,1,0:T(8,128)(2,1)S(1)}, u32[]{:S(2)}, u32[]{:S(2)}) %collective-permute-start.21) | collective-permute-done | bytes 720928 | tf_op jit(solution)/shard_map/ppermute | solution.py:32
  234.8 14.0 %collective-permute-done.22.refs_3_.refs_8_.refs_13_.refs_12_ = bf16[4,176,512]{2,1,0:T(8,128)(2,1)S(1)} collective-permute-done((bf16[4,176,512]{2,1,0:T(8,128)(2,1)}, bf16[4,176,512]{2,1,0:T(8,128)(2,1)S(1)}, u32[]{:S(2)}, u32[]{:S(2)}) %collective-permute-start.22) | collective-permute-done | bytes 720928 | tf_op jit(solution)/shard_map/ppermute | solution.py:32
  251.5 4.6 %multiply_reduce_fusion = (f32[1024]{0:T(1024)S(1)}, bf16[1024,512]{0,1:T(8,128)(2,1)}) fusion(bf16[1024,128]{0,1:T(8,128)(2,1)} %copy.68, bf16[1024,128]{0,1:T(8,128)(2,1)} %copy.67, bf16[1024,256]{0,1:T(8,128)(2,1)} %copy.66, bf16[1024,512]{1,0:T(8,128)(2,1)} %get-tuple-element.201, bf16[1024,1024]{1,0:T(8,128)(2,1)} %constant_dynamic-update-slice_fusion, ...), kind=kOutput, calls=%fused_computation.16 | convolution fusion | flops 1082653696 | bytes 5255168 | tf_op jit(solution)/shard_map/dot_general | solution.py:28
  272.8 3.0 sum_pieces.3
  307.0 5.2 %fusion.11 = bf16[1,256,1024]{2,1,0:T(8,128)(2,1)} fusion(f32[256,1024]{1,0:T(8,128)S(1)} %copy-done.6, bf16[256,2816]{1,0:T(8,128)(2,1)S(1)} %copy-done.26, bf16[2816,1024]{1,0:T(8,128)(2,1)} %param.41), kind=kOutput, calls=%fused_computation.36 | convolution fusion | flops 1476919296 | bytes 8781824 | tf_op jit(solution)/shard_map/dot_general | solution.py:28
  313.8 3.0 combine.4
  320.2 3.0 collective-permute-start.44
  329.2 8.8 %collective-permute-done.43.refs_7_ = bf16[1,256,512]{2,1,0:T(8,128)(2,1)S(1)} collective-permute-done((bf16[1,256,512]{2,1,0:T(8,128)(2,1)}, bf16[1,256,512]{2,1,0:T(8,128)(2,1)S(1)}, u32[]{:S(2)}, u32[]{:S(2)}) %collective-permute-start.43) | collective-permute-done | bytes 262176 | tf_op jit(solution)/shard_map/ppermute | solution.py:32
  339.5 3.1 finish.1
  (332 shorter events, 143.5 us)
Async XLA Ops:
  7.2 61.8 %all-gather.2.cloned.1.call-start = ((), (), s32[]{:S(2)}) async-start(), calls=%async_computation.2 | async-start | bytes 1310720 | tf_op jit(solution)/shard_map/all_gather | solution.py:749
  7.3 19.8 %collective-permute-start = (bf16[256,1024]{1,0:T(8,128)(2,1)}, bf16[256,1024]{1,0:T(8,128)(2,1)S(1)}, u32[]{:S(2)}, u32[]{:S(2)}) collective-permute-start(bf16[256,1024]{1,0:T(8,128)(2,1)} %bitcast.77), channel_id=1, source_target_pairs={{0,1},{1,0},{2,3},{3,2},{4,5},{5,4},{6,7},{7,6},{8,9},{9,8},{10,11... | collective-permute-start | bytes 1572872 | tf_op jit(solution)/shard_map/ppermute | solution.py:32
  10.3 18.1 %collective-permute-start.1 = (bf16[256,1024]{1,0:T(8,128)(2,1)}, bf16[256,1024]{1,0:T(8,128)(2,1)}, u32[]{:S(2)}, u32[]{:S(2)}) collective-permute-start(bf16[256,1024]{1,0:T(8,128)(2,1)} %bitcast.78), channel_id=1, source_target_pairs={{0,2},{1,3},{2,0},{3,1},{4,6},{5,7},{6,4},{7,5},{8,10},{9,11},{10,... | collective-permute-start | bytes 1572872 | tf_op jit(solution)/shard_map/ppermute | solution.py:32
  37.7 280.5 %reduce-scatter.3.cloned.1.call-start = ((), (), s32[]{:S(2)}) async-start(), calls=%async_computation.3 | async-start | bytes 3244032 | tf_op jit(solution)/shard_map/reduce_scatter | solution.py:876
  111.5 43.6 %collective-permute-start.12 = (bf16[16,176,512]{2,1,0:T(8,128)(2,1)}, bf16[16,176,512]{2,1,0:T(8,128)(2,1)S(1)}, u32[]{:S(2)}, u32[]{:S(2)}) collective-permute-start(bf16[16,176,512]{2,1,0:T(8,128)(2,1)} %get-tuple-element.151), channel_id=1, source_target_pairs={{0,4},{4,0},{8,12},{12,8},{16,20},{20,16},{24,28},{28,24},{1,5},{5... | collective-permute-start | bytes 8650760 | tf_op jit(solution)/shard_map/ppermute | solution.py:32
  113.4 18.8 %collective-permute-start.9 = (bf16[256,1408]{1,0:T(8,128)(2,1)}, bf16[256,1408]{1,0:T(8,128)(2,1)S(1)}, u32[]{:S(2)}, u32[]{:S(2)}) collective-permute-start(bf16[256,1408]{1,0:T(8,128)(2,1)} %get-tuple-element.139), channel_id=1, source_target_pairs={{0,1},{1,0},{2,3},{3,2},{4,5},{5,4},{6,7},{7,6},{8,9},{9,8},{10,11... | collective-permute-start | bytes 2162696 | tf_op jit(solution)/shard_map/ppermute | solution.py:32
  113.9 18.5 %collective-permute-start.10 = (bf16[256,1408]{1,0:T(8,128)(2,1)}, bf16[256,1408]{1,0:T(8,128)(2,1)S(1)}, u32[]{:S(2)}, u32[]{:S(2)}) collective-permute-start(bf16[256,1408]{1,0:T(8,128)(2,1)} %get-tuple-element.140), channel_id=1, source_target_pairs={{0,2},{1,3},{2,0},{3,1},{4,6},{5,7},{6,4},{7,5},{8,10},{9,11},{10,... | collective-permute-start | bytes 2162696 | tf_op jit(solution)/shard_map/ppermute | solution.py:32
  132.4 22.8 %collective-permute-start.11 = (bf16[256,1408]{1,0:T(8,128)(2,1)}, bf16[256,1408]{1,0:T(8,128)(2,1)}, u32[]{:S(2)}, u32[]{:S(2)}) collective-permute-start(bf16[256,1408]{1,0:T(8,128)(2,1)} %get-tuple-element.150), channel_id=1, source_target_pairs={{0,3},{1,2},{2,1},{3,0},{4,7},{5,6},{6,5},{7,4},{8,11},{9,10},{10,... | collective-permute-start | bytes 2162696 | tf_op jit(solution)/shard_map/ppermute | solution.py:32
  134.5 25.7 %collective-permute-start.13 = (bf16[128,1024]{1,0:T(8,128)(2,1)}, bf16[128,1024]{1,0:T(8,128)(2,1)S(1)}, u32[]{:S(2)}, u32[]{:S(2)}) collective-permute-start(bf16[128,1024]{1,0:T(8,128)(2,1)} %slice.95), channel_id=1, source_target_pairs={{0,2},{1,3},{2,0},{3,1},{4,6},{5,7},{6,4},{7,5},{8,10},{9,11},{10,... | collective-permute-start | bytes 786440 | tf_op jit(solution)/shard_map/ppermute | solution.py:32
  138.3 22.0 %collective-permute-start.14 = (bf16[128,1024]{1,0:T(8,128)(2,1)}, bf16[128,1024]{1,0:T(8,128)(2,1)}, u32[]{:S(2)}, u32[]{:S(2)}) collective-permute-start(bf16[128,1024]{1,0:T(8,128)(2,1)} %slice.96), channel_id=1, source_target_pairs={{0,1},{1,0},{2,3},{3,2},{4,5},{5,4},{6,7},{7,6},{8,9},{9,8},{10,11... | collective-permute-start | bytes 786440 | tf_op jit(solution)/shard_map/ppermute | solution.py:32
  179.6 139.6 %reduce-scatter.5.cloned.1.call-start = ((), (), s32[]{:S(2)}) async-start(), calls=%async_computation.4 | async-start | bytes 1179648 | tf_op jit(solution)/shard_map/reduce_scatter | solution.py:891
  193.0 55.8 %collective-permute-start.19 = (bf16[8,128,512]{2,1,0:T(8,128)(2,1)}, bf16[8,128,512]{2,1,0:T(8,128)(2,1)S(1)}, u32[]{:S(2)}, u32[]{:S(2)}) collective-permute-start(bf16[8,128,512]{2,1,0:T(8,128)(2,1)} %get-tuple-element.196), channel_id=1, source_target_pairs={{0,1},{1,0},{2,3},{3,2},{4,5},{5,4},{6,7},{7,6},{8,9},{9,8},{10,11... | collective-permute-start | bytes 3145736 | tf_op jit(solution)/shard_map/ppermute | solution.py:32
  193.6 55.2 %collective-permute-start.20 = (bf16[8,128,512]{2,1,0:T(8,128)(2,1)}, bf16[8,128,512]{2,1,0:T(8,128)(2,1)S(1)}, u32[]{:S(2)}, u32[]{:S(2)}) collective-permute-start(bf16[8,128,512]{2,1,0:T(8,128)(2,1)} %get-tuple-element.197), channel_id=1, source_target_pairs={{0,2},{1,3},{2,0},{3,1},{4,6},{5,7},{6,4},{7,5},{8,10},{9,11},{10,... | collective-permute-start | bytes 3145736 | tf_op jit(solution)/shard_map/ppermute | solution.py:32
  199.5 35.3 %collective-permute-start.21 = (bf16[4,176,512]{2,1,0:T(8,128)(2,1)}, bf16[4,176,512]{2,1,0:T(8,128)(2,1)S(1)}, u32[]{:S(2)}, u32[]{:S(2)}) collective-permute-start(bf16[4,176,512]{2,1,0:T(8,128)(2,1)} %get-tuple-element.198), channel_id=1, source_target_pairs={{0,1},{1,0},{2,3},{3,2},{4,5},{5,4},{6,7},{7,6},{8,9},{9,8},{10,11... | collective-permute-start | bytes 2162696 | tf_op jit(solution)/shard_map/ppermute | solution.py:32
  200.0 48.8 %collective-permute-start.22 = (bf16[4,176,512]{2,1,0:T(8,128)(2,1)}, bf16[4,176,512]{2,1,0:T(8,128)(2,1)S(1)}, u32[]{:S(2)}, u32[]{:S(2)}) collective-permute-start(bf16[4,176,512]{2,1,0:T(8,128)(2,1)} %get-tuple-element.199), channel_id=1, source_target_pairs={{0,2},{1,3},{2,0},{3,1},{4,6},{5,7},{6,4},{7,5},{8,10},{9,11},{10,... | collective-permute-start | bytes 2162696 | tf_op jit(solution)/shard_map/ppermute | solution.py:32
  201.5 47.2 %collective-permute-start.23 = (bf16[4,176,512]{2,1,0:T(8,128)(2,1)}, bf16[4,176,512]{2,1,0:T(8,128)(2,1)S(1)}, u32[]{:S(2)}, u32[]{:S(2)}) collective-permute-start(bf16[4,176,512]{2,1,0:T(8,128)(2,1)} %get-tuple-element.200), channel_id=1, source_target_pairs={{0,3},{1,2},{2,1},{3,0},{4,7},{5,6},{6,5},{7,4},{8,11},{9,10},{10,... | collective-permute-start | bytes 2162696 | tf_op jit(solution)/shard_map/ppermute | solution.py:32
  262.8 21.9 %collective-permute-start.24 = (bf16[256,512]{1,0:T(8,128)(2,1)}, bf16[256,512]{1,0:T(8,128)(2,1)}, u32[]{:S(2)}, u32[]{:S(2)}) collective-permute-start(bf16[256,512]{1,0:T(8,128)(2,1)} %get-tuple-element.304), channel_id=1, source_target_pairs={{0,1},{1,0},{2,3},{3,2},{4,5},{5,4},{6,7},{7,6},{8,9},{9,8},{10,11... | collective-permute-start | bytes 786440 | tf_op jit(solution)/shard_map/ppermute | solution.py:32
  264.7 20.3 %collective-permute-start.25 = (bf16[256,512]{1,0:T(8,128)(2,1)}, bf16[256,512]{1,0:T(8,128)(2,1)S(1)}, u32[]{:S(2)}, u32[]{:S(2)}) collective-permute-start(bf16[256,512]{1,0:T(8,128)(2,1)} %get-tuple-element.303), channel_id=1, source_target_pairs={{0,2},{1,3},{2,0},{3,1},{4,6},{5,7},{6,4},{7,5},{8,10},{9,11},{10,... | collective-permute-start | bytes 786440 | tf_op jit(solution)/shard_map/ppermute | solution.py:32
  265.0 13.6 %collective-permute-start.35 = (f32[28,128]{1,0:T(8,128)S(1)}, f32[28,128]{1,0:T(8,128)S(1)}, u32[]{:S(2)}, u32[]{:S(2)}) collective-permute-start(f32[28,128]{1,0:T(8,128)S(1)} %add_add_fusion.1), channel_id=1, source_target_pairs={{0,16},{4,20},{8,24},{12,28},{16,0},{20,4},{24,8},{28,12},{1,17},{... | collective-permute-start | bytes 43016 | tf_op jit(solution)/shard_map/ppermute | solution.py:32
  280.1 15.9 %collective-permute-start.29 = (bf16[2,128,512]{2,1,0:T(8,128)(2,1)}, bf16[2,128,512]{2,1,0:T(8,128)(2,1)}, u32[]{:S(2)}, u32[]{:S(2)}) collective-permute-start(bf16[2,128,512]{2,1,0:T(8,128)(2,1)} %get-tuple-element.292), channel_id=1, source_target_pairs={{0,3},{1,2},{2,1},{3,0},{4,7},{5,6},{6,5},{7,4},{8,11},{9,10},{10,... | collective-permute-start | bytes 786440 | tf_op jit(solution)/shard_map/ppermute | solution.py:32
  281.6 16.1 %collective-permute-start.28 = (bf16[2,128,512]{2,1,0:T(8,128)(2,1)}, bf16[2,128,512]{2,1,0:T(8,128)(2,1)}, u32[]{:S(2)}, u32[]{:S(2)}) collective-permute-start(bf16[2,128,512]{2,1,0:T(8,128)(2,1)} %get-tuple-element.293), channel_id=1, source_target_pairs={{0,2},{1,3},{2,0},{3,1},{4,6},{5,7},{6,4},{7,5},{8,10},{9,11},{10,... | collective-permute-start | bytes 786440 | tf_op jit(solution)/shard_map/ppermute | solution.py:32
  284.7 15.6 %collective-permute-start.27 = (bf16[2,128,512]{2,1,0:T(8,128)(2,1)}, bf16[2,128,512]{2,1,0:T(8,128)(2,1)S(1)}, u32[]{:S(2)}, u32[]{:S(2)}) collective-permute-start(bf16[2,128,512]{2,1,0:T(8,128)(2,1)} %get-tuple-element.291), channel_id=1, source_target_pairs={{0,1},{1,0},{2,3},{3,2},{4,5},{5,4},{6,7},{7,6},{8,9},{9,8},{10,11... | collective-permute-start | bytes 786440 | tf_op jit(solution)/shard_map/ppermute | solution.py:32
  284.9 27.3 %collective-permute-start.40 = (bf16[4,128,512]{2,1,0:T(8,128)(2,1)}, bf16[4,128,512]{2,1,0:T(8,128)(2,1)S(1)}, u32[]{:S(2)}, u32[]{:S(2)}) collective-permute-start(bf16[4,128,512]{2,1,0:T(8,128)(2,1)} %get-tuple-element.215), channel_id=1, source_target_pairs={{0,2},{1,3},{2,0},{3,1},{4,6},{5,7},{6,4},{7,5},{8,10},{9,11},{10,... | collective-permute-start | bytes 1572872 | tf_op jit(solution)/shard_map/ppermute | solution.py:32
  289.6 22.6 %collective-permute-start.41 = (bf16[4,128,512]{2,1,0:T(8,128)(2,1)}, bf16[4,128,512]{2,1,0:T(8,128)(2,1)S(1)}, u32[]{:S(2)}, u32[]{:S(2)}) collective-permute-start(bf16[4,128,512]{2,1,0:T(8,128)(2,1)} %get-tuple-element.216), channel_id=1, source_target_pairs={{0,1},{1,0},{2,3},{3,2},{4,5},{5,4},{6,7},{7,6},{8,9},{9,8},{10,11... | collective-permute-start | bytes 1572872 | tf_op jit(solution)/shard_map/ppermute | solution.py:32
  295.9 24.2 %collective-permute-start.45 = (bf16[1,176,512]{2,1,0:T(8,128)(2,1)}, bf16[1,176,512]{2,1,0:T(8,128)(2,1)}, u32[]{:S(2)}, u32[]{:S(2)}) collective-permute-start(bf16[1,176,512]{2,1,0:T(8,128)(2,1)} %get-tuple-element.223), channel_id=1, source_target_pairs={{0,8},{4,12},{8,0},{12,4},{16,24},{20,28},{24,16},{28,20},{1,9},{5... | collective-permute-start | bytes 540680 | tf_op jit(solution)/shard_map/ppermute | solution.py:32
  297.7 26.2 %collective-permute-start.46 = (bf16[1,176,512]{2,1,0:T(8,128)(2,1)}, bf16[1,176,512]{2,1,0:T(8,128)(2,1)}, u32[]{:S(2)}, u32[]{:S(2)}) collective-permute-start(bf16[1,176,512]{2,1,0:T(8,128)(2,1)} %get-tuple-element.224), channel_id=1, source_target_pairs={{0,16},{4,20},{8,24},{12,28},{16,0},{20,4},{24,8},{28,12},{1,17},{... | collective-permute-start | bytes 540680 | tf_op jit(solution)/shard_map/ppermute | solution.py:32
  300.4 23.7 %collective-permute-start.47 = (bf16[1,176,512]{2,1,0:T(8,128)(2,1)}, bf16[1,176,512]{2,1,0:T(8,128)(2,1)}, u32[]{:S(2)}, u32[]{:S(2)}) collective-permute-start(bf16[1,176,512]{2,1,0:T(8,128)(2,1)} %get-tuple-element.225), channel_id=1, source_target_pairs={{0,24},{4,28},{8,16},{12,20},{16,8},{20,12},{24,0},{28,4},{1,25},{... | collective-permute-start | bytes 540680 | tf_op jit(solution)/shard_map/ppermute | solution.py:32
  317.2 20.9 %collective-permute-start.43 = (bf16[1,256,512]{2,1,0:T(8,128)(2,1)}, bf16[1,256,512]{2,1,0:T(8,128)(2,1)S(1)}, u32[]{:S(2)}, u32[]{:S(2)}) collective-permute-start(bf16[1,256,512]{2,1,0:T(8,128)(2,1)} %get-tuple-element.218), channel_id=1, source_target_pairs={{0,16},{4,20},{8,24},{12,28},{16,0},{20,4},{24,8},{28,12},{1,17},{... | collective-permute-start | bytes 786440 | tf_op jit(solution)/shard_map/ppermute | solution.py:32
  320.2 17.8 %collective-permute-start.44 = (bf16[1,256,512]{2,1,0:T(8,128)(2,1)}, bf16[1,256,512]{2,1,0:T(8,128)(2,1)S(1)}, u32[]{:S(2)}, u32[]{:S(2)}) collective-permute-start(bf16[1,256,512]{2,1,0:T(8,128)(2,1)} %get-tuple-element.219), channel_id=1, source_target_pairs={{0,24},{4,28},{8,16},{12,20},{16,8},{20,12},{24,0},{28,4},{1,25},{... | collective-permute-start | bytes 786440 | tf_op jit(solution)/shard_map/ppermute | solution.py:32
  323.9 18.7 %collective-permute-start.37 = (bf16[32,1920]{1,0:T(8,128)(2,1)S(1)}, bf16[32,1920]{1,0:T(8,128)(2,1)S(1)}, u32[]{:S(2)}, u32[]{:S(2)}) collective-permute-start(bf16[32,1920]{1,0:T(8,128)(2,1)S(1)} %get-tuple-element.315), channel_id=1, source_target_pairs={{0,1},{1,0},{2,3},{3,2},{4,5},{5,4},{6,7},{7,6},{8,9},{9,8},{10,11... | collective-permute-start | bytes 368648 | tf_op jit(solution)/shard_map/ppermute | solution.py:32
  324.1 18.5 %collective-permute-start.38 = (bf16[32,1920]{1,0:T(8,128)(2,1)S(1)}, bf16[32,1920]{1,0:T(8,128)(2,1)S(1)}, u32[]{:S(2)}, u32[]{:S(2)}) collective-permute-start(bf16[32,1920]{1,0:T(8,128)(2,1)S(1)} %get-tuple-element.314), channel_id=1, source_target_pairs={{0,2},{1,3},{2,0},{3,1},{4,6},{5,7},{6,4},{7,5},{8,10},{9,11},{10,... | collective-permute-start | bytes 368648 | tf_op jit(solution)/shard_map/ppermute | solution.py:32
  326.5 16.1 %collective-permute-start.39 = (bf16[32,1920]{1,0:T(8,128)(2,1)S(1)}, bf16[32,1920]{1,0:T(8,128)(2,1)S(1)}, u32[]{:S(2)}, u32[]{:S(2)}) collective-permute-start(bf16[32,1920]{1,0:T(8,128)(2,1)S(1)} %get-tuple-element.313), channel_id=1, source_target_pairs={{0,3},{1,2},{2,1},{3,0},{4,7},{5,6},{6,5},{7,4},{8,11},{9,10},{10,... | collective-permute-start | bytes 368648 | tf_op jit(solution)/shard_map/ppermute | solution.py:32
  (97 other events, 782.9 us)
Sparse Core Ops, SparseCore 0:
  37.8 28.2 all-gather.1
  179.8 39.2 reduce-scatter.2
  272.9 33.1 reduce-scatter.4

commit v3 on v2

v3 whole, which is shorter than its diff:
```python
import functools

import jax
import jax.numpy as jnp
from jax import lax
from jax.experimental import pallas as pl
from jax.experimental.pallas import tpu as pltpu
from jax.sharding import PartitionSpec as P

HEAD_DIM = 64
EPSILON = 1e-06
NEGATIVE = -1e30
SCALE = HEAD_DIM ** (-0.5)
LANES = 128
PAIR = 2 * HEAD_DIM
SLAB = 512
STEP_ELEMENTS = 768 * 1024
F32 = jnp.float32
BF16 = jnp.bfloat16
VMEM_LIMIT = 56 * 1024 * 1024

NT = (((1,), (1,)), ((), ()))
NN = (((1,), (0,)), ((), ()))
TN = (((0,), (0,)), ((), ()))


def dot32(a, b, dims=NN):
    return lax.dot_general(a, b, dims, preferred_element_type=F32)


def swap(x, axis, bit):
    return lax.ppermute(x, axis, [(i, i ^ bit) for i in range(lax.axis_size(axis))])


def trade(parts, axis, bit):
    return [swap(part, axis, k * bit) for k, part in enumerate(parts) if k]


def tie(*groups):
    return lax.optimization_barrier(groups)


def row_blocks(x, count):
    length = x.shape[0] // count
    return [x[k * length : (k + 1) * length] for k in range(count)]


def column_blocks(x, count):
    width = x.shape[1] // count
    return [x[:, k * width : (k + 1) * width] for k in range(count)]


def add16(a, b):
    return (a.astype(F32) + b.astype(F32)).astype(BF16)


def sum_axis(x, axis, last, bit=1):
    while bit <= last:
        x = x + swap(x, axis, bit)
        bit *= 2
    return x


def sum_rows(x, first_blk_bit):
    dp_bits = lax.axis_size("dp").bit_length() - 1
    blk_bits = lax.axis_size("blk").bit_length() - 1
    rest = [("dp", k) for k in reversed(range(dp_bits))] + [("blk", k) for k in reversed(range(blk_bits))]
    rows, width = x.shape
    x = x.reshape((2,) * len(rest) + (rows >> len(rest), width))
    order = [("dp", 0)]
    order += [("blk", (first_blk_bit + k) % blk_bits) for k in range(blk_bits)]
    order += [("dp", k) for k in range(1, dp_bits)]
    for axis, k in order:
        place = rest.index((axis, k))
        mine = (lax.axis_index(axis) >> k) & 1
        out = lax.dynamic_index_in_dim(x, 1 - mine, place, keepdims=False)
        keep = lax.dynamic_index_in_dim(x, mine, place, keepdims=False)
        got = swap(out, axis, 1 << k)
        rest.pop(place)
        x = keep.astype(F32) + got.astype(F32)
        if rest:
            x = x.astype(BF16)
    return x


def stacked(ref, kv):
    low = kv * PAIR
    return jnp.concatenate([ref[:, low : low + HEAD_DIM], ref[:, low + HEAD_DIM : low + PAIR]], axis=0)


def unstack(ref, kv, columns):
    length = columns.shape[1] // 2
    rows = columns.T
    low = kv * PAIR
    ref[:, low : low + HEAD_DIM] = rows[:length].astype(ref.dtype)
    ref[:, low + HEAD_DIM : low + PAIR] = rows[length:].astype(ref.dtype)


def spread_bias(bias_ref, tile_ref):
    heads, width = bias_ref.shape
    for h in range(heads):
        line = jnp.broadcast_to(bias_ref[h : h + 1, :], (LANES, width))
        tile_ref[h] = pltpu.roll(line, 0, 1, stride=1, stride_axis=0)


def bias_tile(tile_ref, kv, start, length):
    heads = []
    for g in range(2):
        parts = [
            tile_ref[2 * kv + g, :, pl.ds(pl.multiple_of(start - LANES * m, LANES), length)]
            for m in range(length // LANES)
        ]
        heads.append(jnp.concatenate(parts, axis=0))
    return jnp.concatenate(heads, axis=1)


def head_columns(kv_local, kv):
    return kv * PAIR, kv_local * PAIR + kv * HEAD_DIM, kv_local * (PAIR + HEAD_DIM) + kv * HEAD_DIM


def two_heads(ref, rows, low):
    return jnp.concatenate([ref[rows, low : low + HEAD_DIM], ref[rows, low + HEAD_DIM : low + PAIR]], axis=0)


def self_forward_kernel(blocks, kv_local, my_ref, qkv_ref, bias_ref, *refs):
    mix_refs, (lse_ref, tile_ref, top_ref, sum_ref, acc_ref) = refs[:blocks], refs[blocks:]
    a = pl.program_id(0)
    length = qkv_ref.shape[0] // blocks
    my = my_ref[0]
    mine = my ^ a

    @pl.when(a == 0)
    def _():
        spread_bias(bias_ref, tile_ref)

    rows = pl.ds(pl.multiple_of(a * length, length), length)
    top_ref[...] = jnp.full_like(top_ref, NEGATIVE)
    sum_ref[...] = jnp.zeros_like(sum_ref)
    acc_ref[...] = jnp.zeros_like(acc_ref)
    for b in range(blocks):
        source = my ^ b
        keys_at = slice(b * length, (b + 1) * length)

        @pl.when(source <= mine)
        def _(source=source, keys_at=keys_at):
            start = length + length * (mine - source)
            for kv in range(kv_local):
                q_at, k_at, v_at = head_columns(kv_local, kv)
                qq = two_heads(qkv_ref, rows, q_at)
                keys = qkv_ref[keys_at, k_at : k_at + HEAD_DIM]
                values = qkv_ref[keys_at, v_at : v_at + HEAD_DIM]
                scores = dot32(keys, qq, NT) * SCALE + bias_tile(tile_ref, kv, start, length)
                old = top_ref[kv]
                new = jnp.maximum(old, jnp.max(scores, axis=0, keepdims=True))
                weights = jnp.exp(scores - new)
                shrink = jnp.exp(old - new)
                top_ref[kv] = new
                sum_ref[kv] = sum_ref[kv] * shrink + jnp.sum(weights, axis=0, keepdims=True)
                acc_ref[kv] = acc_ref[kv] * shrink + dot32(values, weights.astype(BF16), TN)

    for kv in range(kv_local):
        lse_ref[0, kv] = top_ref[kv] + jnp.log(sum_ref[kv])
    for b, mix_ref in enumerate(mix_refs):

        @pl.when(a == b)
        def _(mix_ref=mix_ref):
            for kv in range(kv_local):
                unstack(mix_ref, kv, acc_ref[kv] / sum_ref[kv])


def self_backward_kernel(blocks, kv_local, my_ref, qkv_ref, bias_ref, lse_ref, *refs):
    mix_refs, grad_refs, out_refs = refs[:blocks], refs[blocks : 2 * blocks], refs[2 * blocks : 3 * blocks]
    dbias_ref, tile_ref, diag_ref, dq_ref, dk_ref, dv_ref, grad_ref, mix_ref = refs[3 * blocks :]
    a = pl.program_id(0)
    length = qkv_ref.shape[0] // blocks
    width = bias_ref.shape[1]
    my = my_ref[0]
    mine = my ^ a

    @pl.when(a == 0)
    def _():
        spread_bias(bias_ref, tile_ref)
        diag_ref[...] = jnp.zeros_like(diag_ref)
        dk_ref[...] = jnp.zeros_like(dk_ref)
        dv_ref[...] = jnp.zeros_like(dv_ref)

    rows = pl.ds(pl.multiple_of(a * length, length), length)
    every = slice(0, length)
    for b in range(blocks):

        @pl.when(a == b)
        def _(b=b):
            grad_ref[...] = grad_refs[b][...]
            mix_ref[...] = mix_refs[b][...]

    dq_ref[...] = jnp.zeros_like(dq_ref)
    deltas = []
    for kv in range(kv_local):
        both = two_heads(grad_ref, every, kv * PAIR).astype(F32) * two_heads(mix_ref, every, kv * PAIR).astype(F32)
        deltas.append(jnp.sum(both.T, axis=0, keepdims=True))
    for b in range(blocks):
        source = my ^ b
        keys_at = slice(b * length, (b + 1) * length)

        @pl.when(source <= mine)
        def _(source=source, keys_at=keys_at):
            start = length + length * (mine - source)
            for kv in range(kv_local):
                q_at, k_at, v_at = head_columns(kv_local, kv)
                qq = two_heads(qkv_ref, rows, q_at)
                dd = two_heads(grad_ref, every, q_at)
                keys = qkv_ref[keys_at, k_at : k_at + HEAD_DIM]
                values = qkv_ref[keys_at, v_at : v_at + HEAD_DIM]
                scores = dot32(keys, qq, NT) * SCALE + bias_tile(tile_ref, kv, start, length)
                probs = jnp.exp(scores - lse_ref[0, kv])
                dv_ref[kv, keys_at, :] += dot32(probs.astype(BF16), dd)
                change = dot32(values, dd, NT) - deltas[kv]
                ds = (probs * change).astype(BF16)
                dk_ref[kv, keys_at, :] += dot32(ds, qq)
                dq_ref[kv] += dot32(keys, ds, TN)
                ds = ds.astype(F32)
                for g in range(2):
                    for m in range(length // LANES):
                        where = pl.ds(pl.multiple_of(start - LANES * m, LANES), length)
                        diag_ref[2 * kv + g, :, where] += ds[m * LANES : (m + 1) * LANES, g * length : (g + 1) * length]

    for b in range(blocks):

        @pl.when(a == b)
        def _(out_ref=out_refs[b]):
            for kv in range(kv_local):
                back = (dq_ref[kv] * SCALE).T.astype(BF16)
                out_ref[:, kv * PAIR : kv * PAIR + HEAD_DIM] = back[:length]
                out_ref[:, kv * PAIR + HEAD_DIM : (kv + 1) * PAIR] = back[length:]

    @pl.when(a == blocks - 1)
    def _():
        for kv in range(kv_local):
            _, k_at, v_at = head_columns(kv_local, kv)
            for b, out_ref in enumerate(out_refs):
                keys_at = slice(b * length, (b + 1) * length)
                out_ref[:, k_at : k_at + HEAD_DIM] = (dk_ref[kv, keys_at, :] * SCALE).astype(BF16)
                out_ref[:, v_at : v_at + HEAD_DIM] = dv_ref[kv, keys_at, :].astype(BF16)
        for h in range(2 * kv_local):
            part = diag_ref[h]
            half = LANES // 2
            while half:
                part = part[:half] + pltpu.roll(part[half:], width - half, 1)
                half //= 2
            dbias_ref[h : h + 1, :] = part


def cross_forward_kernel(allow_ref, q_ref, k_ref, v_ref, mix_ref, lse_ref):
    allow = allow_ref[...] > 0
    for kv in range(2):
        low = kv * HEAD_DIM
        qq = stacked(q_ref, kv)
        scores = dot32(k_ref[:, low : low + HEAD_DIM], qq, NT) * SCALE
        scores = jnp.where(allow, scores, NEGATIVE)
        top = jnp.max(scores, axis=0, keepdims=True)
        raised = jnp.exp(scores - top)
        total = jnp.sum(raised, axis=0, keepdims=True)
        probs = (raised * (1.0 / total)).astype(BF16)
        unstack(mix_ref, kv, dot32(v_ref[:, low : low + HEAD_DIM], probs, TN))
        lse_ref[kv] = top + jnp.log(total)


def cross_backward_kernel(allow_ref, q_ref, k_ref, v_ref, lse_ref, grad_ref, dq_ref, dkv_ref):
    allow = allow_ref[...] > 0
    for kv in range(2):
        low = kv * HEAD_DIM
        qq = stacked(q_ref, kv)
        dd = stacked(grad_ref, kv)
        keys = k_ref[:, low : low + HEAD_DIM]
        scores = jnp.where(allow, dot32(keys, qq, NT) * SCALE, NEGATIVE)
        probs = jnp.exp(scores - lse_ref[kv])
        change = dot32(v_ref[:, low : low + HEAD_DIM], dd, NT)
        delta = jnp.sum(probs * change, axis=0, keepdims=True)
        ds = (probs * (change - delta)).astype(BF16)
        dkv_ref[1, :, low : low + HEAD_DIM] = dot32(probs.astype(BF16), dd).astype(BF16)
        dkv_ref[0, :, low : low + HEAD_DIM] = (dot32(ds, qq) * SCALE).astype(BF16)
        unstack(dq_ref, kv, dot32(keys, ds, TN) * SCALE)


TINY = pl.CostEstimate(flops=1, transcendentals=0, bytes_accessed=1)


def params():
    return pltpu.CompilerParams(dimension_semantics=("arbitrary",), vmem_limit_bytes=VMEM_LIMIT)


def cost(length, keys, heads, passes, moved):
    return pl.CostEstimate(
        flops=2 * length * keys * heads * HEAD_DIM * passes,
        transcendentals=length * keys * heads,
        bytes_accessed=moved,
    )


def lane_block(rows, width):
    return pl.BlockSpec((rows, width), lambda i: (0, i))


def self_forward(blocks, my, qkv, bias):
    tokens, columns = qkv.shape
    length, kv_local, width = tokens // blocks, columns // (2 * PAIR), bias.shape[1]
    q_width = kv_local * PAIR
    return pl.pallas_call(
        functools.partial(self_forward_kernel, blocks, kv_local),
        grid=(blocks,),
        in_specs=[
            pl.BlockSpec(memory_space=pltpu.SMEM),
            pl.BlockSpec((tokens, columns), lambda i: (0, 0)),
            pl.BlockSpec(bias.shape, lambda i: (0, 0)),
        ],
        out_specs=[pl.BlockSpec((length, q_width), lambda i: (0, 0))] * blocks
        + [pl.BlockSpec((1, kv_local, 1, 2 * length), lambda i: (i, 0, 0, 0))],
        out_shape=[jax.ShapeDtypeStruct((length, q_width), BF16)] * blocks
        + [jax.ShapeDtypeStruct((blocks, kv_local, 1, 2 * length), F32)],
        scratch_shapes=[
            pltpu.VMEM((2 * kv_local, LANES, width), F32),
            pltpu.VMEM((kv_local, 1, 2 * length), F32),
            pltpu.VMEM((kv_local, 1, 2 * length), F32),
            pltpu.VMEM((kv_local, HEAD_DIM, 2 * length), F32),
        ],
        compiler_params=params(),
        cost_estimate=TINY,
        name="self_forward",
    )(my, qkv, bias)


def self_backward(blocks, my, qkv, bias, mixes, lse, grads):
    tokens, columns = qkv.shape
    length, kv_local, width = tokens // blocks, columns // (2 * PAIR), bias.shape[1]
    q_width = kv_local * PAIR
    lines = pl.BlockSpec(bias.shape, lambda i: (0, 0))
    *outs, d_bias = pl.pallas_call(
        functools.partial(self_backward_kernel, blocks, kv_local),
        grid=(blocks,),
        in_specs=[
            pl.BlockSpec(memory_space=pltpu.SMEM),
            pl.BlockSpec((tokens, columns), lambda i: (0, 0)),
            lines,
            pl.BlockSpec((1, kv_local, 1, 2 * length), lambda i: (i, 0, 0, 0)),
        ]
        + [pl.BlockSpec((length, q_width), lambda i: (0, 0))] * (2 * blocks),
        out_specs=[pl.BlockSpec((length, columns), lambda i: (0, 0))] * blocks + [lines],
        out_shape=[jax.ShapeDtypeStruct((length, columns), BF16)] * blocks + [jax.ShapeDtypeStruct(bias.shape, F32)],
        scratch_shapes=[
            pltpu.VMEM((2 * kv_local, LANES, width), F32),
            pltpu.VMEM((2 * kv_local, LANES, width), F32),
            pltpu.VMEM((kv_local, HEAD_DIM, 2 * length), F32),
            pltpu.VMEM((kv_local, tokens, HEAD_DIM), F32),
            pltpu.VMEM((kv_local, tokens, HEAD_DIM), F32),
            pltpu.VMEM((length, q_width), BF16),
            pltpu.VMEM((length, q_width), BF16),
        ],
        compiler_params=params(),
        cost_estimate=TINY,
        name="self_backward",
    )(my, qkv, bias, lse, *mixes, *grads)
    return outs, d_bias


def cross_forward(allow, q, k, v):
    length, keys, kv_heads = q.shape[0], k.shape[0], k.shape[1] // HEAD_DIM
    return pl.pallas_call(
        cross_forward_kernel,
        grid=(kv_heads // 2,),
        in_specs=[
            pl.BlockSpec((keys, 1), lambda i: (0, 0)),
            lane_block(length, 2 * PAIR),
            lane_block(keys, PAIR),
            lane_block(keys, PAIR),
        ],
        out_specs=[
            lane_block(length, 2 * PAIR),
            pl.BlockSpec((2, 1, 2 * length), lambda i: (i, 0, 0)),
        ],
        out_shape=[
            jax.ShapeDtypeStruct(q.shape, BF16),
            jax.ShapeDtypeStruct((kv_heads, 1, 2 * length), F32),
        ],
        compiler_params=params(),
        cost_estimate=TINY,
        name="cross_forward",
    )(allow, q, k, v)


def cross_backward(allow, q, k, v, lse, grad):
    length, keys, kv_heads = q.shape[0], k.shape[0], k.shape[1] // HEAD_DIM
    return pl.pallas_call(
        cross_backward_kernel,
        grid=(kv_heads // 2,),
        in_specs=[
            pl.BlockSpec((keys, 1), lambda i: (0, 0)),
            lane_block(length, 2 * PAIR),
            lane_block(keys, PAIR),
            lane_block(keys, PAIR),
            pl.BlockSpec((2, 1, 2 * length), lambda i: (i, 0, 0)),
            lane_block(length, 2 * PAIR),
        ],
        out_specs=[
            lane_block(length, 2 * PAIR),
            pl.BlockSpec((2, keys, PAIR), lambda i: (0, 0, i)),
        ],
        out_shape=[
            jax.ShapeDtypeStruct(q.shape, BF16),
            jax.ShapeDtypeStruct((2,) + k.shape, BF16),
        ],
        compiler_params=params(),
        cost_estimate=TINY,
        name="cross_backward",
    )(allow, q, k, v, lse, grad)


def slab_kernel(kind, later, x_count, g_count, gained, order_ref, *refs):
    xs, gs = refs[:x_count], refs[x_count : x_count + g_count]
    turned_ref, whole_ref = refs[-2:]
    keep_ref, send_ref = refs[-5:-3] if gained else refs[-4:-2]
    slab = pl.program_id(0)
    kind = jnp.where(slab < later, 0, 1) if kind is None else kind

    @pl.when(slab == 0)
    def _():
        low = 0
        for x in xs:
            turned_ref[low : low + x.shape[1], :] = x[...].T
            low += x.shape[1]

    chunks, rows, width = whole_ref.shape
    g = gs[0][...] if g_count == 1 else jnp.concatenate([ref[...] for ref in gs], axis=0)
    full = dot32(turned_ref[...], g)
    whole_ref[...] = full.reshape(chunks, rows, width)
    half = chunks // 2
    for c in range(half):
        keep_ref[c] = whole_ref[order_ref[kind, c]].astype(BF16)
        send_ref[c] = whole_ref[order_ref[kind, half + c]].astype(BF16)
    if gained:
        refs[-3][...] = jnp.sum(full * refs[x_count + g_count][...].astype(F32), axis=1, keepdims=True)


def slabs(order, x, g, total, at, later, buffers, kind=None, slab=SLAB, weight=None):
    xs = x if isinstance(x, list) else [x]
    tokens, features = xs[0].shape[0], sum(part.shape[1] for part in xs)
    chunks = order.shape[1]
    rows = features // chunks
    gs = g if isinstance(g, list) else [g]
    if len(gs) > 1:
        count, g_specs = 1, whole_blocks(gs)
    elif g.ndim == 3:
        count, g_specs = g.shape[0], [pl.BlockSpec((None, tokens, slab), lambda i: (i, 0, 0))]
    else:
        count, g_specs = g.shape[1] // slab, [pl.BlockSpec((tokens, slab), lambda i: (0, i))]
    assert at % rows == 0 and features % chunks == 0 and rows % 8 == 0
    out = pl.BlockSpec((chunks // 2, rows, slab), lambda i: (0, at // rows + i, 0))
    shapes = [jax.ShapeDtypeStruct((chunks // 2, total, slab), BF16)] * 2
    outs = [out, out]
    extra = [] if buffers is None else list(buffers)
    first = 1 + len(xs) + len(gs)
    weights = []
    if weight is not None:
        weights = [weight]
        shapes.append(jax.ShapeDtypeStruct((features, 1), F32))
        outs.append(pl.BlockSpec((features, 1), lambda i: (0, 0)))
    return pl.pallas_call(
        functools.partial(slab_kernel, kind, later, len(xs), len(gs), weight is not None),
        grid=(count,),
        in_specs=[pl.BlockSpec(memory_space=pltpu.SMEM)]
        + whole_blocks(xs)
        + g_specs
        + whole_blocks(weights)
        + [pl.BlockSpec(memory_space=pl.ANY)] * len(extra),
        out_specs=outs,
        out_shape=shapes,
        scratch_shapes=[pltpu.VMEM((features, tokens), BF16), pltpu.VMEM((chunks, rows, slab), F32)],
        input_output_aliases={first: 0, first + 1: 1} if extra else {},
        compiler_params=params(),
        cost_estimate=TINY,
        name="slabs",
    )(order, *xs, *gs, *weights, *extra)


def cover(*ranges):
    held, row = [], 0
    for low, high in ranges:
        held.append((low, high, row))
        row += high - low
    return held


def add_range(sources, refs, low, high):
    total = None
    for number, segments in sources:
        for start, stop, row in segments:
            if start <= low and high <= stop:
                part = refs[number][:, row + low - start : row + high - start, :].astype(F32)
                total = part if total is None else total + part
    return total


def cut_points(pieces, low, high):
    marks = {low, high}
    for _, segments in pieces:
        marks |= {m for start, stop, _ in segments for m in (start, stop) if low < m < high}
    marks = sorted(marks)
    return list(zip(marks[:-1], marks[1:]))


def total_kernel(plan, *refs):
    inputs, results = refs[: -len(plan)], refs[-len(plan) :]
    for (sources, writes), result in zip(plan, results):
        for row, low, high in writes:
            result[:, row : row + high - low, :] = add_range(sources, inputs, low, high).astype(result.dtype)


def totals(pieces, groups, steps):
    plan, specs, arrays, shapes, outs = [], [], [], [], []
    width = pieces[0][0].shape[2]
    for first, count, ranges in groups:
        step = count // steps
        sources = []
        for array, segments in pieces:
            sources.append((len(arrays), segments))
            arrays.append(array)
            specs.append(pl.BlockSpec((step,) + array.shape[1:], lambda i, low=first // step: (low + i, 0, 0)))
        writes, rows = [], 0
        for low, high in ranges:
            for a, b in cut_points(pieces, low, high):
                writes.append((rows, a, b))
                rows += b - a
        plan.append((sources, writes))
        outs.append(pl.BlockSpec((step, rows, width), lambda i: (i, 0, 0)))
        shapes.append(jax.ShapeDtypeStruct((count, rows, width), BF16))
    return pl.pallas_call(
        functools.partial(total_kernel, plan),
        grid=(steps,),
        in_specs=specs,
        out_specs=outs,
        out_shape=shapes,
        compiler_params=params(),
        cost_estimate=TINY,
        name="totals",
    )(*arrays)


def finish_kernel(sources, outs, dealt, my_ref, *refs):
    inputs, results = refs[: len(sources)], refs[len(sources) :]
    for row, rows, number, column in outs:
        results[number][:, column : column + SLAB] = add_range(sources, inputs, row, row + rows)[0]
    for j, row, rows, parts in dealt:
        block = add_range(sources, inputs, row, row + rows)[0]
        low = 0
        for number, width in parts:
            columns = pl.ds(pl.multiple_of((my_ref[0] ^ j) * width, LANES), width)
            results[number][:, columns] = block[:, low : low + width]
            low += width


def finish(my, pieces, shapes, outs, dealt):
    sources = [(number, segments) for number, (_, segments) in enumerate(pieces)]
    return pl.pallas_call(
        functools.partial(finish_kernel, sources, outs, dealt),
        grid=(1,),
        in_specs=[pl.BlockSpec(memory_space=pltpu.SMEM)]
        + [pl.BlockSpec((1,) + array.shape[1:], lambda i: (0, 0, 0)) for array, _ in pieces],
        out_specs=[pl.BlockSpec(shape, lambda i: (0, 0)) for shape in shapes],
        out_shape=[jax.ShapeDtypeStruct(shape, F32) for shape in shapes],
        compiler_params=params(),
        cost_estimate=TINY,
        name="finish",
    )(my, *[array for array, _ in pieces])


def pair_dot_kernel(x_count, *refs):
    result = refs[-1]
    xs, gs = refs[:x_count], refs[x_count:-1]
    x = jnp.concatenate([ref[...] for ref in xs], axis=0)
    g = jnp.concatenate([ref[...] for ref in gs], axis=0)
    result[...] = dot32(x, g, TN).astype(BF16)


def whole_blocks(arrays):
    return [pl.BlockSpec(a.shape, lambda i, n=a.ndim: (0,) * n) for a in arrays]


def pair_dot(xs, gs):
    features, width = xs[0].shape[1], gs[0].shape[1]
    return pl.pallas_call(
        functools.partial(pair_dot_kernel, len(xs)),
        grid=(1,),
        in_specs=whole_blocks(list(xs) + list(gs)),
        out_specs=pl.BlockSpec((features, width), lambda i: (0, 0)),
        out_shape=jax.ShapeDtypeStruct((features, width), BF16),
        compiler_params=params(),
        cost_estimate=TINY,
        name="pair_dot",
    )(*xs, *gs)


def dot_gain_kernel(x_ref, g_ref, w_ref, out_ref, gain_ref):
    full = dot32(x_ref[...], g_ref[...], TN)
    out_ref[...] = full.astype(BF16)
    gain_ref[...] = jnp.sum(full * w_ref[...].astype(F32), axis=1, keepdims=True)


def dot_gain(x, g, w):
    features, width = w.shape
    return pl.pallas_call(
        dot_gain_kernel,
        grid=(1,),
        in_specs=whole_blocks([x, g, w]),
        out_specs=[pl.BlockSpec((features, width), lambda i: (0, 0)), pl.BlockSpec((features, 1), lambda i: (0, 0))],
        out_shape=[jax.ShapeDtypeStruct((features, width), BF16), jax.ShapeDtypeStruct((features, 1), F32)],
        compiler_params=params(),
        cost_estimate=TINY,
        name="dot_gain",
    )(x, g, w)


def add_norm_kernel(count, has_next, *refs):
    xs, ws = refs[:count], refs[count : 2 * count]
    base_ref, gain_ref = refs[2 * count : 2 * count + 2]
    total = base_ref[...].astype(F32)
    for x, w in zip(xs, ws):
        total = total + dot32(x[...], w[...])
    normed = (total * inverse_rms(total) * gain_ref[...]).astype(BF16)
    if has_next:
        next_ref, total_ref, normed_ref, out_ref = refs[2 * count + 2 :]
        out_ref[...] = dot32(normed, next_ref[...]).astype(BF16)
    else:
        total_ref, normed_ref = refs[2 * count + 2 :]
    total_ref[...] = total
    normed_ref[...] = normed


def add_norm(base, xs, ws, gain, after=None):
    shapes = [jax.ShapeDtypeStruct(base.shape, F32), jax.ShapeDtypeStruct(base.shape, BF16)]
    inputs = [*xs, *ws, base, gain[None]]
    if after is not None:
        inputs.append(after)
        shapes.append(jax.ShapeDtypeStruct((base.shape[0], after.shape[1]), BF16))
    return pl.pallas_call(
        functools.partial(add_norm_kernel, len(xs), after is not None),
        grid=(1,),
        in_specs=whole_blocks(inputs),
        out_specs=whole_blocks(shapes),
        out_shape=shapes,
        compiler_params=params(),
        cost_estimate=TINY,
        name="add_norm",
    )(*inputs)


def norm_grad_kernel(count, nexts, *refs):
    gs, ws = refs[:count], refs[count : 2 * count]
    x_ref, gain_ref, base_ref = refs[2 * count : 2 * count + 3]
    after = refs[2 * count + 3 : 2 * count + 3 + nexts]
    grad_ref, low_ref, gain_grad_ref = refs[2 * count + 3 + nexts : 2 * count + 6 + nexts]
    outs, acc_ref = refs[2 * count + 6 + nexts : -1], refs[-1]
    step = pl.program_id(0)

    @pl.when(step == 0)
    def _():
        acc_ref[...] = jnp.zeros_like(acc_ref)

    part = None
    for g, w in zip(gs, ws):
        term = dot32(g[...], w[...], NT)
        part = term if part is None else part + term
    acc_ref[...] += part

    @pl.when(step == pl.num_programs(0) - 1)
    def _():
        total = acc_ref[...]
        x = x_ref[...].astype(F32)
        d_x, d_gain = norm_back(x, inverse_rms(x), gain_ref[...], total)
        grad = base_ref[...].astype(F32) + d_x
        low = grad.astype(BF16)
        grad_ref[...] = grad
        low_ref[...] = low
        gain_grad_ref[...] = d_gain[None]
        for w, out in zip(after, outs):
            out[...] = dot32(low, w[...], NT).astype(BF16)


def norm_grad(base, gs, ws, x, gain, after, tile):
    length, width = x.shape
    inner = gs[0].shape[1]
    fixed = [x, gain[None], base, *after]
    shapes = [
        jax.ShapeDtypeStruct(x.shape, F32),
        jax.ShapeDtypeStruct(x.shape, BF16),
        jax.ShapeDtypeStruct((1, width), F32),
    ] + [jax.ShapeDtypeStruct((length, w.shape[0]), BF16) for w in after]
    grad, low, d_gain, *outs = pl.pallas_call(
        functools.partial(norm_grad_kernel, len(gs), len(after)),
        grid=(inner // tile,),
        in_specs=[pl.BlockSpec((length, tile), lambda i: (0, i))] * len(gs)
        + [pl.BlockSpec((width, tile), lambda i: (0, i))] * len(ws)
        + whole_blocks(fixed),
        out_specs=whole_blocks(shapes),
        out_shape=shapes,
        scratch_shapes=[pltpu.VMEM((length, width), F32)],
        compiler_params=params(),
        cost_estimate=TINY,
        name="norm_grad",
    )(*gs, *ws, *fixed)
    return grad, low, d_gain[0], outs


def norm_dot_kernel(count, *refs):
    gain_ref, w_ref, normed_ref, out_ref = refs[count:]
    for k, ref in enumerate(refs[:count]):
        length = ref.shape[0]
        rows = slice(k * length, (k + 1) * length)
        x = ref[...].astype(F32)
        normed = (x * inverse_rms(x) * gain_ref[...]).astype(BF16)
        normed_ref[rows, :] = normed
        out_ref[rows, :] = dot32(normed, w_ref[...]).astype(BF16)


def norm_dot(xs, gain, w):
    rows = len(xs) * xs[0].shape[0]
    shapes = [(rows, w.shape[0]), (rows, w.shape[1])]
    return pl.pallas_call(
        functools.partial(norm_dot_kernel, len(xs)),
        grid=(1,),
        in_specs=whole_blocks([*xs, gain, w]),
        out_specs=[pl.BlockSpec(shape, lambda i: (0, 0)) for shape in shapes],
        out_shape=[jax.ShapeDtypeStruct(shape, BF16) for shape in shapes],
        compiler_params=params(),
        cost_estimate=TINY,
        name="norm_dot",
    )(*xs, gain, w)


def turn_kernel(my_ref, x_ref, *refs):
    results, chunk_ref = refs[:-1], refs[-1]
    count = len(results)
    chunk_ref[...] = x_ref[...].astype(F32).T.reshape(chunk_ref.shape)
    for j, result in enumerate(results):
        for k in range(result.shape[0]):
            result[k] = chunk_ref[k * count + (my_ref[0] ^ j)].astype(BF16)


def turn_chunks(my, x, blocks, devices):
    tokens, features = x.shape
    shape = (devices // blocks, features // devices, tokens)
    return pl.pallas_call(
        turn_kernel,
        grid=(1,),
        in_specs=[pl.BlockSpec(memory_space=pltpu.SMEM)] + whole_blocks([x]),
        out_specs=[pl.BlockSpec(shape, lambda i: (0, 0, 0))] * blocks,
        out_shape=[jax.ShapeDtypeStruct(shape, BF16)] * blocks,
        scratch_shapes=[pltpu.VMEM((devices, features // devices, tokens), F32)],
        compiler_params=params(),
        cost_estimate=TINY,
        name="turn_chunks",
    )(my, x)


def turned_dot_kernel(count, my_ref, *refs):
    xs, (g_ref, result) = refs[:count], refs[count:]
    chunks, rows, tokens = xs[0].shape
    total = None
    for j, ref in enumerate(xs):
        x = ref[...].astype(F32).reshape(chunks * rows, tokens).astype(BF16)
        term = dot32(x, g_ref[my_ref[0] ^ j])
        total = term if total is None else total + term
    result[...] = total.reshape(result.shape).astype(BF16)


def turned_dot(my, xs, g):
    chunks, rows, tokens = xs[0].shape
    width = g.shape[1]
    g = g.reshape(len(xs), tokens, width)
    return pl.pallas_call(
        functools.partial(turned_dot_kernel, len(xs)),
        grid=(1,),
        in_specs=[pl.BlockSpec(memory_space=pltpu.SMEM)] + whole_blocks([*xs, g]),
        out_specs=pl.BlockSpec((chunks, rows, width), lambda i: (0, 0, 0)),
        out_shape=jax.ShapeDtypeStruct((chunks, rows, width), BF16),
        compiler_params=params(),
        cost_estimate=TINY,
        name="turned_dot",
    )(my, *xs, g)


def place_kernel(my_ref, *refs):
    parts, results = refs[:-2], refs[-2:]
    per_half = len(parts) // 2
    share = parts[0].shape[1]
    for j, part in enumerate(parts):
        owner = my_ref[0] ^ j
        for number, result in enumerate(results):

            @pl.when(owner // per_half == number)
            def _(part=part, result=result, number=number, owner=owner):
                columns = pl.ds(pl.multiple_of((owner - number * per_half) * share, LANES), share)
                result[:, columns] = part[...].astype(F32)


def place(my, parts):
    shape = (parts[0].shape[0], len(parts) // 2 * parts[0].shape[1])
    return pl.pallas_call(
        place_kernel,
        grid=(1,),
        in_specs=[pl.BlockSpec(memory_space=pltpu.SMEM)] + whole_blocks(parts),
        out_specs=[pl.BlockSpec(shape, lambda i: (0, 0))] * 2,
        out_shape=[jax.ShapeDtypeStruct(shape, F32)] * 2,
        compiler_params=params(),
        cost_estimate=TINY,
        name="place",
    )(my, *parts)


def exchange_order():
    dp, blk = lax.axis_size("dp"), lax.axis_size("blk")
    dp_bits, blk_bits = dp.bit_length() - 1, blk.bit_length() - 1
    mine = lax.axis_index("dp") * blk + lax.axis_index("blk")
    deep = list(range(blk_bits + 1, blk_bits + dp_bits))
    up, down = list(range(blk_bits)), list(reversed(range(blk_bits)))
    tables = []
    for order in (up + deep, down + deep, deep + down):
        order = [blk_bits] + order
        table = []
        for place in range(dp * blk):
            relative = 0
            for k, bit in enumerate(order):
                relative |= ((place >> (len(order) - 1 - k)) & 1) << bit
            table.append(relative)
        tables.append(table)
    return jnp.array(tables, jnp.int32) ^ mine.astype(jnp.int32)


class Halves:
    def __init__(self, keep, got, over_x, over_y):
        self.rows = [(0, keep.shape[1])]
        self.pieces = [(keep, cover(*self.rows)), (got, cover(*self.rows))]
        self.parts, self.chunks = (over_x, over_y), keep.shape[0]

    def pack(self, deep=False):
        half = self.chunks // 2
        parts = [self.rows] if deep else self.parts
        self.out = totals(self.pieces, [(half, half, part) for part in parts], 2 if half > 4 else 1)
        self.chunks = half

    def hop(self, bits):
        self.got = [swap(out, "blk", bit) for out, bit in zip(self.out, bits)]

    def join(self, pieces, end):
        self.pieces += pieces
        self.rows = [(0, end)]

    def hop_deep(self, bit):
        self.got = [swap(self.out[0], "dp", bit)]

    def arrive(self):
        parts = [self.rows] if len(self.got) == 1 else self.parts
        self.pieces += [(array, cover(*part)) for array, part in zip(self.got, parts)]


def turn_rows(x, rows):
    my = lax.axis_index("blk")
    return jnp.concatenate([lax.dynamic_slice_in_dim(x, (my ^ j) * rows, rows, 0) for j in range(lax.axis_size("blk"))], axis=0)


def inverse_rms(x):
    return lax.rsqrt(jnp.mean(x * x, axis=-1, keepdims=True) + EPSILON)


def norm_back(x, inverse, gain, grad):
    scaled = grad * gain
    along = jnp.mean(scaled * x, axis=-1, keepdims=True)
    d_x = inverse * scaled - x * (inverse * inverse * inverse * along)
    return d_x, jnp.sum(grad * (x * inverse), axis=0)


def body(
    block_in,
    memory,
    memory_len,
    cross_mask,
    buckets,
    bias_table,
    norm_self,
    w_query,
    w_key,
    w_value,
    w_out,
    norm_cross,
    cross_query,
    cross_key,
    cross_value,
    cross_out,
    norm_ffn,
    w_gate,
    w_up,
    w_down,
    grad_out,
):
    seq_count, length, model_width = block_in.shape
    assert seq_count == 1
    mem_rows = memory.shape[1]
    mem_total = cross_mask.shape[1]
    blocks = lax.axis_size("blk")
    my = lax.axis_index("blk")
    kv_width = w_key.shape[1]
    head_count = w_query.shape[1] // HEAD_DIM
    bucket_count = bias_table.shape[0]
    my_ref = my.reshape(1).astype(jnp.int32)

    x_parts = [block_in[0]] + trade([block_in[0]] * blocks, "blk", 1)

    own_heads = head_count // blocks
    own_q, own_kv = own_heads * HEAD_DIM, kv_width // blocks
    turned_qkv = [
        jnp.concatenate(
            [
                lax.dynamic_slice_in_dim(w, (my ^ j) * width, width, 1)
                for w, width in ((w_query, own_q), (w_key, own_kv), (w_value, own_kv))
            ],
            axis=1,
        )
        for j in range(blocks)
    ]
    out_turned = [lax.dynamic_slice_in_dim(w_out, (my ^ j) * own_q, own_q, 0) for j in range(blocks)]

    bucket_hot = (buckets[:, None] == jnp.arange(bucket_count)[None, :]).astype(F32)
    own_table = lax.dynamic_slice_in_dim(bias_table, my * own_heads, own_heads, 1)
    dist_bias = lax.dot_general(own_table, bucket_hot, (((0,), (1,)), ((), ())), precision=lax.Precision.HIGHEST)
    bias = jnp.concatenate([jnp.full((own_heads, length), NEGATIVE, F32), dist_bias], axis=1)

    mem_places = jnp.arange(mem_total)
    allowed = (mem_places == 0) | (mem_places < memory_len[0]) & (cross_mask[0] == 1)
    allow = allowed.astype(F32).reshape(blocks, mem_rows)[my ^ jnp.arange(blocks)].reshape(mem_total, 1)

    d_hidden = dot32(grad_out[0], w_down, NT)
    x_parts, mem_own, turned_qkv, out_turned, d_hidden, bias, allow, top_own = tie(
        x_parts, memory[0], turned_qkv, out_turned, d_hidden, bias, allow, grad_out[0]
    )
    top_all = lax.all_gather(top_own, "blk", axis=0, tiled=True)
    mem_all = jnp.concatenate([mem_own] + trade([mem_own] * blocks, "blk", 1), axis=0)
    self_all, qkv = norm_dot(x_parts, norm_self[None], turned_qkv[0])
    *own_mix, lse = self_forward(blocks, my_ref, qkv, bias)
    mem_key = dot32(mem_all, cross_key).astype(BF16)
    mem_value = dot32(mem_all, cross_value).astype(BF16)
    mix_got, mem_key, mem_value = tie(trade(own_mix, "blk", 1), mem_key, mem_value)
    mixes = [own_mix[0]] + mix_got
    after_self, cross_in, cross_q = add_norm(block_in[0], mixes, out_turned, norm_cross, cross_query)
    cross_mix, cross_lse = cross_forward(allow, cross_q, mem_key, mem_value)
    after_cross, ffn_in = add_norm(after_self, [cross_mix], [cross_out], norm_ffn)
    devices = blocks * lax.axis_size("dp")
    d, ff = model_width, w_gate.shape[1]
    share = 2 * ff // blocks
    fast = (
        blocks == 4
        and lax.axis_size("dp") == 8
        and d % (8 * devices) == 0
        and ff % (8 * devices) == 0
        and kv_width == SLAB
        and d % SLAB == 0
        and share % LANES == 0
    )
    gate = dot32(ffn_in, w_gate)
    up = dot32(ffn_in, w_up)
    (act, hidden_full), gated_back = jax.vjp(lambda g, u: (jax.nn.gelu(g, approximate=True), jax.nn.gelu(g, approximate=True) * u), gate, up)
    hidden = hidden_full.astype(BF16)

    ffn_grad = grad_out[0]
    gate_full, up_full = gated_back((jnp.zeros_like(act), d_hidden))
    gate_grad, up_grad = gate_full.astype(BF16), up_full.astype(BF16)
    if fast:
        order = exchange_order()
        turned = order ^ ((my * (devices // blocks)).astype(jnp.int32))
        small, large = d // devices, ff // devices
        d_slabs = d // SLAB
        half = length // 2
        near = trade([ffn_in] * 3, "blk", 1)
        gate_grad, up_grad, top_all, near = tie(gate_grad, up_grad, top_all, near)
        far = [swap(near[0][:half], "blk", 2), swap(near[1][half:], "blk", 1)]
        both_grad = jnp.concatenate([gate_grad, up_grad], axis=1)
        shares = [lax.dynamic_slice_in_dim(both_grad, (my ^ j) * share, share, 1) for j in range(blocks)]
        shares, hidden = tie(shares, hidden)
        shares_near = trade(shares[:3], "blk", 1)
        hidden_parts = turn_chunks(my_ref, hidden, blocks, devices)
    else:
        dw_down = sum_rows(dot32(hidden, ffn_grad, TN).astype(BF16), 1)
        ffn_outs = (
            sum_rows(dot32(ffn_in, gate_grad, TN).astype(BF16), 0),
            sum_rows(dot32(ffn_in, up_grad, TN).astype(BF16), 1),
            dw_down,
        )
    tile = ff // 2 if ff % (2 * LANES) == 0 else ff
    grad_cross, cross_grad, d_gain_ffn, (mix_grad,) = norm_grad(
        ffn_grad, [gate_grad, up_grad], [w_gate, w_up], after_cross, norm_ffn, [cross_out], tile
    )
    if fast:
        mix_grad, shares_near, shares[3], hidden_parts, far = tie(mix_grad, shares_near, shares[3], hidden_parts, far)
        ffn_parts = [ffn_in] + near + far
        share_far = swap(shares[3], "blk", 3)
        hidden_got = trade(hidden_parts, "blk", 1)
    block_out = (after_cross + dot32(hidden, w_down)).astype(BF16)
    cq_grad, mem_part = cross_backward(allow, cross_q, mem_key, mem_value, cross_lse, mix_grad)
    if fast:
        total = 4 * d_slabs * small
        held = slabs(order, cross_mix, cross_grad, total, 0, total, None)
        cq_grad, mem_part, share_far, hidden_got, block_out, held = tie(cq_grad, mem_part, share_far, hidden_got, block_out, held)
    grad_self, self_grad, d_gain_cross, grad_parts = norm_grad(
        grad_cross, [cq_grad], [cross_query], after_self, norm_cross, out_turned, d
    )
    grad_got = trade(grad_parts, "blk", 1)
    if fast:
        shares_near, held, cq_late, self_late = tie(shares_near, held, cq_grad, self_grad)
        wide = pair_dot(ffn_parts, [shares[0]] + shares_near + [share_far])
        grad_got, wide, held, mem_late = tie(grad_got, wide, held, mem_part)
        wide = lax.psum_scatter(wide, "dp", scatter_dimension=0, tiled=True)
        held = slabs(order, cross_in, cq_late, total, d_slabs * small, total, held)
        held = slabs(order, mem_all, mem_late, total, 2 * d_slabs * small, 0, held)
        keep, send = slabs(turned, mixes, self_late, total, 3 * d_slabs * small, 0, held)
        got = swap(send, "dp", 1)
        hidden_got, keep = tie(hidden_got, keep)
        down = turned_dot(my_ref, [hidden_parts[0]] + hidden_got, top_all)
        down, got = tie(down, got)
        cross = Halves(keep, got, [(0, total // 2)], [(total // 2, total)])
        cross.pack()
        grad_got, cross.out = tie(grad_got, cross.out)
        cross.hop((1, 2))
    qkv_parts, bias_grad = self_backward(blocks, my_ref, qkv, bias, own_mix, lse, [grad_parts[0]] + grad_got)
    d_table = lax.dot_general(bucket_hot, bias_grad[:, length:], (((0,), (1,)), ((), ())), precision=lax.Precision.HIGHEST)
    d_table = lax.dynamic_update_slice_in_dim(jnp.zeros_like(bias_table), d_table, my * own_heads, 1)
    if fast:
        qkv_parts, mem_part, cross.got, wide = tie(qkv_parts, mem_part, cross.got, wide)
        down = lax.psum_scatter(down, "dp", scatter_dimension=0, tiled=True)
        cross.arrive()
        cross.pack()
        qkv_parts, cross.out = tie(qkv_parts, cross.out)
        cross.hop((2, 1))
        own = own_q + 2 * own_kv
        keep, send, gain_part = slabs(order, self_all, qkv_parts, small, 0, 0, None, 2, own, turned_qkv[0])
        gain_part = gain_part[:, 0]
        view = (-1, blocks * small, own)
        got = swap(send, "dp", 1)
        wides = [lax.dynamic_slice_in_dim(wide, (my ^ j) * small, small, 0) for j in range(blocks)]
        wides, got = tie(wides, got)
        sides = [(keep.reshape(view), cover((0, view[1]))), (got.reshape(view), cover((0, view[1])))]
        sides = totals(sides, [(0, cross.chunks, [(j * small, (j + 1) * small)]) for j in range(blocks)], 1)
        sides = [sides[0]] + trade(sides, "blk", 1)
        gain_part, cross.got, sides = tie(gain_part, cross.got, sides)
        cross.arrive()
        cross.join([(side, cover((total + j * small, total + (j + 1) * small))) for j, side in enumerate(sides)], total + view[1])
        cross.pack(True)
        gain_part, qkv_parts, cross.out, wides, d_table = tie(gain_part, qkv_parts, cross.out, wides, d_table)
        cross.hop_deep(2)
    else:
        attn, gain_part = dot_gain(self_all, jnp.concatenate(qkv_parts, axis=0), turned_qkv[0])
        gain_part = gain_part[:, 0]
    d_gain_self = gain_part / norm_self
    qkv_got = trade(qkv_parts, "blk", 1)
    d_block_in, _, _, _ = norm_grad(
        grad_self, [qkv_parts[0]] + qkv_got, turned_qkv, block_in[0], norm_self, [], own_q + 2 * own_kv
    )
    lines = jnp.concatenate([d_gain_self, d_gain_cross, d_gain_ffn, d_table.reshape(-1)]).reshape(-1, LANES)
    if fast:
        lines = sum_axis(sum_axis(lines, "dp", 1), "blk", blocks // 2)
        d_block_in, cross.got, mem_part, lines, down = tie(d_block_in, cross.got, mem_part, lines, down)
        cross.arrive()
        cross.pack(True)
        mem_part, lines, wides, cross.out = tie(mem_part, lines, wides, cross.out)
        cross.hop_deep(4)
        wides = [wides[0]] + trade(wides, "blk", 1)
    mem_blocks = mem_part.reshape(2, blocks, mem_rows, kv_width)
    bit = blocks // 2
    while bit:
        mem_blocks = add16(mem_blocks[:, :bit], swap(mem_blocks[:, bit:], "blk", bit))
        bit //= 2
    mem_grad = mem_blocks[:, 0]
    d_memory = dot32(mem_grad[0], cross_key, NT) + dot32(mem_grad[1], cross_value, NT)
    if fast:
        cross.arrive()
        lines = sum_axis(lines, "dp", lax.axis_size("dp") // 2, 2).reshape(-1)
    else:
        lines = sum_axis(sum_axis(lines, "dp", lax.axis_size("dp") // 2), "blk", blocks // 2).reshape(-1)
    gain_self, gain_cross, gain_ffn = lines[:d], lines[d : 2 * d], lines[2 * d : 3 * d]
    table_sum = lines[3 * d :].reshape(bias_table.shape)
    if fast:
        dw_gate, dw_up = place(my_ref, wides)
        shapes = [(small, d), (small, d), (small, kv_width), (small, kv_width), (small, d)]
        outs, row = [], 0
        for number, (_, width) in enumerate(shapes):
            for k in range(width // SLAB):
                outs.append((row, small, number, k * SLAB))
                row += small
        shapes += [(small, d), (small, kv_width), (small, kv_width)]
        dealt = [(j, row + j * small, small, ((5, own_q), (6, own_kv), (7, own_kv))) for j in range(blocks)]
        dw_co, dw_cq, dw_ck, dw_cv, dw_o, dw_q, dw_k, dw_v = finish(my_ref, cross.pieces, shapes, outs, dealt)
        dw_down = down[0].astype(F32)
        ffn_outs = (dw_gate, dw_up, dw_down)
    else:
        dw_co = sum_rows(dot32(cross_mix, cross_grad, TN).astype(BF16), 0)
        dw_cq = sum_rows(dot32(cross_in, cq_grad, TN).astype(BF16), 1)
        dw_ck = sum_rows(dot32(mem_all, mem_part[0], TN).astype(BF16), 0)
        dw_cv = sum_rows(dot32(mem_all, mem_part[1], TN).astype(BF16), 1)
        dw_o = sum_rows(turn_rows(dot32(jnp.concatenate(mixes, axis=1), self_grad, TN).astype(BF16), own_q), 0)
        dw_q, dw_k, dw_v = [
            sum_rows(lax.dynamic_update_slice_in_dim(jnp.zeros((d, width), BF16), attn[:, low : low + width // blocks], my * (width // blocks), 1), 0)
            for width, low in ((blocks * own_q, 0), (kv_width, own_q), (kv_width, own_q + own_kv))
        ]
    return (
        block_out[None],
        d_block_in[None],
        d_memory[None],
        table_sum,
        gain_self,
        dw_q,
        dw_k,
        dw_v,
        dw_o,
        gain_cross,
        dw_cq,
        dw_ck,
        dw_cv,
        dw_co,
        gain_ffn,
        *ffn_outs,
    )


def solution(mesh):
    rows = P("dp", "blk", None)
    split = P(("dp", "blk"), None)
    whole = P()
    return jax.shard_map(
        body,
        mesh=mesh,
        in_specs=(rows, rows, P("dp"), P("dp", None)) + (whole,) * 16 + (rows,),
        out_specs=(rows, rows, rows, whole, whole)
        + (split,) * 4
        + (whole,)
        + (split,) * 4
        + (whole,)
        + (split,) * 3,
        check_vma=False,
    )
```

time: 358 us -> 338 us (0.944)
  Pallas kernels: 99.4 us -> 142 us
  matrix products: 64.6 us -> 22.7 us
  local copies, waits for them, and re-layouts: 44.8 us -> 27.1 us
    pallas_call x12 -> x20, Pallas kernels: 43.4 us -> 85.5 us  [the longest x3 22.1 us: norm_grad(): pl.pallas_call(functools.partial(norm_grad_kernel, len(gs), len(after)),...]
    dot_general x22 -> x8, matrix products: 62.2 us -> 20.2 us  [dot32(): return lax.dot_general(a, b, dims, preferred_element_type=F32)]
    unnamed x166 -> x133, local copies, waits for them, and re-layouts: 21 us -> 13 us
    slice x6 -> x2, local copies, waits for them, and re-layouts: 6.28 us -> 0.05 us  [body(): mem_blocks[:, bit:]]
    ppermute x48 -> x46, waiting for transfers between devices: 55.6 us -> 53.2 us  [swap(): lax.ppermute(x, axis, [(i, i ^ bit) for i in range(lax.axis_size(axis))])]
    ppermute x48 -> x46, starting transfers between devices: 58.5 us -> 56.2 us  [swap(): lax.ppermute(x, axis, [(i, i ^ bit) for i in range(lax.axis_size(axis))])]
  transfers between devices with their start and end apart: 51 -> 49, of which waited for: 12 -> 20; matrix products, arithmetic and copies ran while one was open for 30% -> 16% of each run, Pallas kernels for 20% -> 40%
where the time goes in v3:
time: 338 us; the launch traced here: 332 us
  Pallas kernels  142 us (42%)
  starting transfers between devices  56.4 us (17%)
  waiting for transfers between devices  53.3 us (16%)
  local copies, waits for them, and re-layouts  27.1 us (8%)
  matrix products  22.7 us (7%)
  other arithmetic  15.3 us (5%)
  between operations  15.3 us (5%)
    ppermute x46, starting transfers between devices, swap(): lax.ppermute(x, axis, [(i, i ^ bit) for i in range(lax.axis_size(axis))])  56.2 us
    ppermute x46, waiting for transfers between devices, swap(): lax.ppermute(x, axis, [(i, i ^ bit) for i in range(lax.axis_size(axis))])  53.2 us
    pallas_call x3, Pallas kernels, norm_grad(): pl.pallas_call(functools.partial(norm_grad_kernel, len(gs), len(after)),...  22.1 us
    dot_general x8, matrix products, dot32(): return lax.dot_general(a, b, dims, preferred_element_type=F32)  20.2 us
    pallas_call x5, Pallas kernels, slabs(): pl.pallas_call(functools.partial(slab_kernel, kind, later, len(xs), len(g...  19.7 us
    pallas_call x1, Pallas kernels, self_backward(): pl.pallas_call(functools.partial(self_backward_kernel, blocks, kv_local),...  18.8 us
    pallas_call x5, Pallas kernels, totals(): pl.pallas_call(functools.partial(total_kernel, plan), grid=(steps,), in_s...  17.7 us
    unnamed x133, local copies, waits for them, and re-layouts  13 us
  transfers between devices with their start and end apart: 49, of which 20 were waited for; matrix products, arithmetic and copies ran while one was open for 16% of the time, Pallas kernels for 40%

profile of v3, /device:TPU:0, one launch (start us, length us, event | category | flops | bytes accessed | tf_op | source)
XLA Modules:
  0.0 332.3 jit_solution(3200853125389328047)
XLA Ops:
  7.3 4.0 %collective-permute-start.2 = (bf16[256,1024]{1,0:T(8,128)(2,1)}, bf16[256,1024]{1,0:T(8,128)(2,1)}, u32[]{:S(2)}, u32[]{:S(2)}) collective-permute-start(bf16[256,1024]{1,0:T(8,128)(2,1)} %bitcast.72), channel_id=1, source_target_pairs={{0,3},{1,2},{2,1},{3,0},{4,7},{5,6},{6,5},{7,4},{8,11},{9,10},{10,... | collective-permute-start | bytes 1572872 | tf_op jit(solution)/shard_map/ppermute | solution.py:32
  13.2 2.9 constant_dynamic-slice_fusion.15
  26.1 6.0 %fusion.20 = f32[256,2816]{1,0:T(8,128)} fusion(bf16[2816,1024]{1,0:T(8,128)(2,1)} %param.41, bf16[1,256,1024]{2,1,0:T(8,128)(2,1)S(1)} %copy-done.12), kind=kOutput, calls=%fused_computation.81 | convolution fusion | flops 1476395008 | bytes 9175040 | tf_op jit(solution)/shard_map/dot_general | solution.py:28
  39.6 4.8 %norm_dot.1 = (bf16[1024,1024]{1,0:T(8,128)(2,1)}, bf16[1024,512]{1,0:T(8,128)(2,1)}) custom-call(bf16[256,1024]{1,0:T(8,128)(2,1)} %bitcast.75, bf16[256,1024]{1,0:T(8,128)(2,1)} %collective-permute-done.refs_1_, bf16[256,1024]{1,0:T(8,128)(2,1)} %collective-permute-done.1.refs_2_, bf16[256,1024]{1,0:T(8,128)(2,1)} %collective-permute-done.2.refs_3_, ...), custom_call_target="tpu_custom_call" | custom-call | flops 1 | bytes 1 | tf_op jit(solution)/shard_map/norm_dot/pallas_call | solution.py:726
  44.3 12.9 %self_forward.1 = (bf16[256,256]{1,0:T(8,128)(2,1)}, bf16[256,256]{1,0:T(8,128)(2,1)}, bf16[256,256]{1,0:T(8,128)(2,1)}, bf16[256,256]{1,0:T(8,128)(2,1)}, f32[4,2,1,512]{3,2,1,0:T(1,128)}) custom-call(s32[1]{0:T(128)} %bitcast.6.my_ref, bf16[1024,512]{1,0:T(8,128)(2,1)} %get-tuple-element.214.qkv_ref, f32[4,1280]{1,0:T(4,128)} %concatenate.28.bias_ref), custom_call_target="tpu_custom_call" | custom-call | flops 1 | bytes 1 | tf_op jit(solution)/shard_map/self_forward/pallas_call | solution.py:308
  70.5 5.0 %add_norm.2 = (f32[256,1024]{1,0:T(8,128)}, bf16[256,1024]{1,0:T(8,128)(2,1)}, bf16[256,1024]{1,0:T(8,128)(2,1)}) custom-call(bf16[256,256]{1,0:T(8,128)(2,1)} %get-tuple-element.216.refs_0_, bf16[256,256]{1,0:T(8,128)(2,1)} %copy-done.31, bf16[256,256]{1,0:T(8,128)(2,1)} %copy-done.32, bf16[256,256]{1,0:T(8,128)(2,1)} %copy-done.33, ...), custom_call_target="tpu_custom_call" | custom-call | flops 1 | bytes 1 | tf_op jit(solution)/shard_map/add_norm/pallas_call | solution.py:643
  75.5 8.2 %cross_forward.1 = (bf16[256,1024]{1,0:T(8,128)(2,1)}, f32[8,1,512]{2,1,0:T(1,128)}) custom-call(f32[512,1]{1,0:T(8,128)} %copy.47.allow_ref, bf16[256,1024]{1,0:T(8,128)(2,1)} %get-tuple-element.228.q_ref, bf16[512,512]{1,0:T(8,128)(2,1)} %convolution_convert_fusion.1.k_ref, bf16[512,512]{1,0:T(8,128)(2,1)} %convolution_convert_fusion.v_ref), custom_call_target="tpu_custom_call" | custom-call | flops 1 | bytes 1 | tf_op jit(solution)/shard_map/cross_forward/pallas_call | solution.py:367
  83.6 3.9 %add_norm.3 = (f32[256,1024]{1,0:T(8,128)}, bf16[256,1024]{1,0:T(8,128)(2,1)}) custom-call(bf16[256,1024]{1,0:T(8,128)(2,1)} %get-tuple-element.233.refs_0_, bf16[1024,1024]{1,0:T(8,128)(2,1)} %refs_7_.1, f32[256,1024]{1,0:T(8,128)} %get-tuple-element.234.refs_2_, f32[1,1024]{1,0:T(1,128)} %bitcast.91), custom_call_target="tpu_custom_call" | custom-call | flops 1 | bytes 1 | tf_op jit(solution)/shard_map/add_norm/pallas_call | solution.py:643
  95.7 4.9 %multiply_convert_fusion = (bf16[256,2816]{1,0:T(8,128)(2,1)}, bf16[256,2816]{1,0:T(8,128)(2,1)S(1)}, bf16[256,2816]{1,0:T(8,128)(2,1)}) fusion(f32[256,2816]{1,0:T(8,128)S(1)} %fusion.23, f32[256,2816]{1,0:T(8,128)S(1)} %fusion.24, f32[256,2816]{1,0:T(8,128)S(1)} %copy-done.11), kind=kLoop, calls=%fused_computation.7 | loop fusion | flops 25231360 | bytes 12976128 | tf_op jit(solution)/shard_map/convert_element_type | solution.py:969
  110.1 10.6 %norm_grad.3 = (f32[256,1024]{1,0:T(8,128)}, bf16[256,1024]{1,0:T(8,128)(2,1)}, f32[1,1024]{1,0:T(1,128)}, bf16[256,1024]{1,0:T(8,128)(2,1)}) custom-call(bf16[256,2816]{1,0:T(8,128)(2,1)} %copy-done.3, bf16[256,2816]{1,0:T(8,128)(2,1)} %get-tuple-element.238.refs_1_, bf16[1024,2816]{1,0:T(8,128)(2,1)} %refs_2_.1, bf16[1024,2816]{1,0:T(8,128)(2,1)} %refs_3_.1, ...), custom_call_target="tpu_custom_call" | custom-call | flops 1 | bytes 1 | tf_op jit(solution)/shard_map/norm_grad/pallas_call | solution.py:696
  120.8 2.9 turn_chunks.1
  124.2 8.4 %collective-permute-done.13.refs_3_ = bf16[128,1024]{1,0:T(8,128)(2,1)S(1)} collective-permute-done((bf16[128,1024]{1,0:T(8,128)(2,1)}, bf16[128,1024]{1,0:T(8,128)(2,1)S(1)}, u32[]{:S(2)}, u32[]{:S(2)}) %collective-permute-start.13) | collective-permute-done | bytes 262176 | tf_op jit(solution)/shard_map/ppermute | solution.py:32
  133.5 3.4 %slabs.5 = (bf16[16,256,512]{2,1,0:T(8,128)(2,1)}, bf16[16,256,512]{2,1,0:T(8,128)(2,1)}) custom-call(s32[3,32]{1,0:T(4,128)} %get-tuple-element.447.order_ref, bf16[256,1024]{1,0:T(8,128)(2,1)} %get-tuple-element.233.refs_0_, bf16[256,1024]{1,0:T(8,128)(2,1)} %get-tuple-element.258.refs_1_), custom_call_target="tpu_custom_call" | custom-call | flops 1 | bytes 1 | tf_op jit(solution)/shard_map/slabs/pallas_call | solution.py:466
  140.4 5.1 %fusion.4 = bf16[256,1024]{1,0:T(8,128)(2,1)} fusion(f32[256,1024]{1,0:T(8,128)S(1)} %copy-done.24, bf16[256,2816]{1,0:T(8,128)(2,1)S(1)} %copy-done.6, bf16[2816,1024]{1,0:T(8,128)(2,1)} %param.41), kind=kOutput, calls=%fused_computation.12 | convolution fusion | flops 1476919296 | bytes 8781824 | tf_op jit(solution)/shard_map/dot_general | solution.py:28
  145.5 9.5 %cross_backward.1 = (bf16[256,1024]{1,0:T(8,128)(2,1)}, bf16[2,512,512]{2,1,0:T(8,128)(2,1)}) custom-call(f32[512,1]{1,0:T(8,128)} %copy.47.allow_ref, bf16[256,1024]{1,0:T(8,128)(2,1)} %get-tuple-element.228.q_ref, bf16[512,512]{1,0:T(8,128)(2,1)} %convolution_convert_fusion.1.k_ref, bf16[512,512]{1,0:T(8,128)(2,1)} %convolution_convert_fusion.v_ref, ...), custom_call_target="tpu_custom_call" | custom-call | flops 1 | bytes 1 | tf_op jit(solution)/shard_map/cross_backward/pallas_call | solution.py:392
  155.5 5.9 %norm_grad.4 = (f32[256,1024]{1,0:T(8,128)}, bf16[256,1024]{1,0:T(8,128)(2,1)}, f32[1,1024]{1,0:T(1,128)}, bf16[256,256]{1,0:T(8,128)(2,1)}, bf16[256,256]{1,0:T...) custom-call(bf16[256,1024]{1,0:T(8,128)(2,1)} %get-tuple-element.293.refs_0_.refs_1_, ...), custom_call_target="tpu_custom_call" | custom-call | flops 1 | bytes 1 | tf_op jit(solution)/shard_map/norm_grad/pallas_call | solution.py:696
  165.0 7.5 %pair_dot.1 = bf16[1024,1408]{1,0:T(8,128)(2,1)} custom-call(bf16[256,1024]{1,0:T(8,128)(2,1)} %get-tuple-element.235.refs_0_, bf16[256,1024]{1,0:T(8,128)(2,1)} %copy-done.23, bf16[256,1024]{1,0:T(8,128)(2,1)} %copy-done.22, bf16[128,1024]{1,0:T(8,128)(2,1)} %copy-done.42, bf16[128,1024]{1,0:T(8,128)(2,1)} %copy-done.41, ...), custom_call_target="tpu_custom_call" | custom-call | flops 1 | bytes 1 | tf_op jit(solution)/shard_map/pair_dot/pallas_call | solution.py:589
  172.6 3.7 %slabs.6 = (bf16[16,256,512]{2,1,0:T(8,128)(2,1)}, bf16[16,256,512]{2,1,0:T(8,128)(2,1)}) custom-call(s32[3,32]{1,0:T(4,128)} %get-tuple-element.447.order_ref, bf16[256,1024]{1,0:T(8,128)(2,1)} %get-tuple-element.292.refs_0_, bf16[256,1024]{1,0:T(8,128)(2,1)} %get-tuple-element.293.refs_0_.refs_1_, ...), custom_call_target="tpu_custom_call", output_to_operand_aliasing={{0}: (3, {}), {1}: (4, {})} | custom-call | flops 1 | bytes 1 | tf_op jit(solution)/shard_map/slabs/pallas_call | solution.py:466
  176.3 4.4 %slabs.7 = (bf16[16,256,512]{2,1,0:T(8,128)(2,1)}, bf16[16,256,512]{2,1,0:T(8,128)(2,1)}) custom-call(s32[3,32]{1,0:T(4,128)} %get-tuple-element.447.order_ref, bf16[512,1024]{1,0:T(8,128)(2,1)} %copy-done.18, bf16[2,512,512]{2,1,0:T(8,128)(2,1)} %get-tuple-element.380.refs_1_, ...), custom_call_target="tpu_custom_call", output_to_operand_aliasing={{0}: (3, {}), {1}: (4, {})} | custom-call | flops 1 | bytes 1 | tf_op jit(solution)/shard_map/slabs/pallas_call | solution.py:466
  180.7 3.4 %slabs.8 = (bf16[16,256,512]{2,1,0:T(8,128)(2,1)}, bf16[16,256,512]{2,1,0:T(8,128)(2,1)}) custom-call(s32[3,32]{1,0:T(4,128)} %get-tuple-element.446.order_ref, bf16[256,256]{1,0:T(8,128)(2,1)} %get-tuple-element.216.refs_0_, bf16[256,256]{1,0:T(8,128)(2,1)} %copy-done.31, ...), custom_call_target="tpu_custom_call", output_to_operand_aliasing={{0}: (6, {}), {1}: (7, {})} | custom-call | flops 1 | bytes 1 | tf_op jit(solution)/shard_map/slabs/pallas_call | solution.py:466
  184.1 4.8 %turned_dot.1 = bf16[8,88,1024]{2,1,0:T(8,128)(2,1)} custom-call(s32[1]{0:T(128)} %bitcast.6.my_ref, bf16[8,88,256]{2,1,0:T(8,128)(2,1)} %get-tuple-element.302.refs_0_, bf16[8,88,256]{2,1,0:T(8,128)(2,1)} %copy-done.38, bf16[8,88,256]{2,1,0:T(8,128)(2,1)} %copy-done.39, bf16[8,88,256]{2,1,0:T(8,128)(2,1)} %copy-done.40, bf16[4,256,1024]{2,1,0:T(8,128)(2,1)} %bitcast.82), custom_call_target="tpu_custom_call" | custom-call | flops 1 | bytes 1 | tf_op jit(solution)/shard_map/turned_dot/pallas_call | solution.py:778
  191.6 5.0 %totals.5 = (bf16[8,128,512]{2,1,0:T(8,128)(2,1)}, bf16[8,128,512]{2,1,0:T(8,128)(2,1)}) custom-call(bf16[16,256,512]{2,1,0:T(8,128)(2,1)} %get-tuple-element.301.refs_0_.refs_2_.refs_4_, bf16[16,256,512]{2,1,0:T(8,128)(2,1)} %collective-permute-done.22.refs_1_.refs_3_.refs_5_, bf16[16,256,512]{2,1,0:T(8,128)(2,1)} %get-tuple-element.301.refs_0_.refs_2_.refs_4_, ...), custom_call_target="tpu_custom_call" | custom-call | flops 1 | bytes 1 | tf_op jit(solution)/shard_map/totals/pallas_call | solution.py:535
  199.6 18.8 %self_backward.1 = (bf16[256,512]{1,0:T(8,128)(2,1)}, bf16[256,512]{1,0:T(8,128)(2,1)}, bf16[256,512]{1,0:T(8,128)(2,1)}, bf16[256,512]{1,0:T(8,128)(2,1)}, f32[4,1280]{1,0:T(4,128)}) custom-call(s32[1]{0:T(128)} %bitcast.6.my_ref, bf16[1024,512]{1,0:T(8,128)(2,1)} %get-tuple-element.214.qkv_ref, f32[4,1280]{1,0:T(4,128)} %concatenate.28.bias_ref, ...), custom_call_target="tpu_custom_call" | custom-call | flops 1 | bytes 1 | tf_op jit(solution)/shard_map/self_backward/pallas_call | solution.py:337
  218.4 3.7 %collective-permute-done.23.refs_2_.refs_6_ = bf16[8,128,512]{2,1,0:T(8,128)(2,1)S(1)} collective-permute-done((bf16[8,128,512]{2,1,0:T(8,128)(2,1)}, bf16[8,128,512]{2,1,0:T(8,128)(2,1)S(1)}, u32[]{:S(2)}, u32[]{:S(2)}) %collective-permute-start.23) | collective-permute-done | bytes 1048608 | tf_op jit(solution)/shard_map/ppermute | solution.py:32
  224.0 4.1 %totals.6 = (bf16[4,128,512]{2,1,0:T(8,128)(2,1)}, bf16[4,128,512]{2,1,0:T(8,128)(2,1)}) custom-call(bf16[16,256,512]{2,1,0:T(8,128)(2,1)} %get-tuple-element.301.refs_0_.refs_2_.refs_4_, bf16[16,256,512]{2,1,0:T(8,128)(2,1)} %collective-permute-done.22.refs_1_.refs_3_.refs_5_, bf16[8,128,512]{2,1,0:T(8,128)(2,1)} %copy-done.1, ...), custom_call_target="tpu_custom_call" | custom-call | flops 1 | bytes 1 | tf_op jit(solution)/shard_map/totals/pallas_call | solution.py:535
  228.0 4.8 %slabs.9 = (bf16[16,32,512]{2,1,0:T(8,128)(2,1)}, bf16[16,32,512]{2,1,0:T(8,128)(2,1)}, f32[1024,1]{1,0:T(8,128)}) custom-call(s32[3,32]{1,0:T(4,128)} %get-tuple-element.447.order_ref, bf16[1024,1024]{1,0:T(8,128)(2,1)} %get-tuple-element.262.refs_0_, bf16[256,512]{1,0:T(8,128)(2,1)} %get-tuple-element.356.refs_1_.refs_0_, ...), custom_call_target="tpu_custom_call" | custom-call | flops 1 | bytes 1 | tf_op jit(solution)/shard_map/slabs/pallas_call | solution.py:466
  236.8 3.4 %totals.7 = (bf16[4,32,512]{2,1,0:T(8,128)(2,1)}, bf16[4,32,512]{2,1,0:T(8,128)(2,1)}, bf16[4,32,512]{2,1,0:T(8,128)(2,1)}, bf16[4,32,512]{2,1,0:T(8,128)(2,1)}) custom-call(bf16[4,128,512]{2,1,0:T(8,128)(2,1)} %bitcast.60, bf16[4,128,512]{2,1,0:T(8,128)(2,1)} %bitcast.64, bf16[4,128,512]{2,1,0:T(8,128)(2,1)} %bitcast.61, bf16[4,128,512]{2,1,0:T(8,128)(2,1)} %bitcast.65, ...), custom_call_target="tpu_custom_call" | custom-call | flops 1 | bytes 1 | tf_op jit(solution)/shard_map/totals/pallas_call | solution.py:535
  266.4 9.3 %collective-permute-done.36 = f32[28,128]{1,0:T(8,128)S(1)} collective-permute-done((f32[28,128]{1,0:T(8,128)S(1)}, f32[28,128]{1,0:T(8,128)S(1)}, u32[]{:S(2)}, u32[]{:S(2)}) %collective-permute-start.36) | collective-permute-done | bytes 14368 | tf_op jit(solution)/shard_map/ppermute | solution.py:32
  281.1 5.6 %norm_grad.5 = (f32[256,1024]{1,0:T(8,128)}, bf16[256,1024]{1,0:T(8,128)(2,1)}, f32[1,1024]{1,0:T(1,128)}) custom-call(bf16[256,512]{1,0:T(8,128)(2,1)} %get-tuple-element.356.refs_1_.refs_0_, bf16[256,512]{1,0:T(8,128)(2,1)} %copy-done.43, bf16[256,512]{1,0:T(8,128)(2,1)} %copy-done.44, bf16[256,512]{1,0:T(8,128)(2,1)} %copy-done.45, ...), custom_call_target="tpu_custom_call" | custom-call | flops 1 | bytes 1 | tf_op jit(solution)/shard_map/norm_grad/pallas_call | solution.py:696
  295.6 3.2 collective-permute-start.41
  298.8 3.9 %collective-permute-done.38 = bf16[2,2,128,512]{3,2,1,0:T(8,128)(2,1)S(1)} collective-permute-done((bf16[2,2,128,512]{3,2,1,0:T(8,128)(2,1)S(1)}, bf16[2,2,128,512]{3,2,1,0:T(8,128)(2,1)S(1)}, u32[]{:S(2)}, u32[]{:S(2)}) %collective-permute-start.38) | collective-permute-done | bytes 524320 | tf_op jit(solution)/shard_map/ppermute | solution.py:32
  307.3 4.4 %collective-permute-done.41 = f32[28,128]{1,0:T(8,128)S(1)} collective-permute-done((f32[28,128]{1,0:T(8,128)S(1)}, f32[28,128]{1,0:T(8,128)S(1)}, u32[]{:S(2)}, u32[]{:S(2)}) %collective-permute-start.41) | collective-permute-done | bytes 14368 | tf_op jit(solution)/shard_map/ppermute | solution.py:32
  (280 shorter events, 128.7 us)
Async XLA Ops:
  7.2 93.4 %all-gather.2.cloned.1.call-start = ((), (), s32[]{:S(2)}) async-start(), calls=%async_computation.2 | async-start | bytes 2621440 | tf_op jit(solution)/shard_map/all_gather | solution.py:943
  7.3 24.8 %collective-permute-start.2 = (bf16[256,1024]{1,0:T(8,128)(2,1)}, bf16[256,1024]{1,0:T(8,128)(2,1)}, u32[]{:S(2)}, u32[]{:S(2)}) collective-permute-start(bf16[256,1024]{1,0:T(8,128)(2,1)} %bitcast.72), channel_id=1, source_target_pairs={{0,3},{1,2},{2,1},{3,0},{4,7},{5,6},{6,5},{7,4},{8,11},{9,10},{10,... | collective-permute-start | bytes 1572872 | tf_op jit(solution)/shard_map/ppermute | solution.py:32
  11.2 23.5 %collective-permute-start.1 = (bf16[256,1024]{1,0:T(8,128)(2,1)}, bf16[256,1024]{1,0:T(8,128)(2,1)}, u32[]{:S(2)}, u32[]{:S(2)}) collective-permute-start(bf16[256,1024]{1,0:T(8,128)(2,1)} %bitcast.73), channel_id=1, source_target_pairs={{0,2},{1,3},{2,0},{3,1},{4,6},{5,7},{6,4},{7,5},{8,10},{9,11},{10,... | collective-permute-start | bytes 1572872 | tf_op jit(solution)/shard_map/ppermute | solution.py:32
  11.7 23.3 %collective-permute-start = (bf16[256,1024]{1,0:T(8,128)(2,1)}, bf16[256,1024]{1,0:T(8,128)(2,1)}, u32[]{:S(2)}, u32[]{:S(2)}) collective-permute-start(bf16[256,1024]{1,0:T(8,128)(2,1)} %bitcast.74), channel_id=1, source_target_pairs={{0,1},{1,0},{2,3},{3,2},{4,5},{5,4},{6,7},{7,6},{8,9},{9,8},{10,11... | collective-permute-start | bytes 1572872 | tf_op jit(solution)/shard_map/ppermute | solution.py:32
  35.0 25.2 %collective-permute-start.6 = (bf16[128,1024]{1,0:T(8,128)(2,1)}, bf16[128,1024]{1,0:T(8,128)(2,1)}, u32[]{:S(2)}, u32[]{:S(2)}) collective-permute-start(bf16[128,1024]{1,0:T(8,128)(2,1)} %bitcast.1), channel_id=1, source_target_pairs={{0,1},{1,0},{2,3},{3,2},{4,5},{5,4},{6,7},{7,6},{8,9},{9,8},{10,11... | collective-permute-start | bytes 786440 | tf_op jit(solution)/shard_map/ppermute | solution.py:32
  36.5 26.1 %collective-permute-start.7 = (bf16[128,1024]{1,0:T(8,128)(2,1)}, bf16[128,1024]{1,0:T(8,128)(2,1)}, u32[]{:S(2)}, u32[]{:S(2)}) collective-permute-start(bf16[128,1024]{1,0:T(8,128)(2,1)} %bitcast.1), channel_id=1, source_target_pairs={{0,2},{1,3},{2,0},{3,1},{4,6},{5,7},{6,4},{7,5},{8,10},{9,11},{10,... | collective-permute-start | bytes 786440 | tf_op jit(solution)/shard_map/ppermute | solution.py:32
  37.1 26.5 %collective-permute-start.8 = (bf16[128,1024]{1,0:T(8,128)(2,1)}, bf16[128,1024]{1,0:T(8,128)(2,1)}, u32[]{:S(2)}, u32[]{:S(2)}) collective-permute-start(bf16[128,1024]{1,0:T(8,128)(2,1)} %bitcast.1), channel_id=1, source_target_pairs={{0,3},{1,2},{2,1},{3,0},{4,7},{5,6},{6,5},{7,4},{8,11},{9,10},{10,... | collective-permute-start | bytes 786440 | tf_op jit(solution)/shard_map/ppermute | solution.py:32
  39.5 183.5 %reduce-scatter.3.cloned.1.call-start = ((), (), s32[]{:S(2)}) async-start(), calls=%async_computation.3 | async-start | bytes 3244032 | tf_op jit(solution)/shard_map/reduce_scatter | solution.py:1018
  87.6 13.0 %collective-permute-start.10 = (bf16[256,1024]{1,0:T(8,128)(2,1)}, bf16[256,1024]{1,0:T(8,128)(2,1)S(1)}, u32[]{:S(2)}, u32[]{:S(2)}) collective-permute-start(bf16[256,1024]{1,0:T(8,128)(2,1)} %get-tuple-element.235.refs_0_), channel_id=1, source_target_pairs={{0,2},{1,3},{2,0},{3,1},{4,6},{5,7},{6,4},{7,5},{8,10},{9,11},{10,... | collective-permute-start | bytes 1572872 | tf_op jit(solution)/shard_map/ppermute | solution.py:32
  104.6 28.0 %collective-permute-start.11 = (bf16[256,1408]{1,0:T(8,128)(2,1)}, bf16[256,1408]{1,0:T(8,128)(2,1)S(1)}, u32[]{:S(2)}, u32[]{:S(2)}) collective-permute-start(bf16[256,1408]{1,0:T(8,128)(2,1)} %get-tuple-element.241), channel_id=1, source_target_pairs={{0,1},{1,0},{2,3},{3,2},{4,5},{5,4},{6,7},{7,6},{8,9},{9,8},{10,11... | collective-permute-start | bytes 2162696 | tf_op jit(solution)/shard_map/ppermute | solution.py:32
  104.7 28.0 %collective-permute-start.12 = (bf16[256,1408]{1,0:T(8,128)(2,1)}, bf16[256,1408]{1,0:T(8,128)(2,1)S(1)}, u32[]{:S(2)}, u32[]{:S(2)}) collective-permute-start(bf16[256,1408]{1,0:T(8,128)(2,1)} %get-tuple-element.242), channel_id=1, source_target_pairs={{0,2},{1,3},{2,0},{3,1},{4,6},{5,7},{6,4},{7,5},{8,10},{9,11},{10,... | collective-permute-start | bytes 2162696 | tf_op jit(solution)/shard_map/ppermute | solution.py:32
  107.0 17.3 %collective-permute-start.14 = (bf16[128,1024]{1,0:T(8,128)(2,1)}, bf16[128,1024]{1,0:T(8,128)(2,1)S(1)}, u32[]{:S(2)}, u32[]{:S(2)}) collective-permute-start(bf16[128,1024]{1,0:T(8,128)(2,1)} %slice.52), channel_id=1, source_target_pairs={{0,1},{1,0},{2,3},{3,2},{4,5},{5,4},{6,7},{7,6},{8,9},{9,8},{10,11... | collective-permute-start | bytes 786440 | tf_op jit(solution)/shard_map/ppermute | solution.py:32
  108.2 24.5 %collective-permute-start.13 = (bf16[128,1024]{1,0:T(8,128)(2,1)}, bf16[128,1024]{1,0:T(8,128)(2,1)S(1)}, u32[]{:S(2)}, u32[]{:S(2)}) collective-permute-start(bf16[128,1024]{1,0:T(8,128)(2,1)} %slice.51), channel_id=1, source_target_pairs={{0,2},{1,3},{2,0},{3,1},{4,6},{5,7},{6,4},{7,5},{8,10},{9,11},{10,... | collective-permute-start | bytes 786440 | tf_op jit(solution)/shard_map/ppermute | solution.py:32
  132.7 22.8 %collective-permute-start.15 = (bf16[256,1408]{1,0:T(8,128)(2,1)S(1)}, bf16[256,1408]{1,0:T(8,128)(2,1)S(1)}, u32[]{:S(2)}, u32[]{:S(2)}) collective-permute-start(bf16[256,1408]{1,0:T(8,128)(2,1)S(1)} %copy-done.27), channel_id=1, source_target_pairs={{0,3},{1,2},{2,1},{3,0},{4,7},{5,6},{6,5},{7,4},{8,11},{9,10},{10,... | collective-permute-start | bytes 2162696 | tf_op jit(solution)/shard_map/ppermute | solution.py:32
  137.0 18.1 %collective-permute-start.16 = (bf16[8,88,256]{2,1,0:T(8,128)(2,1)}, bf16[8,88,256]{2,1,0:T(8,128)(2,1)S(1)}, u32[]{:S(2)}, u32[]{:S(2)}) collective-permute-start(bf16[8,88,256]{2,1,0:T(8,128)(2,1)} %get-tuple-element.255), channel_id=1, source_target_pairs={{0,1},{1,0},{2,3},{3,2},{4,5},{5,4},{6,7},{7,6},{8,9},{9,8},{10,11... | collective-permute-start | bytes 1081352 | tf_op jit(solution)/shard_map/ppermute | solution.py:32
  138.3 17.2 %collective-permute-start.17 = (bf16[8,88,256]{2,1,0:T(8,128)(2,1)}, bf16[8,88,256]{2,1,0:T(8,128)(2,1)S(1)}, u32[]{:S(2)}, u32[]{:S(2)}) collective-permute-start(bf16[8,88,256]{2,1,0:T(8,128)(2,1)} %get-tuple-element.256), channel_id=1, source_target_pairs={{0,2},{1,3},{2,0},{3,1},{4,6},{5,7},{6,4},{7,5},{8,10},{9,11},{10,... | collective-permute-start | bytes 1081352 | tf_op jit(solution)/shard_map/ppermute | solution.py:32
  140.2 15.3 %collective-permute-start.18 = (bf16[8,88,256]{2,1,0:T(8,128)(2,1)}, bf16[8,88,256]{2,1,0:T(8,128)(2,1)S(1)}, u32[]{:S(2)}, u32[]{:S(2)}) collective-permute-start(bf16[8,88,256]{2,1,0:T(8,128)(2,1)} %get-tuple-element.257), channel_id=1, source_target_pairs={{0,3},{1,2},{2,1},{3,0},{4,7},{5,6},{6,5},{7,4},{8,11},{9,10},{10,... | collective-permute-start | bytes 1081352 | tf_op jit(solution)/shard_map/ppermute | solution.py:32
  172.5 114.2 %reduce-scatter.5.cloned.1.call-start = ((), (), s32[]{:S(2)}) async-start(), calls=%async_computation.4 | async-start | bytes 1622016 | tf_op jit(solution)/shard_map/reduce_scatter | solution.py:1035
  196.7 25.4 %collective-permute-start.23 = (bf16[8,128,512]{2,1,0:T(8,128)(2,1)}, bf16[8,128,512]{2,1,0:T(8,128)(2,1)S(1)}, u32[]{:S(2)}, u32[]{:S(2)}) collective-permute-start(bf16[8,128,512]{2,1,0:T(8,128)(2,1)} %get-tuple-element.318), channel_id=1, source_target_pairs={{0,1},{1,0},{2,3},{3,2},{4,5},{5,4},{6,7},{7,6},{8,9},{9,8},{10,11... | collective-permute-start | bytes 3145736 | tf_op jit(solution)/shard_map/ppermute | solution.py:32
  197.8 25.2 %collective-permute-start.24 = (bf16[8,128,512]{2,1,0:T(8,128)(2,1)}, bf16[8,128,512]{2,1,0:T(8,128)(2,1)S(1)}, u32[]{:S(2)}, u32[]{:S(2)}) collective-permute-start(bf16[8,128,512]{2,1,0:T(8,128)(2,1)} %get-tuple-element.319), channel_id=1, source_target_pairs={{0,2},{1,3},{2,0},{3,1},{4,6},{5,7},{6,4},{7,5},{8,10},{9,11},{10,... | collective-permute-start | bytes 3145736 | tf_op jit(solution)/shard_map/ppermute | solution.py:32
  232.8 15.0 %collective-permute-start.25 = (bf16[4,128,512]{2,1,0:T(8,128)(2,1)}, bf16[4,128,512]{2,1,0:T(8,128)(2,1)S(1)}, u32[]{:S(2)}, u32[]{:S(2)}) collective-permute-start(bf16[4,128,512]{2,1,0:T(8,128)(2,1)} %get-tuple-element.334), channel_id=1, source_target_pairs={{0,2},{1,3},{2,0},{3,1},{4,6},{5,7},{6,4},{7,5},{8,10},{9,11},{10,... | collective-permute-start | bytes 1572872 | tf_op jit(solution)/shard_map/ppermute | solution.py:32
  234.6 15.0 %collective-permute-start.26 = (bf16[4,128,512]{2,1,0:T(8,128)(2,1)}, bf16[4,128,512]{2,1,0:T(8,128)(2,1)S(1)}, u32[]{:S(2)}, u32[]{:S(2)}) collective-permute-start(bf16[4,128,512]{2,1,0:T(8,128)(2,1)} %get-tuple-element.335), channel_id=1, source_target_pairs={{0,1},{1,0},{2,3},{3,2},{4,5},{5,4},{6,7},{7,6},{8,9},{9,8},{10,11... | collective-permute-start | bytes 1572872 | tf_op jit(solution)/shard_map/ppermute | solution.py:32
  240.2 12.2 %collective-permute-start.28 = (bf16[4,32,512]{2,1,0:T(8,128)(2,1)}, bf16[4,32,512]{2,1,0:T(8,128)(2,1)S(1)}, u32[]{:S(2)}, u32[]{:S(2)}) collective-permute-start(bf16[4,32,512]{2,1,0:T(8,128)(2,1)} %get-tuple-element.341), channel_id=1, source_target_pairs={{0,1},{1,0},{2,3},{3,2},{4,5},{5,4},{6,7},{7,6},{8,9},{9,8},{10,11... | collective-permute-start | bytes 393224 | tf_op jit(solution)/shard_map/ppermute | solution.py:32
  241.9 12.3 %collective-permute-start.30 = (bf16[4,32,512]{2,1,0:T(8,128)(2,1)}, bf16[4,32,512]{2,1,0:T(8,128)(2,1)S(1)}, u32[]{:S(2)}, u32[]{:S(2)}) collective-permute-start(bf16[4,32,512]{2,1,0:T(8,128)(2,1)} %get-tuple-element.343), channel_id=1, source_target_pairs={{0,3},{1,2},{2,1},{3,0},{4,7},{5,6},{6,5},{7,4},{8,11},{9,10},{10,... | collective-permute-start | bytes 393224 | tf_op jit(solution)/shard_map/ppermute | solution.py:32
  257.6 29.2 %collective-permute-start.34 = (bf16[2,384,512]{2,1,0:T(8,128)(2,1)}, bf16[2,384,512]{2,1,0:T(8,128)(2,1)S(1)}, u32[]{:S(2)}, u32[]{:S(2)}) collective-permute-start(bf16[2,384,512]{2,1,0:T(8,128)(2,1)} %totals.8), channel_id=1, source_target_pairs={{0,8},{4,12},{8,0},{12,4},{16,24},{20,28},{24,16},{28,20},{1,9},{5... | collective-permute-start | bytes 2359304 | tf_op jit(solution)/shard_map/ppermute | solution.py:32
  260.8 19.4 %collective-permute-start.31 = (bf16[256,512]{1,0:T(8,128)(2,1)}, bf16[256,512]{1,0:T(8,128)(2,1)S(1)}, u32[]{:S(2)}, u32[]{:S(2)}) collective-permute-start(bf16[256,512]{1,0:T(8,128)(2,1)} %get-tuple-element.357.refs_2_), channel_id=1, source_target_pairs={{0,1},{1,0},{2,3},{3,2},{4,5},{5,4},{6,7},{7,6},{8,9},{9,8},{10,11... | collective-permute-start | bytes 786440 | tf_op jit(solution)/shard_map/ppermute | solution.py:32
  262.2 18.0 %collective-permute-start.32 = (bf16[256,512]{1,0:T(8,128)(2,1)S(1)}, bf16[256,512]{1,0:T(8,128)(2,1)S(1)}, u32[]{:S(2)}, u32[]{:S(2)}) collective-permute-start(bf16[256,512]{1,0:T(8,128)(2,1)S(1)} %copy-done.47), channel_id=1, source_target_pairs={{0,2},{1,3},{2,0},{3,1},{4,6},{5,7},{6,4},{7,5},{8,10},{9,11},{10,... | collective-permute-start | bytes 786440 | tf_op jit(solution)/shard_map/ppermute | solution.py:32
  263.1 17.2 %collective-permute-start.33 = (bf16[256,512]{1,0:T(8,128)(2,1)S(1)}, bf16[256,512]{1,0:T(8,128)(2,1)S(1)}, u32[]{:S(2)}, u32[]{:S(2)}) collective-permute-start(bf16[256,512]{1,0:T(8,128)(2,1)S(1)} %copy-done.46), channel_id=1, source_target_pairs={{0,3},{1,2},{2,1},{3,0},{4,7},{5,6},{6,5},{7,4},{8,11},{9,10},{10,... | collective-permute-start | bytes 786440 | tf_op jit(solution)/shard_map/ppermute | solution.py:32
  290.2 12.5 %collective-permute-start.38 = (bf16[2,2,128,512]{3,2,1,0:T(8,128)(2,1)S(1)}, bf16[2,2,128,512]{3,2,1,0:T(8,128)(2,1)S(1)}, u32[]{:S(2)}, u32[]{:S(2)}) collective-permute-start(bf16[2,2,128,512]{3,2,1,0:T(8,128)(2,1)S(1)} %slice.70), channel_id=1, source_target_pairs={{0,2},{1,3},{2,0},{3,1},{4,6},{5,7},{6,4},{7,5},{8,10},{9,11},{10,... | collective-permute-start | bytes 1572872 | tf_op jit(solution)/shard_map/ppermute | solution.py:32
  292.3 27.5 %collective-permute-start.42 = (bf16[1,384,512]{2,1,0:T(8,128)(2,1)}, bf16[1,384,512]{2,1,0:T(8,128)(2,1)S(1)}, u32[]{:S(2)}, u32[]{:S(2)}) collective-permute-start(bf16[1,384,512]{2,1,0:T(8,128)(2,1)} %totals.9), channel_id=1, source_target_pairs={{0,16},{4,20},{8,24},{12,28},{16,0},{20,4},{24,8},{28,12},{1,17},{... | collective-permute-start | bytes 1179656 | tf_op jit(solution)/shard_map/ppermute | solution.py:32
  295.6 16.1 %collective-permute-start.41 = (f32[28,128]{1,0:T(8,128)S(1)}, f32[28,128]{1,0:T(8,128)S(1)}, u32[]{:S(2)}, u32[]{:S(2)}) collective-permute-start(f32[28,128]{1,0:T(8,128)S(1)} %add.146), channel_id=1, source_target_pairs={{0,16},{4,20},{8,24},{12,28},{16,0},{20,4},{24,8},{28,12},{1,17},{... | collective-permute-start | bytes 43016 | tf_op jit(solution)/shard_map/ppermute | solution.py:32
  302.8 20.2 %collective-permute-start.39 = (bf16[2,1,128,512]{3,2,1,0:T(8,128)(2,1)S(1)}, bf16[2,1,128,512]{3,2,1,0:T(8,128)(2,1)S(1)}, u32[]{:S(2)}, u32[]{:S(2)}) collective-permute-start(bf16[2,1,128,512]{3,2,1,0:T(8,128)(2,1)S(1)} %slice.72), channel_id=1, source_target_pairs={{0,1},{1,0},{2,3},{3,2},{4,5},{5,4},{6,7},{7,6},{8,9},{9,8},{10,11... | collective-permute-start | bytes 786440 | tf_op jit(solution)/shard_map/ppermute | solution.py:32
  (81 other events, 657.4 us)
Sparse Core Ops, SparseCore 0:
  39.6 38.7 all-gather.1
  172.6 42.4 reduce-scatter.2
  217.4 33.6 reduce-scatter.4

commit v4 on v3

--- a/solution.py
+++ b/solution.py
@@ -572,10 +572,9 @@
     )(my, *[array for array, _ in pieces])
 
 
-def pair_dot_kernel(x_count, *refs):
-    result = refs[-1]
-    xs, gs = refs[:x_count], refs[x_count:-1]
-    x = jnp.concatenate([ref[...] for ref in xs], axis=0)
+def pair_dot_kernel(my_ref, x_ref, *refs):
+    gs, result = refs[:-1], refs[-1]
+    x = jnp.concatenate([x_ref[my_ref[0] ^ j] for j in range(len(gs))], axis=0)
     g = jnp.concatenate([ref[...] for ref in gs], axis=0)
     result[...] = dot32(x, g, TN).astype(BF16)
 
@@ -584,18 +583,19 @@
     return [pl.BlockSpec(a.shape, lambda i, n=a.ndim: (0,) * n) for a in arrays]
 
 
-def pair_dot(xs, gs):
-    features, width = xs[0].shape[1], gs[0].shape[1]
-    return pl.pallas_call(
-        functools.partial(pair_dot_kernel, len(xs)),
+def pair_dot(my, x, gs):
+    features, width = x.shape[1], gs[0].shape[1]
+    x = x.reshape(len(gs), -1, features)
+    return pl.pallas_call(
+        pair_dot_kernel,
         grid=(1,),
-        in_specs=whole_blocks(list(xs) + list(gs)),
+        in_specs=[pl.BlockSpec(memory_space=pltpu.SMEM)] + whole_blocks([x, *gs]),
         out_specs=pl.BlockSpec((features, width), lambda i: (0, 0)),
         out_shape=jax.ShapeDtypeStruct((features, width), BF16),
         compiler_params=params(),
         cost_estimate=TINY,
         name="pair_dot",
-    )(*xs, *gs)
+    )(my, x, *gs)
 
 
 def dot_gain_kernel(x_ref, g_ref, w_ref, out_ref, gain_ref):
@@ -976,10 +976,8 @@
         turned = order ^ ((my * (devices // blocks)).astype(jnp.int32))
         small, large = d // devices, ff // devices
         d_slabs = d // SLAB
-        half = length // 2
-        near = trade([ffn_in] * 3, "blk", 1)
-        gate_grad, up_grad, top_all, near = tie(gate_grad, up_grad, top_all, near)
-        far = [swap(near[0][:half], "blk", 2), swap(near[1][half:], "blk", 1)]
+        top_all, ffn_late = tie(top_all, ffn_in)
+        ffn_all = lax.all_gather(ffn_late, "blk", axis=0, tiled=True)
         both_grad = jnp.concatenate([gate_grad, up_grad], axis=1)
         shares = [lax.dynamic_slice_in_dim(both_grad, (my ^ j) * share, share, 1) for j in range(blocks)]
         shares, hidden = tie(shares, hidden)
@@ -996,33 +994,31 @@
     grad_cross, cross_grad, d_gain_ffn, (mix_grad,) = norm_grad(
         ffn_grad, [gate_grad, up_grad], [w_gate, w_up], after_cross, norm_ffn, [cross_out], tile
     )
-    if fast:
-        mix_grad, shares_near, shares[3], hidden_parts, far = tie(mix_grad, shares_near, shares[3], hidden_parts, far)
-        ffn_parts = [ffn_in] + near + far
-        share_far = swap(shares[3], "blk", 3)
-        hidden_got = trade(hidden_parts, "blk", 1)
     block_out = (after_cross + dot32(hidden, w_down)).astype(BF16)
-    cq_grad, mem_part = cross_backward(allow, cross_q, mem_key, mem_value, cross_lse, mix_grad)
     if fast:
         total = 4 * d_slabs * small
         held = slabs(order, cross_mix, cross_grad, total, 0, total, None)
-        cq_grad, mem_part, share_far, hidden_got, block_out, held = tie(cq_grad, mem_part, share_far, hidden_got, block_out, held)
+        mix_grad, shares_near, shares[3], hidden_parts, ffn_all, held, block_out = tie(
+            mix_grad, shares_near, shares[3], hidden_parts, ffn_all, held, block_out
+        )
+        share_far = swap(shares[3], "blk", 3)
+    cq_grad, mem_part = cross_backward(allow, cross_q, mem_key, mem_value, cross_lse, mix_grad)
+    if fast:
+        held = slabs(order, cross_in, cq_grad, total, d_slabs * small, total, held)
+        held = slabs(order, mem_all, mem_part, total, 2 * d_slabs * small, 0, held)
+        cq_grad, mem_part, share_far, held = tie(cq_grad, mem_part, share_far, held)
     grad_self, self_grad, d_gain_cross, grad_parts = norm_grad(
         grad_cross, [cq_grad], [cross_query], after_self, norm_cross, out_turned, d
     )
     grad_got = trade(grad_parts, "blk", 1)
     if fast:
-        shares_near, held, cq_late, self_late = tie(shares_near, held, cq_grad, self_grad)
-        wide = pair_dot(ffn_parts, [shares[0]] + shares_near + [share_far])
-        grad_got, wide, held, mem_late = tie(grad_got, wide, held, mem_part)
+        share_far, held, self_late = tie(share_far, held, self_grad)
+        wide = pair_dot(my_ref, ffn_all, [shares[0]] + shares_near + [share_far])
+        keep, send = slabs(turned, mixes, self_late, total, 3 * d_slabs * small, 0, held)
+        grad_got, wide, keep, hidden_parts = tie(grad_got, wide, keep, hidden_parts)
+        got = swap(send, "dp", 1)
+        hidden_got = trade(hidden_parts, "blk", 1)
         wide = lax.psum_scatter(wide, "dp", scatter_dimension=0, tiled=True)
-        held = slabs(order, cross_in, cq_late, total, d_slabs * small, total, held)
-        held = slabs(order, mem_all, mem_late, total, 2 * d_slabs * small, 0, held)
-        keep, send = slabs(turned, mixes, self_late, total, 3 * d_slabs * small, 0, held)
-        got = swap(send, "dp", 1)
-        hidden_got, keep = tie(hidden_got, keep)
-        down = turned_dot(my_ref, [hidden_parts[0]] + hidden_got, top_all)
-        down, got = tie(down, got)
         cross = Halves(keep, got, [(0, total // 2)], [(total // 2, total)])
         cross.pack()
         grad_got, cross.out = tie(grad_got, cross.out)
@@ -1031,61 +1027,65 @@
     d_table = lax.dot_general(bucket_hot, bias_grad[:, length:], (((0,), (1,)), ((), ())), precision=lax.Precision.HIGHEST)
     d_table = lax.dynamic_update_slice_in_dim(jnp.zeros_like(bias_table), d_table, my * own_heads, 1)
     if fast:
-        qkv_parts, mem_part, cross.got, wide = tie(qkv_parts, mem_part, cross.got, wide)
-        down = lax.psum_scatter(down, "dp", scatter_dimension=0, tiled=True)
+        qkv_parts, mem_part, cross.got = tie(qkv_parts, mem_part, cross.got)
         cross.arrive()
         cross.pack()
-        qkv_parts, cross.out = tie(qkv_parts, cross.out)
+        qkv_parts, cross.out, hidden_got = tie(qkv_parts, cross.out, hidden_got)
         cross.hop((2, 1))
         own = own_q + 2 * own_kv
         keep, send, gain_part = slabs(order, self_all, qkv_parts, small, 0, 0, None, 2, own, turned_qkv[0])
         gain_part = gain_part[:, 0]
         view = (-1, blocks * small, own)
         got = swap(send, "dp", 1)
-        wides = [lax.dynamic_slice_in_dim(wide, (my ^ j) * small, small, 0) for j in range(blocks)]
-        wides, got = tie(wides, got)
         sides = [(keep.reshape(view), cover((0, view[1]))), (got.reshape(view), cover((0, view[1])))]
         sides = totals(sides, [(0, cross.chunks, [(j * small, (j + 1) * small)]) for j in range(blocks)], 1)
         sides = [sides[0]] + trade(sides, "blk", 1)
-        gain_part, cross.got, sides = tie(gain_part, cross.got, sides)
+        down = turned_dot(my_ref, [hidden_parts[0]] + hidden_got, top_all)
+        gain_part, cross.got, sides, wide, down = tie(gain_part, cross.got, sides, wide, down)
+        down = lax.psum_scatter(down, "dp", scatter_dimension=0, tiled=True)
         cross.arrive()
         cross.join([(side, cover((total + j * small, total + (j + 1) * small))) for j, side in enumerate(sides)], total + view[1])
         cross.pack(True)
-        gain_part, qkv_parts, cross.out, wides, d_table = tie(gain_part, qkv_parts, cross.out, wides, d_table)
+        gain_part, cross.out, d_table, wide, mem_part = tie(gain_part, cross.out, d_table, wide, mem_part)
         cross.hop_deep(2)
+        wides = [lax.dynamic_slice_in_dim(wide, (my ^ j) * small, small, 0) for j in range(blocks)]
+        wides_got = trade(wides, "blk", 1)
     else:
         attn, gain_part = dot_gain(self_all, jnp.concatenate(qkv_parts, axis=0), turned_qkv[0])
         gain_part = gain_part[:, 0]
     d_gain_self = gain_part / norm_self
-    qkv_got = trade(qkv_parts, "blk", 1)
-    d_block_in, _, _, _ = norm_grad(
-        grad_self, [qkv_parts[0]] + qkv_got, turned_qkv, block_in[0], norm_self, [], own_q + 2 * own_kv
-    )
     lines = jnp.concatenate([d_gain_self, d_gain_cross, d_gain_ffn, d_table.reshape(-1)]).reshape(-1, LANES)
-    if fast:
-        lines = sum_axis(sum_axis(lines, "dp", 1), "blk", blocks // 2)
-        d_block_in, cross.got, mem_part, lines, down = tie(d_block_in, cross.got, mem_part, lines, down)
-        cross.arrive()
-        cross.pack(True)
-        mem_part, lines, wides, cross.out = tie(mem_part, lines, wides, cross.out)
-        cross.hop_deep(4)
-        wides = [wides[0]] + trade(wides, "blk", 1)
     mem_blocks = mem_part.reshape(2, blocks, mem_rows, kv_width)
     bit = blocks // 2
     while bit:
         mem_blocks = add16(mem_blocks[:, :bit], swap(mem_blocks[:, bit:], "blk", bit))
         bit //= 2
     mem_grad = mem_blocks[:, 0]
+    if fast:
+        lines = sum_axis(sum_axis(lines, "dp", 1), "blk", blocks // 2)
+        cross.got, lines, mem_grad, wides_got, qkv_parts = tie(cross.got, lines, mem_grad, wides_got, qkv_parts)
+        cross.arrive()
+        cross.pack(True)
+        lines, mem_grad, qkv_parts, cross.out = tie(lines, mem_grad, qkv_parts, cross.out)
+        cross.hop_deep(4)
+    qkv_got = trade(qkv_parts, "blk", 1)
     d_memory = dot32(mem_grad[0], cross_key, NT) + dot32(mem_grad[1], cross_value, NT)
     if fast:
+        qkv_got, d_memory = tie(qkv_got, d_memory)
+    d_block_in, _, _, _ = norm_grad(
+        grad_self, [qkv_parts[0]] + qkv_got, turned_qkv, block_in[0], norm_self, [], own_q + 2 * own_kv
+    )
+    if fast:
+        lines = sum_axis(lines, "dp", lax.axis_size("dp") // 2, 2).reshape(-1)
+        dw_gate, dw_up = place(my_ref, [wides[0]] + wides_got)
+        dw_down = down[0].astype(F32)
+        d_block_in, cross.got, lines, dw_gate, dw_up, dw_down = tie(d_block_in, cross.got, lines, dw_gate, dw_up, dw_down)
         cross.arrive()
-        lines = sum_axis(lines, "dp", lax.axis_size("dp") // 2, 2).reshape(-1)
     else:
         lines = sum_axis(sum_axis(lines, "dp", lax.axis_size("dp") // 2), "blk", blocks // 2).reshape(-1)
     gain_self, gain_cross, gain_ffn = lines[:d], lines[d : 2 * d], lines[2 * d : 3 * d]
     table_sum = lines[3 * d :].reshape(bias_table.shape)
     if fast:
-        dw_gate, dw_up = place(my_ref, wides)
         shapes = [(small, d), (small, d), (small, kv_width), (small, kv_width), (small, d)]
         outs, row = [], 0
         for number, (_, width) in enumerate(shapes):
@@ -1095,7 +1095,6 @@
         shapes += [(small, d), (small, kv_width), (small, kv_width)]
         dealt = [(j, row + j * small, small, ((5, own_q), (6, own_kv), (7, own_kv))) for j in range(blocks)]
         dw_co, dw_cq, dw_ck, dw_cv, dw_o, dw_q, dw_k, dw_v = finish(my_ref, cross.pieces, shapes, outs, dealt)
-        dw_down = down[0].astype(F32)
         ffn_outs = (dw_gate, dw_up, dw_down)
     else:
         dw_co = sum_rows(dot32(cross_mix, cross_grad, TN).astype(BF16), 0)

time: 338 us -> 330 us (0.976)
  starting transfers between devices: 56.4 us -> 47.8 us
  local copies, waits for them, and re-layouts: 27.1 us -> 19.1 us
  waiting for transfers between devices: 53.3 us -> 59.5 us
  matrix products: 22.7 us -> 26.5 us
    ppermute x46 -> x42, starting transfers between devices: 56.2 us -> 47.4 us  [swap(): lax.ppermute(x, axis, [(i, i ^ bit) for i in range(lax.axis_size(axis))])]
    unnamed x133 -> x130, local copies, waits for them, and re-layouts: 13 us -> 8 us
    dot_general x8, matrix products: 20.2 us -> 24.8 us  [dot32(): return lax.dot_general(a, b, dims, preferred_element_type=F32)]
    ppermute x46 -> x42, waiting for transfers between devices: 53.2 us -> 56.5 us  [swap(): lax.ppermute(x, axis, [(i, i ^ bit) for i in range(lax.axis_size(axis))])]
  transfers between devices with their start and end apart: 49 -> 46, of which waited for: 20 -> 19; matrix products, arithmetic and copies ran while one was open for 16% -> 17% of each run, Pallas kernels for 40% -> 40%
where the time goes in v4:
time: 330 us; the launch traced here: 326 us
  Pallas kernels  142 us (43%)
  waiting for transfers between devices  59.5 us (18%)
  starting transfers between devices  47.8 us (14%)
  matrix products  26.5 us (8%)
  local copies, waits for them, and re-layouts  19.1 us (6%)
  other arithmetic  16.5 us (5%)
  between operations  15.3 us (5%)
    ppermute x42, waiting for transfers between devices, swap(): lax.ppermute(x, axis, [(i, i ^ bit) for i in range(lax.axis_size(axis))])  56.5 us
    ppermute x42, starting transfers between devices, swap(): lax.ppermute(x, axis, [(i, i ^ bit) for i in range(lax.axis_size(axis))])  47.4 us
    dot_general x8, matrix products, dot32(): return lax.dot_general(a, b, dims, preferred_element_type=F32)  24.8 us
    pallas_call x3, Pallas kernels, norm_grad(): pl.pallas_call(functools.partial(norm_grad_kernel, len(gs), len(after)),...  22.1 us
    pallas_call x5, Pallas kernels, slabs(): pl.pallas_call(functools.partial(slab_kernel, kind, later, len(xs), len(g...  20 us
    pallas_call x1, Pallas kernels, self_backward(): pl.pallas_call(functools.partial(self_backward_kernel, blocks, kv_local),...  18.6 us
    pallas_call x5, Pallas kernels, totals(): pl.pallas_call(functools.partial(total_kernel, plan), grid=(steps,), in_s...  17.7 us
    pallas_call x1, Pallas kernels, self_forward(): pl.pallas_call(functools.partial(self_forward_kernel, blocks, kv_local),...  12.7 us
  transfers between devices with their start and end apart: 46, of which 19 were waited for; matrix products, arithmetic and copies ran while one was open for 17% of the time, Pallas kernels for 40%

profile of v4, /device:TPU:0, one launch (start us, length us, event | category | flops | bytes accessed | tf_op | source)
XLA Modules:
  0.0 326.4 jit_solution(12504022086719065443)
XLA Ops:
  7.3 3.0 collective-permute-start
  25.4 6.0 %fusion.28 = f32[256,2816]{1,0:T(8,128)} fusion(bf16[2816,1024]{1,0:T(8,128)(2,1)} %param.41, bf16[1,256,1024]{2,1,0:T(8,128)(2,1)S(1)} %copy-done.12), kind=kOutput, calls=%fused_computation.87 | convolution fusion | flops 1476395008 | bytes 9175040 | tf_op jit(solution)/shard_map/dot_general | solution.py:28
  31.3 3.9 %collective-permute-done.1.refs_2_ = bf16[256,1024]{1,0:T(8,128)(2,1)} collective-permute-done((bf16[256,1024]{1,0:T(8,128)(2,1)}, bf16[256,1024]{1,0:T(8,128)(2,1)}, u32[]{:S(2)}, u32[]{:S(2)}) %collective-permute-start.1) | collective-permute-done | bytes 524320 | tf_op jit(solution)/shard_map/ppermute | solution.py:32
  40.0 4.7 %norm_dot.1 = (bf16[1024,1024]{1,0:T(8,128)(2,1)}, bf16[1024,512]{1,0:T(8,128)(2,1)}) custom-call(bf16[256,1024]{1,0:T(8,128)(2,1)} %bitcast.69, bf16[256,1024]{1,0:T(8,128)(2,1)} %collective-permute-done.refs_1_, bf16[256,1024]{1,0:T(8,128)(2,1)} %collective-permute-done.1.refs_2_, bf16[256,1024]{1,0:T(8,128)(2,1)} %collective-permute-done.2.refs_3_, ...), custom_call_target="tpu_custom_call" | custom-call | flops 1 | bytes 1 | tf_op jit(solution)/shard_map/norm_dot/pallas_call | solution.py:726
  44.7 12.7 %self_forward.1 = (bf16[256,256]{1,0:T(8,128)(2,1)}, bf16[256,256]{1,0:T(8,128)(2,1)}, bf16[256,256]{1,0:T(8,128)(2,1)}, bf16[256,256]{1,0:T(8,128)(2,1)}, f32[4,2,1,512]{3,2,1,0:T(1,128)}) custom-call(s32[1]{0:T(128)} %bitcast.6.my_ref, bf16[1024,512]{1,0:T(8,128)(2,1)} %get-tuple-element.212.qkv_ref, f32[4,1280]{1,0:T(4,128)} %concatenate.28.bias_ref), custom_call_target="tpu_custom_call" | custom-call | flops 1 | bytes 1 | tf_op jit(solution)/shard_map/self_forward/pallas_call | solution.py:308
  70.7 4.9 %add_norm.2 = (f32[256,1024]{1,0:T(8,128)}, bf16[256,1024]{1,0:T(8,128)(2,1)}, bf16[256,1024]{1,0:T(8,128)(2,1)}) custom-call(bf16[256,256]{1,0:T(8,128)(2,1)} %get-tuple-element.214.refs_0_, bf16[256,256]{1,0:T(8,128)(2,1)} %copy-done.28, bf16[256,256]{1,0:T(8,128)(2,1)} %copy-done.29, bf16[256,256]{1,0:T(8,128)(2,1)} %copy-done.30, ...), custom_call_target="tpu_custom_call" | custom-call | flops 1 | bytes 1 | tf_op jit(solution)/shard_map/add_norm/pallas_call | solution.py:643
  75.6 8.2 %cross_forward.1 = (bf16[256,1024]{1,0:T(8,128)(2,1)}, f32[8,1,512]{2,1,0:T(1,128)}) custom-call(f32[512,1]{1,0:T(8,128)} %copy.46.allow_ref, bf16[256,1024]{1,0:T(8,128)(2,1)} %get-tuple-element.226.q_ref, bf16[512,512]{1,0:T(8,128)(2,1)} %convolution_convert_fusion.1.k_ref, bf16[512,512]{1,0:T(8,128)(2,1)} %convolution_convert_fusion.v_ref), custom_call_target="tpu_custom_call" | custom-call | flops 1 | bytes 1 | tf_op jit(solution)/shard_map/cross_forward/pallas_call | solution.py:367
  83.7 3.9 %add_norm.3 = (f32[256,1024]{1,0:T(8,128)}, bf16[256,1024]{1,0:T(8,128)(2,1)}) custom-call(bf16[256,1024]{1,0:T(8,128)(2,1)} %get-tuple-element.229.refs_0_, bf16[1024,1024]{1,0:T(8,128)(2,1)} %refs_7_.1, f32[256,1024]{1,0:T(8,128)} %get-tuple-element.230.refs_2_, f32[1,1024]{1,0:T(1,128)} %bitcast.87), custom_call_target="tpu_custom_call" | custom-call | flops 1 | bytes 1 | tf_op jit(solution)/shard_map/add_norm/pallas_call | solution.py:643
  87.7 4.5 %fusion.32 = f32[256,2816]{1,0:T(8,128)S(1)} fusion(bf16[256,1024]{1,0:T(8,128)(2,1)} %get-tuple-element.243, bf16[1024,2816]{1,0:T(8,128)(2,1)} %refs_3_.1), kind=kOutput, calls=%fused_computation.91 | convolution fusion | flops 1476395008 | bytes 9175040 | tf_op jit(solution)/shard_map/dot_general | solution.py:28
  92.3 4.4 %fusion.33 = f32[256,2816]{1,0:T(8,128)S(1)} fusion(bf16[256,1024]{1,0:T(8,128)(2,1)S(1)} %copy-done.32, bf16[1024,2816]{1,0:T(8,128)(2,1)} %refs_2_.1), kind=kOutput, calls=%fused_computation.92 | convolution fusion | flops 1476395008 | bytes 9175040 | tf_op jit(solution)/shard_map/dot_general | solution.py:28
  96.7 4.6 %multiply_convert_fusion = (bf16[256,2816]{1,0:T(8,128)(2,1)}, bf16[256,2816]{1,0:T(8,128)(2,1)S(1)}, bf16[256,2816]{1,0:T(8,128)(2,1)S(1)}) fusion(f32[256,2816]{1,0:T(8,128)S(1)} %fusion.32, f32[256,2816]{1,0:T(8,128)S(1)} %fusion.33, f32[256,2816]{1,0:T(8,128)S(1)} %copy-done.11), kind=kLoop, calls=%fused_computation.15 | loop fusion | flops 25231360 | bytes 12976128 | tf_op jit(solution)/shard_map/convert_element_type | solution.py:969
  107.2 10.8 %norm_grad.3 = (f32[256,1024]{1,0:T(8,128)}, bf16[256,1024]{1,0:T(8,128)(2,1)}, f32[1,1024]{1,0:T(1,128)}, bf16[256,1024]{1,0:T(8,128)(2,1)}) custom-call(bf16[256,2816]{1,0:T(8,128)(2,1)} %copy-done.3, bf16[256,2816]{1,0:T(8,128)(2,1)} %copy-done.4, bf16[1024,2816]{1,0:T(8,128)(2,1)} %refs_2_.1, bf16[1024,2816]{1,0:T(8,128)(2,1)} %refs_3_.1, ...), custom_call_target="tpu_custom_call" | custom-call | flops 1 | bytes 1 | tf_op jit(solution)/shard_map/norm_grad/pallas_call | solution.py:696
  121.0 3.5 %slabs.5 = (bf16[16,256,512]{2,1,0:T(8,128)(2,1)}, bf16[16,256,512]{2,1,0:T(8,128)(2,1)}) custom-call(s32[3,32]{1,0:T(4,128)} %get-tuple-element.441.order_ref, bf16[256,1024]{1,0:T(8,128)(2,1)} %get-tuple-element.229.refs_0_, bf16[256,1024]{1,0:T(8,128)(2,1)} %get-tuple-element.244.refs_1_), custom_call_target="tpu_custom_call" | custom-call | flops 1 | bytes 1 | tf_op jit(solution)/shard_map/slabs/pallas_call | solution.py:466
  124.4 5.1 %fusion.4 = bf16[256,1024]{1,0:T(8,128)(2,1)} fusion(f32[256,1024]{1,0:T(8,128)S(1)} %copy-done.22, bf16[256,2816]{1,0:T(8,128)(2,1)S(1)} %copy-done.6, bf16[2816,1024]{1,0:T(8,128)(2,1)} %param.41), kind=kOutput, calls=%fused_computation.20 | convolution fusion | flops 1476919296 | bytes 8781824 | tf_op jit(solution)/shard_map/dot_general | solution.py:28
  133.9 9.4 %cross_backward.1 = (bf16[256,1024]{1,0:T(8,128)(2,1)}, bf16[2,512,512]{2,1,0:T(8,128)(2,1)}) custom-call(f32[512,1]{1,0:T(8,128)} %copy.46.allow_ref, bf16[256,1024]{1,0:T(8,128)(2,1)} %get-tuple-element.226.q_ref, bf16[512,512]{1,0:T(8,128)(2,1)} %convolution_convert_fusion.1.k_ref, bf16[512,512]{1,0:T(8,128)(2,1)} %convolution_convert_fusion.v_ref, ...), custom_call_target="tpu_custom_call" | custom-call | flops 1 | bytes 1 | tf_op jit(solution)/shard_map/cross_backward/pallas_call | solution.py:392
  143.4 3.5 %slabs.6 = (bf16[16,256,512]{2,1,0:T(8,128)(2,1)}, bf16[16,256,512]{2,1,0:T(8,128)(2,1)}) custom-call(s32[3,32]{1,0:T(4,128)} %get-tuple-element.441.order_ref, bf16[256,1024]{1,0:T(8,128)(2,1)} %get-tuple-element.255.refs_0_, bf16[256,1024]{1,0:T(8,128)(2,1)} %get-tuple-element.262.refs_1_.refs_0_, ...), custom_call_target="tpu_custom_call", output_to_operand_aliasing={{0}: (3, {}), {1}: (4, {})} | custom-call | flops 1 | bytes 1 | tf_op jit(solution)/shard_map/slabs/pallas_call | solution.py:466
  146.9 4.5 %slabs.7 = (bf16[16,256,512]{2,1,0:T(8,128)(2,1)}, bf16[16,256,512]{2,1,0:T(8,128)(2,1)}) custom-call(s32[3,32]{1,0:T(4,128)} %get-tuple-element.441.order_ref, bf16[512,1024]{1,0:T(8,128)(2,1)} %copy-done.18, bf16[2,512,512]{2,1,0:T(8,128)(2,1)} %get-tuple-element.347.refs_1_, ...), custom_call_target="tpu_custom_call", output_to_operand_aliasing={{0}: (3, {}), {1}: (4, {})} | custom-call | flops 1 | bytes 1 | tf_op jit(solution)/shard_map/slabs/pallas_call | solution.py:466
  151.5 5.6 %norm_grad.4 = (f32[256,1024]{1,0:T(8,128)}, bf16[256,1024]{1,0:T(8,128)(2,1)}, f32[1,1024]{1,0:T(1,128)}, bf16[256,256]{1,0:T(8,128)(2,1)}, bf16[256,256]{1,0:T...) custom-call(bf16[256,1024]{1,0:T(8,128)(2,1)} %get-tuple-element.262.refs_1_.refs_0_, ...), custom_call_target="tpu_custom_call" | custom-call | flops 1 | bytes 1 | tf_op jit(solution)/shard_map/norm_grad/pallas_call | solution.py:696
  157.1 3.6 %slabs.8 = (bf16[16,256,512]{2,1,0:T(8,128)(2,1)}, bf16[16,256,512]{2,1,0:T(8,128)(2,1)}) custom-call(s32[3,32]{1,0:T(4,128)} %get-tuple-element.440.order_ref, bf16[256,256]{1,0:T(8,128)(2,1)} %get-tuple-element.214.refs_0_, bf16[256,256]{1,0:T(8,128)(2,1)} %copy-done.28, ...), custom_call_target="tpu_custom_call", output_to_operand_aliasing={{0}: (6, {}), {1}: (7, {})} | custom-call | flops 1 | bytes 1 | tf_op jit(solution)/shard_map/slabs/pallas_call | solution.py:466
  164.2 7.4 %pair_dot.1 = bf16[1024,1408]{1,0:T(8,128)(2,1)} custom-call(s32[1]{0:T(128)} %bitcast.6.my_ref, bf16[4,256,1024]{2,1,0:T(8,128)(2,1)} %bitcast.77, bf16[256,1408]{1,0:T(8,128)(2,1)} %get-tuple-element.269.refs_0_, bf16[256,1408]{1,0:T(8,128)(2,1)} %copy-done.25, bf16[256,1408]{1,0:T(8,128)(2,1)} %copy-done.26, bf16[256,1408]{1,0:T(8,128)(2,1)} %copy-done.27), custom_call_target="tpu_custom_call" | custom-call | flops 1 | bytes 1 | tf_op jit(solution)/shard_map/pair_dot/pallas_call | solution.py:589
  171.8 5.0 %totals.5 = (bf16[8,128,512]{2,1,0:T(8,128)(2,1)}, bf16[8,128,512]{2,1,0:T(8,128)(2,1)}) custom-call(bf16[16,256,512]{2,1,0:T(8,128)(2,1)} %get-tuple-element.288.refs_0_.refs_2_.refs_4_, bf16[16,256,512]{2,1,0:T(8,128)(2,1)} %collective-permute-done.15.refs_1_.refs_3_.refs_5_, bf16[16,256,512]{2,1,0:T(8,128)(2,1)} %get-tuple-element.288.refs_0_.refs_2_.refs_4_, ...), custom_call_target="tpu_custom_call" | custom-call | flops 1 | bytes 1 | tf_op jit(solution)/shard_map/totals/pallas_call | solution.py:535
  182.3 18.6 %self_backward.1 = (bf16[256,512]{1,0:T(8,128)(2,1)}, bf16[256,512]{1,0:T(8,128)(2,1)}, bf16[256,512]{1,0:T(8,128)(2,1)}, bf16[256,512]{1,0:T(8,128)(2,1)}, f32[4,1280]{1,0:T(4,128)}) custom-call(s32[1]{0:T(128)} %bitcast.6.my_ref, bf16[1024,512]{1,0:T(8,128)(2,1)} %get-tuple-element.212.qkv_ref, f32[4,1280]{1,0:T(4,128)} %concatenate.28.bias_ref, ...), custom_call_target="tpu_custom_call" | custom-call | flops 1 | bytes 1 | tf_op jit(solution)/shard_map/self_backward/pallas_call | solution.py:337
  205.6 4.2 %totals.6 = (bf16[4,128,512]{2,1,0:T(8,128)(2,1)}, bf16[4,128,512]{2,1,0:T(8,128)(2,1)}) custom-call(bf16[16,256,512]{2,1,0:T(8,128)(2,1)} %get-tuple-element.288.refs_0_.refs_2_.refs_4_, bf16[16,256,512]{2,1,0:T(8,128)(2,1)} %collective-permute-done.15.refs_1_.refs_3_.refs_5_, bf16[8,128,512]{2,1,0:T(8,128)(2,1)} %copy-done.1, ...), custom_call_target="tpu_custom_call" | custom-call | flops 1 | bytes 1 | tf_op jit(solution)/shard_map/totals/pallas_call | solution.py:535
  210.8 7.5 %collective-permute-done.19.refs_2_ = bf16[8,88,256]{2,1,0:T(8,128)(2,1)S(1)} collective-permute-done((bf16[8,88,256]{2,1,0:T(8,128)(2,1)S(1)}, bf16[8,88,256]{2,1,0:T(8,128)(2,1)S(1)}, u32[]{:S(2)}, u32[]{:S(2)}) %collective-permute-start.19) | collective-permute-done | bytes 360480 | tf_op jit(solution)/shard_map/ppermute | solution.py:32
  218.3 4.9 %slabs.9 = (bf16[16,32,512]{2,1,0:T(8,128)(2,1)}, bf16[16,32,512]{2,1,0:T(8,128)(2,1)}, f32[1024,1]{1,0:T(8,128)}) custom-call(s32[3,32]{1,0:T(4,128)} %get-tuple-element.441.order_ref, bf16[1024,1024]{1,0:T(8,128)(2,1)} %get-tuple-element.248.refs_0_, bf16[256,512]{1,0:T(8,128)(2,1)} %get-tuple-element.356.refs_1_.refs_0_, ...), custom_call_target="tpu_custom_call" | custom-call | flops 1 | bytes 1 | tf_op jit(solution)/shard_map/slabs/pallas_call | solution.py:466
  226.2 3.4 %totals.7 = (bf16[4,32,512]{2,1,0:T(8,128)(2,1)}, bf16[4,32,512]{2,1,0:T(8,128)(2,1)}, bf16[4,32,512]{2,1,0:T(8,128)(2,1)}, bf16[4,32,512]{2,1,0:T(8,128)(2,1)}) custom-call(bf16[4,128,512]{2,1,0:T(8,128)(2,1)} %bitcast.58, bf16[4,128,512]{2,1,0:T(8,128)(2,1)} %bitcast.62, bf16[4,128,512]{2,1,0:T(8,128)(2,1)} %bitcast.59, bf16[4,128,512]{2,1,0:T(8,128)(2,1)} %bitcast.63, ...), custom_call_target="tpu_custom_call" | custom-call | flops 1 | bytes 1 | tf_op jit(solution)/shard_map/totals/pallas_call | solution.py:535
  233.2 4.9 %turned_dot.1 = bf16[8,88,1024]{2,1,0:T(8,128)(2,1)} custom-call(s32[1]{0:T(128)} %bitcast.6.my_ref, bf16[8,88,256]{2,1,0:T(8,128)(2,1)} %get-tuple-element.327.refs_0_, bf16[8,88,256]{2,1,0:T(8,128)(2,1)} %copy-done.36, bf16[8,88,256]{2,1,0:T(8,128)(2,1)} %copy-done.37, bf16[8,88,256]{2,1,0:T(8,128)(2,1)} %copy-done.38, bf16[4,256,1024]{2,1,0:T(8,128)(2,1)} %bitcast.76), custom_call_target="tpu_custom_call" | custom-call | flops 1 | bytes 1 | tf_op jit(solution)/shard_map/turned_dot/pallas_call | solution.py:778
  241.6 3.0 collective-permute-done.26.refs_9_
  254.5 7.4 %collective-permute-done.31 = bf16[2,2,128,512]{3,2,1,0:T(8,128)(2,1)S(1)} collective-permute-done((bf16[2,2,128,512]{3,2,1,0:T(8,128)(2,1)S(1)}, bf16[2,2,128,512]{3,2,1,0:T(8,128)(2,1)S(1)}, u32[]{:S(2)}, u32[]{:S(2)}) %collective-permute-start.31) | collective-permute-done | bytes 524320 | tf_op jit(solution)/shard_map/ppermute | solution.py:32
  272.9 10.7 %collective-permute-done.27.refs_10_ = bf16[2,384,512]{2,1,0:T(8,128)(2,1)S(1)} collective-permute-done((bf16[2,384,512]{2,1,0:T(8,128)(2,1)}, bf16[2,384,512]{2,1,0:T(8,128)(2,1)S(1)}, u32[]{:S(2)}, u32[]{:S(2)}) %collective-permute-start.27) | collective-permute-done | bytes 786464 | tf_op jit(solution)/shard_map/ppermute | solution.py:32
  302.4 5.6 %norm_grad.5 = (f32[256,1024]{1,0:T(8,128)}, bf16[256,1024]{1,0:T(8,128)(2,1)}, f32[1,1024]{1,0:T(1,128)}) custom-call(bf16[256,512]{1,0:T(8,128)(2,1)} %get-tuple-element.356.refs_1_.refs_0_, bf16[256,512]{1,0:T(8,128)(2,1)} %copy-done.39, bf16[256,512]{1,0:T(8,128)(2,1)} %copy-done.40, bf16[256,512]{1,0:T(8,128)(2,1)} %copy-done.41, ...), custom_call_target="tpu_custom_call" | custom-call | flops 1 | bytes 1 | tf_op jit(solution)/shard_map/norm_grad/pallas_call | solution.py:696
  309.7 6.0 %collective-permute-done.39.refs_11_ = bf16[1,384,512]{2,1,0:T(8,128)(2,1)S(1)} collective-permute-done((bf16[1,384,512]{2,1,0:T(8,128)(2,1)S(1)}, bf16[1,384,512]{2,1,0:T(8,128)(2,1)S(1)}, u32[]{:S(2)}, u32[]{:S(2)}) %collective-permute-start.39) | collective-permute-done | bytes 393248 | tf_op jit(solution)/shard_map/ppermute | solution.py:32
  (267 shorter events, 115.8 us)
Async XLA Ops:
  7.2 80.4 %all-gather.3.cloned.1.call-start = ((), (), s32[]{:S(2)}) async-start(), calls=%async_computation.2 | async-start | bytes 2621440 | tf_op jit(solution)/shard_map/all_gather | solution.py:943
  7.3 24.1 %collective-permute-start = (bf16[256,1024]{1,0:T(8,128)(2,1)}, bf16[256,1024]{1,0:T(8,128)(2,1)}, u32[]{:S(2)}, u32[]{:S(2)}) collective-permute-start(bf16[256,1024]{1,0:T(8,128)(2,1)} %bitcast.66), channel_id=1, source_target_pairs={{0,1},{1,0},{2,3},{3,2},{4,5},{5,4},{6,7},{7,6},{8,9},{9,8},{10,11... | collective-permute-start | bytes 1572872 | tf_op jit(solution)/shard_map/ppermute | solution.py:32
  10.3 24.9 %collective-permute-start.1 = (bf16[256,1024]{1,0:T(8,128)(2,1)}, bf16[256,1024]{1,0:T(8,128)(2,1)}, u32[]{:S(2)}, u32[]{:S(2)}) collective-permute-start(bf16[256,1024]{1,0:T(8,128)(2,1)} %bitcast.67), channel_id=1, source_target_pairs={{0,2},{1,3},{2,0},{3,1},{4,6},{5,7},{6,4},{7,5},{8,10},{9,11},{10,... | collective-permute-start | bytes 1572872 | tf_op jit(solution)/shard_map/ppermute | solution.py:32
  11.8 23.4 %collective-permute-start.2 = (bf16[256,1024]{1,0:T(8,128)(2,1)}, bf16[256,1024]{1,0:T(8,128)(2,1)}, u32[]{:S(2)}, u32[]{:S(2)}) collective-permute-start(bf16[256,1024]{1,0:T(8,128)(2,1)} %bitcast.68), channel_id=1, source_target_pairs={{0,3},{1,2},{2,1},{3,0},{4,7},{5,6},{6,5},{7,4},{8,11},{9,10},{10,... | collective-permute-start | bytes 1572872 | tf_op jit(solution)/shard_map/ppermute | solution.py:32
  35.2 97.2 %all-gather.5.cloned.1.call-start = ((), (), s32[]{:S(2)}) async-start(), calls=%async_computation.3 | async-start | bytes 2621440 | tf_op jit(solution)/shard_map/all_gather | solution.py:980
  35.5 25.0 %collective-permute-start.6 = (bf16[128,1024]{1,0:T(8,128)(2,1)}, bf16[128,1024]{1,0:T(8,128)(2,1)}, u32[]{:S(2)}, u32[]{:S(2)}) collective-permute-start(bf16[128,1024]{1,0:T(8,128)(2,1)} %bitcast.1), channel_id=1, source_target_pairs={{0,1},{1,0},{2,3},{3,2},{4,5},{5,4},{6,7},{7,6},{8,9},{9,8},{10,11... | collective-permute-start | bytes 786440 | tf_op jit(solution)/shard_map/ppermute | solution.py:32
  36.8 25.9 %collective-permute-start.7 = (bf16[128,1024]{1,0:T(8,128)(2,1)}, bf16[128,1024]{1,0:T(8,128)(2,1)}, u32[]{:S(2)}, u32[]{:S(2)}) collective-permute-start(bf16[128,1024]{1,0:T(8,128)(2,1)} %bitcast.1), channel_id=1, source_target_pairs={{0,2},{1,3},{2,0},{3,1},{4,6},{5,7},{6,4},{7,5},{8,10},{9,11},{10,... | collective-permute-start | bytes 786440 | tf_op jit(solution)/shard_map/ppermute | solution.py:32
  37.6 26.1 %collective-permute-start.8 = (bf16[128,1024]{1,0:T(8,128)(2,1)}, bf16[128,1024]{1,0:T(8,128)(2,1)}, u32[]{:S(2)}, u32[]{:S(2)}) collective-permute-start(bf16[128,1024]{1,0:T(8,128)(2,1)} %bitcast.1), channel_id=1, source_target_pairs={{0,3},{1,2},{2,1},{3,0},{4,7},{5,6},{6,5},{7,4},{8,11},{9,10},{10,... | collective-permute-start | bytes 786440 | tf_op jit(solution)/shard_map/ppermute | solution.py:32
  87.7 156.9 %reduce-scatter.3.cloned.1.call-start = ((), (), s32[]{:S(2)}) async-start(), calls=%async_computation.4 | async-start | bytes 3244032 | tf_op jit(solution)/shard_map/reduce_scatter | solution.py:1021
  103.4 26.1 %collective-permute-start.9 = (bf16[256,1408]{1,0:T(8,128)(2,1)S(1)}, bf16[256,1408]{1,0:T(8,128)(2,1)S(1)}, u32[]{:S(2)}, u32[]{:S(2)}) collective-permute-start(bf16[256,1408]{1,0:T(8,128)(2,1)S(1)} %get-tuple-element.234), channel_id=1, source_target_pairs={{0,1},{1,0},{2,3},{3,2},{4,5},{5,4},{6,7},{7,6},{8,9},{9,8},{10,11... | collective-permute-start | bytes 2162696 | tf_op jit(solution)/shard_map/ppermute | solution.py:32
  104.3 25.2 %collective-permute-start.10 = (bf16[256,1408]{1,0:T(8,128)(2,1)S(1)}, bf16[256,1408]{1,0:T(8,128)(2,1)S(1)}, u32[]{:S(2)}, u32[]{:S(2)}) collective-permute-start(bf16[256,1408]{1,0:T(8,128)(2,1)S(1)} %get-tuple-element.235), channel_id=1, source_target_pairs={{0,2},{1,3},{2,0},{3,1},{4,6},{5,7},{6,4},{7,5},{8,10},{9,11},{10,... | collective-permute-start | bytes 2162696 | tf_op jit(solution)/shard_map/ppermute | solution.py:32
  132.5 19.0 %collective-permute-start.11 = (bf16[256,1408]{1,0:T(8,128)(2,1)S(1)}, bf16[256,1408]{1,0:T(8,128)(2,1)S(1)}, u32[]{:S(2)}, u32[]{:S(2)}) collective-permute-start(bf16[256,1408]{1,0:T(8,128)(2,1)S(1)} %get-tuple-element.254), channel_id=1, source_target_pairs={{0,3},{1,2},{2,1},{3,0},{4,7},{5,6},{6,5},{7,4},{8,11},{9,10},{10,... | collective-permute-start | bytes 2162696 | tf_op jit(solution)/shard_map/ppermute | solution.py:32
  160.7 11.1 %collective-permute-start.15 = (bf16[16,256,512]{2,1,0:T(8,128)(2,1)}, bf16[16,256,512]{2,1,0:T(8,128)(2,1)}, u32[]{:S(2)}, u32[]{:S(2)}) collective-permute-start(bf16[16,256,512]{2,1,0:T(8,128)(2,1)} %get-tuple-element.289), channel_id=1, source_target_pairs={{0,4},{4,0},{8,12},{12,8},{16,20},{20,16},{24,28},{28,24},{1,5},{5... | collective-permute-start | bytes 12582920 | tf_op jit(solution)/shard_map/ppermute | solution.py:32
  160.7 11.0 %collective-permute-start.12 = (bf16[256,256]{1,0:T(8,128)(2,1)S(1)}, bf16[256,256]{1,0:T(8,128)(2,1)S(1)}, u32[]{:S(2)}, u32[]{:S(2)}) collective-permute-start(bf16[256,256]{1,0:T(8,128)(2,1)S(1)} %copy-done.60), channel_id=1, source_target_pairs={{0,1},{1,0},{2,3},{3,2},{4,5},{5,4},{6,7},{7,6},{8,9},{9,8},{10,11... | collective-permute-start | bytes 393224 | tf_op jit(solution)/shard_map/ppermute | solution.py:32
  171.7 136.3 %reduce-scatter.5.cloned.1.call-start = ((), (), s32[]{:S(2)}) async-start(), calls=%async_computation.5 | async-start | bytes 1622016 | tf_op jit(solution)/shard_map/reduce_scatter | solution.py:1045
  176.8 26.4 %collective-permute-start.16 = (bf16[8,128,512]{2,1,0:T(8,128)(2,1)}, bf16[8,128,512]{2,1,0:T(8,128)(2,1)S(1)}, u32[]{:S(2)}, u32[]{:S(2)}) collective-permute-start(bf16[8,128,512]{2,1,0:T(8,128)(2,1)} %get-tuple-element.300), channel_id=1, source_target_pairs={{0,1},{1,0},{2,3},{3,2},{4,5},{5,4},{6,7},{7,6},{8,9},{9,8},{10,11... | collective-permute-start | bytes 3145736 | tf_op jit(solution)/shard_map/ppermute | solution.py:32
  178.3 26.3 %collective-permute-start.17 = (bf16[8,128,512]{2,1,0:T(8,128)(2,1)}, bf16[8,128,512]{2,1,0:T(8,128)(2,1)S(1)}, u32[]{:S(2)}, u32[]{:S(2)}) collective-permute-start(bf16[8,128,512]{2,1,0:T(8,128)(2,1)} %get-tuple-element.301), channel_id=1, source_target_pairs={{0,2},{1,3},{2,0},{3,1},{4,6},{5,7},{6,4},{7,5},{8,10},{9,11},{10,... | collective-permute-start | bytes 3145736 | tf_op jit(solution)/shard_map/ppermute | solution.py:32
  178.8 32.0 %collective-permute-start.18 = (bf16[8,88,256]{2,1,0:T(8,128)(2,1)S(1)}, bf16[8,88,256]{2,1,0:T(8,128)(2,1)S(1)}, u32[]{:S(2)}, u32[]{:S(2)}) collective-permute-start(bf16[8,88,256]{2,1,0:T(8,128)(2,1)S(1)} %copy-done.57), channel_id=1, source_target_pairs={{0,1},{1,0},{2,3},{3,2},{4,5},{5,4},{6,7},{7,6},{8,9},{9,8},{10,11... | collective-permute-start | bytes 1081352 | tf_op jit(solution)/shard_map/ppermute | solution.py:32
  180.3 38.0 %collective-permute-start.19 = (bf16[8,88,256]{2,1,0:T(8,128)(2,1)S(1)}, bf16[8,88,256]{2,1,0:T(8,128)(2,1)S(1)}, u32[]{:S(2)}, u32[]{:S(2)}) collective-permute-start(bf16[8,88,256]{2,1,0:T(8,128)(2,1)S(1)} %copy-done.56), channel_id=1, source_target_pairs={{0,2},{1,3},{2,0},{3,1},{4,6},{5,7},{6,4},{7,5},{8,10},{9,11},{10,... | collective-permute-start | bytes 1081352 | tf_op jit(solution)/shard_map/ppermute | solution.py:32
  180.9 37.4 %collective-permute-start.20 = (bf16[8,88,256]{2,1,0:T(8,128)(2,1)S(1)}, bf16[8,88,256]{2,1,0:T(8,128)(2,1)S(1)}, u32[]{:S(2)}, u32[]{:S(2)}) collective-permute-start(bf16[8,88,256]{2,1,0:T(8,128)(2,1)S(1)} %copy-done.55), channel_id=1, source_target_pairs={{0,3},{1,2},{2,1},{3,0},{4,7},{5,6},{6,5},{7,4},{8,11},{9,10},{10,... | collective-permute-start | bytes 1081352 | tf_op jit(solution)/shard_map/ppermute | solution.py:32
  223.3 15.6 %collective-permute-start.21 = (bf16[4,128,512]{2,1,0:T(8,128)(2,1)}, bf16[4,128,512]{2,1,0:T(8,128)(2,1)S(1)}, u32[]{:S(2)}, u32[]{:S(2)}) collective-permute-start(bf16[4,128,512]{2,1,0:T(8,128)(2,1)} %get-tuple-element.318), channel_id=1, source_target_pairs={{0,2},{1,3},{2,0},{3,1},{4,6},{5,7},{6,4},{7,5},{8,10},{9,11},{10,... | collective-permute-start | bytes 1572872 | tf_op jit(solution)/shard_map/ppermute | solution.py:32
  223.8 15.1 %collective-permute-start.22 = (bf16[4,128,512]{2,1,0:T(8,128)(2,1)}, bf16[4,128,512]{2,1,0:T(8,128)(2,1)S(1)}, u32[]{:S(2)}, u32[]{:S(2)}) collective-permute-start(bf16[4,128,512]{2,1,0:T(8,128)(2,1)} %get-tuple-element.319), channel_id=1, source_target_pairs={{0,1},{1,0},{2,3},{3,2},{4,5},{5,4},{6,7},{7,6},{8,9},{9,8},{10,11... | collective-permute-start | bytes 1572872 | tf_op jit(solution)/shard_map/ppermute | solution.py:32
  229.6 12.0 %collective-permute-start.24 = (bf16[4,32,512]{2,1,0:T(8,128)(2,1)}, bf16[4,32,512]{2,1,0:T(8,128)(2,1)S(1)}, u32[]{:S(2)}, u32[]{:S(2)}) collective-permute-start(bf16[4,32,512]{2,1,0:T(8,128)(2,1)} %get-tuple-element.323), channel_id=1, source_target_pairs={{0,1},{1,0},{2,3},{3,2},{4,5},{5,4},{6,7},{7,6},{8,9},{9,8},{10,11... | collective-permute-start | bytes 393224 | tf_op jit(solution)/shard_map/ppermute | solution.py:32
  230.2 11.4 %collective-permute-start.25 = (bf16[4,32,512]{2,1,0:T(8,128)(2,1)}, bf16[4,32,512]{2,1,0:T(8,128)(2,1)S(1)}, u32[]{:S(2)}, u32[]{:S(2)}) collective-permute-start(bf16[4,32,512]{2,1,0:T(8,128)(2,1)} %get-tuple-element.324), channel_id=1, source_target_pairs={{0,2},{1,3},{2,0},{3,1},{4,6},{5,7},{6,4},{7,5},{8,10},{9,11},{10,... | collective-permute-start | bytes 393224 | tf_op jit(solution)/shard_map/ppermute | solution.py:32
  231.7 12.9 %collective-permute-start.26 = (bf16[4,32,512]{2,1,0:T(8,128)(2,1)}, bf16[4,32,512]{2,1,0:T(8,128)(2,1)S(1)}, u32[]{:S(2)}, u32[]{:S(2)}) collective-permute-start(bf16[4,32,512]{2,1,0:T(8,128)(2,1)} %get-tuple-element.325), channel_id=1, source_target_pairs={{0,3},{1,2},{2,1},{3,0},{4,7},{5,6},{6,5},{7,4},{8,11},{9,10},{10,... | collective-permute-start | bytes 393224 | tf_op jit(solution)/shard_map/ppermute | solution.py:32
  248.6 13.3 %collective-permute-start.31 = (bf16[2,2,128,512]{3,2,1,0:T(8,128)(2,1)S(1)}, bf16[2,2,128,512]{3,2,1,0:T(8,128)(2,1)S(1)}, u32[]{:S(2)}, u32[]{:S(2)}) collective-permute-start(bf16[2,2,128,512]{3,2,1,0:T(8,128)(2,1)S(1)} %slice.55), channel_id=1, source_target_pairs={{0,2},{1,3},{2,0},{3,1},{4,6},{5,7},{6,4},{7,5},{8,10},{9,11},{10,... | collective-permute-start | bytes 1572872 | tf_op jit(solution)/shard_map/ppermute | solution.py:32
  250.8 32.7 %collective-permute-start.27 = (bf16[2,384,512]{2,1,0:T(8,128)(2,1)}, bf16[2,384,512]{2,1,0:T(8,128)(2,1)S(1)}, u32[]{:S(2)}, u32[]{:S(2)}) collective-permute-start(bf16[2,384,512]{2,1,0:T(8,128)(2,1)} %totals.8), channel_id=1, source_target_pairs={{0,8},{4,12},{8,0},{12,4},{16,24},{20,28},{24,16},{28,20},{1,9},{5... | collective-permute-start | bytes 2359304 | tf_op jit(solution)/shard_map/ppermute | solution.py:32
  253.0 9.8 %collective-permute-start.29 = (f32[28,128]{1,0:T(8,128)S(1)}, f32[28,128]{1,0:T(8,128)S(1)}, u32[]{:S(2)}, u32[]{:S(2)}) collective-permute-start(f32[28,128]{1,0:T(8,128)S(1)} %fusion.30), channel_id=1, source_target_pairs={{0,1},{1,0},{2,3},{3,2},{4,5},{5,4},{6,7},{7,6},{8,9},{9,8},{10,11... | collective-permute-start | bytes 43016 | tf_op jit(solution)/shard_map/ppermute | solution.py:32
  286.8 13.5 %collective-permute-start.36 = (bf16[256,512]{1,0:T(8,128)(2,1)S(1)}, bf16[256,512]{1,0:T(8,128)(2,1)S(1)}, u32[]{:S(2)}, u32[]{:S(2)}) collective-permute-start(bf16[256,512]{1,0:T(8,128)(2,1)S(1)} %copy-done.44), channel_id=1, source_target_pairs={{0,1},{1,0},{2,3},{3,2},{4,5},{5,4},{6,7},{7,6},{8,9},{9,8},{10,11... | collective-permute-start | bytes 786440 | tf_op jit(solution)/shard_map/ppermute | solution.py:32
  288.3 13.3 %collective-permute-start.37 = (bf16[256,512]{1,0:T(8,128)(2,1)S(1)}, bf16[256,512]{1,0:T(8,128)(2,1)S(1)}, u32[]{:S(2)}, u32[]{:S(2)}) collective-permute-start(bf16[256,512]{1,0:T(8,128)(2,1)S(1)} %copy-done.43), channel_id=1, source_target_pairs={{0,2},{1,3},{2,0},{3,1},{4,6},{5,7},{6,4},{7,5},{8,10},{9,11},{10,... | collective-permute-start | bytes 786440 | tf_op jit(solution)/shard_map/ppermute | solution.py:32
  289.8 11.8 %collective-permute-start.38 = (bf16[256,512]{1,0:T(8,128)(2,1)S(1)}, bf16[256,512]{1,0:T(8,128)(2,1)S(1)}, u32[]{:S(2)}, u32[]{:S(2)}) collective-permute-start(bf16[256,512]{1,0:T(8,128)(2,1)S(1)} %copy-done.42), channel_id=1, source_target_pairs={{0,3},{1,2},{2,1},{3,0},{4,7},{5,6},{6,5},{7,4},{8,11},{9,10},{10,... | collective-permute-start | bytes 786440 | tf_op jit(solution)/shard_map/ppermute | solution.py:32
  297.4 18.4 %collective-permute-start.39 = (bf16[1,384,512]{2,1,0:T(8,128)(2,1)S(1)}, bf16[1,384,512]{2,1,0:T(8,128)(2,1)S(1)}, u32[]{:S(2)}, u32[]{:S(2)}) collective-permute-start(bf16[1,384,512]{2,1,0:T(8,128)(2,1)S(1)} %copy-done.34), channel_id=1, source_target_pairs={{0,16},{4,20},{8,24},{12,28},{16,0},{20,4},{24,8},{28,12},{1,17},{... | collective-permute-start | bytes 1179656 | tf_op jit(solution)/shard_map/ppermute | solution.py:32
  (77 other events, 648.1 us)
Sparse Core Ops, SparseCore 0:
  35.3 42.0 all-gather.2
  87.8 44.6 all-gather.4
  171.8 38.7 reduce-scatter.2
  244.8 39.3 reduce-scatter.4

commit v5 on v4

--- a/solution.py
+++ b/solution.py
@@ -17,7 +17,8 @@
 STEP_ELEMENTS = 768 * 1024
 F32 = jnp.float32
 BF16 = jnp.bfloat16
-VMEM_LIMIT = 56 * 1024 * 1024
+VMEM_SMALL = 28 * 1024 * 1024
+VMEM_LARGE = 56 * 1024 * 1024
 
 NT = (((1,), (1,)), ((), ()))
 NN = (((1,), (0,)), ((), ()))
@@ -285,8 +286,8 @@
 TINY = pl.CostEstimate(flops=1, transcendentals=0, bytes_accessed=1)
 
 
-def params():
-    return pltpu.CompilerParams(dimension_semantics=("arbitrary",), vmem_limit_bytes=VMEM_LIMIT)
+def params(limit=VMEM_SMALL):
+    return pltpu.CompilerParams(dimension_semantics=("arbitrary",), vmem_limit_bytes=limit)
 
 
 def cost(length, keys, heads, passes, moved):
@@ -475,7 +476,7 @@
         out_shape=shapes,
         scratch_shapes=[pltpu.VMEM((features, tokens), BF16), pltpu.VMEM((chunks, rows, slab), F32)],
         input_output_aliases={first: 0, first + 1: 1} if extra else {},
-        compiler_params=params(),
+        compiler_params=params(VMEM_LARGE),
         cost_estimate=TINY,
         name="slabs",
     )(order, *xs, *gs, *weights, *extra)
@@ -538,7 +539,7 @@
         in_specs=specs,
         out_specs=outs,
         out_shape=shapes,
-        compiler_params=params(),
+        compiler_params=params(VMEM_LARGE),
         cost_estimate=TINY,
         name="totals",
     )(*arrays)
@@ -566,7 +567,7 @@
         + [pl.BlockSpec((1,) + array.shape[1:], lambda i: (0, 0, 0)) for array, _ in pieces],
         out_specs=[pl.BlockSpec(shape, lambda i: (0, 0)) for shape in shapes],
         out_shape=[jax.ShapeDtypeStruct(shape, F32) for shape in shapes],
-        compiler_params=params(),
+        compiler_params=params(VMEM_LARGE),
         cost_estimate=TINY,
         name="finish",
     )(my, *[array for array, _ in pieces])
@@ -809,7 +810,7 @@
         in_specs=[pl.BlockSpec(memory_space=pltpu.SMEM)] + whole_blocks(parts),
         out_specs=[pl.BlockSpec(shape, lambda i: (0, 0))] * 2,
         out_shape=[jax.ShapeDtypeStruct(shape, F32)] * 2,
-        compiler_params=params(),
+        compiler_params=params(VMEM_LARGE),
         cost_estimate=TINY,
         name="place",
     )(my, *parts)

time: 330 us -> 326 us (0.988)
  Pallas kernels: 142 us -> 108 us
  local copies, waits for them, and re-layouts: 19.1 us -> 36.4 us
  waiting for transfers between devices: 59.5 us -> 66.2 us
  matrix products: 26.5 us -> 30.5 us
    unnamed x130 -> x242, local copies, waits for them, and re-layouts: 8 us -> 24.3 us
    pallas_call x3, Pallas kernels: 22.1 us -> 10.2 us  [norm_grad(): pl.pallas_call(functools.partial(norm_grad_kernel, len(gs), len(after)),...]
    ppermute x42, waiting for transfers between devices: 56.5 us -> 65.5 us  [swap(): lax.ppermute(x, axis, [(i, i ^ bit) for i in range(lax.axis_size(axis))])]
    pallas_call x2, Pallas kernels: 8.84 us -> 2.27 us  [add_norm(): pl.pallas_call(functools.partial(add_norm_kernel, len(xs), after is not N...]
    dot_general x8, matrix products: 24.8 us -> 28.7 us  [dot32(): return lax.dot_general(a, b, dims, preferred_element_type=F32)]
  transfers between devices with their start and end apart: 46 -> 46, of which waited for: 19 -> 20; matrix products, arithmetic and copies ran while one was open for 17% -> 20% of each run, Pallas kernels for 40% -> 31%
where the time goes in v5:
time: 326 us; the launch traced here: 322 us
  Pallas kernels  108 us (33%)
  waiting for transfers between devices  66.2 us (20%)
  starting transfers between devices  46.7 us (14%)
  local copies, waits for them, and re-layouts  36.4 us (11%)
  matrix products  30.5 us (9%)
  other arithmetic  17.8 us (5%)
  between operations  16.2 us (5%)
    ppermute x42, waiting for transfers between devices, swap(): lax.ppermute(x, axis, [(i, i ^ bit) for i in range(lax.axis_size(axis))])  65.5 us
    ppermute x42, starting transfers between devices, swap(): lax.ppermute(x, axis, [(i, i ^ bit) for i in range(lax.axis_size(axis))])  46.4 us
    dot_general x8, matrix products, dot32(): return lax.dot_general(a, b, dims, preferred_element_type=F32)  28.7 us
    unnamed x242, local copies, waits for them, and re-layouts  24.3 us
    pallas_call x5, Pallas kernels, slabs(): pl.pallas_call(functools.partial(slab_kernel, kind, later, len(xs), len(g...  20.3 us
    pallas_call x5, Pallas kernels, totals(): pl.pallas_call(functools.partial(total_kernel, plan), grid=(steps,), in_s...  17.8 us
    pallas_call x1, Pallas kernels, self_backward(): pl.pallas_call(functools.partial(self_backward_kernel, blocks, kv_local),...  16.8 us
    pallas_call x1, Pallas kernels, self_forward(): pl.pallas_call(functools.partial(self_forward_kernel, blocks, kv_local),...  10.6 us
  transfers between devices with their start and end apart: 46, of which 20 were waited for; matrix products, arithmetic and copies ran while one was open for 20% of the time, Pallas kernels for 31%

profile of v5, /device:TPU:0, one launch (start us, length us, event | category | flops | bytes accessed | tf_op | source)
XLA Modules:
  0.0 321.7 jit_solution(5654029773211046748)
XLA Ops:
  7.3 3.0 collective-permute-start
  11.8 2.9 constant_dynamic-slice_fusion.11
  23.9 6.0 %fusion.28 = f32[256,2816]{1,0:T(8,128)} fusion(bf16[2816,1024]{1,0:T(8,128)(2,1)} %param.41, bf16[1,256,1024]{2,1,0:T(8,128)(2,1)S(1)} %copy-done.30), kind=kOutput, calls=%fused_computation.87 | convolution fusion | flops 1476395008 | bytes 9175040 | tf_op jit(solution)/shard_map/dot_general | solution.py:29
  29.9 5.3 %collective-permute-done.1.refs_2_ = bf16[256,1024]{1,0:T(8,128)(2,1)} collective-permute-done((bf16[256,1024]{1,0:T(8,128)(2,1)}, bf16[256,1024]{1,0:T(8,128)(2,1)}, u32[]{:S(2)}, u32[]{:S(2)}) %collective-permute-start.1) | collective-permute-done | bytes 524320 | tf_op jit(solution)/shard_map/ppermute | solution.py:33
  40.7 2.8 norm_dot.1
  44.8 10.6 %self_forward.1 = (bf16[256,256]{1,0:T(8,128)(2,1)S(1)}, bf16[256,256]{1,0:T(8,128)(2,1)S(1)}, bf16[256,256]{1,0:T(8,128)(2,1)S(1)}, bf16[256,256]{1,0:T(8,128)(2,1)S(1)}, f32[4,2,1,512]{3,2,1,0:T(1,128)S(1)}) custom-call(s32[1]{0:T(128)} %bitcast.6.my_ref, bf16[1024,512]{1,0:T(8,128)(2,1)S(1)} %get-tuple-element.212.qkv_ref, f32[4,1280]{1,0:T(4,128)S(1)} %concatenate.28.bias_ref), custom_call_target="tpu_custom_call" | custom-call | flops 1 | bytes 1 | tf_op jit(solution)/shard_map/self_forward/pallas_call | solution.py:309
  70.1 6.3 %cross_forward.1 = (bf16[256,1024]{1,0:T(8,128)(2,1)S(1)}, f32[8,1,512]{2,1,0:T(1,128)S(1)}) custom-call(f32[512,1]{1,0:T(8,128)S(1)} %copy.46.allow_ref, bf16[256,1024]{1,0:T(8,128)(2,1)S(1)} %get-tuple-element.226.q_ref, bf16[512,512]{1,0:T(8,128)(2,1)S(1)} %convolution_convert_fusion.1.k_ref, bf16[512,512]{1,0:T(8,128)(2,1)S(1)} %convolution_convert_fusion.v_ref), custom_call_target="tpu_custom_call" | custom-call | flops 1 | bytes 1 | tf_op jit(solution)/shard_map/cross_forward/pallas_call | solution.py:368
  79.9 4.5 %fusion.32 = f32[256,2816]{1,0:T(8,128)S(1)} fusion(bf16[256,1024]{1,0:T(8,128)(2,1)} %copy-done.55, bf16[1024,2816]{1,0:T(8,128)(2,1)} %refs_3_.1), kind=kOutput, calls=%fused_computation.91 | convolution fusion | flops 1476395008 | bytes 9175040 | tf_op jit(solution)/shard_map/dot_general | solution.py:29
  84.5 4.6 %fusion.33 = f32[256,2816]{1,0:T(8,128)S(1)} fusion(bf16[256,1024]{1,0:T(8,128)(2,1)S(1)} %copy-done.56, bf16[1024,2816]{1,0:T(8,128)(2,1)} %refs_2_.1), kind=kOutput, calls=%fused_computation.92 | convolution fusion | flops 1476395008 | bytes 9175040 | tf_op jit(solution)/shard_map/dot_general | solution.py:29
  89.1 3.8 %multiply_convert_fusion = (bf16[256,2816]{1,0:T(8,128)(2,1)S(1)}, bf16[256,2816]{1,0:T(8,128)(2,1)S(1)}, bf16[256,2816]{1,0:T(8,128)(2,1)S(1)}) fusion(f32[256,2816]{1,0:T(8,128)S(1)} %fusion.32, f32[256,2816]{1,0:T(8,128)S(1)} %fusion.33, f32[256,2816]{1,0:T(8,128)S(1)} %copy-done.100), kind=kLoop, calls=%fused_computation.15 | loop fusion | flops 25231360 | bytes 12976128 | tf_op jit(solution)/shard_map/convert_element_type | solution.py:970
  98.1 5.9 %norm_grad.3 = (f32[256,1024]{1,0:T(8,128)S(1)}, bf16[256,1024]{1,0:T(8,128)(2,1)S(1)}, f32[1,1024]{1,0:T(1,128)S(1)}, bf16[256,1024]{1,0:T(8,128)(2,1)S(1)}) custom-call(bf16[256,2816]{1,0:T(8,128)(2,1)S(1)} %get-tuple-element.411.refs_0_, bf16[256,2816]{1,0:T(8,128)(2,1)S(1)} %get-tuple-element.412.refs_1_, bf16[1024,2816]{1,0:T(8,128)(2,1)S(1)} %bitcast.61, ...), custom_call_target="tpu_custom_call" | custom-call | flops 1 | bytes 1 | tf_op jit(solution)/shard_map/norm_grad/pallas_call | solution.py:697
  107.2 3.9 %slabs.5 = (bf16[16,256,512]{2,1,0:T(8,128)(2,1)}, bf16[16,256,512]{2,1,0:T(8,128)(2,1)}) custom-call(s32[3,32]{1,0:T(4,128)} %get-tuple-element.441.order_ref, bf16[256,1024]{1,0:T(8,128)(2,1)} %copy-done.40, bf16[256,1024]{1,0:T(8,128)(2,1)} %copy-done.57), custom_call_target="tpu_custom_call" | custom-call | flops 1 | bytes 1 | tf_op jit(solution)/shard_map/slabs/pallas_call | solution.py:467
  111.1 5.5 %fusion.4 = bf16[256,1024]{1,0:T(8,128)(2,1)} fusion(f32[256,1024]{1,0:T(8,128)} %copy-done.44, bf16[256,2816]{1,0:T(8,128)(2,1)S(1)} %get-tuple-element.237.x_ref, bf16[2816,1024]{1,0:T(8,128)(2,1)} %param.41), kind=kOutput, calls=%fused_computation.20 | convolution fusion | flops 1476919296 | bytes 8781824 | tf_op jit(solution)/shard_map/dot_general | solution.py:29
  116.7 4.8 %collective-permute-done.9.refs_1_ = bf16[256,1408]{1,0:T(8,128)(2,1)} collective-permute-done((bf16[256,1408]{1,0:T(8,128)(2,1)}, bf16[256,1408]{1,0:T(8,128)(2,1)}, u32[]{:S(2)}, u32[]{:S(2)}) %collective-permute-start.9) | collective-permute-done | bytes 720928 | tf_op jit(solution)/shard_map/ppermute | solution.py:33
  125.0 8.0 %cross_backward.1 = (bf16[256,1024]{1,0:T(8,128)(2,1)S(1)}, bf16[2,512,512]{2,1,0:T(8,128)(2,1)S(1)}) custom-call(f32[512,1]{1,0:T(8,128)S(1)} %copy.46.allow_ref, bf16[256,1024]{1,0:T(8,128)(2,1)S(1)} %copy-done.38, bf16[512,512]{1,0:T(8,128)(2,1)S(1)} %copy-done.34, bf16[512,512]{1,0:T(8,128)(2,1)S(1)} %copy-done.36, ...), custom_call_target="tpu_custom_call" | custom-call | flops 1 | bytes 1 | tf_op jit(solution)/shard_map/cross_backward/pallas_call | solution.py:393
  134.8 3.4 %slabs.6 = (bf16[16,256,512]{2,1,0:T(8,128)(2,1)}, bf16[16,256,512]{2,1,0:T(8,128)(2,1)}) custom-call(s32[3,32]{1,0:T(4,128)} %get-tuple-element.441.order_ref, bf16[256,1024]{1,0:T(8,128)(2,1)} %copy-done.53, bf16[256,1024]{1,0:T(8,128)(2,1)} %copy-done.28, ...), custom_call_target="tpu_custom_call", output_to_operand_aliasing={{0}: (3, {}), {1}: (4, {})} | custom-call | flops 1 | bytes 1 | tf_op jit(solution)/shard_map/slabs/pallas_call | solution.py:467
  138.2 4.7 %slabs.7 = (bf16[16,256,512]{2,1,0:T(8,128)(2,1)}, bf16[16,256,512]{2,1,0:T(8,128)(2,1)}) custom-call(s32[3,32]{1,0:T(4,128)} %get-tuple-element.441.order_ref, bf16[512,1024]{1,0:T(8,128)(2,1)} %constant_dynamic-update-slice_fusion.refs_0_, bf16[2,512,512]{2,1,0:T(8,128)(2,1)} %copy-done.25, ...), custom_call_target="tpu_custom_call", output_to_operand_aliasing={{0}: (3, {}), {1}: (4, {})} | custom-call | flops 1 | bytes 1 | tf_op jit(solution)/shard_map/slabs/pallas_call | solution.py:467
  148.0 3.6 %slabs.8 = (bf16[16,256,512]{2,1,0:T(8,128)(2,1)}, bf16[16,256,512]{2,1,0:T(8,128)(2,1)}) custom-call(s32[3,32]{1,0:T(4,128)} %get-tuple-element.440.order_ref, bf16[256,256]{1,0:T(8,128)(2,1)} %copy-done.42, bf16[256,256]{1,0:T(8,128)(2,1)} %copy-done.50, bf16[256,256]{1,0:T(8,128)(2,1)} %copy-done.51, ...), custom_call_target="tpu_custom_call", output_to_operand_aliasing={{0}: (6, {}), {1}: (7, {})} | custom-call | flops 1 | bytes 1 | tf_op jit(solution)/shard_map/slabs/pallas_call | solution.py:467
  155.2 5.0 %pair_dot.1 = bf16[1024,1408]{1,0:T(8,128)(2,1)S(1)} custom-call(s32[1]{0:T(128)} %bitcast.6.my_ref, bf16[4,256,1024]{2,1,0:T(8,128)(2,1)S(1)} %bitcast.73, bf16[256,1408]{1,0:T(8,128)(2,1)S(1)} %copy-done.27, bf16[256,1408]{1,0:T(8,128)(2,1)} %collective-permute-done.9.refs_1_, bf16[256,1408]{1,0:T(8,128)(2,1)} %collective-permute-done.10.refs_2_, ...), custom_call_target="tpu_custom_call" | custom-call | flops 1 | bytes 1 | tf_op jit(solution)/shard_map/pair_dot/pallas_call | solution.py:590
  164.1 5.2 %totals.5 = (bf16[8,128,512]{2,1,0:T(8,128)(2,1)}, bf16[8,128,512]{2,1,0:T(8,128)(2,1)}) custom-call(bf16[16,256,512]{2,1,0:T(8,128)(2,1)} %get-tuple-element.288.refs_0_.refs_2_.refs_4_, bf16[16,256,512]{2,1,0:T(8,128)(2,1)} %collective-permute-done.15.refs_1_.refs_3_.refs_5_, bf16[16,256,512]{2,1,0:T(8,128)(2,1)} %get-tuple-element.288.refs_0_.refs_2_.refs_4_, ...), custom_call_target="tpu_custom_call" | custom-call | flops 1 | bytes 1 | tf_op jit(solution)/shard_map/totals/pallas_call | solution.py:536
  175.0 16.8 %self_backward.1 = (bf16[256,512]{1,0:T(8,128)(2,1)S(1)}, bf16[256,512]{1,0:T(8,128)(2,1)}, bf16[256,512]{1,0:T(8,128)(2,1)}, bf16[256,512]{1,0:T(8,128)(2,1)S(1)}, f32[4,1280]{1,0:T(4,128)S(1)}) custom-call(s32[1]{0:T(128)} %bitcast.6.my_ref, bf16[1024,512]{1,0:T(8,128)(2,1)S(1)} %copy-done.19, f32[4,1280]{1,0:T(4,128)S(1)} %copy-done.65, ...), custom_call_target="tpu_custom_call" | custom-call | flops 1 | bytes 1 | tf_op jit(solution)/shard_map/self_backward/pallas_call | solution.py:338
  197.0 4.1 %totals.6 = (bf16[4,128,512]{2,1,0:T(8,128)(2,1)}, bf16[4,128,512]{2,1,0:T(8,128)(2,1)}) custom-call(bf16[16,256,512]{2,1,0:T(8,128)(2,1)} %get-tuple-element.288.refs_0_.refs_2_.refs_4_, bf16[16,256,512]{2,1,0:T(8,128)(2,1)} %collective-permute-done.15.refs_1_.refs_3_.refs_5_, bf16[8,128,512]{2,1,0:T(8,128)(2,1)} %copy-done.95, ...), custom_call_target="tpu_custom_call" | custom-call | flops 1 | bytes 1 | tf_op jit(solution)/shard_map/totals/pallas_call | solution.py:536
  203.3 7.3 %collective-permute-done.19.refs_2_ = bf16[8,88,256]{2,1,0:T(8,128)(2,1)S(1)} collective-permute-done((bf16[8,88,256]{2,1,0:T(8,128)(2,1)S(1)}, bf16[8,88,256]{2,1,0:T(8,128)(2,1)S(1)}, u32[]{:S(2)}, u32[]{:S(2)}) %collective-permute-start.19) | collective-permute-done | bytes 360480 | tf_op jit(solution)/shard_map/ppermute | solution.py:33
  210.6 4.7 %slabs.9 = (bf16[16,32,512]{2,1,0:T(8,128)(2,1)}, bf16[16,32,512]{2,1,0:T(8,128)(2,1)}, f32[1024,1]{1,0:T(8,128)}) custom-call(s32[3,32]{1,0:T(4,128)} %get-tuple-element.441.order_ref, bf16[1024,1024]{1,0:T(8,128)(2,1)} %copy-done.39, bf16[256,512]{1,0:T(8,128)(2,1)} %copy-done.48, bf16[256,512]{1,0:T(8,128)(2,1)} %get-tuple-element.357.refs_2_, ...), custom_call_target="tpu_custom_call" | custom-call | flops 1 | bytes 1 | tf_op jit(solution)/shard_map/slabs/pallas_call | solution.py:467
  218.4 3.3 %totals.7 = (bf16[4,32,512]{2,1,0:T(8,128)(2,1)}, bf16[4,32,512]{2,1,0:T(8,128)(2,1)}, bf16[4,32,512]{2,1,0:T(8,128)(2,1)}, bf16[4,32,512]{2,1,0:T(8,128)(2,1)}) custom-call(bf16[4,128,512]{2,1,0:T(8,128)(2,1)} %bitcast.86, bf16[4,128,512]{2,1,0:T(8,128)(2,1)} %bitcast.90, bf16[4,128,512]{2,1,0:T(8,128)(2,1)} %bitcast.87, bf16[4,128,512]{2,1,0:T(8,128)(2,1)} %bitcast.91, ...), custom_call_target="tpu_custom_call" | custom-call | flops 1 | bytes 1 | tf_op jit(solution)/shard_map/totals/pallas_call | solution.py:536
  225.2 2.8 turned_dot.1
  231.3 2.8 collective-permute-done.24.refs_7_
  234.1 2.7 collective-permute-done.26.refs_9_
  238.0 2.8 totals.8
  245.7 9.4 %collective-permute-done.31 = bf16[2,2,128,512]{3,2,1,0:T(8,128)(2,1)} collective-permute-done((bf16[2,2,128,512]{3,2,1,0:T(8,128)(2,1)}, bf16[2,2,128,512]{3,2,1,0:T(8,128)(2,1)}, u32[]{:S(2)}, u32[]{:S(2)}) %collective-permute-start.31) | collective-permute-done | bytes 524320 | tf_op jit(solution)/shard_map/ppermute | solution.py:33
  267.6 8.4 %collective-permute-done.27.refs_10_ = bf16[2,384,512]{2,1,0:T(8,128)(2,1)S(1)} collective-permute-done((bf16[2,384,512]{2,1,0:T(8,128)(2,1)}, bf16[2,384,512]{2,1,0:T(8,128)(2,1)S(1)}, u32[]{:S(2)}, u32[]{:S(2)}) %collective-permute-start.27) | collective-permute-done | bytes 786464 | tf_op jit(solution)/shard_map/ppermute | solution.py:33
  300.8 10.3 %collective-permute-done.39.refs_11_ = bf16[1,384,512]{2,1,0:T(8,128)(2,1)} collective-permute-done((bf16[1,384,512]{2,1,0:T(8,128)(2,1)}, bf16[1,384,512]{2,1,0:T(8,128)(2,1)}, u32[]{:S(2)}, u32[]{:S(2)}) %collective-permute-start.39) | collective-permute-done | bytes 393248 | tf_op jit(solution)/shard_map/ppermute | solution.py:33
  (381 shorter events, 130.5 us)
Async XLA Ops:
  7.2 72.6 %all-gather.3.cloned.1.call-start = ((), (), s32[]{:S(2)}) async-start(), calls=%async_computation.2 | async-start | bytes 2621440 | tf_op jit(solution)/shard_map/all_gather | solution.py:944
  7.3 22.6 %collective-permute-start = (bf16[256,1024]{1,0:T(8,128)(2,1)}, bf16[256,1024]{1,0:T(8,128)(2,1)}, u32[]{:S(2)}, u32[]{:S(2)}) collective-permute-start(bf16[256,1024]{1,0:T(8,128)(2,1)} %bitcast.62), channel_id=1, source_target_pairs={{0,1},{1,0},{2,3},{3,2},{4,5},{5,4},{6,7},{7,6},{8,9},{9,8},{10,11... | collective-permute-start | bytes 1572872 | tf_op jit(solution)/shard_map/ppermute | solution.py:33
  10.3 24.9 %collective-permute-start.1 = (bf16[256,1024]{1,0:T(8,128)(2,1)}, bf16[256,1024]{1,0:T(8,128)(2,1)}, u32[]{:S(2)}, u32[]{:S(2)}) collective-permute-start(bf16[256,1024]{1,0:T(8,128)(2,1)} %bitcast.63), channel_id=1, source_target_pairs={{0,2},{1,3},{2,0},{3,1},{4,6},{5,7},{6,4},{7,5},{8,10},{9,11},{10,... | collective-permute-start | bytes 1572872 | tf_op jit(solution)/shard_map/ppermute | solution.py:33
  11.8 23.4 %collective-permute-start.2 = (bf16[256,1024]{1,0:T(8,128)(2,1)}, bf16[256,1024]{1,0:T(8,128)(2,1)}, u32[]{:S(2)}, u32[]{:S(2)}) collective-permute-start(bf16[256,1024]{1,0:T(8,128)(2,1)} %bitcast.64), channel_id=1, source_target_pairs={{0,3},{1,2},{2,1},{3,0},{4,7},{5,6},{6,5},{7,4},{8,11},{9,10},{10,... | collective-permute-start | bytes 1572872 | tf_op jit(solution)/shard_map/ppermute | solution.py:33
  35.2 88.4 %all-gather.5.cloned.1.call-start = ((), (), s32[]{:S(2)}) async-start(), calls=%async_computation.3 | async-start | bytes 2621440 | tf_op jit(solution)/shard_map/all_gather | solution.py:981
  35.5 23.3 %collective-permute-start.6 = (bf16[128,1024]{1,0:T(8,128)(2,1)}, bf16[128,1024]{1,0:T(8,128)(2,1)S(1)}, u32[]{:S(2)}, u32[]{:S(2)}) collective-permute-start(bf16[128,1024]{1,0:T(8,128)(2,1)} %bitcast.1), channel_id=1, source_target_pairs={{0,1},{1,0},{2,3},{3,2},{4,5},{5,4},{6,7},{7,6},{8,9},{9,8},{10,11... | collective-permute-start | bytes 786440 | tf_op jit(solution)/shard_map/ppermute | solution.py:33
  36.8 24.1 %collective-permute-start.7 = (bf16[128,1024]{1,0:T(8,128)(2,1)}, bf16[128,1024]{1,0:T(8,128)(2,1)S(1)}, u32[]{:S(2)}, u32[]{:S(2)}) collective-permute-start(bf16[128,1024]{1,0:T(8,128)(2,1)} %bitcast.1), channel_id=1, source_target_pairs={{0,2},{1,3},{2,0},{3,1},{4,6},{5,7},{6,4},{7,5},{8,10},{9,11},{10,... | collective-permute-start | bytes 786440 | tf_op jit(solution)/shard_map/ppermute | solution.py:33
  37.6 24.0 %collective-permute-start.8 = (bf16[128,1024]{1,0:T(8,128)(2,1)}, bf16[128,1024]{1,0:T(8,128)(2,1)}, u32[]{:S(2)}, u32[]{:S(2)}) collective-permute-start(bf16[128,1024]{1,0:T(8,128)(2,1)} %bitcast.1), channel_id=1, source_target_pairs={{0,3},{1,2},{2,1},{3,0},{4,7},{5,6},{6,5},{7,4},{8,11},{9,10},{10,... | collective-permute-start | bytes 786440 | tf_op jit(solution)/shard_map/ppermute | solution.py:33
  56.6 11.0 %collective-permute-start.3 = (bf16[256,256]{1,0:T(8,128)(2,1)S(1)}, bf16[256,256]{1,0:T(8,128)(2,1)S(1)}, u32[]{:S(2)}, u32[]{:S(2)}) collective-permute-start(bf16[256,256]{1,0:T(8,128)(2,1)S(1)} %get-tuple-element.215.refs_1_), channel_id=1, source_target_pairs={{0,1},{1,0},{2,3},{3,2},{4,5},{5,4},{6,7},{7,6},{8,9},{9,8},{10,11... | collective-permute-start | bytes 393224 | tf_op jit(solution)/shard_map/ppermute | solution.py:33
  79.9 157.0 %reduce-scatter.3.cloned.1.call-start = ((), (), s32[]{:S(2)}) async-start(), calls=%async_computation.4 | async-start | bytes 3244032 | tf_op jit(solution)/shard_map/reduce_scatter | solution.py:1022
  95.4 26.1 %collective-permute-start.9 = (bf16[256,1408]{1,0:T(8,128)(2,1)}, bf16[256,1408]{1,0:T(8,128)(2,1)}, u32[]{:S(2)}, u32[]{:S(2)}) collective-permute-start(bf16[256,1408]{1,0:T(8,128)(2,1)} %get-tuple-element.234), channel_id=1, source_target_pairs={{0,1},{1,0},{2,3},{3,2},{4,5},{5,4},{6,7},{7,6},{8,9},{9,8},{10,11... | collective-permute-start | bytes 2162696 | tf_op jit(solution)/shard_map/ppermute | solution.py:33
  96.5 26.5 %collective-permute-start.10 = (bf16[256,1408]{1,0:T(8,128)(2,1)}, bf16[256,1408]{1,0:T(8,128)(2,1)}, u32[]{:S(2)}, u32[]{:S(2)}) collective-permute-start(bf16[256,1408]{1,0:T(8,128)(2,1)} %get-tuple-element.235), channel_id=1, source_target_pairs={{0,2},{1,3},{2,0},{3,1},{4,6},{5,7},{6,4},{7,5},{8,10},{9,11},{10,... | collective-permute-start | bytes 2162696 | tf_op jit(solution)/shard_map/ppermute | solution.py:33
  123.7 19.3 %collective-permute-start.11 = (bf16[256,1408]{1,0:T(8,128)(2,1)}, bf16[256,1408]{1,0:T(8,128)(2,1)}, u32[]{:S(2)}, u32[]{:S(2)}) collective-permute-start(bf16[256,1408]{1,0:T(8,128)(2,1)} %get-tuple-element.254), channel_id=1, source_target_pairs={{0,3},{1,2},{2,1},{3,0},{4,7},{5,6},{6,5},{7,4},{8,11},{9,10},{10,... | collective-permute-start | bytes 2162696 | tf_op jit(solution)/shard_map/ppermute | solution.py:33
  151.6 12.4 %collective-permute-start.15 = (bf16[16,256,512]{2,1,0:T(8,128)(2,1)}, bf16[16,256,512]{2,1,0:T(8,128)(2,1)}, u32[]{:S(2)}, u32[]{:S(2)}) collective-permute-start(bf16[16,256,512]{2,1,0:T(8,128)(2,1)} %get-tuple-element.289), channel_id=1, source_target_pairs={{0,4},{4,0},{8,12},{12,8},{16,20},{20,16},{24,28},{28,24},{1,5},{5... | collective-permute-start | bytes 12582920 | tf_op jit(solution)/shard_map/ppermute | solution.py:33
  163.9 135.2 %reduce-scatter.5.cloned.1.call-start = ((), (), s32[]{:S(2)}) async-start(), calls=%async_computation.5 | async-start | bytes 1622016 | tf_op jit(solution)/shard_map/reduce_scatter | solution.py:1046
  169.3 26.3 %collective-permute-start.16 = (bf16[8,128,512]{2,1,0:T(8,128)(2,1)}, bf16[8,128,512]{2,1,0:T(8,128)(2,1)S(1)}, u32[]{:S(2)}, u32[]{:S(2)}) collective-permute-start(bf16[8,128,512]{2,1,0:T(8,128)(2,1)} %get-tuple-element.300), channel_id=1, source_target_pairs={{0,1},{1,0},{2,3},{3,2},{4,5},{5,4},{6,7},{7,6},{8,9},{9,8},{10,11... | collective-permute-start | bytes 3145736 | tf_op jit(solution)/shard_map/ppermute | solution.py:33
  170.6 26.4 %collective-permute-start.17 = (bf16[8,128,512]{2,1,0:T(8,128)(2,1)}, bf16[8,128,512]{2,1,0:T(8,128)(2,1)}, u32[]{:S(2)}, u32[]{:S(2)}) collective-permute-start(bf16[8,128,512]{2,1,0:T(8,128)(2,1)} %get-tuple-element.301), channel_id=1, source_target_pairs={{0,2},{1,3},{2,0},{3,1},{4,6},{5,7},{6,4},{7,5},{8,10},{9,11},{10,... | collective-permute-start | bytes 3145736 | tf_op jit(solution)/shard_map/ppermute | solution.py:33
  171.5 31.8 %collective-permute-start.18 = (bf16[8,88,256]{2,1,0:T(8,128)(2,1)S(1)}, bf16[8,88,256]{2,1,0:T(8,128)(2,1)S(1)}, u32[]{:S(2)}, u32[]{:S(2)}) collective-permute-start(bf16[8,88,256]{2,1,0:T(8,128)(2,1)S(1)} %copy-done.90), channel_id=1, source_target_pairs={{0,1},{1,0},{2,3},{3,2},{4,5},{5,4},{6,7},{7,6},{8,9},{9,8},{10,11... | collective-permute-start | bytes 1081352 | tf_op jit(solution)/shard_map/ppermute | solution.py:33
  172.7 37.9 %collective-permute-start.19 = (bf16[8,88,256]{2,1,0:T(8,128)(2,1)S(1)}, bf16[8,88,256]{2,1,0:T(8,128)(2,1)S(1)}, u32[]{:S(2)}, u32[]{:S(2)}) collective-permute-start(bf16[8,88,256]{2,1,0:T(8,128)(2,1)S(1)} %copy-done.88), channel_id=1, source_target_pairs={{0,2},{1,3},{2,0},{3,1},{4,6},{5,7},{6,4},{7,5},{8,10},{9,11},{10,... | collective-permute-start | bytes 1081352 | tf_op jit(solution)/shard_map/ppermute | solution.py:33
  173.3 37.3 %collective-permute-start.20 = (bf16[8,88,256]{2,1,0:T(8,128)(2,1)S(1)}, bf16[8,88,256]{2,1,0:T(8,128)(2,1)S(1)}, u32[]{:S(2)}, u32[]{:S(2)}) collective-permute-start(bf16[8,88,256]{2,1,0:T(8,128)(2,1)S(1)} %copy-done.86), channel_id=1, source_target_pairs={{0,3},{1,2},{2,1},{3,0},{4,7},{5,6},{6,5},{7,4},{8,11},{9,10},{10,... | collective-permute-start | bytes 1081352 | tf_op jit(solution)/shard_map/ppermute | solution.py:33
  215.4 15.0 %collective-permute-start.21 = (bf16[4,128,512]{2,1,0:T(8,128)(2,1)}, bf16[4,128,512]{2,1,0:T(8,128)(2,1)S(1)}, u32[]{:S(2)}, u32[]{:S(2)}) collective-permute-start(bf16[4,128,512]{2,1,0:T(8,128)(2,1)} %get-tuple-element.318), channel_id=1, source_target_pairs={{0,2},{1,3},{2,0},{3,1},{4,6},{5,7},{6,4},{7,5},{8,10},{9,11},{10,... | collective-permute-start | bytes 1572872 | tf_op jit(solution)/shard_map/ppermute | solution.py:33
  216.3 15.0 %collective-permute-start.22 = (bf16[4,128,512]{2,1,0:T(8,128)(2,1)}, bf16[4,128,512]{2,1,0:T(8,128)(2,1)S(1)}, u32[]{:S(2)}, u32[]{:S(2)}) collective-permute-start(bf16[4,128,512]{2,1,0:T(8,128)(2,1)} %get-tuple-element.319), channel_id=1, source_target_pairs={{0,1},{1,0},{2,3},{3,2},{4,5},{5,4},{6,7},{7,6},{8,9},{9,8},{10,11... | collective-permute-start | bytes 1572872 | tf_op jit(solution)/shard_map/ppermute | solution.py:33
  221.7 12.4 %collective-permute-start.24 = (bf16[4,32,512]{2,1,0:T(8,128)(2,1)}, bf16[4,32,512]{2,1,0:T(8,128)(2,1)S(1)}, u32[]{:S(2)}, u32[]{:S(2)}) collective-permute-start(bf16[4,32,512]{2,1,0:T(8,128)(2,1)} %get-tuple-element.323), channel_id=1, source_target_pairs={{0,1},{1,0},{2,3},{3,2},{4,5},{5,4},{6,7},{7,6},{8,9},{9,8},{10,11... | collective-permute-start | bytes 393224 | tf_op jit(solution)/shard_map/ppermute | solution.py:33
  222.4 11.7 %collective-permute-start.25 = (bf16[4,32,512]{2,1,0:T(8,128)(2,1)}, bf16[4,32,512]{2,1,0:T(8,128)(2,1)S(1)}, u32[]{:S(2)}, u32[]{:S(2)}) collective-permute-start(bf16[4,32,512]{2,1,0:T(8,128)(2,1)} %get-tuple-element.324), channel_id=1, source_target_pairs={{0,2},{1,3},{2,0},{3,1},{4,6},{5,7},{6,4},{7,5},{8,10},{9,11},{10,... | collective-permute-start | bytes 393224 | tf_op jit(solution)/shard_map/ppermute | solution.py:33
  223.7 13.1 %collective-permute-start.26 = (bf16[4,32,512]{2,1,0:T(8,128)(2,1)}, bf16[4,32,512]{2,1,0:T(8,128)(2,1)}, u32[]{:S(2)}, u32[]{:S(2)}) collective-permute-start(bf16[4,32,512]{2,1,0:T(8,128)(2,1)} %get-tuple-element.325), channel_id=1, source_target_pairs={{0,3},{1,2},{2,1},{3,0},{4,7},{5,6},{6,5},{7,4},{8,11},{9,10},{10,... | collective-permute-start | bytes 393224 | tf_op jit(solution)/shard_map/ppermute | solution.py:33
  241.6 13.5 %collective-permute-start.31 = (bf16[2,2,128,512]{3,2,1,0:T(8,128)(2,1)}, bf16[2,2,128,512]{3,2,1,0:T(8,128)(2,1)}, u32[]{:S(2)}, u32[]{:S(2)}) collective-permute-start(bf16[2,2,128,512]{3,2,1,0:T(8,128)(2,1)} %slice.55), channel_id=1, source_target_pairs={{0,2},{1,3},{2,0},{3,1},{4,6},{5,7},{6,4},{7,5},{8,10},{9,11},{10,... | collective-permute-start | bytes 1572872 | tf_op jit(solution)/shard_map/ppermute | solution.py:33
  242.8 33.2 %collective-permute-start.27 = (bf16[2,384,512]{2,1,0:T(8,128)(2,1)}, bf16[2,384,512]{2,1,0:T(8,128)(2,1)S(1)}, u32[]{:S(2)}, u32[]{:S(2)}) collective-permute-start(bf16[2,384,512]{2,1,0:T(8,128)(2,1)} %totals.8), channel_id=1, source_target_pairs={{0,8},{4,12},{8,0},{12,4},{16,24},{20,28},{24,16},{28,20},{1,9},{5... | collective-permute-start | bytes 2359304 | tf_op jit(solution)/shard_map/ppermute | solution.py:33
  244.4 12.8 %collective-permute-start.29 = (f32[28,128]{1,0:T(8,128)S(1)}, f32[28,128]{1,0:T(8,128)S(1)}, u32[]{:S(2)}, u32[]{:S(2)}) collective-permute-start(f32[28,128]{1,0:T(8,128)S(1)} %fusion.30), channel_id=1, source_target_pairs={{0,1},{1,0},{2,3},{3,2},{4,5},{5,4},{6,7},{7,6},{8,9},{9,8},{10,11... | collective-permute-start | bytes 43016 | tf_op jit(solution)/shard_map/ppermute | solution.py:33
  279.3 17.1 %collective-permute-start.36 = (bf16[256,512]{1,0:T(8,128)(2,1)}, bf16[256,512]{1,0:T(8,128)(2,1)S(1)}, u32[]{:S(2)}, u32[]{:S(2)}) collective-permute-start(bf16[256,512]{1,0:T(8,128)(2,1)} %get-tuple-element.357.refs_2_), channel_id=1, source_target_pairs={{0,1},{1,0},{2,3},{3,2},{4,5},{5,4},{6,7},{7,6},{8,9},{9,8},{10,11... | collective-permute-start | bytes 786440 | tf_op jit(solution)/shard_map/ppermute | solution.py:33
  280.9 15.5 %collective-permute-start.37 = (bf16[256,512]{1,0:T(8,128)(2,1)}, bf16[256,512]{1,0:T(8,128)(2,1)S(1)}, u32[]{:S(2)}, u32[]{:S(2)}) collective-permute-start(bf16[256,512]{1,0:T(8,128)(2,1)} %get-tuple-element.358.refs_3_), channel_id=1, source_target_pairs={{0,2},{1,3},{2,0},{3,1},{4,6},{5,7},{6,4},{7,5},{8,10},{9,11},{10,... | collective-permute-start | bytes 786440 | tf_op jit(solution)/shard_map/ppermute | solution.py:33
  281.5 14.8 %collective-permute-start.38 = (bf16[256,512]{1,0:T(8,128)(2,1)S(1)}, bf16[256,512]{1,0:T(8,128)(2,1)S(1)}, u32[]{:S(2)}, u32[]{:S(2)}) collective-permute-start(bf16[256,512]{1,0:T(8,128)(2,1)S(1)} %copy-done.63), channel_id=1, source_target_pairs={{0,3},{1,2},{2,1},{3,0},{4,7},{5,6},{6,5},{7,4},{8,11},{9,10},{10,... | collective-permute-start | bytes 786440 | tf_op jit(solution)/shard_map/ppermute | solution.py:33
  292.7 18.4 %collective-permute-start.39 = (bf16[1,384,512]{2,1,0:T(8,128)(2,1)}, bf16[1,384,512]{2,1,0:T(8,128)(2,1)}, u32[]{:S(2)}, u32[]{:S(2)}) collective-permute-start(bf16[1,384,512]{2,1,0:T(8,128)(2,1)} %totals.9), channel_id=1, source_target_pairs={{0,16},{4,20},{8,24},{12,28},{16,0},{20,4},{24,8},{28,12},{1,17},{... | collective-permute-start | bytes 1179656 | tf_op jit(solution)/shard_map/ppermute | solution.py:33
  (133 other events, 1035.4 us)
Sparse Core Ops, SparseCore 0:
  35.3 40.4 all-gather.2
  80.0 43.6 all-gather.4
  164.0 39.0 reduce-scatter.2
  237.0 39.4 reduce-scatter.4

commit v6 on v5

--- a/solution.py
+++ b/solution.py
@@ -1016,8 +1016,8 @@
         share_far, held, self_late = tie(share_far, held, self_grad)
         wide = pair_dot(my_ref, ffn_all, [shares[0]] + shares_near + [share_far])
         keep, send = slabs(turned, mixes, self_late, total, 3 * d_slabs * small, 0, held)
-        grad_got, wide, keep, hidden_parts = tie(grad_got, wide, keep, hidden_parts)
         got = swap(send, "dp", 1)
+        grad_got, wide, keep, hidden_parts, got = tie(grad_got, wide, keep, hidden_parts, got)
         hidden_got = trade(hidden_parts, "blk", 1)
         wide = lax.psum_scatter(wide, "dp", scatter_dimension=0, tiled=True)
         cross = Halves(keep, got, [(0, total // 2)], [(total // 2, total)])
@@ -1031,8 +1031,11 @@
         qkv_parts, mem_part, cross.got = tie(qkv_parts, mem_part, cross.got)
         cross.arrive()
         cross.pack()
-        qkv_parts, cross.out, hidden_got = tie(qkv_parts, cross.out, hidden_got)
+        qkv_parts, cross.out, hidden_got, wide = tie(qkv_parts, cross.out, hidden_got, wide)
         cross.hop((2, 1))
+        down = turned_dot(my_ref, [hidden_parts[0]] + hidden_got, top_all)
+        qkv_parts, down = tie(qkv_parts, down)
+        down = lax.psum_scatter(down, "dp", scatter_dimension=0, tiled=True)
         own = own_q + 2 * own_kv
         keep, send, gain_part = slabs(order, self_all, qkv_parts, small, 0, 0, None, 2, own, turned_qkv[0])
         gain_part = gain_part[:, 0]
@@ -1041,9 +1044,7 @@
         sides = [(keep.reshape(view), cover((0, view[1]))), (got.reshape(view), cover((0, view[1])))]
         sides = totals(sides, [(0, cross.chunks, [(j * small, (j + 1) * small)]) for j in range(blocks)], 1)
         sides = [sides[0]] + trade(sides, "blk", 1)
-        down = turned_dot(my_ref, [hidden_parts[0]] + hidden_got, top_all)
-        gain_part, cross.got, sides, wide, down = tie(gain_part, cross.got, sides, wide, down)
-        down = lax.psum_scatter(down, "dp", scatter_dimension=0, tiled=True)
+        gain_part, cross.got, sides = tie(gain_part, cross.got, sides)
         cross.arrive()
         cross.join([(side, cover((total + j * small, total + (j + 1) * small))) for j, side in enumerate(sides)], total + view[1])
         cross.pack(True)

time: 326 us -> 318 us (0.975)
  waiting for transfers between devices: 66.2 us -> 53.8 us
  local copies, waits for them, and re-layouts: 36.4 us -> 40.8 us
  other arithmetic: 17.8 us -> 14.1 us
  starting transfers between devices: 46.7 us -> 50.2 us
    ppermute x42, waiting for transfers between devices: 65.5 us -> 53.1 us  [swap(): lax.ppermute(x, axis, [(i, i ^ bit) for i in range(lax.axis_size(axis))])]
    unnamed x242 -> x248, local copies, waits for them, and re-layouts: 24.3 us -> 29.4 us
    ppermute x42, starting transfers between devices: 46.4 us -> 49.9 us  [swap(): lax.ppermute(x, axis, [(i, i ^ bit) for i in range(lax.axis_size(axis))])]
  transfers between devices with their start and end apart: 46 -> 46, of which waited for: 20 -> 20; matrix products, arithmetic and copies ran while one was open for 20% -> 19% of each run, Pallas kernels for 31% -> 30%
where the time goes in v6:
time: 318 us; the launch traced here: 314 us
  Pallas kernels  108 us (34%)
  waiting for transfers between devices  53.8 us (17%)
  starting transfers between devices  50.2 us (16%)
  local copies, waits for them, and re-layouts  40.8 us (13%)
  matrix products  30.4 us (10%)
  between operations  16.1 us (5%)
  other arithmetic  14.1 us (4%)
    ppermute x42, waiting for transfers between devices, swap(): lax.ppermute(x, axis, [(i, i ^ bit) for i in range(lax.axis_size(axis))])  53.1 us
    ppermute x42, starting transfers between devices, swap(): lax.ppermute(x, axis, [(i, i ^ bit) for i in range(lax.axis_size(axis))])  49.9 us
    unnamed x248, local copies, waits for them, and re-layouts  29.4 us
    dot_general x8, matrix products, dot32(): return lax.dot_general(a, b, dims, preferred_element_type=F32)  28.7 us
    pallas_call x5, Pallas kernels, slabs(): pl.pallas_call(functools.partial(slab_kernel, kind, later, len(xs), len(g...  20.6 us
    pallas_call x5, Pallas kernels, totals(): pl.pallas_call(functools.partial(total_kernel, plan), grid=(steps,), in_s...  18 us
    pallas_call x1, Pallas kernels, self_backward(): pl.pallas_call(functools.partial(self_backward_kernel, blocks, kv_local),...  16.8 us
    pallas_call x1, Pallas kernels, self_forward(): pl.pallas_call(functools.partial(self_forward_kernel, blocks, kv_local),...  10.6 us
  transfers between devices with their start and end apart: 46, of which 20 were waited for; matrix products, arithmetic and copies ran while one was open for 19% of the time, Pallas kernels for 30%

profile of v6, /device:TPU:0, one launch (start us, length us, event | category | flops | bytes accessed | tf_op | source)
XLA Modules:
  0.0 313.9 jit_solution(14182928109122714283)
XLA Ops:
  7.3 3.0 collective-permute-start
  11.8 2.9 constant_dynamic-slice_fusion.11
  23.9 6.0 %fusion.28 = f32[256,2816]{1,0:T(8,128)} fusion(bf16[2816,1024]{1,0:T(8,128)(2,1)} %param.41, bf16[1,256,1024]{2,1,0:T(8,128)(2,1)S(1)} %copy-done.30), kind=kOutput, calls=%fused_computation.87 | convolution fusion | flops 1476395008 | bytes 9175040 | tf_op jit(solution)/shard_map/dot_general | solution.py:29
  29.9 5.3 %collective-permute-done.1.refs_2_ = bf16[256,1024]{1,0:T(8,128)(2,1)} collective-permute-done((bf16[256,1024]{1,0:T(8,128)(2,1)}, bf16[256,1024]{1,0:T(8,128)(2,1)}, u32[]{:S(2)}, u32[]{:S(2)}) %collective-permute-start.1) | collective-permute-done | bytes 524320 | tf_op jit(solution)/shard_map/ppermute | solution.py:33
  40.7 2.8 norm_dot.1
  44.8 10.6 %self_forward.1 = (bf16[256,256]{1,0:T(8,128)(2,1)S(1)}, bf16[256,256]{1,0:T(8,128)(2,1)S(1)}, bf16[256,256]{1,0:T(8,128)(2,1)S(1)}, bf16[256,256]{1,0:T(8,128)(2,1)S(1)}, f32[4,2,1,512]{3,2,1,0:T(1,128)S(1)}) custom-call(s32[1]{0:T(128)} %bitcast.6.my_ref, bf16[1024,512]{1,0:T(8,128)(2,1)S(1)} %get-tuple-element.217.qkv_ref, f32[4,1280]{1,0:T(4,128)S(1)} %concatenate.28.bias_ref), custom_call_target="tpu_custom_call" | custom-call | flops 1 | bytes 1 | tf_op jit(solution)/shard_map/self_forward/pallas_call | solution.py:309
  70.1 6.3 %cross_forward.1 = (bf16[256,1024]{1,0:T(8,128)(2,1)S(1)}, f32[8,1,512]{2,1,0:T(1,128)S(1)}) custom-call(f32[512,1]{1,0:T(8,128)S(1)} %copy.46.allow_ref, bf16[256,1024]{1,0:T(8,128)(2,1)S(1)} %get-tuple-element.231.q_ref, bf16[512,512]{1,0:T(8,128)(2,1)S(1)} %convolution_convert_fusion.1.k_ref, bf16[512,512]{1,0:T(8,128)(2,1)S(1)} %convolution_convert_fusion.v_ref), custom_call_target="tpu_custom_call" | custom-call | flops 1 | bytes 1 | tf_op jit(solution)/shard_map/cross_forward/pallas_call | solution.py:368
  80.0 4.5 %fusion.32 = f32[256,2816]{1,0:T(8,128)S(1)} fusion(bf16[256,1024]{1,0:T(8,128)(2,1)} %copy-done.57, bf16[1024,2816]{1,0:T(8,128)(2,1)} %refs_3_.1), kind=kOutput, calls=%fused_computation.91 | convolution fusion | flops 1476395008 | bytes 9175040 | tf_op jit(solution)/shard_map/dot_general | solution.py:29
  84.5 4.6 %fusion.33 = f32[256,2816]{1,0:T(8,128)S(1)} fusion(bf16[256,1024]{1,0:T(8,128)(2,1)S(1)} %copy-done.58, bf16[1024,2816]{1,0:T(8,128)(2,1)} %refs_2_.1), kind=kOutput, calls=%fused_computation.92 | convolution fusion | flops 1476395008 | bytes 9175040 | tf_op jit(solution)/shard_map/dot_general | solution.py:29
  89.1 3.8 %multiply_convert_fusion = (bf16[256,2816]{1,0:T(8,128)(2,1)S(1)}, bf16[256,2816]{1,0:T(8,128)(2,1)S(1)}, bf16[256,2816]{1,0:T(8,128)(2,1)S(1)}) fusion(f32[256,2816]{1,0:T(8,128)S(1)} %fusion.32, f32[256,2816]{1,0:T(8,128)S(1)} %fusion.33, f32[256,2816]{1,0:T(8,128)S(1)} %copy-done.101), kind=kLoop, calls=%fused_computation.15 | loop fusion | flops 25231360 | bytes 12976128 | tf_op jit(solution)/shard_map/convert_element_type | solution.py:970
  98.1 5.9 %norm_grad.3 = (f32[256,1024]{1,0:T(8,128)S(1)}, bf16[256,1024]{1,0:T(8,128)(2,1)S(1)}, f32[1,1024]{1,0:T(1,128)S(1)}, bf16[256,1024]{1,0:T(8,128)(2,1)S(1)}) custom-call(bf16[256,2816]{1,0:T(8,128)(2,1)S(1)} %get-tuple-element.421.refs_0_, bf16[256,2816]{1,0:T(8,128)(2,1)S(1)} %get-tuple-element.422.refs_1_, bf16[1024,2816]{1,0:T(8,128)(2,1)S(1)} %bitcast.61, ...), custom_call_target="tpu_custom_call" | custom-call | flops 1 | bytes 1 | tf_op jit(solution)/shard_map/norm_grad/pallas_call | solution.py:697
  107.3 3.9 %slabs.5 = (bf16[16,256,512]{2,1,0:T(8,128)(2,1)}, bf16[16,256,512]{2,1,0:T(8,128)(2,1)}) custom-call(s32[3,32]{1,0:T(4,128)} %get-tuple-element.451.order_ref, bf16[256,1024]{1,0:T(8,128)(2,1)} %copy-done.40, bf16[256,1024]{1,0:T(8,128)(2,1)} %copy-done.59), custom_call_target="tpu_custom_call" | custom-call | flops 1 | bytes 1 | tf_op jit(solution)/shard_map/slabs/pallas_call | solution.py:467
  111.2 5.5 %fusion.4 = bf16[256,1024]{1,0:T(8,128)(2,1)} fusion(f32[256,1024]{1,0:T(8,128)} %copy-done.44, bf16[256,2816]{1,0:T(8,128)(2,1)S(1)} %get-tuple-element.242.x_ref, bf16[2816,1024]{1,0:T(8,128)(2,1)} %param.41), kind=kOutput, calls=%fused_computation.20 | convolution fusion | flops 1476919296 | bytes 8781824 | tf_op jit(solution)/shard_map/dot_general | solution.py:29
  116.7 4.7 %collective-permute-done.9.refs_1_ = bf16[256,1408]{1,0:T(8,128)(2,1)} collective-permute-done((bf16[256,1408]{1,0:T(8,128)(2,1)}, bf16[256,1408]{1,0:T(8,128)(2,1)}, u32[]{:S(2)}, u32[]{:S(2)}) %collective-permute-start.9) | collective-permute-done | bytes 720928 | tf_op jit(solution)/shard_map/ppermute | solution.py:33
  125.0 8.0 %cross_backward.1 = (bf16[256,1024]{1,0:T(8,128)(2,1)S(1)}, bf16[2,512,512]{2,1,0:T(8,128)(2,1)S(1)}) custom-call(f32[512,1]{1,0:T(8,128)S(1)} %copy.46.allow_ref, bf16[256,1024]{1,0:T(8,128)(2,1)S(1)} %copy-done.38, bf16[512,512]{1,0:T(8,128)(2,1)S(1)} %copy-done.34, bf16[512,512]{1,0:T(8,128)(2,1)S(1)} %copy-done.36, ...), custom_call_target="tpu_custom_call" | custom-call | flops 1 | bytes 1 | tf_op jit(solution)/shard_map/cross_backward/pallas_call | solution.py:393
  134.8 3.6 %slabs.6 = (bf16[16,256,512]{2,1,0:T(8,128)(2,1)}, bf16[16,256,512]{2,1,0:T(8,128)(2,1)}) custom-call(s32[3,32]{1,0:T(4,128)} %get-tuple-element.451.order_ref, bf16[256,1024]{1,0:T(8,128)(2,1)} %copy-done.55, bf16[256,1024]{1,0:T(8,128)(2,1)} %copy-done.28, ...), custom_call_target="tpu_custom_call", output_to_operand_aliasing={{0}: (3, {}), {1}: (4, {})} | custom-call | flops 1 | bytes 1 | tf_op jit(solution)/shard_map/slabs/pallas_call | solution.py:467
  138.4 4.7 %slabs.7 = (bf16[16,256,512]{2,1,0:T(8,128)(2,1)}, bf16[16,256,512]{2,1,0:T(8,128)(2,1)}) custom-call(s32[3,32]{1,0:T(4,128)} %get-tuple-element.451.order_ref, bf16[512,1024]{1,0:T(8,128)(2,1)} %constant_dynamic-update-slice_fusion.refs_0_, bf16[2,512,512]{2,1,0:T(8,128)(2,1)} %copy-done.25, ...), custom_call_target="tpu_custom_call", output_to_operand_aliasing={{0}: (3, {}), {1}: (4, {})} | custom-call | flops 1 | bytes 1 | tf_op jit(solution)/shard_map/slabs/pallas_call | solution.py:467
  147.3 3.7 %slabs.8 = (bf16[16,256,512]{2,1,0:T(8,128)(2,1)}, bf16[16,256,512]{2,1,0:T(8,128)(2,1)}) custom-call(s32[3,32]{1,0:T(4,128)} %get-tuple-element.450.order_ref, bf16[256,256]{1,0:T(8,128)(2,1)} %copy-done.42, bf16[256,256]{1,0:T(8,128)(2,1)} %copy-done.52, bf16[256,256]{1,0:T(8,128)(2,1)} %copy-done.53, ...), custom_call_target="tpu_custom_call", output_to_operand_aliasing={{0}: (6, {}), {1}: (7, {})} | custom-call | flops 1 | bytes 1 | tf_op jit(solution)/shard_map/slabs/pallas_call | solution.py:467
  154.6 5.0 %pair_dot.1 = bf16[1024,1408]{1,0:T(8,128)(2,1)S(1)} custom-call(s32[1]{0:T(128)} %bitcast.6.my_ref, bf16[4,256,1024]{2,1,0:T(8,128)(2,1)S(1)} %bitcast.73, bf16[256,1408]{1,0:T(8,128)(2,1)S(1)} %copy-done.27, bf16[256,1408]{1,0:T(8,128)(2,1)} %collective-permute-done.9.refs_1_, bf16[256,1408]{1,0:T(8,128)(2,1)} %collective-permute-done.10.refs_2_, ...), custom_call_target="tpu_custom_call" | custom-call | flops 1 | bytes 1 | tf_op jit(solution)/shard_map/pair_dot/pallas_call | solution.py:590
  161.3 5.2 %totals.5 = (bf16[8,128,512]{2,1,0:T(8,128)(2,1)}, bf16[8,128,512]{2,1,0:T(8,128)(2,1)}) custom-call(bf16[16,256,512]{2,1,0:T(8,128)(2,1)} %get-tuple-element.294.refs_0_.refs_2_.refs_4_, bf16[16,256,512]{2,1,0:T(8,128)(2,1)} %collective-permute-done.15.refs_1_.refs_3_.refs_5_, bf16[16,256,512]{2,1,0:T(8,128)(2,1)} %get-tuple-element.294.refs_0_.refs_2_.refs_4_, ...), custom_call_target="tpu_custom_call" | custom-call | flops 1 | bytes 1 | tf_op jit(solution)/shard_map/totals/pallas_call | solution.py:536
  172.3 16.8 %self_backward.1 = (bf16[256,512]{1,0:T(8,128)(2,1)S(1)}, bf16[256,512]{1,0:T(8,128)(2,1)}, bf16[256,512]{1,0:T(8,128)(2,1)}, bf16[256,512]{1,0:T(8,128)(2,1)S(1)}, f32[4,1280]{1,0:T(4,128)S(1)}) custom-call(s32[1]{0:T(128)} %bitcast.6.my_ref, bf16[1024,512]{1,0:T(8,128)(2,1)S(1)} %copy-done.19, f32[4,1280]{1,0:T(4,128)S(1)} %copy-done.73, ...), custom_call_target="tpu_custom_call" | custom-call | flops 1 | bytes 1 | tf_op jit(solution)/shard_map/self_backward/pallas_call | solution.py:338
  195.0 4.2 %totals.6 = (bf16[4,128,512]{2,1,0:T(8,128)(2,1)}, bf16[4,128,512]{2,1,0:T(8,128)(2,1)}) custom-call(bf16[16,256,512]{2,1,0:T(8,128)(2,1)} %get-tuple-element.294.refs_0_.refs_2_.refs_4_, bf16[16,256,512]{2,1,0:T(8,128)(2,1)} %collective-permute-done.15.refs_1_.refs_3_.refs_5_, bf16[8,128,512]{2,1,0:T(8,128)(2,1)} %copy-done.95, ...), custom_call_target="tpu_custom_call" | custom-call | flops 1 | bytes 1 | tf_op jit(solution)/shard_map/totals/pallas_call | solution.py:536
  201.3 5.1 %collective-permute-done.19.refs_2_ = bf16[8,88,256]{2,1,0:T(8,128)(2,1)S(1)} collective-permute-done((bf16[8,88,256]{2,1,0:T(8,128)(2,1)S(1)}, bf16[8,88,256]{2,1,0:T(8,128)(2,1)S(1)}, u32[]{:S(2)}, u32[]{:S(2)}) %collective-permute-start.19) | collective-permute-done | bytes 360480 | tf_op jit(solution)/shard_map/ppermute | solution.py:33
  211.5 2.8 turned_dot.1
  214.3 4.7 %slabs.9 = (bf16[16,32,512]{2,1,0:T(8,128)(2,1)}, bf16[16,32,512]{2,1,0:T(8,128)(2,1)}, f32[1024,1]{1,0:T(8,128)}) custom-call(s32[3,32]{1,0:T(4,128)} %get-tuple-element.451.order_ref, bf16[1024,1024]{1,0:T(8,128)(2,1)} %copy-done.39, bf16[256,512]{1,0:T(8,128)(2,1)} %copy-done.50, bf16[256,512]{1,0:T(8,128)(2,1)} %get-tuple-element.367.refs_2_, ...), custom_call_target="tpu_custom_call" | custom-call | flops 1 | bytes 1 | tf_op jit(solution)/shard_map/slabs/pallas_call | solution.py:467
  223.0 3.2 %totals.7 = (bf16[4,32,512]{2,1,0:T(8,128)(2,1)}, bf16[4,32,512]{2,1,0:T(8,128)(2,1)}, bf16[4,32,512]{2,1,0:T(8,128)(2,1)}, bf16[4,32,512]{2,1,0:T(8,128)(2,1)}) custom-call(bf16[4,128,512]{2,1,0:T(8,128)(2,1)} %bitcast.86, bf16[4,128,512]{2,1,0:T(8,128)(2,1)} %bitcast.90, bf16[4,128,512]{2,1,0:T(8,128)(2,1)} %bitcast.87, bf16[4,128,512]{2,1,0:T(8,128)(2,1)} %bitcast.91, ...), custom_call_target="tpu_custom_call" | custom-call | flops 1 | bytes 1 | tf_op jit(solution)/shard_map/totals/pallas_call | solution.py:536
  231.0 3.1 collective-permute-done.21.refs_4_
  235.9 2.8 collective-permute-done.24.refs_7_
  241.2 2.8 totals.8
  249.0 8.7 %collective-permute-done.31 = bf16[2,2,128,512]{3,2,1,0:T(8,128)(2,1)} collective-permute-done((bf16[2,2,128,512]{3,2,1,0:T(8,128)(2,1)S(1)}, bf16[2,2,128,512]{3,2,1,0:T(8,128)(2,1)}, u32[]{:S(2)}, u32[]{:S(2)}) %collective-permute-start.31) | collective-permute-done | bytes 524320 | tf_op jit(solution)/shard_map/ppermute | solution.py:33
  289.6 2.7 norm_grad.5
  294.0 9.3 %collective-permute-done.39.refs_11_ = bf16[1,384,512]{2,1,0:T(8,128)(2,1)} collective-permute-done((bf16[1,384,512]{2,1,0:T(8,128)(2,1)}, bf16[1,384,512]{2,1,0:T(8,128)(2,1)}, u32[]{:S(2)}, u32[]{:S(2)}) %collective-permute-start.39) | collective-permute-done | bytes 393248 | tf_op jit(solution)/shard_map/ppermute | solution.py:33
  (387 shorter events, 131.6 us)
Async XLA Ops:
  7.2 72.7 %all-gather.3.cloned.1.call-start = ((), (), s32[]{:S(2)}) async-start(), calls=%async_computation.2 | async-start | bytes 2621440 | tf_op jit(solution)/shard_map/all_gather | solution.py:944
  7.3 22.6 %collective-permute-start = (bf16[256,1024]{1,0:T(8,128)(2,1)}, bf16[256,1024]{1,0:T(8,128)(2,1)}, u32[]{:S(2)}, u32[]{:S(2)}) collective-permute-start(bf16[256,1024]{1,0:T(8,128)(2,1)} %bitcast.62), channel_id=1, source_target_pairs={{0,1},{1,0},{2,3},{3,2},{4,5},{5,4},{6,7},{7,6},{8,9},{9,8},{10,11... | collective-permute-start | bytes 1572872 | tf_op jit(solution)/shard_map/ppermute | solution.py:33
  10.3 24.9 %collective-permute-start.1 = (bf16[256,1024]{1,0:T(8,128)(2,1)}, bf16[256,1024]{1,0:T(8,128)(2,1)}, u32[]{:S(2)}, u32[]{:S(2)}) collective-permute-start(bf16[256,1024]{1,0:T(8,128)(2,1)} %bitcast.63), channel_id=1, source_target_pairs={{0,2},{1,3},{2,0},{3,1},{4,6},{5,7},{6,4},{7,5},{8,10},{9,11},{10,... | collective-permute-start | bytes 1572872 | tf_op jit(solution)/shard_map/ppermute | solution.py:33
  11.8 23.4 %collective-permute-start.2 = (bf16[256,1024]{1,0:T(8,128)(2,1)}, bf16[256,1024]{1,0:T(8,128)(2,1)}, u32[]{:S(2)}, u32[]{:S(2)}) collective-permute-start(bf16[256,1024]{1,0:T(8,128)(2,1)} %bitcast.64), channel_id=1, source_target_pairs={{0,3},{1,2},{2,1},{3,0},{4,7},{5,6},{6,5},{7,4},{8,11},{9,10},{10,... | collective-permute-start | bytes 1572872 | tf_op jit(solution)/shard_map/ppermute | solution.py:33
  35.2 88.4 %all-gather.5.cloned.1.call-start = ((), (), s32[]{:S(2)}) async-start(), calls=%async_computation.3 | async-start | bytes 2621440 | tf_op jit(solution)/shard_map/all_gather | solution.py:981
  35.5 23.3 %collective-permute-start.6 = (bf16[128,1024]{1,0:T(8,128)(2,1)}, bf16[128,1024]{1,0:T(8,128)(2,1)S(1)}, u32[]{:S(2)}, u32[]{:S(2)}) collective-permute-start(bf16[128,1024]{1,0:T(8,128)(2,1)} %bitcast.1), channel_id=1, source_target_pairs={{0,1},{1,0},{2,3},{3,2},{4,5},{5,4},{6,7},{7,6},{8,9},{9,8},{10,11... | collective-permute-start | bytes 786440 | tf_op jit(solution)/shard_map/ppermute | solution.py:33
  36.8 24.1 %collective-permute-start.7 = (bf16[128,1024]{1,0:T(8,128)(2,1)}, bf16[128,1024]{1,0:T(8,128)(2,1)S(1)}, u32[]{:S(2)}, u32[]{:S(2)}) collective-permute-start(bf16[128,1024]{1,0:T(8,128)(2,1)} %bitcast.1), channel_id=1, source_target_pairs={{0,2},{1,3},{2,0},{3,1},{4,6},{5,7},{6,4},{7,5},{8,10},{9,11},{10,... | collective-permute-start | bytes 786440 | tf_op jit(solution)/shard_map/ppermute | solution.py:33
  37.6 24.1 %collective-permute-start.8 = (bf16[128,1024]{1,0:T(8,128)(2,1)}, bf16[128,1024]{1,0:T(8,128)(2,1)}, u32[]{:S(2)}, u32[]{:S(2)}) collective-permute-start(bf16[128,1024]{1,0:T(8,128)(2,1)} %bitcast.1), channel_id=1, source_target_pairs={{0,3},{1,2},{2,1},{3,0},{4,7},{5,6},{6,5},{7,4},{8,11},{9,10},{10,... | collective-permute-start | bytes 786440 | tf_op jit(solution)/shard_map/ppermute | solution.py:33
  56.6 11.0 %collective-permute-start.3 = (bf16[256,256]{1,0:T(8,128)(2,1)S(1)}, bf16[256,256]{1,0:T(8,128)(2,1)S(1)}, u32[]{:S(2)}, u32[]{:S(2)}) collective-permute-start(bf16[256,256]{1,0:T(8,128)(2,1)S(1)} %get-tuple-element.220.refs_1_), channel_id=1, source_target_pairs={{0,1},{1,0},{2,3},{3,2},{4,5},{5,4},{6,7},{7,6},{8,9},{9,8},{10,11... | collective-permute-start | bytes 393224 | tf_op jit(solution)/shard_map/ppermute | solution.py:33
  79.9 128.6 %reduce-scatter.3.cloned.1.call-start = ((), (), s32[]{:S(2)}) async-start(), calls=%async_computation.4 | async-start | bytes 3244032 | tf_op jit(solution)/shard_map/reduce_scatter | solution.py:1022
  95.4 26.1 %collective-permute-start.9 = (bf16[256,1408]{1,0:T(8,128)(2,1)}, bf16[256,1408]{1,0:T(8,128)(2,1)}, u32[]{:S(2)}, u32[]{:S(2)}) collective-permute-start(bf16[256,1408]{1,0:T(8,128)(2,1)} %get-tuple-element.239), channel_id=1, source_target_pairs={{0,1},{1,0},{2,3},{3,2},{4,5},{5,4},{6,7},{7,6},{8,9},{9,8},{10,11... | collective-permute-start | bytes 2162696 | tf_op jit(solution)/shard_map/ppermute | solution.py:33
  96.5 26.5 %collective-permute-start.10 = (bf16[256,1408]{1,0:T(8,128)(2,1)}, bf16[256,1408]{1,0:T(8,128)(2,1)}, u32[]{:S(2)}, u32[]{:S(2)}) collective-permute-start(bf16[256,1408]{1,0:T(8,128)(2,1)} %get-tuple-element.240), channel_id=1, source_target_pairs={{0,2},{1,3},{2,0},{3,1},{4,6},{5,7},{6,4},{7,5},{8,10},{9,11},{10,... | collective-permute-start | bytes 2162696 | tf_op jit(solution)/shard_map/ppermute | solution.py:33
  123.7 19.5 %collective-permute-start.11 = (bf16[256,1408]{1,0:T(8,128)(2,1)}, bf16[256,1408]{1,0:T(8,128)(2,1)}, u32[]{:S(2)}, u32[]{:S(2)}) collective-permute-start(bf16[256,1408]{1,0:T(8,128)(2,1)} %get-tuple-element.259), channel_id=1, source_target_pairs={{0,3},{1,2},{2,1},{3,0},{4,7},{5,6},{6,5},{7,4},{8,11},{9,10},{10,... | collective-permute-start | bytes 2162696 | tf_op jit(solution)/shard_map/ppermute | solution.py:33
  151.0 10.1 %collective-permute-start.15 = (bf16[16,256,512]{2,1,0:T(8,128)(2,1)}, bf16[16,256,512]{2,1,0:T(8,128)(2,1)}, u32[]{:S(2)}, u32[]{:S(2)}) collective-permute-start(bf16[16,256,512]{2,1,0:T(8,128)(2,1)} %get-tuple-element.290), channel_id=1, source_target_pairs={{0,4},{4,0},{8,12},{12,8},{16,20},{20,16},{24,28},{28,24},{1,5},{5... | collective-permute-start | bytes 12582920 | tf_op jit(solution)/shard_map/ppermute | solution.py:33
  161.2 131.1 %reduce-scatter.5.cloned.1.call-start = ((), (), s32[]{:S(2)}) async-start(), calls=%async_computation.5 | async-start | bytes 1622016 | tf_op jit(solution)/shard_map/reduce_scatter | solution.py:1038
  166.6 26.3 %collective-permute-start.16 = (bf16[8,128,512]{2,1,0:T(8,128)(2,1)}, bf16[8,128,512]{2,1,0:T(8,128)(2,1)S(1)}, u32[]{:S(2)}, u32[]{:S(2)}) collective-permute-start(bf16[8,128,512]{2,1,0:T(8,128)(2,1)} %get-tuple-element.306), channel_id=1, source_target_pairs={{0,1},{1,0},{2,3},{3,2},{4,5},{5,4},{6,7},{7,6},{8,9},{9,8},{10,11... | collective-permute-start | bytes 3145736 | tf_op jit(solution)/shard_map/ppermute | solution.py:33
  167.7 26.3 %collective-permute-start.17 = (bf16[8,128,512]{2,1,0:T(8,128)(2,1)}, bf16[8,128,512]{2,1,0:T(8,128)(2,1)S(1)}, u32[]{:S(2)}, u32[]{:S(2)}) collective-permute-start(bf16[8,128,512]{2,1,0:T(8,128)(2,1)} %get-tuple-element.307), channel_id=1, source_target_pairs={{0,2},{1,3},{2,0},{3,1},{4,6},{5,7},{6,4},{7,5},{8,10},{9,11},{10,... | collective-permute-start | bytes 3145736 | tf_op jit(solution)/shard_map/ppermute | solution.py:33
  168.8 31.8 %collective-permute-start.18 = (bf16[8,88,256]{2,1,0:T(8,128)(2,1)S(1)}, bf16[8,88,256]{2,1,0:T(8,128)(2,1)S(1)}, u32[]{:S(2)}, u32[]{:S(2)}) collective-permute-start(bf16[8,88,256]{2,1,0:T(8,128)(2,1)S(1)} %copy-done.90), channel_id=1, source_target_pairs={{0,1},{1,0},{2,3},{3,2},{4,5},{5,4},{6,7},{7,6},{8,9},{9,8},{10,11... | collective-permute-start | bytes 1081352 | tf_op jit(solution)/shard_map/ppermute | solution.py:33
  170.1 36.3 %collective-permute-start.19 = (bf16[8,88,256]{2,1,0:T(8,128)(2,1)S(1)}, bf16[8,88,256]{2,1,0:T(8,128)(2,1)S(1)}, u32[]{:S(2)}, u32[]{:S(2)}) collective-permute-start(bf16[8,88,256]{2,1,0:T(8,128)(2,1)S(1)} %copy-done.88), channel_id=1, source_target_pairs={{0,2},{1,3},{2,0},{3,1},{4,6},{5,7},{6,4},{7,5},{8,10},{9,11},{10,... | collective-permute-start | bytes 1081352 | tf_op jit(solution)/shard_map/ppermute | solution.py:33
  170.6 37.2 %collective-permute-start.20 = (bf16[8,88,256]{2,1,0:T(8,128)(2,1)S(1)}, bf16[8,88,256]{2,1,0:T(8,128)(2,1)S(1)}, u32[]{:S(2)}, u32[]{:S(2)}) collective-permute-start(bf16[8,88,256]{2,1,0:T(8,128)(2,1)S(1)} %copy-done.86), channel_id=1, source_target_pairs={{0,3},{1,2},{2,1},{3,0},{4,7},{5,6},{6,5},{7,4},{8,11},{9,10},{10,... | collective-permute-start | bytes 1081352 | tf_op jit(solution)/shard_map/ppermute | solution.py:33
  219.1 15.0 %collective-permute-start.21 = (bf16[4,128,512]{2,1,0:T(8,128)(2,1)}, bf16[4,128,512]{2,1,0:T(8,128)(2,1)S(1)}, u32[]{:S(2)}, u32[]{:S(2)}) collective-permute-start(bf16[4,128,512]{2,1,0:T(8,128)(2,1)} %get-tuple-element.334), channel_id=1, source_target_pairs={{0,2},{1,3},{2,0},{3,1},{4,6},{5,7},{6,4},{7,5},{8,10},{9,11},{10,... | collective-permute-start | bytes 1572872 | tf_op jit(solution)/shard_map/ppermute | solution.py:33
  220.9 15.0 %collective-permute-start.22 = (bf16[4,128,512]{2,1,0:T(8,128)(2,1)}, bf16[4,128,512]{2,1,0:T(8,128)(2,1)S(1)}, u32[]{:S(2)}, u32[]{:S(2)}) collective-permute-start(bf16[4,128,512]{2,1,0:T(8,128)(2,1)} %get-tuple-element.335), channel_id=1, source_target_pairs={{0,1},{1,0},{2,3},{3,2},{4,5},{5,4},{6,7},{7,6},{8,9},{9,8},{10,11... | collective-permute-start | bytes 1572872 | tf_op jit(solution)/shard_map/ppermute | solution.py:33
  226.2 12.5 %collective-permute-start.24 = (bf16[4,32,512]{2,1,0:T(8,128)(2,1)}, bf16[4,32,512]{2,1,0:T(8,128)(2,1)S(1)}, u32[]{:S(2)}, u32[]{:S(2)}) collective-permute-start(bf16[4,32,512]{2,1,0:T(8,128)(2,1)} %get-tuple-element.339), channel_id=1, source_target_pairs={{0,1},{1,0},{2,3},{3,2},{4,5},{5,4},{6,7},{7,6},{8,9},{9,8},{10,11... | collective-permute-start | bytes 393224 | tf_op jit(solution)/shard_map/ppermute | solution.py:33
  226.9 11.7 %collective-permute-start.25 = (bf16[4,32,512]{2,1,0:T(8,128)(2,1)}, bf16[4,32,512]{2,1,0:T(8,128)(2,1)S(1)}, u32[]{:S(2)}, u32[]{:S(2)}) collective-permute-start(bf16[4,32,512]{2,1,0:T(8,128)(2,1)} %get-tuple-element.340), channel_id=1, source_target_pairs={{0,2},{1,3},{2,0},{3,1},{4,6},{5,7},{6,4},{7,5},{8,10},{9,11},{10,... | collective-permute-start | bytes 393224 | tf_op jit(solution)/shard_map/ppermute | solution.py:33
  228.2 12.3 %collective-permute-start.26 = (bf16[4,32,512]{2,1,0:T(8,128)(2,1)}, bf16[4,32,512]{2,1,0:T(8,128)(2,1)S(1)}, u32[]{:S(2)}, u32[]{:S(2)}) collective-permute-start(bf16[4,32,512]{2,1,0:T(8,128)(2,1)} %get-tuple-element.341), channel_id=1, source_target_pairs={{0,3},{1,2},{2,1},{3,0},{4,7},{5,6},{6,5},{7,4},{8,11},{9,10},{10,... | collective-permute-start | bytes 393224 | tf_op jit(solution)/shard_map/ppermute | solution.py:33
  244.1 13.6 %collective-permute-start.31 = (bf16[2,2,128,512]{3,2,1,0:T(8,128)(2,1)S(1)}, bf16[2,2,128,512]{3,2,1,0:T(8,128)(2,1)}, u32[]{:S(2)}, u32[]{:S(2)}) collective-permute-start(bf16[2,2,128,512]{3,2,1,0:T(8,128)(2,1)S(1)} %slice.55), channel_id=1, source_target_pairs={{0,2},{1,3},{2,0},{3,1},{4,6},{5,7},{6,4},{7,5},{8,10},{9,11},{10,... | collective-permute-start | bytes 1572872 | tf_op jit(solution)/shard_map/ppermute | solution.py:33
  246.0 25.3 %collective-permute-start.27 = (bf16[2,384,512]{2,1,0:T(8,128)(2,1)}, bf16[2,384,512]{2,1,0:T(8,128)(2,1)S(1)}, u32[]{:S(2)}, u32[]{:S(2)}) collective-permute-start(bf16[2,384,512]{2,1,0:T(8,128)(2,1)} %totals.8), channel_id=1, source_target_pairs={{0,8},{4,12},{8,0},{12,4},{16,24},{20,28},{24,16},{28,20},{1,9},{5... | collective-permute-start | bytes 2359304 | tf_op jit(solution)/shard_map/ppermute | solution.py:33
  247.7 12.8 %collective-permute-start.29 = (f32[28,128]{1,0:T(8,128)S(1)}, f32[28,128]{1,0:T(8,128)S(1)}, u32[]{:S(2)}, u32[]{:S(2)}) collective-permute-start(f32[28,128]{1,0:T(8,128)S(1)} %fusion.30), channel_id=1, source_target_pairs={{0,1},{1,0},{2,3},{3,2},{4,5},{5,4},{6,7},{7,6},{8,9},{9,8},{10,11... | collective-permute-start | bytes 43016 | tf_op jit(solution)/shard_map/ppermute | solution.py:33
  274.7 14.8 %collective-permute-start.36 = (bf16[256,512]{1,0:T(8,128)(2,1)}, bf16[256,512]{1,0:T(8,128)(2,1)S(1)}, u32[]{:S(2)}, u32[]{:S(2)}) collective-permute-start(bf16[256,512]{1,0:T(8,128)(2,1)} %get-tuple-element.367.refs_2_), channel_id=1, source_target_pairs={{0,1},{1,0},{2,3},{3,2},{4,5},{5,4},{6,7},{7,6},{8,9},{9,8},{10,11... | collective-permute-start | bytes 786440 | tf_op jit(solution)/shard_map/ppermute | solution.py:33
  276.1 13.5 %collective-permute-start.37 = (bf16[256,512]{1,0:T(8,128)(2,1)}, bf16[256,512]{1,0:T(8,128)(2,1)S(1)}, u32[]{:S(2)}, u32[]{:S(2)}) collective-permute-start(bf16[256,512]{1,0:T(8,128)(2,1)} %get-tuple-element.368.refs_3_), channel_id=1, source_target_pairs={{0,2},{1,3},{2,0},{3,1},{4,6},{5,7},{6,4},{7,5},{8,10},{9,11},{10,... | collective-permute-start | bytes 786440 | tf_op jit(solution)/shard_map/ppermute | solution.py:33
  277.3 12.3 %collective-permute-start.38 = (bf16[256,512]{1,0:T(8,128)(2,1)S(1)}, bf16[256,512]{1,0:T(8,128)(2,1)S(1)}, u32[]{:S(2)}, u32[]{:S(2)}) collective-permute-start(bf16[256,512]{1,0:T(8,128)(2,1)S(1)} %copy-done.71), channel_id=1, source_target_pairs={{0,3},{1,2},{2,1},{3,0},{4,7},{5,6},{6,5},{7,4},{8,11},{9,10},{10,... | collective-permute-start | bytes 786440 | tf_op jit(solution)/shard_map/ppermute | solution.py:33
  287.0 16.4 %collective-permute-start.39 = (bf16[1,384,512]{2,1,0:T(8,128)(2,1)}, bf16[1,384,512]{2,1,0:T(8,128)(2,1)}, u32[]{:S(2)}, u32[]{:S(2)}) collective-permute-start(bf16[1,384,512]{2,1,0:T(8,128)(2,1)} %totals.9), channel_id=1, source_target_pairs={{0,16},{4,20},{8,24},{12,28},{16,0},{20,4},{24,8},{28,12},{1,17},{... | collective-permute-start | bytes 1179656 | tf_op jit(solution)/shard_map/ppermute | solution.py:33
  (136 other events, 970.9 us)
Sparse Core Ops, SparseCore 0:
  35.3 40.4 all-gather.2
  80.0 43.6 all-gather.4
  161.3 39.1 reduce-scatter.2
  219.2 35.5 reduce-scatter.4
